TPU v7x, 32 devices: a whole 2x2x4 slice. The times are simulated.
32 devices in a mesh: dp: 2 (over z_hi), expert: 8 (over y, x, core), tensor: 2 (over z_lo).
Axes of the slice: x: 2, y: 2, z: 4 (z_hi: 2, z_lo: 2; z = z_hi * 2 + z_lo), core: 2. Of those that a mesh axis runs over, the one named last changes fastest.
Arguments:
- tokens: bfloat16 [15760, 768], P(('dp', 'expert')), may hold values from -6 to 6
- cotangent: bfloat16 [15760, 768], P(('dp', 'expert')), may hold values from -6 to 6
- ln1_gain: float32 [768], P(('dp', 'expert')), may hold values from 0.5 to 1.5
- ln1_bias: float32 [768], P(('dp', 'expert')), may hold values from -0.625 to 0.625
- ln2_gain: float32 [768], P(('dp', 'expert')), may hold values from 0.5 to 1.5
- ln2_bias: float32 [768], P(('dp', 'expert')), may hold values from -0.625 to 0.625
- w_query: float32 [768, 768], P(('dp', 'expert'), 'tensor'), may hold values from -0.3125 to 0.3125
- w_key: float32 [768, 768], P(('dp', 'expert'), 'tensor'), may hold values from -0.3125 to 0.3125
- w_value: float32 [768, 768], P(('dp', 'expert'), 'tensor'), may hold values from -0.21875 to 0.21875
- w_out: float32 [768, 768], P('tensor', ('dp', 'expert')), may hold values from -1.5 to 1.5
- w_router: float32 [768, 8], P(('dp', 'expert')), may hold values from -0.15625 to 0.15625
- w_in: float32 [8, 768, 3072], P('expert', 'dp', 'tensor'), may hold values from -0.21875 to 0.21875
- w_back: float32 [8, 3072, 768], P('expert', 'tensor', 'dp'), may hold values from -0.875 to 0.875
- expert_ids: int32 [15760, 2], P(('dp', 'expert')), may hold values from 0 to 7, all different within a row; in each aligned block of 985 rows (0 to 984, 985 to 1969, ...) at most 312 rows name the same one
Outputs:
- block_out: bfloat16 [15760, 768], P(('dp', 'expert'))
- grad_tokens: float32 [15760, 768], P(('dp', 'expert'))
- grad_ln1_gain: float32 [768], P(('dp', 'expert'))
- grad_ln1_bias: float32 [768], P(('dp', 'expert'))
- grad_ln2_gain: float32 [768], P(('dp', 'expert'))
- grad_ln2_bias: float32 [768], P(('dp', 'expert'))
- grad_query: float32 [768, 768], P(('dp', 'expert'), 'tensor')
- grad_key: float32 [768, 768], P(('dp', 'expert'), 'tensor')
- grad_value: float32 [768, 768], P(('dp', 'expert'), 'tensor')
- grad_out: float32 [768, 768], P('tensor', ('dp', 'expert'))
- grad_router: float32 [768, 8], P(('dp', 'expert'))
- grad_in: float32 [8, 768, 3072], P('expert', 'dp', 'tensor')
- grad_back: float32 [8, 3072, 768], P('expert', 'tensor', 'dp')
Inputs may be any that keep to these rules, and one draw needn't show every extreme that they name: `expert_ids`: each row names two different experts; in each aligned block of 985 rows (the tokens of one group) no expert is named more than 312 times, and in every draw some expert is named exactly 312 times in some block.
All inputs are finite; a program needn't handle non-finite values.
Results may differ from a plain program's by a relative error of at most 0.014.
The roundings to bfloat16 on the way count: a program that leaves them out, or rounds other values in their place, can miss the bound.
Values may be sent and summed in bfloat16 or wider, within the bound.
No kernel may reach another device: no remote copies, remote signals or barrier semaphores. Data moves between devices by JAX's collectives and lax.ppermute only.
A program may use at most 192 MiB of HBM per device.

v0:
```python
import jax
import jax.numpy as jnp
from jax import lax
from jax.sharding import PartitionSpec as P

D = 768
HEADS = 12
SEQ = 197


EPSILON = 1e-06
HIGH = lax.Precision.HIGHEST


def norm_rows(values, gain, bias):
    average = jnp.mean(values, axis=-1, keepdims=True)
    centred = values - average
    variance = jnp.mean(centred * centred, axis=-1, keepdims=True)
    return centred * lax.rsqrt(variance + EPSILON) * gain + bias


def gelu_exact(values):
    return jax.nn.gelu(values, approximate=False)


def slot_table(routes, expert_count):
    total = routes.shape[0]
    sequence = jnp.transpose(routes).reshape(-1)
    onehot = (sequence[:, None] == jnp.arange(expert_count, dtype=jnp.int32)[None, :]).astype(
        jnp.int32
    )
    before = jnp.cumsum(onehot, axis=0) - onehot
    placed = jnp.sum(before * onehot, axis=1).reshape(2, total)
    return jnp.transpose(placed)


def on_device(
    tokens,
    cotangent,
    ln1_gain,
    ln1_bias,
    ln2_gain,
    ln2_bias,
    w_query,
    w_key,
    w_value,
    w_out,
    w_router,
    w_in,
    w_back,
    expert_ids,
):
    expert_count = lax.axis_size("expert")
    tok_count = tokens.shape[0]
    feat_width = tokens.shape[1]
    capacity = (10 * tok_count + 32 * expert_count - 1) // (32 * expert_count) * 8
    head_size = D // HEADS
    score_scale = head_size ** (-0.5)
    images = tok_count // SEQ
    gain_one, bias_one, gain_two, bias_two, query_w, key_w, value_w, out_w, router_w = (
        lax.all_gather(ln1_gain.astype(jnp.bfloat16), ("dp", "expert"), axis=0, tiled=True),
        lax.all_gather(ln1_bias.astype(jnp.bfloat16), ("dp", "expert"), axis=0, tiled=True),
        lax.all_gather(ln2_gain.astype(jnp.bfloat16), ("dp", "expert"), axis=0, tiled=True),
        lax.all_gather(ln2_bias.astype(jnp.bfloat16), ("dp", "expert"), axis=0, tiled=True),
        lax.all_gather(w_query.astype(jnp.bfloat16), ("dp", "expert"), axis=0, tiled=True),
        lax.all_gather(w_key.astype(jnp.bfloat16), ("dp", "expert"), axis=0, tiled=True),
        lax.all_gather(w_value.astype(jnp.bfloat16), ("dp", "expert"), axis=0, tiled=True),
        lax.all_gather(w_out.astype(jnp.bfloat16), ("dp", "expert"), axis=1, tiled=True),
        lax.all_gather(w_router.astype(jnp.bfloat16), ("dp", "expert"), axis=0, tiled=True),
    )
    first_all, second_all = (
        lax.all_gather(w_in.astype(jnp.bfloat16), "dp", axis=1, tiled=True),
        lax.all_gather(w_back.astype(jnp.bfloat16), "dp", axis=2, tiled=True),
    )
    first_w = first_all[0]
    second_w = second_all[0]
    heads_here = query_w.shape[1] // head_size
    gain_a = gain_one.astype(jnp.float32)
    bias_a = bias_one.astype(jnp.float32)
    gain_b = gain_two.astype(jnp.float32)
    bias_b = bias_two.astype(jnp.float32)
    inputs = tokens.astype(jnp.float32)
    a_rows = norm_rows(inputs, gain_a, bias_a).astype(jnp.bfloat16)
    query = jnp.dot(a_rows, query_w, preferred_element_type=jnp.float32).astype(jnp.bfloat16)
    keys = jnp.dot(a_rows, key_w, preferred_element_type=jnp.float32).astype(jnp.bfloat16)
    values = jnp.dot(a_rows, value_w, preferred_element_type=jnp.float32).astype(jnp.bfloat16)
    query_heads = query.reshape(images, SEQ, heads_here, head_size)
    key_heads = keys.reshape(images, SEQ, heads_here, head_size)
    value_heads = values.reshape(images, SEQ, heads_here, head_size)
    scores = (
        jnp.einsum("bqhd,bkhd->bhqk", query_heads, key_heads, preferred_element_type=jnp.float32)
        * score_scale
    )
    log_total = jax.nn.logsumexp(scores, axis=-1, keepdims=True)
    weights = jnp.exp(scores - log_total)
    attended = (
        jnp.einsum(
            "bhqk,bkhd->bqhd",
            weights.astype(jnp.bfloat16),
            value_heads,
            preferred_element_type=jnp.float32,
        )
        .astype(jnp.bfloat16)
        .reshape(tok_count, -1)
    )
    head_part = jnp.dot(attended, out_w, preferred_element_type=jnp.float32)
    middle = inputs + lax.psum(head_part, "tensor")
    h_rows = norm_rows(middle, gain_b, bias_b).astype(jnp.bfloat16)
    router_probs = jax.nn.softmax(
        jnp.dot(h_rows, router_w, preferred_element_type=jnp.float32), axis=-1
    )
    gate_values = jnp.take_along_axis(router_probs, expert_ids, axis=1)
    slots = slot_table(expert_ids, expert_count)
    slot_index = (expert_ids * capacity + slots).reshape(-1)
    outgoing = (
        jnp.zeros((expert_count * capacity, feat_width), jnp.bfloat16)
        .at[slot_index]
        .set(jnp.repeat(h_rows, 2, axis=0))
        .reshape(expert_count, capacity, feat_width)
    )
    arrived = lax.all_to_all(outgoing, "expert", split_axis=0, concat_axis=0, tiled=True).reshape(
        -1, feat_width
    )
    pre_act = jnp.dot(arrived, first_w, preferred_element_type=jnp.float32)
    hidden = gelu_exact(pre_act).astype(jnp.bfloat16)
    expert_part = jnp.dot(hidden, second_w, preferred_element_type=jnp.float32)
    returned = lax.psum(expert_part, "tensor").astype(jnp.bfloat16)
    came_back = lax.all_to_all(
        returned.reshape(expert_count, capacity, -1),
        "expert",
        split_axis=0,
        concat_axis=0,
        tiled=True,
    )
    picked = (
        jnp.take(came_back.reshape(-1, feat_width), slot_index, axis=0)
        .reshape(tok_count, 2, feat_width)
        .astype(jnp.float32)
    )
    block_out = (middle + jnp.sum(gate_values[:, :, None] * picked, axis=1)).astype(jnp.bfloat16)
    grad_result = cotangent.astype(jnp.float32)
    grad_gates = jnp.sum(picked * grad_result[:, None, :], axis=2)
    grad_slots = (
        (gate_values[:, :, None] * grad_result[:, None, :])
        .astype(jnp.bfloat16)
        .reshape(-1, feat_width)
    )
    grad_outgoing = (
        jnp.zeros((expert_count * capacity, feat_width), jnp.bfloat16)
        .at[slot_index]
        .set(grad_slots)
        .reshape(expert_count, capacity, feat_width)
    )
    grad_arrived = lax.all_to_all(
        grad_outgoing, "expert", split_axis=0, concat_axis=0, tiled=True
    ).reshape(-1, feat_width)
    grad_second = jnp.einsum("rf,rd->fd", hidden, grad_arrived, preferred_element_type=jnp.float32)
    grad_hidden = jnp.einsum(
        "rd,fd->rf", grad_arrived, second_w, preferred_element_type=jnp.float32
    )
    gelu_value, gelu_pull = jax.vjp(gelu_exact, pre_act)
    grad_pre = gelu_pull(grad_hidden)[0].astype(jnp.bfloat16)
    grad_first = jnp.einsum("rd,rf->df", arrived, grad_pre, preferred_element_type=jnp.float32)
    input_part = jnp.einsum("rf,df->rd", grad_pre, first_w, preferred_element_type=jnp.float32)
    grad_rows = lax.psum(input_part, "tensor").astype(jnp.bfloat16)
    grad_home = lax.all_to_all(
        grad_rows.reshape(expert_count, capacity, -1),
        "expert",
        split_axis=0,
        concat_axis=0,
        tiled=True,
    )
    grad_taken = (
        jnp.take(grad_home.reshape(-1, feat_width), slot_index, axis=0)
        .reshape(tok_count, 2, feat_width)
        .astype(jnp.float32)
    )
    grad_h = jnp.sum(grad_taken, axis=1)
    onehot = (
        expert_ids[:, :, None] == jnp.arange(expert_count, dtype=jnp.int32)[None, None, :]
    ).astype(jnp.float32)
    grad_probs = jnp.sum(onehot * grad_gates[:, :, None], axis=1)
    grad_logits = router_probs * (
        grad_probs - jnp.sum(router_probs * grad_probs, axis=-1, keepdims=True)
    )
    h_float = h_rows.astype(jnp.float32)
    grad_router = jnp.dot(jnp.transpose(h_float), grad_logits, precision=HIGH)
    grad_h = grad_h + jnp.dot(
        grad_logits, jnp.transpose(router_w.astype(jnp.float32)), precision=HIGH
    )
    norm_two_value, norm_two_pull = jax.vjp(norm_rows, middle, gain_b, bias_b)
    grad_mid_norm, grad_gain_two, grad_bias_two = norm_two_pull(grad_h)
    grad_middle = grad_result + grad_mid_norm
    grad_branch = grad_middle.astype(jnp.bfloat16)
    grad_outw = jnp.einsum("tc,td->cd", attended, grad_branch, preferred_element_type=jnp.float32)
    grad_att = jnp.einsum(
        "td,cd->tc", grad_branch, out_w, preferred_element_type=jnp.float32
    ).astype(jnp.bfloat16)
    grad_att_heads = grad_att.reshape(images, SEQ, heads_here, head_size)
    again = (
        jnp.einsum("bqhd,bkhd->bhqk", query_heads, key_heads, preferred_element_type=jnp.float32)
        * score_scale
    )
    weights_again = jnp.exp(again - log_total)
    grad_value_heads = jnp.einsum(
        "bhqk,bqhd->bkhd",
        weights_again.astype(jnp.bfloat16),
        grad_att_heads,
        preferred_element_type=jnp.float32,
    ).astype(jnp.bfloat16)
    grad_weights = jnp.einsum(
        "bqhd,bkhd->bhqk", grad_att_heads, value_heads, preferred_element_type=jnp.float32
    )
    grad_scores = (
        weights_again
        * (grad_weights - jnp.sum(weights_again * grad_weights, axis=-1, keepdims=True))
    ).astype(jnp.bfloat16)
    grad_query_heads = (
        jnp.einsum("bhqk,bkhd->bqhd", grad_scores, key_heads, preferred_element_type=jnp.float32)
        * score_scale
    ).astype(jnp.bfloat16)
    grad_key_heads = (
        jnp.einsum("bhqk,bqhd->bkhd", grad_scores, query_heads, preferred_element_type=jnp.float32)
        * score_scale
    ).astype(jnp.bfloat16)
    grad_q_rows = grad_query_heads.reshape(tok_count, -1)
    grad_k_rows = grad_key_heads.reshape(tok_count, -1)
    grad_v_rows = grad_value_heads.reshape(tok_count, -1)
    grad_wq = jnp.einsum("td,tc->dc", a_rows, grad_q_rows, preferred_element_type=jnp.float32)
    grad_wk = jnp.einsum("td,tc->dc", a_rows, grad_k_rows, preferred_element_type=jnp.float32)
    grad_wv = jnp.einsum("td,tc->dc", a_rows, grad_v_rows, preferred_element_type=jnp.float32)
    norm_part = (
        jnp.einsum("tc,dc->td", grad_q_rows, query_w, preferred_element_type=jnp.float32)
        + jnp.einsum("tc,dc->td", grad_k_rows, key_w, preferred_element_type=jnp.float32)
        + jnp.einsum("tc,dc->td", grad_v_rows, value_w, preferred_element_type=jnp.float32)
    )
    grad_normed = lax.psum(norm_part, "tensor")
    norm_one_value, norm_one_pull = jax.vjp(norm_rows, inputs, gain_a, bias_a)
    grad_in_norm, grad_gain_one, grad_bias_one = norm_one_pull(grad_normed)
    grad_tokens = grad_middle + grad_in_norm
    layer_parts = (
        lax.psum_scatter(grad_gain_one, ("dp", "expert"), scatter_dimension=0, tiled=True),
        lax.psum_scatter(grad_bias_one, ("dp", "expert"), scatter_dimension=0, tiled=True),
        lax.psum_scatter(grad_gain_two, ("dp", "expert"), scatter_dimension=0, tiled=True),
        lax.psum_scatter(grad_bias_two, ("dp", "expert"), scatter_dimension=0, tiled=True),
        lax.psum_scatter(grad_wq, ("dp", "expert"), scatter_dimension=0, tiled=True),
        lax.psum_scatter(grad_wk, ("dp", "expert"), scatter_dimension=0, tiled=True),
        lax.psum_scatter(grad_wv, ("dp", "expert"), scatter_dimension=0, tiled=True),
        lax.psum_scatter(grad_outw, ("dp", "expert"), scatter_dimension=1, tiled=True),
        lax.psum_scatter(grad_router, ("dp", "expert"), scatter_dimension=0, tiled=True),
    )
    expert_parts = (
        lax.psum_scatter(grad_first[None], "dp", scatter_dimension=1, tiled=True),
        lax.psum_scatter(grad_second[None], "dp", scatter_dimension=2, tiled=True),
    )
    return (
        block_out,
        grad_tokens,
        layer_parts[0],
        layer_parts[1],
        layer_parts[2],
        layer_parts[3],
        layer_parts[4],
        layer_parts[5],
        layer_parts[6],
        layer_parts[7],
        layer_parts[8],
        expert_parts[0],
        expert_parts[1],
    )


def solution(mesh):
    in_specs = (
        P(("dp", "expert"), None),
        P(("dp", "expert"), None),
        P(("dp", "expert")),
        P(("dp", "expert")),
        P(("dp", "expert")),
        P(("dp", "expert")),
        P(("dp", "expert"), "tensor"),
        P(("dp", "expert"), "tensor"),
        P(("dp", "expert"), "tensor"),
        P("tensor", ("dp", "expert")),
        P(("dp", "expert"), None),
        P("expert", "dp", "tensor"),
        P("expert", "tensor", "dp"),
        P(("dp", "expert"), None),
    )
    out_specs = (
        P(("dp", "expert"), None),
        P(("dp", "expert"), None),
        P(("dp", "expert")),
        P(("dp", "expert")),
        P(("dp", "expert")),
        P(("dp", "expert")),
        P(("dp", "expert"), "tensor"),
        P(("dp", "expert"), "tensor"),
        P(("dp", "expert"), "tensor"),
        P("tensor", ("dp", "expert")),
        P(("dp", "expert"), None),
        P("expert", "dp", "tensor"),
        P("expert", "tensor", "dp"),
    )
    return jax.shard_map(
        on_device, mesh=mesh, in_specs=in_specs, out_specs=out_specs, check_vma=False
    )
```

profile of v0, /device:TPU:0, one launch (start us, length us, event | category | flops | bytes accessed | tf_op | source)
XLA Modules:
  0.0 1706.8 jit_solution(8788566759606359939)
XLA Ops:
  13.7 35.4 %all-reduce.11 = (bf16[768]{0:T(1024)(128)(2,1)S(1)}, bf16[768]{0:T(1024)(128)(2,1)S(1)}, bf16[768]{0:T(1024)(128)(2,1)S(1)}, bf16[768]{0:T(1024)(128)(2,1)S(1)}) all-reduce(bf16[768]{0:T(1024)(128)(2,1)S(1)} %dynamic-update-slice.1, ...), channel_id=1, replica_groups=mesh['dp'=2,'expert'=8,'tensor'=2] {'dp','expert'}, use_global_device_ids=true, to_apply=%add.2 | all-reduce | flops 3072 | bytes 12288
  52.9 20.5 %all_gather.38 = bf16[384,768]{0,1:T(8,128)(2,1)} all-gather(bf16[384,48]{0,1:T(8,128)(2,1)S(1)} %convert_element_type.159), channel_id=1, replica_groups=mesh['dp'=2,'expert'=8,'tensor'=2] {'dp','expert'}, dimensions={1}, use_global_device_ids=true | all-gather | bytes 626688 | tf_op jit(solution)/shard_map/all_gather | solution.py:68
  73.4 20.7 %all_gather.35 = bf16[768,384]{1,0:T(8,128)(2,1)S(1)} all-gather(bf16[48,384]{1,0:T(8,128)(2,1)S(1)} %convert_element_type.150), channel_id=1, replica_groups=mesh['dp'=2,'expert'=8,'tensor'=2] {'dp','expert'}, dimensions={0}, use_global_device_ids=true | all-gather | bytes 626688 | tf_op jit(solution)/shard_map/all_gather | solution.py:67
  94.1 19.5 %all_gather.37 = bf16[768,384]{1,0:T(8,128)(2,1)S(1)} all-gather(bf16[48,384]{1,0:T(8,128)(2,1)S(1)} %convert_element_type.154), channel_id=1, replica_groups=mesh['dp'=2,'expert'=8,'tensor'=2] {'dp','expert'}, dimensions={0}, use_global_device_ids=true | all-gather | bytes 626688 | tf_op jit(solution)/shard_map/all_gather | solution.py:66
  113.6 20.8 %all_gather.36 = bf16[768,384]{1,0:T(8,128)(2,1)S(1)} all-gather(bf16[48,384]{1,0:T(8,128)(2,1)S(1)} %convert_element_type.152), channel_id=1, replica_groups=mesh['dp'=2,'expert'=8,'tensor'=2] {'dp','expert'}, dimensions={0}, use_global_device_ids=true | all-gather | bytes 626688 | tf_op jit(solution)/shard_map/all_gather | solution.py:65
  146.1 3.7 reshape.346
  166.6 3.9 fusion.55
  177.5 101.0 %all-reduce.16.cloned.1.call-done = f32[985,768]{1,0:T(8,128)} async-done(((f32[985,768]{1,0:T(8,128)}), f32[985,768]{1,0:T(8,128)}) %all-reduce.16.cloned.1.call-update) | async-done | bytes 3025936 | tf_op jit(solution)/shard_map/psum | solution.py:107
  286.1 7.3 reshape.294
  293.5 13.6 scatter_custom_fusion
  307.1 4.5 all-to-all-start
  314.6 55.4 %all-gather = bf16[16,48,8]{1,2,0:T(8,128)(2,1)S(1)} all-gather(bf16[1,48,8]{1,2,0:T(8,128)(2,1)S(1)} %convert_bitcast_fusion.1), channel_id=1, replica_groups=mesh['dp'=2,'expert'=8,'tensor'=2] {'dp','expert'}, dimensions={0}, use_global_device_ids=true | all-gather | bytes 13056 | tf_op jit(solution)/shard_map/all_gather | solution.py:69
  372.4 4.8 mul.245
  377.3 8.2 mul.246
  387.3 18.5 %gather_fusion = f32[1970]{0:T(1024)S(1)} fusion(f32[985,8]{0,1:T(8,128)S(1)} %fusion.41, s32[1970]{0:T(1024)S(1)} %reshape.284), kind=kCustom, calls=%fused_computation.2 | custom fusion | bytes 31520 | tf_op jit(solution)/shard_map/jit(take_along_axis)/gather | solution.py:112
  407.0 19.9 %scatter_custom_fusion.1 = bf16[2496,768]{1,0:T(8,128)(2,1)} fusion(s32[1970]{0:T(1024)} %bitcast.127, f32[1970,768]{1,0:T(8,128)} %mul.246, f32[1970]{0:T(1024)S(1)} %mul.243, bf16[]{:T(256)} %constant.61.clone.1), kind=kCustom, calls=%fused_computation.57 | custom fusion | flops 3025920 | bytes 9912520 | tf_op jit(solution)/shard_map/scatter | solution.py:151
  426.9 4.7 all-to-all-start.2
  431.6 41.0 %multiply_convert_fusion = (bf16[2496,1536]{1,0:T(8,128)(2,1)}, f32[2496,1536]{1,0:T(8,128)}, f32[2496,1536]{1,0:T(8,128)}) fusion(bf16[2496,768]{1,0:T(8,128)(2,1)} %bitcast.9, bf16[1,768,1536]{2,1,0:T(8,128)(2,1)} %all-gather.4.cloned.1.call-done), kind=kOutput, calls=%fused_computation.8 | convolution fusion | flops 6138003456 | bytes 44531712 | tf_op jit(solution)/shard_map/dot_general | solution.py:124
  472.6 11.0 fusion.21
  483.6 21.0 %add_convert_fusion = bf16[2496,1536]{1,0:T(8,128)(2,1)} fusion(f32[2496,1536]{1,0:T(8,128)} %get-tuple-element.34, f32[2496,1536]{1,0:T(8,128)} %get-tuple-element.44, bf16[2496,768]{1,0:T(8,128)(2,1)} %bitcast.15, bf16[1,1536,768]{2,1,0:T(8,128)(2,1)} %all-gather.6.cloned.1.call-done), kind=kOutput, calls=%fused_computation.7 | convolution fusion | flops 5942476800 | bytes 44531712 | tf_op jit(solution)/shard_map/rd,fd->rf/dot_general | solution.py:158
  504.6 10.3 fusion.23
  514.9 351.3 %all-reduce.19 = (bf16[2496,768]{1,0:T(8,128)(2,1)}, bf16[2496,768]{1,0:T(8,128)(2,1)}) all-reduce(f32[2496,768]{1,0:T(8,128)} %fusion.21, f32[2496,768]{1,0:T(8,128)} %fusion.23), channel_id=1, replica_groups=mesh['dp'=2,'expert'=8,'tensor'=2] {'tensor'}, use_global_device_ids=true, to_apply=%region_13.14 | all-reduce | flops 3833856 | bytes 23003136 | tf_op jit(solution)/shard_map/psum | solution.py:127
  866.2 49.6 %all_to_all.20 = bf16[8,312,768]{2,1,0:T(8,128)(2,1)} all-to-all(bf16[8,312,768]{2,1,0:T(8,128)(2,1)} %bitcast.121), channel_id=1, replica_groups=mesh['dp'=2,'expert'=8,'tensor'=2] {'expert'}, dimensions={0} | all-to-all | bytes 7667712 | tf_op jit(solution)/shard_map/all_to_all | solution.py:166
  915.9 4.6 all-to-all-start.1
  920.9 12.9 gather_fusion.2
  933.7 32.0 %all-to-all-done.1 = bf16[8,312,768]{2,1,0:T(8,128)(2,1)} async-done(((bf16[8,312,768]{2,1,0:T(8,128)(2,1)}), bf16[8,312,768]{2,1,0:T(8,128)(2,1)}, u32[]{:S(2)}, u32[]{:S(2)}) %all-to-all-start.1) | async-done | bytes 3833888 | tf_op jit(solution)/shard_map/all_to_all | solution.py:128
  965.8 11.2 gather_fusion.1
  983.1 3.9 fusion.43
  987.0 6.4 select_convert_fusion
  993.4 8.3 reshape.267
  1001.8 11.7 reduce_sum.197
  1013.5 5.7 multiply_reduce_fusion.4
  1019.2 7.9 reshape.266
  1027.2 30.6 %multiply_reduce_fusion.2 = f32[985,768]{1,0:T(8,128)S(1)} fusion(f32[985,2,768]{2,1,0:T(2,128)} %reshape.266, f32[985,2]{1,0:T(8,128)} %copy-done.21), kind=kLoop, calls=%fused_computation.28 | loop fusion | flops 2269440 | bytes 9085640 | tf_op jit(solution)/shard_map/reduce_sum | solution.py:140
  1065.4 3.5 copy.145
  1068.9 5.1 fusion.31
  1095.7 3.9 fusion.34
  1099.6 3.8 fusion.60
  1108.1 11.3 convolution_bitcast_fusion
  1119.4 11.4 convolution_bitcast_fusion.1
  1133.8 84.9 %all-reduce.18.cloned.1.call-done = f32[985,768]{1,0:T(8,128)} async-done(((f32[985,768]{1,0:T(8,128)}), f32[985,768]{1,0:T(8,128)}) %all-reduce.18.cloned.1.call-update) | async-done | bytes 3025936 | tf_op jit(solution)/shard_map/psum | solution.py:237
  1223.5 61.2 %all-reduce.9 = (f32[768]{0:T(1024)S(1)}, f32[768]{0:T(1024)S(1)}, f32[768]{0:T(1024)S(1)}, f32[768]{0:T(1024)S(1)}) all-reduce(f32[768]{0:T(1024)S(1)} %get-tuple-element.16, f32[768]{0:T(1024)S(1)} %get-tuple-element.19, f32[768]{0:T(1024)S(1)} %get-tuple-element.14, ...), channel_id=2, replica_groups=mesh['dp'=2,'expert'=8,'tensor'=2] {'dp','expert'}, use_global_device_ids=true, to_apply=%region_28.30.clone | all-reduce | flops 3072 | bytes 24576
  1287.0 4.6 add_add_fusion.2
  1291.6 54.1 %reduce-scatter.14.cloned.1.call-done = f32[48,384]{1,0:T(8,128)} async-done(((f32[768,384]{1,0:T(8,128)}), f32[48,384]{1,0:T(8,128)}) %reduce-scatter.14.cloned.1.call-update) | async-done | bytes 73744 | tf_op jit(solution)/shard_map/reduce_scatter | solution.py:248
  1345.7 63.1 %reduce-scatter.10.cloned.1.call-done = f32[48,384]{1,0:T(8,128)} async-done(((f32[768,384]{1,0:T(8,128)}), f32[48,384]{1,0:T(8,128)}) %reduce-scatter.10.cloned.1.call-update) | async-done | bytes 73744 | tf_op jit(solution)/shard_map/reduce_scatter | solution.py:246
  1408.8 63.2 %reduce-scatter.12.cloned.1.call-done = f32[48,384]{1,0:T(8,128)} async-done(((f32[768,384]{1,0:T(8,128)}), f32[48,384]{1,0:T(8,128)}) %reduce-scatter.12.cloned.1.call-update) | async-done | bytes 73744 | tf_op jit(solution)/shard_map/reduce_scatter | solution.py:247
  1472.0 113.7 %reduce-scatter.20.cloned.1.call-done = f32[1,1536,384]{2,1,0:T(8,128)} async-done(((f32[1,1536,768]{2,1,0:T(8,128)}), f32[1,1536,384]{2,1,0:T(8,128)}) %reduce-scatter.20.cloned.1.call-update) | async-done | bytes 2359312 | tf_op jit(solution)/shard_map/reduce_scatter | solution.py:254
  1585.7 113.5 %reduce-scatter.18.cloned.1.call-done = f32[1,384,1536]{2,1,0:T(8,128)} async-done(((f32[1,768,1536]{2,1,0:T(8,128)}), f32[1,384,1536]{2,1,0:T(8,128)}) %reduce-scatter.18.cloned.1.call-update) | async-done | bytes 2359312 | tf_op jit(solution)/shard_map/reduce_scatter | solution.py:253
  (297 shorter events, 109.2 us)
Async XLA Ops:
  8.0 44.8 %copy-start.53 = (f32[48,384]{1,0:T(8,128)S(1)}, f32[48,384]{1,0:T(8,128)}, u32[]{:S(2)}) copy-start(f32[48,384]{1,0:T(8,128)} %param.22) | copy-start | bytes 221188
  8.0 44.8 %copy-start.54 = (f32[48,384]{1,0:T(8,128)S(1)}, f32[48,384]{1,0:T(8,128)}, u32[]{:S(2)}) copy-start(f32[48,384]{1,0:T(8,128)} %param.23) | copy-start | bytes 221188
  8.0 44.8 %copy-start.55 = (f32[48,384]{1,0:T(8,128)S(1)}, f32[48,384]{1,0:T(8,128)}, u32[]{:S(2)}) copy-start(f32[48,384]{1,0:T(8,128)} %param.24) | copy-start | bytes 221188
  8.0 44.8 %copy-start.56 = (f32[384,48]{0,1:T(8,128)S(1)}, f32[384,48]{0,1:T(8,128)}, u32[]{:S(2)}) copy-start(f32[384,48]{0,1:T(8,128)} %param.25) | copy-start | bytes 221188
  8.1 270.4 %all-reduce.16.cloned.1.call-start = ((), (), s32[]{:S(2)}) async-start(), calls=%async_computation.11 | async-start | bytes 6094848 | tf_op jit(solution)/shard_map/psum | solution.py:107
  10.8 123.6 %copy-start.5 = (bf16[985,768]{1,0:T(8,128)(2,1)S(1)}, bf16[985,768]{1,0:T(8,128)(2,1)}, u32[]{:S(2)}) copy-start(bf16[985,768]{1,0:T(8,128)(2,1)} %param.16) | copy-start | bytes 4538884
  49.1 86.0 %copy-start.51 = (f32[768]{0:T(1024)}, f32[768]{0:T(1024)S(1)}, u32[]{:S(2)}) copy-start(f32[768]{0:T(1024)S(1)} %convert_element_type.146) | copy-start | bytes 9220
  50.8 84.3 %copy-start.45 = (f32[985]{0:T(1024)}, f32[985]{0:T(1024)S(1)}, u32[]{:S(2)}) copy-start(f32[985]{0:T(1024)S(1)} %broadcast_multiply_fusion.1) | copy-start | bytes 11824
  52.8 60.8 %copy-start.65 = (f32[985]{0:T(1024)}, f32[985]{0:T(1024)S(1)}, u32[]{:S(2)}) copy-start(f32[985]{0:T(1024)S(1)} %fusion.16) | copy-start | bytes 11824
  52.8 84.1 %copy-start.61 = (f32[985]{0:T(1024)}, f32[985]{0:T(1024)S(1)}, u32[]{:S(2)}) copy-start(f32[985]{0:T(1024)S(1)} %fusion.44) | copy-start | bytes 11824
  94.1 44.6 %copy-start.29 = (bf16[768,384]{1,0:T(8,128)(2,1)}, bf16[768,384]{1,0:T(8,128)(2,1)S(1)}, u32[]{:S(2)}) copy-start(bf16[768,384]{1,0:T(8,128)(2,1)S(1)} %all_gather.35) | copy-start | bytes 1769476
  113.6 23.3 %copy-start.31 = (bf16[768,384]{1,0:T(8,128)(2,1)}, bf16[768,384]{1,0:T(8,128)(2,1)S(1)}, u32[]{:S(2)}) copy-start(bf16[768,384]{1,0:T(8,128)(2,1)S(1)} %all_gather.37) | copy-start | bytes 1769476
  170.6 261.0 %all-gather.4.cloned.1.call-start = ((), (), s32[]{:S(2)}) async-start(), calls=%async_computation.12 | async-start | bytes 3538944 | tf_op jit(solution)/shard_map/all_gather | solution.py:72
  173.5 107.8 %copy-start.57 = (f32[768]{0:T(1024)}, f32[768]{0:T(1024)S(1)}, u32[]{:S(2)}) copy-start(f32[768]{0:T(1024)S(1)} %convert_element_type.161) | copy-start | bytes 9220
  177.1 103.6 %copy-start.22 = (s32[985,2]{1,0:T(8,128)}, s32[985,2]{1,0:T(8,128)S(1)}, u32[]{:S(2)}) copy-start(s32[985,2]{1,0:T(8,128)S(1)} %copy.140) | copy-start | bytes 23644
  177.5 116.0 %copy-start.71 = (s32[1970,1]{0,1:T(1,128)}, s32[1970,1]{0,1:T(1,128)S(1)}, u32[]{:S(2)}) copy-start(s32[1970,1]{0,1:T(1,128)S(1)} %compare_select_fusion) | copy-start | bytes 23644
  282.9 102.6 %copy-start.8 = (bf16[985,768]{1,0:T(8,128)(2,1)}, bf16[985,768]{1,0:T(8,128)(2,1)S(1)}, u32[]{:S(2)}) copy-start(bf16[985,768]{1,0:T(8,128)(2,1)S(1)} %add_convert_fusion.2) | copy-start | bytes 4538884
  307.1 119.8 %all-to-all-start = ((bf16[8,312,768]{2,1,0:T(8,128)(2,1)}), bf16[8,312,768]{2,1,0:T(8,128)(2,1)}, u32[]{:S(2)}, u32[]{:S(2)}) async-start(bf16[8,312,768]{2,1,0:T(8,128)(2,1)} %bitcast.119), calls=%async_computation | async-start | bytes 7667712 | tf_op jit(solution)/shard_map/all_to_all | solution.py:121
  311.6 60.9 %copy-start.18 = (bf16[985,768]{1,0:T(8,128)(2,1)S(1)}, bf16[985,768]{1,0:T(8,128)(2,1)}, u32[]{:S(2)}) copy-start(bf16[985,768]{1,0:T(8,128)(2,1)} %param.17) | copy-start | bytes 4538884
  311.6 161.0 %all-gather.6.cloned.1.call-start = ((), (), s32[]{:S(2)}) async-start(), calls=%async_computation.13 | async-start | bytes 3538944 | tf_op jit(solution)/shard_map/all_gather | solution.py:73
  370.1 15.4 copy-start.47
  386.0 19.7 %copy-start.63 = (f32[985]{0:T(1024)}, f32[985]{0:T(1024)S(1)}, u32[]{:S(2)}) copy-start(f32[985]{0:T(1024)S(1)} %get-tuple-element.45) | copy-start | bytes 11824
  387.3 18.5 %copy-start = (f32[985,8]{0,1:T(8,128)}, f32[985,8]{0,1:T(8,128)S(1)}, u32[]{:S(2)}) copy-start(f32[985,8]{0,1:T(8,128)S(1)} %fusion.41) | copy-start | bytes 94564
  387.3 19.2 %copy-start.43 = (s32[985,2]{0,1:T(2,128)S(1)}, s32[985,2]{0,1:T(2,128)}, u32[]{:S(2)}) copy-start(s32[985,2]{0,1:T(2,128)} %param.29) | copy-start | bytes 23644
  406.7 20.2 %copy-start.21 = (f32[985,2]{1,0:T(8,128)}, f32[985,2]{1,0:T(8,128)S(1)}, u32[]{:S(2)}) copy-start(f32[985,2]{1,0:T(8,128)S(1)} %copy.139) | copy-start | bytes 23644
  426.9 56.7 %all-to-all-start.2 = ((bf16[8,312,768]{2,1,0:T(8,128)(2,1)}), bf16[8,312,768]{2,1,0:T(8,128)(2,1)}, u32[]{:S(2)}, u32[]{:S(2)}) async-start(bf16[8,312,768]{2,1,0:T(8,128)(2,1)} %bitcast.118), calls=%async_computation.2 | async-start | bytes 7667712 | tf_op jit(solution)/shard_map/all_to_all | solution.py:154
  483.6 21.0 %copy-start.73 = (bf16[1,768,1536]{2,1,0:T(8,128)(2,1)S(1)}, bf16[1,768,1536]{2,1,0:T(8,128)(2,1)}, u32[]{:S(2)}) copy-start(bf16[1,768,1536]{2,1,0:T(8,128)(2,1)} %all-gather.4.cloned.1.call-done) | copy-start | bytes 7077892
  915.9 49.9 %all-to-all-start.1 = ((bf16[8,312,768]{2,1,0:T(8,128)(2,1)}), bf16[8,312,768]{2,1,0:T(8,128)(2,1)}, u32[]{:S(2)}, u32[]{:S(2)}) async-start(bf16[8,312,768]{2,1,0:T(8,128)(2,1)} %bitcast.120), calls=%async_computation.1 | async-start | bytes 7667712 | tf_op jit(solution)/shard_map/all_to_all | solution.py:128
  920.5 211.9 %reduce-scatter.22.cloned.1.call-start = ((), (), s32[]{:S(2)}) async-start(), calls=%async_computation.21 | async-start | bytes 417792
  1001.7 11.7 copy-start.4
  1001.7 11.7 copy-start.48
  1001.8 11.7 copy-start.50
  1001.8 11.7 copy-start.58
  1001.8 11.7 copy-start.60
  1027.2 30.6 %copy-start.11 = (f32[985,768]{1,0:T(8,128)S(1)}, f32[985,768]{1,0:T(8,128)}, u32[]{:S(2)}) copy-start(f32[985,768]{1,0:T(8,128)} %get-tuple-element.47) | copy-start | bytes 9077764
  1079.3 139.4 %all-reduce.18.cloned.1.call-start = ((), (), s32[]{:S(2)}) async-start(), calls=%async_computation.14 | async-start | bytes 6094848 | tf_op jit(solution)/shard_map/psum | solution.py:237
  1093.8 197.8 %reduce-scatter.16.cloned.1.call-start = ((), (), s32[]{:S(2)}) async-start(), calls=%async_computation.18 | async-start | bytes 1253376 | tf_op jit(solution)/shard_map/reduce_scatter | solution.py:249
  1099.6 246.1 %reduce-scatter.14.cloned.1.call-start = ((), (), s32[]{:S(2)}) async-start(), calls=%async_computation.17 | async-start | bytes 1253376 | tf_op jit(solution)/shard_map/reduce_scatter | solution.py:248
  1103.5 305.3 %reduce-scatter.10.cloned.1.call-start = ((), (), s32[]{:S(2)}) async-start(), calls=%async_computation.15 | async-start | bytes 1253376 | tf_op jit(solution)/shard_map/reduce_scatter | solution.py:246
  1105.6 366.4 %reduce-scatter.12.cloned.1.call-start = ((), (), s32[]{:S(2)}) async-start(), calls=%async_computation.16 | async-start | bytes 1253376 | tf_op jit(solution)/shard_map/reduce_scatter | solution.py:247
  1107.8 478.0 %reduce-scatter.20.cloned.1.call-start = ((), (), s32[]{:S(2)}) async-start(), calls=%async_computation.20 | async-start | bytes 7077888 | tf_op jit(solution)/shard_map/reduce_scatter | solution.py:254
  1119.4 579.9 %reduce-scatter.18.cloned.1.call-start = ((), (), s32[]{:S(2)}) async-start(), calls=%async_computation.19 | async-start | bytes 7077888 | tf_op jit(solution)/shard_map/reduce_scatter | solution.py:253
  1130.8 88.0 %copy-start.6 = (bf16[985,768]{1,0:T(8,128)(2,1)S(1)}, bf16[985,768]{1,0:T(8,128)(2,1)}, u32[]{:S(2)}) copy-start(bf16[985,768]{1,0:T(8,128)(2,1)} %param.16) | copy-start | bytes 4538884
  1130.8 88.0 %copy-start.46 = (f32[985]{0:T(1024)S(1)}, f32[985]{0:T(1024)}, u32[]{:S(2)}) copy-start(f32[985]{0:T(1024)} %copy-done.45) | copy-start | bytes 11824
  1130.8 88.0 %copy-start.52 = (f32[768]{0:T(1024)S(1)}, f32[768]{0:T(1024)}, u32[]{:S(2)}) copy-start(f32[768]{0:T(1024)} %copy-done.51) | copy-start | bytes 9220
  1130.8 90.8 %copy-start.66 = (f32[985]{0:T(1024)S(1)}, f32[985]{0:T(1024)}, u32[]{:S(2)}) copy-start(f32[985]{0:T(1024)} %copy-done.65) | copy-start | bytes 11824
  1130.9 90.8 %copy-start.62 = (f32[985]{0:T(1024)S(1)}, f32[985]{0:T(1024)}, u32[]{:S(2)}) copy-start(f32[985]{0:T(1024)} %copy-done.61) | copy-start | bytes 11824
  1221.7 65.3 %copy-start.20 = (bf16[985,768]{1,0:T(8,128)(2,1)S(1)}, bf16[985,768]{1,0:T(8,128)(2,1)}, u32[]{:S(2)}) copy-start(bf16[985,768]{1,0:T(8,128)(2,1)} %param.17) | copy-start | bytes 4538884
  (42 other events, 152.6 us)
Sparse Core Ops, SparseCore 0:
  170.7 107.7 all-reduce.15
  1079.5 52.9 reduce-scatter.21
  1135.4 83.3 all-reduce.17
  1223.2 59.3 reduce-scatter.15
  1287.1 58.5 reduce-scatter.13
  1350.2 58.5 reduce-scatter.9
  1413.4 58.5 reduce-scatter.11
  1474.9 110.8 reduce-scatter.19
  1588.6 110.5 reduce-scatter.17
Sparse Core Ops, SparseCore 1:
  173.6 59.2 all-gather.3
  314.7 62.7 all-gather.5
where the time goes:
time: 1710 us
  blocking collectives  634 us (37%)
  waiting for transfers between devices  627 us (37%)
  matrix products  155 us (9%)
  local copies, waits for them, and re-layouts  152 us (9%)
  other arithmetic  106 us (6%)
  between operations  18.5 us (1%)
    psum x1, blocking collectives, on_device(): returned = lax.psum(expert_part, 'tensor').astype(jnp.bfloat16)  351 us
    reduce_scatter x1, waiting for transfers between devices, on_device(): lax.psum_scatter(grad_second[None], 'dp', scatter_dimension=2, tiled=True)  114 us
    reduce_scatter x1, waiting for transfers between devices, on_device(): lax.psum_scatter(grad_first[None], 'dp', scatter_dimension=1, tiled=True)  113 us
    psum x1, waiting for transfers between devices, on_device(): middle = inputs + lax.psum(head_part, 'tensor')  101 us
    unnamed x2, blocking collectives  96.5 us
    psum x1, waiting for transfers between devices, on_device(): grad_normed = lax.psum(norm_part, 'tensor')  84.9 us
    reduce_scatter x1, waiting for transfers between devices, on_device(): lax.psum_scatter(grad_wk, ('dp', 'expert'), scatter_dimension=0, tiled=True)  63.2 us
    reduce_scatter x1, waiting for transfers between devices, on_device(): lax.psum_scatter(grad_wq, ('dp', 'expert'), scatter_dimension=0, tiled=True)  63.1 us
  transfers between devices with their start and end apart: 14, of which 9 were waited for; matrix products, arithmetic and copies ran while one was open for 13% of the time, Pallas kernels for 0%

commit v1 on v0

v1 whole, which is shorter than its diff:
```python
import functools

import jax
import jax.numpy as jnp
from jax import lax
from jax.experimental import pallas as pl
from jax.experimental.pallas import tpu as pltpu
from jax.sharding import PartitionSpec as P

D = 768
HEADS = 12
SEQ = 197
HEAD = D // HEADS
SCALE = HEAD ** (-0.5)
EPSILON = 1e-06
HIGH = lax.Precision.HIGHEST
BF = jnp.bfloat16
F32 = jnp.float32


def norm_rows(values, gain, bias):
    average = jnp.mean(values, axis=-1, keepdims=True)
    centred = values - average
    variance = jnp.mean(centred * centred, axis=-1, keepdims=True)
    return centred * lax.rsqrt(variance + EPSILON) * gain + bias


def gelu_exact(values):
    return jax.nn.gelu(values, approximate=False)


def slot_table(routes, expert_count):
    total = routes.shape[0]
    sequence = jnp.transpose(routes).reshape(-1)
    onehot = (sequence[:, None] == jnp.arange(expert_count, dtype=jnp.int32)[None, :]).astype(
        jnp.int32
    )
    before = jnp.cumsum(onehot, axis=0) - onehot
    return jnp.sum(before * onehot, axis=1).reshape(2, total)


def hop(value, axis, offset):
    count = lax.axis_size(axis)
    return lax.ppermute(value, axis, [(i, i ^ offset) for i in range(count)])


def after(value, *others):
    return lax.optimization_barrier((value,) + others)[0]


def in_order(first, own, other, axis):
    return jnp.where(
        first, jnp.concatenate([own, other], axis), jnp.concatenate([other, own], axis)
    )


def gather_rows(shard):
    count = lax.axis_size("expert")
    here_dp = lax.axis_index("dp")
    here = lax.axis_index("expert")
    across = hop(shard, "dp", 1)
    pair = jnp.where(here_dp == 0, jnp.stack([shard, across]), jnp.stack([across, shard]))
    same = [pair] + [hop(pair, "expert", k) for k in range(2, count, 2)]
    flipped = [hop(p, "expert", 1) for p in same]
    buffer = jnp.zeros((2, count) + shard.shape, shard.dtype)
    for j in range(count // 2):
        buffer = lax.dynamic_update_slice(buffer, same[j][:, None], (0, here ^ (2 * j), 0, 0))
        buffer = lax.dynamic_update_slice(
            buffer, flipped[j][:, None], (0, here ^ (2 * j + 1), 0, 0)
        )
    return buffer.reshape(-1, shard.shape[1]), across


def scatter_sum(grad, wide):
    count = lax.axis_size("expert")
    here_dp = lax.axis_index("dp")
    here = lax.axis_index("expert")
    core = here & 1
    chip = here >> 1
    blocks = grad.reshape((2, count // 2, 2, -1) + grad.shape[1:])
    pick = lambda array, index, axis: lax.dynamic_index_in_dim(array, index, axis, False)
    total = pick(blocks, core, 2) + hop(
        pick(blocks, 1 - core, 2).astype(wide), "expert", 1
    ).astype(F32)
    summed = pick(total, chip, 1)
    for k in range(1, count // 2):
        summed = summed + hop(pick(total, chip ^ k, 1).astype(wide), "expert", 2 * k).astype(F32)
    return pick(summed, here_dp, 0) + hop(
        pick(summed, 1 - here_dp, 0).astype(wide), "dp", 1
    ).astype(F32)


def trade_blocks(blocks):
    return [blocks[0]] + [hop(blocks[k], "expert", k) for k in range(1, len(blocks))]


def send_kernel(rows_ref, values_ref, gates_ref, out_ref, *, gated):
    capacity = out_ref.shape[1]
    base = pl.program_id(0) * capacity
    places = lax.broadcasted_iota(jnp.int32, (capacity, 1), 0) + base
    first = places == rows_ref[0:1, :]
    second = places == rows_ref[1:2, :]
    chosen = jnp.where(first | second, 1.0, 0.0).astype(BF)
    picked = jnp.dot(chosen, values_ref[...], preferred_element_type=F32)
    if gated:
        weight = jnp.where(first, gates_ref[0:1, :], 0.0) + jnp.where(
            second, gates_ref[1:2, :], 0.0
        )
        picked = picked * jnp.sum(weight, axis=1, keepdims=True)
    out_ref[0] = picked.astype(BF)


def send_rows(rows, values, gates, count, capacity, gated):
    total = values.shape[0]
    return pl.pallas_call(
        functools.partial(send_kernel, gated=gated),
        grid=(count,),
        in_specs=[
            pl.BlockSpec((2, total), lambda i: (0, 0)),
            pl.BlockSpec((total, D), lambda i: (0, 0)),
            pl.BlockSpec((2, total), lambda i: (0, 0)),
        ],
        out_specs=pl.BlockSpec((1, capacity, D), lambda i: (i, 0, 0)),
        out_shape=jax.ShapeDtypeStruct((count, capacity, D), BF),
        name="send_gated" if gated else "send_rows",
        cost_estimate=pl.CostEstimate(
            flops=2 * count * capacity * total * D, bytes_accessed=8_000_000, transcendentals=0
        ),
    )(rows, values, gates)


TILE = 200


def home_kernel(rows_ref, back_ref, middle_ref, grad_ref, gates_ref, out_ref, dgate_ref):
    total = back_ref.shape[0]
    places = lax.broadcasted_iota(jnp.int32, (1, total), 1)
    value = middle_ref[...]
    columns = lax.broadcasted_iota(jnp.int32, (TILE, 128), 1)
    found = jnp.zeros((TILE, 128), F32)
    for c in range(2):
        chosen = jnp.where(rows_ref[:, c : c + 1] == places, 1.0, 0.0).astype(BF)
        picked = jnp.dot(chosen, back_ref[...], preferred_element_type=F32)
        value = value + gates_ref[:, c : c + 1] * picked
        dgate = jnp.sum(picked * grad_ref[...].astype(F32), axis=1, keepdims=True)
        found = jnp.where(columns == c, dgate, found)
    out_ref[...] = value.astype(BF)
    dgate_ref[...] = found


def bring_home(rows, back, middle, grad, gates):
    total, width = middle.shape
    count = back.shape[0]
    tile = lambda w: pl.BlockSpec((TILE, w), lambda i: (i, 0))
    return pl.pallas_call(
        home_kernel,
        grid=(pl.cdiv(total, TILE),),
        in_specs=[
            tile(2),
            pl.BlockSpec((count, width), lambda i: (0, 0)),
            tile(width),
            tile(width),
            tile(2),
        ],
        out_specs=[tile(width), tile(128)],
        out_shape=[
            jax.ShapeDtypeStruct((total, width), BF),
            jax.ShapeDtypeStruct((total, 128), F32),
        ],
        name="bring_home",
        cost_estimate=pl.CostEstimate(
            flops=4 * count * total * width, bytes_accessed=8_000_000, transcendentals=0
        ),
    )(rows, back, middle, grad, gates)


def sum_kernel(rows_ref, back_ref, out_ref):
    places = lax.broadcasted_iota(jnp.int32, (1, back_ref.shape[0]), 1)
    chosen = (rows_ref[:, 0:1] == places) | (rows_ref[:, 1:2] == places)
    out_ref[...] = jnp.dot(
        jnp.where(chosen, 1.0, 0.0).astype(BF), back_ref[...], preferred_element_type=F32
    ).astype(BF)


def sum_home(rows, back):
    total = rows.shape[0]
    count, width = back.shape
    tile = lambda w: pl.BlockSpec((TILE, w), lambda i: (i, 0))
    return pl.pallas_call(
        sum_kernel,
        grid=(pl.cdiv(total, TILE),),
        in_specs=[tile(2), pl.BlockSpec((count, width), lambda i: (0, 0))],
        out_specs=tile(width),
        out_shape=jax.ShapeDtypeStruct((total, width), BF),
        name="sum_home",
        cost_estimate=pl.CostEstimate(
            flops=2 * count * total * width, bytes_accessed=6_000_000, transcendentals=0
        ),
    )(rows, back)


def on_device(
    tokens,
    cotangent,
    ln1_gain,
    ln1_bias,
    ln2_gain,
    ln2_bias,
    w_query,
    w_key,
    w_value,
    w_out,
    w_router,
    w_in,
    w_back,
    expert_ids,
):
    count = lax.axis_size("expert")
    tok = tokens.shape[0]
    capacity = (10 * tok + 32 * count - 1) // (32 * count) * 8
    images = tok // SEQ
    here = lax.axis_index("expert")
    here_dp = lax.axis_index("dp")
    here_t = lax.axis_index("tensor")
    half = D // 2

    small = jnp.stack([ln1_gain, ln1_bias, ln2_gain, ln2_bias], axis=1)
    narrow = jnp.concatenate([small, w_router], axis=1)
    narrow = jnp.pad(narrow, ((0, 0), (0, 128 - narrow.shape[1])))
    first_pack = jnp.concatenate([w_query, w_key, w_value, narrow], axis=1).astype(BF)
    packed, crossed = gather_rows(first_pack)
    query_w = packed[:, :half]
    key_w = packed[:, half : 2 * half]
    value_w = packed[:, 2 * half : 3 * half]
    vectors = packed[:, 3 * half : 3 * half + 4].astype(F32)
    gain_a, bias_a, gain_b, bias_b = (vectors[:, i] for i in range(4))
    router_w = packed[:, 3 * half + 4 : 3 * half + 4 + count]
    out_own = jnp.transpose(w_out).astype(BF)
    out_pair = in_order(here_t == 0, out_own, hop(after(out_own, crossed), "tensor", 1), 1)
    out_t, crossed_out = gather_rows(out_pair)
    out_here = lax.dynamic_slice_in_dim(out_t, here_t * half, half, 1)

    in_own = w_in[0].astype(BF)
    back_own = w_back[0].astype(BF)
    first_w = in_order(here_dp == 0, in_own, hop(after(in_own, crossed_out), "dp", 1), 0)
    second_w = in_order(here_dp == 0, back_own, hop(after(back_own, first_w[:8]), "dp", 1), 1)

    slots = slot_table(expert_ids, count)
    ids = jnp.transpose(expert_ids)
    rows_lane = (ids ^ here) * capacity + slots
    rows = jnp.transpose(rows_lane)

    inputs = tokens.astype(F32)
    a_rows = norm_rows(inputs, gain_a, bias_a).astype(BF)
    dot = functools.partial(jnp.dot, preferred_element_type=F32)
    ein = functools.partial(jnp.einsum, preferred_element_type=F32)
    heads_here = half // HEAD
    shape = (images, SEQ, heads_here, HEAD)
    query = dot(a_rows, query_w).astype(BF).reshape(shape)
    keys = dot(a_rows, key_w).astype(BF).reshape(shape)
    values = dot(a_rows, value_w).astype(BF).reshape(shape)
    scores = ein("bqhd,bkhd->bhqk", query, keys) * SCALE
    log_total = jax.nn.logsumexp(scores, axis=-1, keepdims=True)
    weights = jnp.exp(scores - log_total)
    attended = ein("bhqk,bkhd->bqhd", weights.astype(BF), values).astype(BF).reshape(tok, -1)
    attended_all = in_order(here_t == 0, attended, hop(attended, "tensor", 1), 1)
    middle = inputs + ein("tc,dc->td", attended_all, out_t)

    h_rows = norm_rows(middle, gain_b, bias_b).astype(BF)
    router_probs = jax.nn.softmax(dot(h_rows, router_w), axis=-1)
    lanes = jnp.arange(count, dtype=jnp.int32)[None, :]
    chosen = [(expert_ids[:, c : c + 1] == lanes).astype(F32) for c in range(2)]
    gates = jnp.stack([jnp.sum(router_probs * chosen[c], axis=1) for c in range(2)], axis=1)
    gates_lane = jnp.transpose(gates)
    outgoing = send_rows(rows_lane, h_rows, gates_lane, count, capacity, False)
    arrived = jnp.concatenate(trade_blocks([outgoing[k] for k in range(count)]), axis=0)
    grad_out_rows = send_rows(
        rows_lane, cotangent, after(gates_lane, outgoing[0, :8]), count, capacity, True
    )
    grad_arrived = jnp.concatenate(trade_blocks([grad_out_rows[k] for k in range(count)]), axis=0)

    pre_act = dot(arrived, first_w)
    hidden = gelu_exact(pre_act).astype(BF)
    second_there = lax.dynamic_slice_in_dim(second_w, (1 - here_t) * half, half, 1)
    second_here = lax.dynamic_slice_in_dim(second_w, here_t * half, half, 1)
    part_there = dot(hidden, second_there).astype(BF)
    part_here = dot(hidden, second_here)
    returned = (part_here + hop(part_there, "tensor", 1).astype(F32)).astype(BF)
    returned = returned.reshape(count, capacity, half)
    came_back = jnp.concatenate(trade_blocks([returned[k] for k in range(count)]), axis=0)

    grad_second = ein("rf,rd->fd", hidden, grad_arrived)
    grad_hidden = ein("rd,fd->rf", grad_arrived, second_w)
    _, gelu_pull = jax.vjp(gelu_exact, pre_act)
    grad_pre = gelu_pull(grad_hidden)[0].astype(BF)
    first_there = lax.dynamic_slice_in_dim(first_w, (1 - here_t) * half, half, 0)
    first_here = lax.dynamic_slice_in_dim(first_w, here_t * half, half, 0)
    input_there = ein("rf,df->rd", grad_pre, first_there).astype(BF)
    input_here = ein("rf,df->rd", grad_pre, first_here)
    grad_rows = (input_here + hop(input_there, "tensor", 1).astype(F32)).astype(BF)
    grad_rows = grad_rows.reshape(count, capacity, half)
    grad_home = jnp.concatenate(trade_blocks([grad_rows[k] for k in range(count)]), axis=0)
    grad_first = ein("rd,rf->df", arrived, grad_pre)

    def share(grad, axis):
        size = grad.shape[axis] // 2
        there = lax.dynamic_slice_in_dim(grad, (1 - here_dp) * size, size, axis).astype(BF)
        own = lax.dynamic_slice_in_dim(grad, here_dp * size, size, axis)
        return own + hop(there, "dp", 1).astype(F32)

    grad_back = share(grad_second, 1)[None]
    grad_in = share(grad_first, 0)[None]

    middle_half = lax.dynamic_slice_in_dim(middle, here_t * half, half, 1)
    cot_half = lax.dynamic_slice_in_dim(cotangent, here_t * half, half, 1)
    out_half, dgate_part = bring_home(rows, came_back, middle_half, cot_half, gates)
    block_out = in_order(here_t == 0, out_half, hop(out_half, "tensor", 1), 1)
    dgate_part = jnp.transpose(dgate_part[:, :2])
    grad_gates = jnp.transpose(dgate_part + hop(dgate_part, "tensor", 1))
    grad_probs = sum(chosen[c] * grad_gates[:, c : c + 1] for c in range(2))
    grad_logits = router_probs * (
        grad_probs - jnp.sum(router_probs * grad_probs, axis=-1, keepdims=True)
    )
    h_float = h_rows.astype(F32)
    grad_router = jnp.dot(jnp.transpose(h_float), grad_logits, precision=HIGH)
    grad_h_router = jnp.dot(grad_logits, jnp.transpose(router_w.astype(F32)), precision=HIGH)

    moe_half = sum_home(rows, grad_home)
    moe_all = in_order(here_t == 0, moe_half, hop(moe_half, "tensor", 1), 1)
    grad_h = moe_all.astype(F32) + grad_h_router
    _, norm_two_pull = jax.vjp(norm_rows, middle, gain_b, bias_b)
    grad_mid_norm, grad_gain_two, grad_bias_two = norm_two_pull(grad_h)
    grad_middle = cotangent.astype(F32) + grad_mid_norm

    grad_branch = grad_middle.astype(BF)
    grad_outw = ein("td,tc->dc", grad_branch, attended)
    grad_att = dot(grad_branch, out_here).astype(BF).reshape(shape)
    again = ein("bqhd,bkhd->bhqk", query, keys) * SCALE
    weights_again = jnp.exp(again - log_total)
    grad_value = ein("bhqk,bqhd->bkhd", weights_again.astype(BF), grad_att).astype(BF)
    grad_weights = ein("bqhd,bkhd->bhqk", grad_att, values)
    grad_scores = (
        weights_again
        * (grad_weights - jnp.sum(weights_again * grad_weights, axis=-1, keepdims=True))
    ).astype(BF)
    grad_query = (ein("bhqk,bkhd->bqhd", grad_scores, keys) * SCALE).astype(BF)
    grad_key = (ein("bhqk,bqhd->bkhd", grad_scores, query) * SCALE).astype(BF)
    grad_qkv = jnp.concatenate(
        [g.reshape(tok, half) for g in (grad_query, grad_key, grad_value)], axis=1
    )
    qkv_w = packed[:, : 3 * half]
    norm_part = ein("tc,dc->td", grad_qkv, qkv_w).astype(BF)
    grad_normed = norm_part.astype(F32) + hop(norm_part, "tensor", 1).astype(F32)
    grad_wqkv = ein("td,tc->dc", a_rows, grad_qkv)
    _, norm_one_pull = jax.vjp(norm_rows, inputs, gain_a, bias_a)
    grad_in_norm, grad_gain_one, grad_bias_one = norm_one_pull(grad_normed)
    grad_tokens = grad_middle + grad_in_norm

    shard_outw = jnp.transpose(scatter_sum(grad_outw, BF))
    shard_qkv = scatter_sum(grad_wqkv, BF)
    tiny = jnp.concatenate(
        [
            jnp.transpose(grad_router),
            jnp.stack([grad_gain_one, grad_bias_one, grad_gain_two, grad_bias_two]),
        ],
        axis=0,
    )
    for offset in [1 << b for b in range(count.bit_length() - 1)]:
        tiny = tiny + hop(tiny, "expert", offset)
    tiny = tiny + hop(tiny, "dp", 1)
    width = ln1_gain.shape[0]
    tiny = tiny.reshape(-1, 2 * count, width)
    tiny = lax.dynamic_index_in_dim(tiny, here_dp * count + here, 1, False)
    return (
        block_out,
        grad_tokens,
        tiny[count],
        tiny[count + 1],
        tiny[count + 2],
        tiny[count + 3],
        shard_qkv[:, :half],
        shard_qkv[:, half : 2 * half],
        shard_qkv[:, 2 * half :],
        shard_outw,
        jnp.transpose(tiny[:count]),
        grad_in,
        grad_back,
    )


def solution(mesh):
    rows = ("dp", "expert")
    in_specs = (
        P(rows, None),
        P(rows, None),
        P(rows),
        P(rows),
        P(rows),
        P(rows),
        P(rows, "tensor"),
        P(rows, "tensor"),
        P(rows, "tensor"),
        P("tensor", rows),
        P(rows, None),
        P("expert", "dp", "tensor"),
        P("expert", "tensor", "dp"),
        P(rows, None),
    )
    out_specs = (
        P(rows, None),
        P(rows, None),
        P(rows),
        P(rows),
        P(rows),
        P(rows),
        P(rows, "tensor"),
        P(rows, "tensor"),
        P(rows, "tensor"),
        P("tensor", rows),
        P(rows, None),
        P("expert", "dp", "tensor"),
        P("expert", "tensor", "dp"),
    )
    return jax.shard_map(
        on_device, mesh=mesh, in_specs=in_specs, out_specs=out_specs, check_vma=False
    )
```

time: 1710 us -> 699 us (0.41)
  blocking collectives: 634 us -> 0 us
  waiting for transfers between devices: 627 us -> 286 us
  starting transfers between devices: 14.8 us -> 86.7 us
  other arithmetic: 106 us -> 44.3 us
  local copies, waits for them, and re-layouts: 152 us -> 96.8 us
  Pallas kernels: 0 us -> 34 us
    reduce_scatter x6 -> x0, waiting for transfers between devices: 408 us -> none  [the longest x1 114 us: on_device(): lax.psum_scatter(grad_second[None], 'dp', scatter_dimension=2, tiled=True)]
    psum x1 -> x0, blocking collectives: 351 us -> none  [on_device(): returned = lax.psum(expert_part, 'tensor').astype(jnp.bfloat16)]
    ppermute x0 -> x70, waiting for transfers between devices: none -> 286 us  [hop(): return lax.ppermute(value, axis, [(i, i ^ offset) for i in range(count)])]
    psum x2 -> x0, waiting for transfers between devices: 186 us -> none  [the longest x1 101 us: on_device(): middle = inputs + lax.psum(head_part, 'tensor')]
    all_gather x5 -> x0, blocking collectives: 137 us -> none  [the longest x1 55.4 us: on_device(): lax.all_gather(w_router.astype(jnp.bfloat16), ('dp', 'expert'), axis=0, t...]
    unnamed x2 -> x0, blocking collectives: 96.5 us -> none
    ppermute x0 -> x70, starting transfers between devices: none -> 86.7 us  [hop(): return lax.ppermute(value, axis, [(i, i ^ offset) for i in range(count)])]
    all_to_all x1 -> x0, blocking collectives: 49.6 us -> none  [on_device(): lax.all_to_all(grad_rows.reshape(expert_count, capacity, -1), 'expert', s...]
  transfers between devices with their start and end apart: 14 -> 70, of which waited for: 9 -> 30; matrix products, arithmetic and copies ran while one was open for 13% -> 34% of each run, Pallas kernels for 0% -> 5%
where the time goes in v1:
time: 699 us; the launch traced here: 689 us
  waiting for transfers between devices  286 us (41%)
  matrix products  139 us (20%)
  local copies, waits for them, and re-layouts  96.8 us (14%)
  starting transfers between devices  86.7 us (12%)
  other arithmetic  44.3 us (6%)
  Pallas kernels  34 us (5%)
    ppermute x70, waiting for transfers between devices, hop(): return lax.ppermute(value, axis, [(i, i ^ offset) for i in range(count)])  286 us
    ppermute x70, starting transfers between devices, hop(): return lax.ppermute(value, axis, [(i, i ^ offset) for i in range(count)])  86.7 us
    dot_general x1, matrix products, on_device(): pre_act = dot(arrived, first_w)  40 us
    unnamed x205, local copies, waits for them, and re-layouts  28.3 us
    dot_general x1, matrix products, on_device(): grad_hidden = ein('rd,fd->rf', grad_arrived, second_w)  19.5 us
    pallas_call x2, Pallas kernels, send_rows(): pl.pallas_call(functools.partial(send_kernel, gated=gated), grid=(count,)...  17.5 us
  transfers between devices with their start and end apart: 70, of which 30 were waited for; matrix products, arithmetic and copies ran while one was open for 34% of the time, Pallas kernels for 5%

profile of v1, /device:TPU:0, one launch (start us, length us, event | category | flops | bytes accessed | tf_op | source)
XLA Modules:
  0.0 689.4 jit_solution(10525556261405716079)
XLA Ops:
  5.1 4.1 collective-permute-start
  24.6 19.9 %collective-permute-start.9 = (bf16[48,384]{1,0:T(8,128)(2,1)S(1)}, bf16[48,384]{1,0:T(8,128)(2,1)S(1)}, u32[]{:S(2)}, u32[]{:S(2)}) collective-permute-start(bf16[48,384]{1,0:T(8,128)(2,1)S(1)} %get-tuple-element.17), channel_id=1, source_target_pairs={{0,1},{1,0},{2,3},{3,2},{4,5},{5,4},{6,7},{7,6},{8,9},{9,8},{10,11... | collective-permute-start | bytes 110600 | tf_op jit(solution)/shard_map/ppermute | solution.py:44
  44.7 22.0 %collective-permute-done.9 = bf16[48,384]{1,0:T(8,128)(2,1)S(1)} collective-permute-done((bf16[48,384]{1,0:T(8,128)(2,1)S(1)}, bf16[48,384]{1,0:T(8,128)(2,1)S(1)}, u32[]{:S(2)}, u32[]{:S(2)}) %collective-permute-start.9) | collective-permute-done | bytes 36896 | tf_op jit(solution)/shard_map/ppermute | solution.py:44
  68.2 5.2 collective-permute-done.10
  78.0 5.8 collective-permute-done.12
  88.5 4.9 collective-permute-done.16
  101.5 3.3 copy.170
  107.3 3.8 copy.171
  119.3 3.3 copy.172
  122.7 4.4 fusion.33
  128.9 2.9 reshape.581
  136.1 4.0 maximum_select_fusion.1
  140.1 18.4 %collective-permute-done.8 = bf16[985,384]{1,0:T(8,128)(2,1)S(1)} collective-permute-done((bf16[985,384]{1,0:T(8,128)(2,1)}, bf16[985,384]{1,0:T(8,128)(2,1)S(1)}, u32[]{:S(2)}, u32[]{:S(2)}) %collective-permute-start.8) | collective-permute-done | bytes 756512 | tf_op jit(solution)/shard_map/ppermute | solution.py:44
  164.9 8.2 %send_rows.1 = bf16[8,312,768]{2,1,0:T(8,128)(2,1)} custom-call(s32[2,985]{1,0:T(2,128)} %copy.184.rows_ref, bf16[985,768]{1,0:T(8,128)(2,1)} %copy-done.7, f32[2,985]{1,0:T(2,128)} %get-tuple-element.85.gates_ref), custom_call_target="tpu_custom_call" | custom-call | flops 3776348160 | bytes 8000000 | tf_op jit(solution)/shard_map/send_rows/pallas_call | solution.py:115
  173.1 3.2 slice_bitcast_fusion.9
  178.2 9.3 %send_gated.1 = bf16[8,312,768]{2,1,0:T(8,128)(2,1)} custom-call(s32[2,985]{1,0:T(2,128)} %copy.184.rows_ref, bf16[985,768]{1,0:T(8,128)(2,1)} %values_ref.1, f32[2,985]{1,0:T(2,128)} %get-tuple-element.85.gates_ref), custom_call_target="tpu_custom_call" | custom-call | flops 3776348160 | bytes 8000000 | tf_op jit(solution)/shard_map/send_gated/pallas_call | solution.py:115
  187.5 3.4 slice_bitcast_fusion.1
  203.7 3.2 collective-permute-done.19
  208.0 8.1 %collective-permute-done.20 = bf16[312,768]{1,0:T(8,128)(2,1)} collective-permute-done((bf16[312,768]{1,0:T(8,128)(2,1)}, bf16[312,768]{1,0:T(8,128)(2,1)}, u32[]{:S(2)}, u32[]{:S(2)}) %collective-permute-start.20) | collective-permute-done | bytes 479264 | tf_op jit(solution)/shard_map/ppermute | solution.py:44
  219.8 19.6 %collective-permute-done.22 = bf16[312,768]{1,0:T(8,128)(2,1)S(1)} collective-permute-done((bf16[312,768]{1,0:T(8,128)(2,1)S(1)}, bf16[312,768]{1,0:T(8,128)(2,1)S(1)}, u32[]{:S(2)}, u32[]{:S(2)}) %collective-permute-start.22) | collective-permute-done | bytes 479264 | tf_op jit(solution)/shard_map/ppermute | solution.py:44
  241.9 40.0 %multiply_convert_fusion = (bf16[2496,1536]{1,0:T(8,128)(2,1)}, f32[2496,1536]{1,0:T(8,128)}, f32[2496,1536]{1,0:T(8,128)}) fusion(bf16[2496,768]{1,0:T(8,128)(2,1)S(1)} %constant_dynamic-update-slice_fusion, bf16[768,1536]{1,0:T(8,128)(2,1)S(1)} %maximum_select_fusion), kind=kOutput, calls=%fused_computation.3 | convolution fusion | flops 6138003456 | bytes 44531712 | tf_op jit(solution)/shard_map/dot_general | solution.py:282
  285.2 11.6 %collective-permute-done.41 = bf16[312,768]{1,0:T(8,128)(2,1)S(1)} collective-permute-done((bf16[312,768]{1,0:T(8,128)(2,1)S(1)}, bf16[312,768]{1,0:T(8,128)(2,1)S(1)}, u32[]{:S(2)}, u32[]{:S(2)}) %collective-permute-start.41) | collective-permute-done | bytes 479264 | tf_op jit(solution)/shard_map/ppermute | solution.py:44
  296.8 9.5 %collective-permute-done.42 = bf16[312,768]{1,0:T(8,128)(2,1)S(1)} collective-permute-done((bf16[312,768]{1,0:T(8,128)(2,1)S(1)}, bf16[312,768]{1,0:T(8,128)(2,1)S(1)}, u32[]{:S(2)}, u32[]{:S(2)}) %collective-permute-start.42) | collective-permute-done | bytes 479264 | tf_op jit(solution)/shard_map/ppermute | solution.py:44
  308.2 19.5 %add_convert_fusion = bf16[2496,1536]{1,0:T(8,128)(2,1)} fusion(f32[2496,1536]{1,0:T(8,128)} %get-tuple-element.38, f32[2496,1536]{1,0:T(8,128)} %get-tuple-element.94, bf16[2496,768]{1,0:T(8,128)(2,1)} %copy-done.67, bf16[1536,768]{1,0:T(8,128)(2,1)S(1)} %copy-done.26), kind=kOutput, calls=%fused_computation.2 | convolution fusion | flops 5942476800 | bytes 44531712 | tf_op jit(solution)/shard_map/rd,fd->rf/dot_general | solution.py:293
  327.7 10.1 %fusion.118 = f32[768,1536]{1,0:T(8,128)S(1)} fusion(bf16[2496,768]{1,0:T(8,128)(2,1)} %copy-done.70, bf16[2496,1536]{1,0:T(8,128)(2,1)} %add_convert_fusion), kind=kOutput, calls=%fused_computation.299 | convolution fusion | flops 5888802816 | bytes 16220160 | tf_op jit(solution)/shard_map/rd,rf->df/dot_general | solution.py:303
  338.1 9.2 %fusion.119 = f32[1536,768]{1,0:T(8,128)S(1)} fusion(bf16[2496,1536]{1,0:T(8,128)(2,1)} %get-tuple-element.37, bf16[2496,768]{1,0:T(8,128)(2,1)S(1)} %copy-done.68), kind=kOutput, calls=%fused_computation.300 | convolution fusion | flops 5888802816 | bytes 16220160 | tf_op jit(solution)/shard_map/rf,rd->fd/dot_general | solution.py:292
  347.4 4.2 convolution_convert_fusion.1
  354.8 7.3 %convolution_convert_fusion = bf16[2496,384]{1,0:T(8,128)(2,1)S(1)} fusion(bf16[2496,1536]{1,0:T(8,128)(2,1)} %add_convert_fusion, bf16[768,1536]{1,0:T(8,128)(2,1)S(1)} %copy-done.28, s32[]{:T(128)S(6)} %select_n.230), kind=kOutput, calls=%fused_computation.33 | convolution fusion | flops 2945359872 | bytes 10764292 | tf_op jit(solution)/shard_map/rf,df->rd/dot_general | solution.py:298
  364.2 27.4 %collective-permute-done.68 = bf16[384,1536]{1,0:T(8,128)(2,1)S(1)} collective-permute-done((bf16[384,1536]{1,0:T(8,128)(2,1)S(1)}, bf16[384,1536]{1,0:T(8,128)(2,1)S(1)}, u32[]{:S(2)}, u32[]{:S(2)}) %collective-permute-start.68) | collective-permute-done | bytes 1179680 | tf_op jit(solution)/shard_map/ppermute | solution.py:44
  393.3 48.8 %collective-permute-done.69 = bf16[1536,384]{1,0:T(8,128)(2,1)S(1)} collective-permute-done((bf16[1536,384]{1,0:T(8,128)(2,1)S(1)}, bf16[1536,384]{1,0:T(8,128)(2,1)S(1)}, u32[]{:S(2)}, u32[]{:S(2)}) %collective-permute-start.69) | collective-permute-done | bytes 1179680 | tf_op jit(solution)/shard_map/ppermute | solution.py:44
  443.7 3.0 collective-permute-done.27
  446.7 4.4 fusion.10
  455.1 32.0 %collective-permute-done.43 = bf16[2496,384]{1,0:T(8,128)(2,1)S(1)} collective-permute-done((bf16[2496,384]{1,0:T(8,128)(2,1)S(1)}, bf16[2496,384]{1,0:T(8,128)(2,1)S(1)}, u32[]{:S(2)}, u32[]{:S(2)}) %collective-permute-start.43) | collective-permute-done | bytes 1916960 | tf_op jit(solution)/shard_map/ppermute | solution.py:44
  487.7 7.4 %fusion.11 = bf16[2496,384]{1,0:T(8,128)(2,1)S(1)} fusion(bf16[2496,1536]{1,0:T(8,128)(2,1)} %add_convert_fusion, bf16[2496,384]{1,0:T(8,128)(2,1)S(1)} %collective-permute-done.43, bf16[768,1536]{1,0:T(8,128)(2,1)S(1)} %copy-done.28, s32[]{:T(128)S(6)} %select_n.229), kind=kOutput, calls=%fused_computation.36 | convolution fusion | flops 2947276800 | bytes 12681220 | tf_op jit(solution)/shard_map/rf,df->rd/dot_general | solution.py:299
  501.8 3.4 collective-permute-done.33
  506.7 4.3 collective-permute-done.34
  512.6 9.9 %bring_home.1 = (bf16[985,384]{1,0:T(8,128)(2,1)}, f32[985,128]{1,0:T(8,128)}) custom-call(s32[985,2]{1,0:T(8,128)} %bitcast.291, bf16[2496,384]{1,0:T(8,128)(2,1)} %copy-done.81, f32[985,384]{1,0:T(8,128)} %constant_dynamic-slice_fusion.7.middle_ref, bf16[985,384]{1,0:T(8,128)(2,1)} %constant_dynamic-slice_fusion.6.grad_ref, f32[985,2]{1,0:T(8,128)} %copy.185.gates_ref), custom_call_target="tpu_custom_call" | custom-call | flops 3776348160 | bytes 8000000 | tf_op jit(solution)/shard_map/bring_home/pallas_call | solution.py:155
  537.3 6.7 sum_home.1
  544.0 14.3 %collective-permute-done.52 = f32[2,985]{0,1:T(8,128)S(1)} collective-permute-done((f32[2,985]{0,1:T(8,128)S(1)}, f32[2,985]{0,1:T(8,128)S(1)}, u32[]{:S(2)}, u32[]{:S(2)}) %collective-permute-start.52) | collective-permute-done | bytes 7912 | tf_op jit(solution)/shard_map/ppermute | solution.py:44
  560.4 14.1 %collective-permute-done.51 = bf16[985,384]{1,0:T(8,128)(2,1)S(1)} collective-permute-done((bf16[985,384]{1,0:T(8,128)(2,1)}, bf16[985,384]{1,0:T(8,128)(2,1)S(1)}, u32[]{:S(2)}, u32[]{:S(2)}) %collective-permute-start.51) | collective-permute-done | bytes 756512 | tf_op jit(solution)/shard_map/ppermute | solution.py:44
  574.5 4.0 multiply_reduce_fusion.2
  586.2 4.2 copy.188
  590.5 5.0 multiply_reduce_fusion
  614.0 4.1 fusion.117
  632.0 2.9 maximum_select_fusion.4
  644.0 18.0 %collective-permute-done.67 = bf16[48,384]{1,0:T(8,128)(2,1)S(1)} collective-permute-done((bf16[48,384]{1,0:T(8,128)(2,1)S(1)}, bf16[48,384]{1,0:T(8,128)(2,1)S(1)}, u32[]{:S(2)}, u32[]{:S(2)}) %collective-permute-start.67) | collective-permute-done | bytes 36896 | tf_op jit(solution)/shard_map/ppermute | solution.py:44
  663.5 3.4 collective-permute-start.62
  683.0 4.7 add_add_fusion.2
  (472 shorter events, 196.1 us)
Async XLA Ops:
  5.1 16.0 %collective-permute-start = (bf16[48,1280]{1,0:T(8,128)(2,1)S(1)}, bf16[48,1280]{1,0:T(8,128)(2,1)S(1)}, u32[]{:S(2)}, u32[]{:S(2)}) collective-permute-start(bf16[48,1280]{1,0:T(8,128)(2,1)S(1)} %pad_maximum_fusion), channel_id=1, source_target_pairs={{0,16},{16,0},{1,17},{17,1},{2,18},{18,2},{3,19},{19,3},{4,20},{20... | collective-permute-start | bytes 368648 | tf_op jit(solution)/shard_map/ppermute | solution.py:44
  12.0 124.1 %collective-permute-start.26 = (bf16[1536,384]{1,0:T(8,128)(2,1)}, bf16[1536,384]{1,0:T(8,128)(2,1)}, u32[]{:S(2)}, u32[]{:S(2)}) collective-permute-start(bf16[1536,384]{1,0:T(8,128)(2,1)} %convert_bitcast_fusion), channel_id=1, source_target_pairs={{0,16},{16,0},{1,17},{17,1},{2,18},{18,2},{3,19},{19,3},{4,20},{20... | collective-permute-start | bytes 3538952 | tf_op jit(solution)/shard_map/ppermute | solution.py:44
  21.1 54.9 %collective-permute-start.1 = (bf16[2,48,1280]{2,1,0:T(8,128)(2,1)S(1)}, bf16[2,48,1280]{2,1,0:T(8,128)(2,1)S(1)}, u32[]{:S(2)}, u32[]{:S(2)}) collective-permute-start(bf16[2,48,1280]{2,1,0:T(8,128)(2,1)S(1)} %maximum_select_fusion.7), channel_id=1, source_target_pairs={{0,2},{2,0},{4,6},{6,4},{8,10},{10,8},{12,14},{14,12},{1,3},{3,1},... | collective-permute-start | bytes 737288 | tf_op jit(solution)/shard_map/ppermute | solution.py:44
  21.2 54.9 %collective-permute-start.2 = (bf16[2,48,1280]{2,1,0:T(8,128)(2,1)S(1)}, bf16[2,48,1280]{2,1,0:T(8,128)(2,1)S(1)}, u32[]{:S(2)}, u32[]{:S(2)}) collective-permute-start(bf16[2,48,1280]{2,1,0:T(8,128)(2,1)S(1)} %maximum_select_fusion.7), channel_id=1, source_target_pairs={{0,4},{2,6},{4,0},{6,2},{8,12},{10,14},{12,8},{14,10},{1,5},{3,7},... | collective-permute-start | bytes 737288 | tf_op jit(solution)/shard_map/ppermute | solution.py:44
  23.0 65.0 %collective-permute-start.4 = (bf16[2,48,1280]{2,1,0:T(8,128)(2,1)S(1)}, bf16[2,48,1280]{2,1,0:T(8,128)(2,1)S(1)}, u32[]{:S(2)}, u32[]{:S(2)}) collective-permute-start(bf16[2,48,1280]{2,1,0:T(8,128)(2,1)S(1)} %maximum_select_fusion.7), channel_id=1, source_target_pairs={{0,8},{2,10},{4,12},{6,14},{8,0},{10,2},{12,4},{14,6},{1,9},{3,11}... | collective-permute-start | bytes 737288 | tf_op jit(solution)/shard_map/ppermute | solution.py:44
  24.6 42.1 %collective-permute-start.9 = (bf16[48,384]{1,0:T(8,128)(2,1)S(1)}, bf16[48,384]{1,0:T(8,128)(2,1)S(1)}, u32[]{:S(2)}, u32[]{:S(2)}) collective-permute-start(bf16[48,384]{1,0:T(8,128)(2,1)S(1)} %get-tuple-element.17), channel_id=1, source_target_pairs={{0,1},{1,0},{2,3},{3,2},{4,5},{5,4},{6,7},{7,6},{8,9},{9,8},{10,11... | collective-permute-start | bytes 110600 | tf_op jit(solution)/shard_map/ppermute | solution.py:44
  73.4 15.1 %collective-permute-start.6 = (bf16[2,48,1280]{2,1,0:T(8,128)(2,1)S(1)}, bf16[2,48,1280]{2,1,0:T(8,128)(2,1)S(1)}, u32[]{:S(2)}, u32[]{:S(2)}) collective-permute-start(bf16[2,48,1280]{2,1,0:T(8,128)(2,1)S(1)} %maximum_select_fusion.7), channel_id=1, source_target_pairs={{0,12},{2,14},{4,8},{6,10},{8,4},{10,6},{12,0},{14,2},{1,13},{3,15... | collective-permute-start | bytes 737288 | tf_op jit(solution)/shard_map/ppermute | solution.py:44
  88.0 110.2 %collective-permute-start.25 = (bf16[384,1536]{1,0:T(8,128)(2,1)}, bf16[384,1536]{1,0:T(8,128)(2,1)}, u32[]{:S(2)}, u32[]{:S(2)}) collective-permute-start(bf16[384,1536]{1,0:T(8,128)(2,1)} %convert_bitcast_fusion.1), channel_id=1, source_target_pairs={{0,16},{16,0},{1,17},{17,1},{2,18},{18,2},{3,19},{19,3},{4,20},{20... | collective-permute-start | bytes 3538952 | tf_op jit(solution)/shard_map/ppermute | solution.py:44
  93.4 41.8 %collective-permute-start.17 = (bf16[2,48,768]{2,1,0:T(8,128)(2,1)}, bf16[2,48,768]{2,1,0:T(8,128)(2,1)}, u32[]{:S(2)}, u32[]{:S(2)}) collective-permute-start(bf16[2,48,768]{2,1,0:T(8,128)(2,1)} %collective-permute-done.16), channel_id=1, source_target_pairs={{0,2},{2,0},{4,6},{6,4},{8,10},{10,8},{12,14},{14,12},{1,3},{3,1},... | collective-permute-start | bytes 442376 | tf_op jit(solution)/shard_map/ppermute | solution.py:44
  132.9 25.6 %collective-permute-start.8 = (bf16[985,384]{1,0:T(8,128)(2,1)}, bf16[985,384]{1,0:T(8,128)(2,1)S(1)}, u32[]{:S(2)}, u32[]{:S(2)}) collective-permute-start(bf16[985,384]{1,0:T(8,128)(2,1)} %copy.176), channel_id=1, source_target_pairs={{0,1},{1,0},{2,3},{3,2},{4,5},{5,4},{6,7},{7,6},{8,9},{9,8},{10,11... | collective-permute-start | bytes 2269448 | tf_op jit(solution)/shard_map/ppermute | solution.py:44
  178.1 23.1 %collective-permute-start.18 = (bf16[312,768]{1,0:T(8,128)(2,1)}, bf16[312,768]{1,0:T(8,128)(2,1)}, u32[]{:S(2)}, u32[]{:S(2)}) collective-permute-start(bf16[312,768]{1,0:T(8,128)(2,1)} %get-tuple-element.52), channel_id=1, source_target_pairs={{0,2},{2,0},{4,6},{6,4},{8,10},{10,8},{12,14},{14,12},{1,3},{3,1},... | collective-permute-start | bytes 1437704 | tf_op jit(solution)/shard_map/ppermute | solution.py:44
  192.7 14.1 %collective-permute-start.19 = (bf16[312,768]{1,0:T(8,128)(2,1)}, bf16[312,768]{1,0:T(8,128)(2,1)}, u32[]{:S(2)}, u32[]{:S(2)}) collective-permute-start(bf16[312,768]{1,0:T(8,128)(2,1)} %get-tuple-element.51), channel_id=1, source_target_pairs={{0,4},{2,6},{4,0},{6,2},{8,12},{10,14},{12,8},{14,10},{1,5},{3,7},... | collective-permute-start | bytes 1437704 | tf_op jit(solution)/shard_map/ppermute | solution.py:44
  194.4 21.8 %collective-permute-start.20 = (bf16[312,768]{1,0:T(8,128)(2,1)}, bf16[312,768]{1,0:T(8,128)(2,1)}, u32[]{:S(2)}, u32[]{:S(2)}) collective-permute-start(bf16[312,768]{1,0:T(8,128)(2,1)} %get-tuple-element.50), channel_id=1, source_target_pairs={{0,6},{2,4},{4,2},{6,0},{8,14},{10,12},{12,10},{14,8},{1,7},{3,5},... | collective-permute-start | bytes 1437704 | tf_op jit(solution)/shard_map/ppermute | solution.py:44
  195.8 22.4 %collective-permute-start.21 = (bf16[312,768]{1,0:T(8,128)(2,1)}, bf16[312,768]{1,0:T(8,128)(2,1)}, u32[]{:S(2)}, u32[]{:S(2)}) collective-permute-start(bf16[312,768]{1,0:T(8,128)(2,1)} %get-tuple-element.49), channel_id=1, source_target_pairs={{0,8},{2,10},{4,12},{6,14},{8,0},{10,2},{12,4},{14,6},{1,9},{3,11}... | collective-permute-start | bytes 1437704 | tf_op jit(solution)/shard_map/ppermute | solution.py:44
  198.2 41.1 %collective-permute-start.22 = (bf16[312,768]{1,0:T(8,128)(2,1)S(1)}, bf16[312,768]{1,0:T(8,128)(2,1)S(1)}, u32[]{:S(2)}, u32[]{:S(2)}) collective-permute-start(bf16[312,768]{1,0:T(8,128)(2,1)S(1)} %get-tuple-element.48), channel_id=1, source_target_pairs={{0,10},{2,8},{4,14},{6,12},{8,2},{10,0},{12,6},{14,4},{1,11},{3,9}... | collective-permute-start | bytes 1437704 | tf_op jit(solution)/shard_map/ppermute | solution.py:44
  201.3 38.9 %collective-permute-start.23 = (bf16[312,768]{1,0:T(8,128)(2,1)S(1)}, bf16[312,768]{1,0:T(8,128)(2,1)S(1)}, u32[]{:S(2)}, u32[]{:S(2)}) collective-permute-start(bf16[312,768]{1,0:T(8,128)(2,1)S(1)} %get-tuple-element.47), channel_id=1, source_target_pairs={{0,12},{2,14},{4,8},{6,10},{8,4},{10,6},{12,0},{14,2},{1,13},{3,15... | collective-permute-start | bytes 1437704 | tf_op jit(solution)/shard_map/ppermute | solution.py:44
  206.9 34.9 %collective-permute-start.24 = (bf16[312,768]{1,0:T(8,128)(2,1)S(1)}, bf16[312,768]{1,0:T(8,128)(2,1)S(1)}, u32[]{:S(2)}, u32[]{:S(2)}) collective-permute-start(bf16[312,768]{1,0:T(8,128)(2,1)S(1)} %get-tuple-element.46), channel_id=1, source_target_pairs={{0,14},{2,12},{4,10},{6,8},{8,6},{10,4},{12,2},{14,0},{1,15},{3,13... | collective-permute-start | bytes 1437704 | tf_op jit(solution)/shard_map/ppermute | solution.py:44
  216.2 65.8 %collective-permute-start.36 = (bf16[312,768]{1,0:T(8,128)(2,1)S(1)}, bf16[312,768]{1,0:T(8,128)(2,1)S(1)}, u32[]{:S(2)}, u32[]{:S(2)}) collective-permute-start(bf16[312,768]{1,0:T(8,128)(2,1)S(1)} %get-tuple-element.45), channel_id=1, source_target_pairs={{0,2},{2,0},{4,6},{6,4},{8,10},{10,8},{12,14},{14,12},{1,3},{3,1},... | collective-permute-start | bytes 1437704 | tf_op jit(solution)/shard_map/ppermute | solution.py:44
  218.2 65.9 %collective-permute-start.37 = (bf16[312,768]{1,0:T(8,128)(2,1)}, bf16[312,768]{1,0:T(8,128)(2,1)S(1)}, u32[]{:S(2)}, u32[]{:S(2)}) collective-permute-start(bf16[312,768]{1,0:T(8,128)(2,1)} %get-tuple-element.44), channel_id=1, source_target_pairs={{0,4},{2,6},{4,0},{6,2},{8,12},{10,14},{12,8},{14,10},{1,5},{3,7},... | collective-permute-start | bytes 1437704 | tf_op jit(solution)/shard_map/ppermute | solution.py:44
  239.3 45.7 %collective-permute-start.38 = (bf16[312,768]{1,0:T(8,128)(2,1)}, bf16[312,768]{1,0:T(8,128)(2,1)S(1)}, u32[]{:S(2)}, u32[]{:S(2)}) collective-permute-start(bf16[312,768]{1,0:T(8,128)(2,1)} %get-tuple-element.43), channel_id=1, source_target_pairs={{0,6},{2,4},{4,2},{6,0},{8,14},{10,12},{12,10},{14,8},{1,7},{3,5},... | collective-permute-start | bytes 1437704 | tf_op jit(solution)/shard_map/ppermute | solution.py:44
  240.2 45.0 %collective-permute-start.39 = (bf16[312,768]{1,0:T(8,128)(2,1)}, bf16[312,768]{1,0:T(8,128)(2,1)S(1)}, u32[]{:S(2)}, u32[]{:S(2)}) collective-permute-start(bf16[312,768]{1,0:T(8,128)(2,1)} %get-tuple-element.42), channel_id=1, source_target_pairs={{0,8},{2,10},{4,12},{6,14},{8,0},{10,2},{12,4},{14,6},{1,9},{3,11}... | collective-permute-start | bytes 1437704 | tf_op jit(solution)/shard_map/ppermute | solution.py:44
  241.8 43.4 %collective-permute-start.40 = (bf16[312,768]{1,0:T(8,128)(2,1)}, bf16[312,768]{1,0:T(8,128)(2,1)S(1)}, u32[]{:S(2)}, u32[]{:S(2)}) collective-permute-start(bf16[312,768]{1,0:T(8,128)(2,1)} %get-tuple-element.41), channel_id=1, source_target_pairs={{0,10},{2,8},{4,14},{6,12},{8,2},{10,0},{12,6},{14,4},{1,11},{3,9}... | collective-permute-start | bytes 1437704 | tf_op jit(solution)/shard_map/ppermute | solution.py:44
  282.0 14.8 %collective-permute-start.41 = (bf16[312,768]{1,0:T(8,128)(2,1)S(1)}, bf16[312,768]{1,0:T(8,128)(2,1)S(1)}, u32[]{:S(2)}, u32[]{:S(2)}) collective-permute-start(bf16[312,768]{1,0:T(8,128)(2,1)S(1)} %get-tuple-element.40), channel_id=1, source_target_pairs={{0,12},{2,14},{4,8},{6,10},{8,4},{10,6},{12,0},{14,2},{1,13},{3,15... | collective-permute-start | bytes 1437704 | tf_op jit(solution)/shard_map/ppermute | solution.py:44
  284.1 22.2 %collective-permute-start.42 = (bf16[312,768]{1,0:T(8,128)(2,1)S(1)}, bf16[312,768]{1,0:T(8,128)(2,1)S(1)}, u32[]{:S(2)}, u32[]{:S(2)}) collective-permute-start(bf16[312,768]{1,0:T(8,128)(2,1)S(1)} %get-tuple-element.39), channel_id=1, source_target_pairs={{0,14},{2,12},{4,10},{6,8},{8,6},{10,4},{12,2},{14,0},{1,15},{3,13... | collective-permute-start | bytes 1437704 | tf_op jit(solution)/shard_map/ppermute | solution.py:44
  338.0 53.6 %collective-permute-start.68 = (bf16[384,1536]{1,0:T(8,128)(2,1)S(1)}, bf16[384,1536]{1,0:T(8,128)(2,1)S(1)}, u32[]{:S(2)}, u32[]{:S(2)}) collective-permute-start(bf16[384,1536]{1,0:T(8,128)(2,1)S(1)} %dynamic-slice_convert_fusion.1), channel_id=1, source_target_pairs={{0,16},{16,0},{1,17},{17,1},{2,18},{18,2},{3,19},{19,3},{4,20},{20... | collective-permute-start | bytes 3538952 | tf_op jit(solution)/shard_map/ppermute | solution.py:44
  351.6 95.2 %collective-permute-start.27 = (bf16[2496,384]{1,0:T(8,128)(2,1)S(1)}, bf16[2496,384]{1,0:T(8,128)(2,1)S(1)}, u32[]{:S(2)}, u32[]{:S(2)}) collective-permute-start(bf16[2496,384]{1,0:T(8,128)(2,1)S(1)} %convolution_convert_fusion.1), channel_id=1, source_target_pairs={{0,1},{1,0},{2,3},{3,2},{4,5},{5,4},{6,7},{7,6},{8,9},{9,8},{10,11... | collective-permute-start | bytes 5750792 | tf_op jit(solution)/shard_map/ppermute | solution.py:44
  353.7 88.5 %collective-permute-start.69 = (bf16[1536,384]{1,0:T(8,128)(2,1)S(1)}, bf16[1536,384]{1,0:T(8,128)(2,1)S(1)}, u32[]{:S(2)}, u32[]{:S(2)}) collective-permute-start(bf16[1536,384]{1,0:T(8,128)(2,1)S(1)} %dynamic-slice_convert_fusion), channel_id=1, source_target_pairs={{0,16},{16,0},{1,17},{17,1},{2,18},{18,2},{3,19},{19,3},{4,20},{20... | collective-permute-start | bytes 3538952 | tf_op jit(solution)/shard_map/ppermute | solution.py:44
  362.1 124.9 %collective-permute-start.43 = (bf16[2496,384]{1,0:T(8,128)(2,1)S(1)}, bf16[2496,384]{1,0:T(8,128)(2,1)S(1)}, u32[]{:S(2)}, u32[]{:S(2)}) collective-permute-start(bf16[2496,384]{1,0:T(8,128)(2,1)S(1)} %convolution_convert_fusion), channel_id=1, source_target_pairs={{0,1},{1,0},{2,3},{3,2},{4,5},{5,4},{6,7},{7,6},{8,9},{9,8},{10,11... | collective-permute-start | bytes 5750792 | tf_op jit(solution)/shard_map/ppermute | solution.py:44
  451.3 44.6 %collective-permute-start.28 = (bf16[312,384]{1,0:T(8,128)(2,1)S(1)}, bf16[312,384]{1,0:T(8,128)(2,1)S(1)}, u32[]{:S(2)}, u32[]{:S(2)}) collective-permute-start(bf16[312,384]{1,0:T(8,128)(2,1)S(1)} %get-tuple-element.67), channel_id=1, source_target_pairs={{0,2},{2,0},{4,6},{6,4},{8,10},{10,8},{12,14},{14,12},{1,3},{3,1},... | collective-permute-start | bytes 718856 | tf_op jit(solution)/shard_map/ppermute | solution.py:44
  451.4 46.6 %collective-permute-start.29 = (bf16[312,384]{1,0:T(8,128)(2,1)S(1)}, bf16[312,384]{1,0:T(8,128)(2,1)S(1)}, u32[]{:S(2)}, u32[]{:S(2)}) collective-permute-start(bf16[312,384]{1,0:T(8,128)(2,1)S(1)} %get-tuple-element.66), channel_id=1, source_target_pairs={{0,4},{2,6},{4,0},{6,2},{8,12},{10,14},{12,8},{14,10},{1,5},{3,7},... | collective-permute-start | bytes 718856 | tf_op jit(solution)/shard_map/ppermute | solution.py:44
  453.2 46.4 %collective-permute-start.30 = (bf16[312,384]{1,0:T(8,128)(2,1)S(1)}, bf16[312,384]{1,0:T(8,128)(2,1)S(1)}, u32[]{:S(2)}, u32[]{:S(2)}) collective-permute-start(bf16[312,384]{1,0:T(8,128)(2,1)S(1)} %get-tuple-element.65), channel_id=1, source_target_pairs={{0,6},{2,4},{4,2},{6,0},{8,14},{10,12},{12,10},{14,8},{1,7},{3,5},... | collective-permute-start | bytes 718856 | tf_op jit(solution)/shard_map/ppermute | solution.py:44
  453.3 46.5 %collective-permute-start.31 = (bf16[312,384]{1,0:T(8,128)(2,1)S(1)}, bf16[312,384]{1,0:T(8,128)(2,1)S(1)}, u32[]{:S(2)}, u32[]{:S(2)}) collective-permute-start(bf16[312,384]{1,0:T(8,128)(2,1)S(1)} %get-tuple-element.64), channel_id=1, source_target_pairs={{0,8},{2,10},{4,12},{6,14},{8,0},{10,2},{12,4},{14,6},{1,9},{3,11}... | collective-permute-start | bytes 718856 | tf_op jit(solution)/shard_map/ppermute | solution.py:44
  487.1 14.2 %collective-permute-start.32 = (bf16[312,384]{1,0:T(8,128)(2,1)S(1)}, bf16[312,384]{1,0:T(8,128)(2,1)S(1)}, u32[]{:S(2)}, u32[]{:S(2)}) collective-permute-start(bf16[312,384]{1,0:T(8,128)(2,1)S(1)} %get-tuple-element.63), channel_id=1, source_target_pairs={{0,10},{2,8},{4,14},{6,12},{8,2},{10,0},{12,6},{14,4},{1,11},{3,9}... | collective-permute-start | bytes 718856 | tf_op jit(solution)/shard_map/ppermute | solution.py:44
  498.0 13.1 %collective-permute-start.34 = (bf16[312,384]{1,0:T(8,128)(2,1)S(1)}, bf16[312,384]{1,0:T(8,128)(2,1)S(1)}, u32[]{:S(2)}, u32[]{:S(2)}) collective-permute-start(bf16[312,384]{1,0:T(8,128)(2,1)S(1)} %get-tuple-element.61), channel_id=1, source_target_pairs={{0,14},{2,12},{4,10},{6,8},{8,6},{10,4},{12,2},{14,0},{1,15},{3,13... | collective-permute-start | bytes 718856 | tf_op jit(solution)/shard_map/ppermute | solution.py:44
  499.6 23.9 %collective-permute-start.44 = (bf16[312,384]{1,0:T(8,128)(2,1)S(1)}, bf16[312,384]{1,0:T(8,128)(2,1)S(1)}, u32[]{:S(2)}, u32[]{:S(2)}) collective-permute-start(bf16[312,384]{1,0:T(8,128)(2,1)S(1)} %get-tuple-element.59), channel_id=1, source_target_pairs={{0,2},{2,0},{4,6},{6,4},{8,10},{10,8},{12,14},{14,12},{1,3},{3,1},... | collective-permute-start | bytes 718856 | tf_op jit(solution)/shard_map/ppermute | solution.py:44
  499.8 26.1 %collective-permute-start.45 = (bf16[312,384]{1,0:T(8,128)(2,1)S(1)}, bf16[312,384]{1,0:T(8,128)(2,1)S(1)}, u32[]{:S(2)}, u32[]{:S(2)}) collective-permute-start(bf16[312,384]{1,0:T(8,128)(2,1)S(1)} %get-tuple-element.58), channel_id=1, source_target_pairs={{0,4},{2,6},{4,0},{6,2},{8,12},{10,14},{12,8},{14,10},{1,5},{3,7},... | collective-permute-start | bytes 718856 | tf_op jit(solution)/shard_map/ppermute | solution.py:44
  501.2 26.1 %collective-permute-start.46 = (bf16[312,384]{1,0:T(8,128)(2,1)S(1)}, bf16[312,384]{1,0:T(8,128)(2,1)S(1)}, u32[]{:S(2)}, u32[]{:S(2)}) collective-permute-start(bf16[312,384]{1,0:T(8,128)(2,1)S(1)} %get-tuple-element.57), channel_id=1, source_target_pairs={{0,6},{2,4},{4,2},{6,0},{8,14},{10,12},{12,10},{14,8},{1,7},{3,5},... | collective-permute-start | bytes 718856 | tf_op jit(solution)/shard_map/ppermute | solution.py:44
  505.3 22.9 %collective-permute-start.47 = (bf16[312,384]{1,0:T(8,128)(2,1)S(1)}, bf16[312,384]{1,0:T(8,128)(2,1)S(1)}, u32[]{:S(2)}, u32[]{:S(2)}) collective-permute-start(bf16[312,384]{1,0:T(8,128)(2,1)S(1)} %get-tuple-element.56), channel_id=1, source_target_pairs={{0,8},{2,10},{4,12},{6,14},{8,0},{10,2},{12,4},{14,6},{1,9},{3,11}... | collective-permute-start | bytes 718856 | tf_op jit(solution)/shard_map/ppermute | solution.py:44
  511.0 19.9 %collective-permute-start.48 = (bf16[312,384]{1,0:T(8,128)(2,1)S(1)}, bf16[312,384]{1,0:T(8,128)(2,1)}, u32[]{:S(2)}, u32[]{:S(2)}) collective-permute-start(bf16[312,384]{1,0:T(8,128)(2,1)S(1)} %get-tuple-element.55), channel_id=1, source_target_pairs={{0,10},{2,8},{4,14},{6,12},{8,2},{10,0},{12,6},{14,4},{1,11},{3,9}... | collective-permute-start | bytes 718856 | tf_op jit(solution)/shard_map/ppermute | solution.py:44
  527.4 104.1 %collective-permute-start.35 = (bf16[985,384]{1,0:T(8,128)(2,1)}, bf16[985,384]{1,0:T(8,128)(2,1)}, u32[]{:S(2)}, u32[]{:S(2)}) collective-permute-start(bf16[985,384]{1,0:T(8,128)(2,1)} %get-tuple-element.19), channel_id=1, source_target_pairs={{0,1},{1,0},{2,3},{3,2},{4,5},{5,4},{6,7},{7,6},{8,9},{9,8},{10,11... | collective-permute-start | bytes 2269448 | tf_op jit(solution)/shard_map/ppermute | solution.py:44
  528.1 30.3 %collective-permute-start.52 = (f32[2,985]{0,1:T(8,128)S(1)}, f32[2,985]{0,1:T(8,128)S(1)}, u32[]{:S(2)}, u32[]{:S(2)}) collective-permute-start(f32[2,985]{0,1:T(8,128)S(1)} %slice_bitcast_fusion), channel_id=1, source_target_pairs={{0,1},{1,0},{2,3},{3,2},{4,5},{5,4},{6,7},{7,6},{8,9},{9,8},{10,11... | collective-permute-start | bytes 23648 | tf_op jit(solution)/shard_map/ppermute | solution.py:44
  544.0 30.5 %collective-permute-start.51 = (bf16[985,384]{1,0:T(8,128)(2,1)}, bf16[985,384]{1,0:T(8,128)(2,1)S(1)}, u32[]{:S(2)}, u32[]{:S(2)}) collective-permute-start(bf16[985,384]{1,0:T(8,128)(2,1)} %sum_home.1), channel_id=1, source_target_pairs={{0,1},{1,0},{2,3},{3,2},{4,5},{5,4},{6,7},{7,6},{8,9},{9,8},{10,11... | collective-permute-start | bytes 2269448 | tf_op jit(solution)/shard_map/ppermute | solution.py:44
  620.9 18.2 %collective-permute-start.58 = (bf16[2,4,48,1152]{3,2,0,1:T(8,128)(2,1)}, bf16[2,4,48,1152]{3,2,0,1:T(8,128)(2,1)}, u32[]{:S(2)}, u32[]{:S(2)}) collective-permute-start(bf16[2,4,48,1152]{3,2,0,1:T(8,128)(2,1)} %fusion.41), channel_id=1, source_target_pairs={{0,2},{2,0},{4,6},{6,4},{8,10},{10,8},{12,14},{14,12},{1,3},{3,1},... | collective-permute-start | bytes 2654216 | tf_op jit(solution)/shard_map/ppermute | solution.py:44
  628.1 38.8 %collective-permute-start.53 = (bf16[985,768]{1,0:T(8,128)(2,1)S(1)}, bf16[985,768]{1,0:T(8,128)(2,1)S(1)}, u32[]{:S(2)}, u32[]{:S(2)}) collective-permute-start(bf16[985,768]{1,0:T(8,128)(2,1)S(1)} %fusion.24), channel_id=1, source_target_pairs={{0,1},{1,0},{2,3},{3,2},{4,5},{5,4},{6,7},{7,6},{8,9},{9,8},{10,11... | collective-permute-start | bytes 4538888 | tf_op jit(solution)/shard_map/ppermute | solution.py:44
  636.2 25.9 %collective-permute-start.67 = (bf16[48,384]{1,0:T(8,128)(2,1)S(1)}, bf16[48,384]{1,0:T(8,128)(2,1)S(1)}, u32[]{:S(2)}, u32[]{:S(2)}) collective-permute-start(bf16[48,384]{1,0:T(8,128)(2,1)S(1)} %fusion.72), channel_id=1, source_target_pairs={{0,16},{16,0},{1,17},{17,1},{2,18},{18,2},{3,19},{19,3},{4,20},{20... | collective-permute-start | bytes 110600 | tf_op jit(solution)/shard_map/ppermute | solution.py:44
  640.5 22.2 %collective-permute-start.61 = (bf16[2,48,1152]{2,1,0:T(8,128)(2,1)S(1)}, bf16[2,48,1152]{2,1,0:T(8,128)(2,1)S(1)}, u32[]{:S(2)}, u32[]{:S(2)}) collective-permute-start(bf16[2,48,1152]{2,1,0:T(8,128)(2,1)S(1)} %get-tuple-element.70), channel_id=1, source_target_pairs={{0,12},{2,14},{4,8},{6,10},{8,4},{10,6},{12,0},{14,2},{1,13},{3,15... | collective-permute-start | bytes 663560 | tf_op jit(solution)/shard_map/ppermute | solution.py:44
  642.1 20.7 %collective-permute-start.60 = (bf16[2,48,1152]{2,1,0:T(8,128)(2,1)S(1)}, bf16[2,48,1152]{2,1,0:T(8,128)(2,1)S(1)}, u32[]{:S(2)}, u32[]{:S(2)}) collective-permute-start(bf16[2,48,1152]{2,1,0:T(8,128)(2,1)S(1)} %get-tuple-element.71), channel_id=1, source_target_pairs={{0,8},{2,10},{4,12},{6,14},{8,0},{10,2},{12,4},{14,6},{1,9},{3,11}... | collective-permute-start | bytes 663560 | tf_op jit(solution)/shard_map/ppermute | solution.py:44
  643.4 19.4 %collective-permute-start.59 = (bf16[2,48,1152]{2,1,0:T(8,128)(2,1)S(1)}, bf16[2,48,1152]{2,1,0:T(8,128)(2,1)S(1)}, u32[]{:S(2)}, u32[]{:S(2)}) collective-permute-start(bf16[2,48,1152]{2,1,0:T(8,128)(2,1)S(1)} %get-tuple-element.69), channel_id=1, source_target_pairs={{0,4},{2,6},{4,0},{6,2},{8,12},{10,14},{12,8},{14,10},{1,5},{3,7},... | collective-permute-start | bytes 663560 | tf_op jit(solution)/shard_map/ppermute | solution.py:44
  (109 other events, 1545.6 us)

commit v2 on v1

v2 whole, which is shorter than its diff:
```python
import functools

import jax
import jax.numpy as jnp
from jax import lax
from jax.experimental import pallas as pl
from jax.experimental.pallas import tpu as pltpu
from jax.sharding import PartitionSpec as P

D = 768
HALF = 384
HEADS = 12
SEQ = 197
ROWS = 208
HEAD = D // HEADS
SCALE = HEAD ** (-0.5)
EPSILON = 1e-06
HIGH = lax.Precision.HIGHEST
BF = jnp.bfloat16
F32 = jnp.float32
LANES = 128
TILE = 512
CHUNKS = 4
TAIL_RATE = 0.305
TAIL = (
    0.12163973686996697,
    0.12246675128071258,
    0.10342128505066615,
    0.12102026121907625,
    -0.03797407148483761,
    0.1857138128109823,
    -0.15298645906475614,
    0.03669873020693663,
)
DENSITY = 0.3989422804014327


def hop(value, axis, offset):
    count = lax.axis_size(axis)
    return lax.ppermute(value, axis, [(i, i ^ offset) for i in range(count)])


class Order:
    def __init__(self):
        self.token = lax.create_token()

    def after(self, value):
        return lax.optimization_barrier((self.token, value))[1]

    def wait(self, value):
        self.token, value = lax.optimization_barrier((self.token, value))
        return value

    def run(self, function, *operands):
        return self.wait(function(*self.after(operands)))


def follow(value, first):
    token = lax.optimization_barrier((lax.create_token(), first))[0]
    return lax.optimization_barrier((token, value))[1]


def dot_nn(a, b):
    return lax.dot_general(a, b, (((1,), (0,)), ((), ())), preferred_element_type=F32)


def dot_nt(a, b):
    return lax.dot_general(a, b, (((1,), (1,)), ((), ())), preferred_element_type=F32)


def dot_tn(a, b):
    return lax.dot_general(a, b, (((0,), (0,)), ((), ())), preferred_element_type=F32)


def cost(flops=1000):
    return pl.CostEstimate(flops=flops, bytes_accessed=1000, transcendentals=0)


def image(width, lo=0):
    return pl.BlockSpec((1, ROWS, width), lambda i, *_: (i + lo, 0, 0))


def images(count, width, kind):
    return jax.ShapeDtypeStruct((count, ROWS, width), kind)


ANY = pl.BlockSpec(memory_space=pl.ANY)


def whole(shape):
    zeros = (0,) * len(shape)
    return pl.BlockSpec(shape, lambda *_: zeros)


def cross(shard):
    across = hop(shard, "dp", 1)
    mine = lax.axis_index("dp") == 0
    return jnp.where(mine, jnp.stack([shard, across]), jnp.stack([across, shard]))


def assemble_kernel(here_ref, same_ref, flip_ref, *out_refs):
    chips, _, rows, _ = same_ref.shape
    for chip in range(chips):
        for b, ref in enumerate((same_ref, flip_ref)):
            place = here_ref[0] ^ (2 * chip + b)
            for d in range(2):
                at = pl.ds(pl.multiple_of((d * 2 * chips + place) * rows, 16), rows)
                lo = 0
                for out_ref in out_refs:
                    out_ref[at, :] = ref[chip, d, :, lo : lo + out_ref.shape[1]]
                    lo += out_ref.shape[1]


def assemble(same, flipped, widths):
    chips, _, rows, columns = same.shape
    here = lax.axis_index("expert").astype(jnp.int32)
    if rows % 16 == 0:
        return pl.pallas_call(
            assemble_kernel,
            grid_spec=pltpu.PrefetchScalarGridSpec(
                num_scalar_prefetch=1,
                grid=(1,),
                in_specs=[whole(same.shape), whole(same.shape)],
                out_specs=[whole((4 * chips * rows, w)) for w in widths],
            ),
            out_shape=[jax.ShapeDtypeStruct((4 * chips * rows, w), same.dtype) for w in widths],
            name="assemble",
            cost_estimate=cost(),
        )(here.reshape(1), same, flipped)
    buffer = jnp.zeros((2, 2 * chips, rows, columns), same.dtype)
    for j in range(chips):
        for b, both in enumerate((same, flipped)):
            buffer = lax.dynamic_update_slice(buffer, both[j][:, None], (0, here ^ (2 * j + b), 0, 0))
    buffer = buffer.reshape(-1, columns)
    cuts = [sum(widths[:n]) for n in range(len(widths) + 1)]
    return [buffer[:, cuts[n] : cuts[n + 1]] for n in range(len(widths))]


def chip_copies(pair):
    count = lax.axis_size("expert")
    return [pair] + [hop(pair, "expert", k) for k in range(2, count, 2)]


def scatter_sum(grad, wide):
    count = lax.axis_size("expert")
    here_dp = lax.axis_index("dp")
    here = lax.axis_index("expert")
    core = here & 1
    chip = here >> 1
    blocks = grad.reshape((2, count // 2, 2, -1) + grad.shape[1:])
    pick = lambda array, index, axis: lax.dynamic_index_in_dim(array, index, axis, False)
    total = pick(blocks, core, 2) + hop(
        pick(blocks, 1 - core, 2).astype(wide), "expert", 1
    ).astype(F32)
    summed = pick(total, chip, 1)
    for k in range(1, count // 2):
        summed = summed + hop(pick(total, chip ^ k, 1).astype(wide), "expert", 2 * k).astype(F32)
    return pick(summed, here_dp, 0), pick(summed, 1 - here_dp, 0).astype(wide)


def normed(values):
    average = jnp.mean(values, axis=-1, keepdims=True)
    centred = values - average
    variance = jnp.mean(centred * centred, axis=-1, keepdims=True)
    scale = lax.rsqrt(variance + EPSILON)
    return centred * scale, scale


def attend_kernel(x_ref, vec_ref, w_ref, *refs):
    a_ref, qkv_ref, o_ref, lse_ref, part_ref = refs[-5:]
    hat, _ = normed(x_ref[0].astype(F32))
    a = (hat * vec_ref[0:1, :] + vec_ref[1:2, :]).astype(BF)
    a_ref[0] = a
    qkv_ref[0] = dot_nn(a, w_ref[...]).astype(BF)
    keys_in = lax.broadcasted_iota(jnp.int32, (ROWS, ROWS), 1) < SEQ
    lane = lax.broadcasted_iota(jnp.int32, (ROWS, LANES), 1)
    lse = jnp.zeros((ROWS, LANES), F32)
    for h in range(HALF // HEAD):
        at = h * HEAD
        q = qkv_ref[0, :, at : at + HEAD]
        k = qkv_ref[0, :, HALF + at : HALF + at + HEAD]
        v = qkv_ref[0, :, 2 * HALF + at : 2 * HALF + at + HEAD]
        s = jnp.where(keys_in, dot_nt(q, k) * SCALE, -1e30)
        top = jnp.max(s, axis=1, keepdims=True)
        total = top + jnp.log(jnp.sum(jnp.exp(s - top), axis=1, keepdims=True))
        weights = jnp.exp(s - total).astype(BF)
        part_ref[0, :, at : at + HEAD] = dot_nn(weights, v).astype(BF)
        lse = jnp.where(lane == h, total, lse)
    lse_ref[0] = lse
    o_ref[0] = part_ref[0]


def attend(x, vectors, weight, lo, hi, held):
    total = x.shape[0]
    return pl.pallas_call(
        attend_kernel,
        grid=(hi - lo,),
        in_specs=[image(D, lo), whole(vectors.shape), whole(weight.shape)] + [ANY] * len(held),
        out_specs=[image(D, lo), image(3 * HALF, lo), image(HALF, lo), image(LANES, lo), image(HALF)],
        out_shape=[
            images(total, D, BF),
            images(total, 3 * HALF, BF),
            images(total, HALF, BF),
            images(total, LANES, F32),
            images(hi - lo, HALF, BF),
        ],
        input_output_aliases={3 + n: n for n in range(len(held))},
        name="attend",
        cost_estimate=cost(),
    )(x, vectors, weight, *held)


def route_kernel(
    which_ref, x_ref, own_ref, got_ref, vec_ref, out_w_ref, router_ref, ids_ref, *refs, count
):
    y_ref, r_ref, g_ref, h_ref = refs[-4:]
    y = x_ref[0].astype(F32) + (
        dot_nt(own_ref[0], out_w_ref[:, :HALF]) + dot_nt(got_ref[0], out_w_ref[:, HALF:])
    )
    y_ref[0] = y
    hat, _ = normed(y)
    h = (hat * vec_ref[2:3, :] + vec_ref[3:4, :]).astype(BF)
    first = which_ref[0] == 0
    h_ref[0, :, :HALF] = jnp.where(first, h[:, :HALF], h[:, HALF:])
    h_ref[0, :, HALF:] = jnp.where(first, h[:, HALF:], h[:, :HALF])
    lane = lax.broadcasted_iota(jnp.int32, (ROWS, LANES), 1)
    logits = jnp.where(lane < count, dot_nn(h, router_ref[...]), -1e30)
    logits = jnp.exp(logits - jnp.max(logits, axis=1, keepdims=True))
    probs = logits / jnp.sum(logits, axis=1, keepdims=True)
    r_ref[0] = probs
    gates = jnp.zeros((ROWS, LANES), F32)
    for c in range(2):
        gate = jnp.sum(jnp.where(lane == ids_ref[0, :, c : c + 1], probs, 0.0), axis=1, keepdims=True)
        gates = jnp.where(lane == c, gate, gates)
    g_ref[0] = gates


def route(which, x, own, got, vectors, out_w, router, ids, count, lo, hi, held):
    total = x.shape[0]
    return pl.pallas_call(
        functools.partial(route_kernel, count=count),
        grid_spec=pltpu.PrefetchScalarGridSpec(
            num_scalar_prefetch=1,
            grid=(hi - lo,),
            in_specs=[
                image(D, lo),
                image(HALF),
                image(HALF),
                whole(vectors.shape),
                whole(out_w.shape),
                whole(router.shape),
                image(2, lo),
            ]
            + [ANY] * len(held),
            out_specs=[image(D, lo), image(LANES, lo), image(LANES, lo), image(D)],
        ),
        out_shape=[
            images(total, D, F32),
            images(total, LANES, F32),
            images(total, LANES, F32),
            images(hi - lo, D, BF),
        ],
        input_output_aliases={8 + n: n for n in range(len(held))},
        name="route",
        cost_estimate=cost(),
    )(which, x, own, got, vectors, out_w, router, ids, *held)


def send_kernel(*refs, parts, chips, gated):
    per = 3 if gated else 2
    groups = [refs[n * per * parts : (n + 1) * per * parts] for n in range(2)]
    out_refs = refs[2 * per * parts :]
    capacity = out_refs[0].shape[1]
    for out_ref, chip in zip(out_refs, chips):
        for r in range(2):
            rows, values, gates = (groups[r][n * parts : (n + 1) * parts] for n in range(3))
            places = lax.broadcasted_iota(jnp.int32, (capacity, 1), 0) + (2 * chip + r) * capacity
            picked = jnp.zeros((capacity, D), F32)
            weight = jnp.zeros((capacity, 1), F32)
            for n in range(parts):
                first = places == rows[n][0:1, :]
                second = places == rows[n][1:2, :]
                chosen = jnp.where(first | second, 1.0, 0.0).astype(BF)
                picked = picked + dot_nn(chosen, values[n][...])
                if gated:
                    each = jnp.where(
                        first, gates[n][0:1, :], jnp.where(second, gates[n][1:2, :], 0.0)
                    )
                    weight = weight + jnp.sum(each, axis=1, keepdims=True)
            if gated:
                picked = picked * weight
            out_ref[r] = picked.astype(BF)


def send_rows(own, other, capacity, chips, gated):
    operands = [part for group in (own, other) for kind in group for part in kind]
    return pl.pallas_call(
        functools.partial(send_kernel, parts=len(own[0]), chips=chips, gated=gated),
        grid=(1,),
        in_specs=[whole(o.shape) for o in operands],
        out_specs=[whole((2, capacity, D))] * len(chips),
        out_shape=[jax.ShapeDtypeStruct((2, capacity, D), BF)] * len(chips),
        name="send_gated" if gated else "send_rows",
        cost_estimate=cost(),
    )(*operands)


def home_kernel(which_ref, rows_ref, middle_ref, grad_ref, gates_ref, own_ref, other_ref, out_ref, dgate_ref):
    value = middle_ref[0]
    grad = grad_ref[0].astype(F32)
    lane = lax.broadcasted_iota(jnp.int32, (ROWS, LANES), 1)
    found = jnp.zeros((ROWS, LANES), F32)
    chips, capacity = own_ref.shape[:2]
    places = lax.broadcasted_iota(jnp.int32, (1, capacity), 1)
    for c in range(2):
        picked = jnp.zeros((ROWS, HALF), F32)
        for chip in range(chips):
            for r, back_ref in enumerate((own_ref, other_ref)):
                at = rows_ref[0, :, c : c + 1] - (2 * chip + r) * capacity
                chosen = jnp.where(at == places, 1.0, 0.0)
                picked = picked + dot_nn(chosen.astype(BF), back_ref[chip])
        value = value + gates_ref[0, :, c : c + 1] * picked
        dgate = jnp.sum(picked * grad, axis=1, keepdims=True)
        found = jnp.where(lane == c, dgate, found)
    out_ref[0] = value.astype(BF)
    dgate_ref[0] = found


def bring_home(which, rows, middle, grad, gates, own, other):
    total = middle.shape[0]
    part = pl.BlockSpec((1, ROWS, HALF), lambda i, s: (i, 0, s[0]))
    return pl.pallas_call(
        home_kernel,
        grid_spec=pltpu.PrefetchScalarGridSpec(
            num_scalar_prefetch=1,
            grid=(total,),
            in_specs=[image(2), part, part, image(LANES), whole(own.shape), whole(other.shape)],
            out_specs=[image(HALF), image(LANES)],
        ),
        out_shape=[images(total, HALF, BF), images(total, LANES, F32)],
        name="bring_home",
        cost_estimate=cost(),
    )(which, rows, middle, grad, gates, own, other)


def sum_kernel(rows_ref, own_ref, other_ref, out_ref):
    chips, capacity = own_ref.shape[:2]
    places = lax.broadcasted_iota(jnp.int32, (1, capacity), 1)
    total = jnp.zeros((ROWS, HALF), F32)
    for chip in range(chips):
        for r, back_ref in enumerate((own_ref, other_ref)):
            base = (2 * chip + r) * capacity
            chosen = (rows_ref[0, :, 0:1] - base == places) | (rows_ref[0, :, 1:2] - base == places)
            total = total + dot_nn(jnp.where(chosen, 1.0, 0.0).astype(BF), back_ref[chip])
    out_ref[0] = total.astype(BF)


def sum_home(rows, own, other, lo, hi):
    return pl.pallas_call(
        sum_kernel,
        grid=(hi - lo,),
        in_specs=[image(2, lo), whole(own.shape), whole(other.shape)],
        out_specs=image(HALF),
        out_shape=images(hi - lo, HALF, BF),
        name="sum_home",
        cost_estimate=cost(),
    )(rows, own, other)


def gelu_parts(u):
    size = jnp.abs(u)
    t = 1.0 / (1.0 + TAIL_RATE * size)
    poly = jnp.full_like(t, TAIL[-1])
    for c in TAIL[-2::-1]:
        poly = poly * t + c
    bell = jnp.exp(-0.5 * (u * u))
    tail = bell * (t * poly)
    normal = jnp.where(u >= 0.0, 1.0 - tail, tail)
    return u * normal, normal + u * (DENSITY * bell)


def forward_kernel(m_ref, w1h, w1t, w2h, w2t, g_ref, s_ref, zt_ref, zh_ref, acc):
    step = pl.program_id(0)
    last = pl.num_programs(0) - 1
    for b in range(m_ref.shape[0]):
        u = dot_nn(m_ref[b, :, :HALF], w1h[...]) + dot_nn(m_ref[b, :, HALF:], w1t[...])
        g, slope = gelu_parts(u)
        g = g.astype(BF)
        g_ref[b] = g
        s_ref[b] = slope.astype(BF)
        away = dot_nn(g, w2t[...])
        near = dot_nn(g, w2h[...])

        @pl.when(step == 0)
        def _():
            acc[b] = away
            zh_ref[b] = near

        @pl.when(step > 0)
        def _():
            acc[b] += away
            zh_ref[b] += near

        @pl.when(step == last)
        def _():
            zt_ref[b] = acc[b].astype(BF)


def expert_forward(rows, w1h, w1t, w2h, w2t):
    blocks, capacity, _ = rows.shape
    hidden = w1h.shape[1]
    across = pl.BlockSpec((HALF, TILE), lambda i: (0, i))
    down = pl.BlockSpec((TILE, HALF), lambda i: (i, 0))
    wide = pl.BlockSpec((blocks, capacity, TILE), lambda i: (0, 0, i))
    make = lambda w, t: jax.ShapeDtypeStruct((blocks, capacity, w), t)
    return pl.pallas_call(
        forward_kernel,
        grid=(hidden // TILE,),
        in_specs=[whole(rows.shape), across, across, down, down],
        out_specs=[wide, wide] + [whole((blocks, capacity, HALF))] * 2,
        out_shape=[make(hidden, BF), make(hidden, BF), make(HALF, BF), make(HALF, F32)],
        scratch_shapes=[pltpu.VMEM((blocks, capacity, HALF), F32)],
        name="expert_forward",
        cost_estimate=cost(),
    )(rows, w1h, w1t, w2h, w2t)


def backward_kernel(z_ref, s_ref, w1h, w1t, w2h, w2t, u_ref, mt_ref, mh_ref, acc):
    step = pl.program_id(0)
    last = pl.num_programs(0) - 1
    for b in range(z_ref.shape[0]):
        grad = dot_nt(z_ref[b, :, :HALF], w2h[...]) + dot_nt(z_ref[b, :, HALF:], w2t[...])
        grad = (grad * s_ref[b].astype(F32)).astype(BF)
        u_ref[b] = grad
        away = dot_nt(grad, w1t[...])
        near = dot_nt(grad, w1h[...])

        @pl.when(step == 0)
        def _():
            acc[b] = away
            mh_ref[b] = near

        @pl.when(step > 0)
        def _():
            acc[b] += away
            mh_ref[b] += near

        @pl.when(step == last)
        def _():
            mt_ref[b] = acc[b].astype(BF)


def expert_backward(rows, slope, w1h, w1t, w2h, w2t):
    blocks, capacity, _ = rows.shape
    hidden = w1h.shape[1]
    across = pl.BlockSpec((HALF, TILE), lambda i: (0, i))
    down = pl.BlockSpec((TILE, HALF), lambda i: (i, 0))
    wide = pl.BlockSpec((blocks, capacity, TILE), lambda i: (0, 0, i))
    make = lambda w, t: jax.ShapeDtypeStruct((blocks, capacity, w), t)
    return pl.pallas_call(
        backward_kernel,
        grid=(hidden // TILE,),
        in_specs=[whole(rows.shape), wide, across, across, down, down],
        out_specs=[wide] + [whole((blocks, capacity, HALF))] * 2,
        out_shape=[make(hidden, BF), make(HALF, BF), make(HALF, F32)],
        scratch_shapes=[pltpu.VMEM((blocks, capacity, HALF), F32)],
        name="expert_backward",
        cost_estimate=cost(),
    )(rows, slope, w1h, w1t, w2h, w2t)


def outer_kernel(which_ref, *refs, chunks, hidden_first, added):
    wides = refs[:chunks]
    narrows = refs[chunks : 2 * chunks]
    out_ref = refs[-1]
    total = None
    for wide_ref, slim_ref in zip(wides, narrows):
        for b in range(wide_ref.shape[0]):
            slim = slim_ref[b]
            term = dot_tn(wide_ref[b], slim) if hidden_first else dot_tn(slim, wide_ref[b])
            total = term if total is None else total + term
    if added:
        total = total + refs[-2][...].astype(F32)
    out_ref[...] = total.astype(out_ref.dtype)


def outer(which, wides, narrows, hidden_first, extra=None):
    per, capacity, hidden = wides[0].shape
    slim = pl.BlockSpec((per, capacity, HALF), lambda i, s: (0, 0, s[0]))
    if hidden_first:
        shape, out = (hidden, HALF), pl.BlockSpec((TILE, HALF), lambda i, s: (i, 0))
    else:
        shape, out = (HALF, hidden), pl.BlockSpec((HALF, TILE), lambda i, s: (0, i))
    specs = [pl.BlockSpec((per, capacity, TILE), lambda i, s: (0, 0, i))] * len(wides)
    specs += [slim] * len(narrows)
    operands = list(wides) + list(narrows)
    if extra is not None:
        specs.append(out)
        operands.append(extra)
    return pl.pallas_call(
        functools.partial(
            outer_kernel,
            chunks=len(wides),
            hidden_first=hidden_first,
            added=extra is not None,
        ),
        grid_spec=pltpu.PrefetchScalarGridSpec(
            num_scalar_prefetch=1, grid=(hidden // TILE,), in_specs=specs, out_specs=out
        ),
        out_shape=jax.ShapeDtypeStruct(shape, BF if extra is None else F32),
        name="outer_send" if extra is None else "outer_keep",
        cost_estimate=cost(),
    )(which, *operands)


def norm_back(grad, hat, scale, gain):
    inner = grad * gain
    return scale * (
        inner
        - jnp.mean(inner, axis=-1, keepdims=True)
        - hat * jnp.mean(inner * hat, axis=-1, keepdims=True)
    )


def add_sums(ref, grad, hat, first):
    sums = [jnp.sum(grad * hat, axis=0, keepdims=True), jnp.sum(grad, axis=0, keepdims=True)]

    @pl.when(first)
    def _():
        ref[...] = jnp.zeros_like(ref)

    ref[0:1, :] += sums[0]
    ref[1:2, :] += sums[1]


def attend_back_kernel(
    which_ref,
    x_ref,
    y_ref,
    near_ref,
    away_ref,
    rout_ref,
    cot_ref,
    vec_ref,
    out_w_ref,
    qkv_ref,
    lse_ref,
    w_ref,
    *refs,
):
    dy_ref, dyb_ref, dqkv_ref, part_ref, sums2_ref, sums1_ref, att_ref = refs[-7:]
    first = which_ref[0] == 0
    start = pl.program_id(0) == 0
    near = near_ref[0].astype(F32)
    away = away_ref[0].astype(F32)
    grad = rout_ref[0] + jnp.concatenate(
        [jnp.where(first, near, away), jnp.where(first, away, near)], axis=1
    )
    hat, scale = normed(y_ref[0])
    add_sums(sums2_ref, grad, hat, start)
    dy = cot_ref[0].astype(F32) + norm_back(grad, hat, scale, vec_ref[2:3, :])
    dy_ref[0] = dy
    dyb = dy.astype(BF)
    dyb_ref[0] = dyb
    att_ref[...] = dot_nn(dyb, out_w_ref[:, :HALF]).astype(BF)
    keys_in = lax.broadcasted_iota(jnp.int32, (ROWS, ROWS), 1) < SEQ
    for h in range(HALF // HEAD):
        at = h * HEAD
        q = qkv_ref[0, :, at : at + HEAD]
        k = qkv_ref[0, :, HALF + at : HALF + at + HEAD]
        v = qkv_ref[0, :, 2 * HALF + at : 2 * HALF + at + HEAD]
        do = att_ref[:, at : at + HEAD]
        s = jnp.where(keys_in, dot_nt(q, k) * SCALE, -1e30)
        weights = jnp.exp(s - lse_ref[0, :, h : h + 1])
        dv = dot_tn(weights.astype(BF), do)
        dp = dot_nt(do, v)
        ds = (weights * (dp - jnp.sum(weights * dp, axis=1, keepdims=True))).astype(BF)
        dqkv_ref[0, :, at : at + HEAD] = (dot_nn(ds, k) * SCALE).astype(BF)
        dqkv_ref[0, :, HALF + at : HALF + at + HEAD] = (dot_tn(ds, q) * SCALE).astype(BF)
        dqkv_ref[0, :, 2 * HALF + at : 2 * HALF + at + HEAD] = dv.astype(BF)
    part = dot_nt(dqkv_ref[0], w_ref[...])
    part_ref[0] = part.astype(BF)
    hat, _ = normed(x_ref[0].astype(F32))
    add_sums(sums1_ref, part, hat, start)


def attend_back(which, x, y, near, away, rout, cot, vectors, out_w, qkv, lse, weight, lo, hi, held):
    total = y.shape[0]
    return pl.pallas_call(
        attend_back_kernel,
        grid_spec=pltpu.PrefetchScalarGridSpec(
            num_scalar_prefetch=1,
            grid=(hi - lo,),
            in_specs=[
                image(D, lo),
                image(D, lo),
                image(HALF),
                image(HALF),
                image(D, lo),
                image(D, lo),
                whole(vectors.shape),
                whole(out_w.shape),
                image(3 * HALF, lo),
                image(LANES, lo),
                whole(weight.shape),
            ]
            + [ANY] * len(held),
            out_specs=[
                image(D, lo),
                image(D, lo),
                image(3 * HALF, lo),
                image(D),
                whole((8, D)),
                whole((8, D)),
            ],
            scratch_shapes=[pltpu.VMEM((ROWS, HALF), BF)],
        ),
        out_shape=[
            images(total, D, F32),
            images(total, D, BF),
            images(total, 3 * HALF, BF),
            images(hi - lo, D, BF),
            jax.ShapeDtypeStruct((8, D), F32),
            jax.ShapeDtypeStruct((8, D), F32),
        ],
        input_output_aliases={12 + n: n for n in range(len(held))},
        name="attend_back",
        cost_estimate=cost(),
    )(which, x, y, near, away, rout, cot, vectors, out_w, qkv, lse, weight, *held)


def token_kernel(x_ref, own_ref, got_ref, dy_ref, vec_ref, *refs):
    out_ref = refs[-1]
    grad = own_ref[0].astype(F32) + got_ref[0].astype(F32)
    hat, scale = normed(x_ref[0].astype(F32))
    out_ref[0] = dy_ref[0] + norm_back(grad, hat, scale, vec_ref[0:1, :])


def token_back(x, own, got, dy, vectors, lo, hi, held):
    total = x.shape[0]
    return pl.pallas_call(
        token_kernel,
        grid=(hi - lo,),
        in_specs=[image(D, lo), image(D), image(D), image(D, lo), whole(vectors.shape)]
        + [ANY] * len(held),
        out_specs=image(D, lo),
        out_shape=images(total, D, F32),
        input_output_aliases={5 + n: n for n in range(len(held))},
        name="token_back",
        cost_estimate=cost(),
    )(x, own, got, dy, vectors, *held)


def slot_table(routes, expert_count):
    total = routes.shape[0]
    sequence = jnp.transpose(routes).reshape(-1)
    onehot = (sequence[:, None] == jnp.arange(expert_count, dtype=jnp.int32)[None, :]).astype(
        jnp.int32
    )
    before = jnp.cumsum(onehot, axis=0) - onehot
    return jnp.sum(before * onehot, axis=1).reshape(2, total)


def images_of(value, fill=0):
    value = value.reshape(-1, SEQ, value.shape[-1])
    return jnp.pad(value, ((0, 0), (0, ROWS - SEQ), (0, 0)), constant_values=fill)


def on_device(
    tokens,
    cotangent,
    ln1_gain,
    ln1_bias,
    ln2_gain,
    ln2_bias,
    w_query,
    w_key,
    w_value,
    w_out,
    w_router,
    w_in,
    w_back,
    expert_ids,
):
    count = lax.axis_size("expert")
    chips = count // 2
    tok = tokens.shape[0]
    capacity = (10 * tok + 32 * count - 1) // (32 * count) * 8
    pictures = tok // SEQ
    rows_all = pictures * ROWS
    here = lax.axis_index("expert")
    here_dp = lax.axis_index("dp")
    here_t = lax.axis_index("tensor")
    which = here_t.astype(jnp.int32).reshape(1)
    same = here_t == here_dp

    order = Order()

    small = jnp.stack([ln1_gain, ln1_bias, ln2_gain, ln2_bias], axis=1)
    narrow = jnp.concatenate([small, w_router], axis=1)
    narrow = jnp.pad(narrow, ((0, 0), (0, LANES - narrow.shape[1])))
    first_pack = jnp.concatenate([w_query, w_key, w_value, narrow], axis=1).astype(BF)
    out_own = jnp.transpose(w_out).astype(BF)
    pair = cross(first_pack)
    out_both = jnp.concatenate([out_own, hop(follow(out_own, first_pack), "tensor", 1)], axis=1)

    slots = slot_table(follow(expert_ids, out_own), count)
    rows = images_of(jnp.transpose((jnp.transpose(expert_ids) ^ here) * capacity + slots), -1)
    rows_lane = jnp.transpose(rows.reshape(-1, 2))
    ids_pad = images_of(expert_ids, -1)
    x = images_of(follow(tokens, out_own))
    cot = images_of(follow(cotangent, out_own))
    cot_flat = cot.reshape(rows_all, D)
    cot_here = jnp.where(
        here_t == 0, cot_flat, jnp.concatenate([cot_flat[:, HALF:], cot_flat[:, :HALF]], axis=1)
    )
    in_own = follow(w_in, out_own)[0].astype(BF)
    back_own = follow(w_back, out_own)[0].astype(BF)

    pair, out_both = order.wait((pair, out_both))
    out_pair = cross(out_both)
    same_chips = jnp.stack(chip_copies(pair))
    same_chips, x, rows_lane, cot_here = order.wait((same_chips, x, rows_lane, cot_here))
    flipped = hop(same_chips, "expert", 1)
    out_pair = order.wait(out_pair)
    in_other = hop(order.after(in_own), "dp", 1)
    qkv_w, narrow_all = order.run(
        lambda *v: assemble(*v, (3 * HALF, LANES)), same_chips, flipped
    )
    vectors = jnp.pad(jnp.transpose(narrow_all[:, :4]).astype(F32), ((0, 4), (0, 0)))
    router_w = narrow_all[:, 4 : 4 + count]
    router_pad = jnp.pad(router_w, ((0, 0), (0, LANES - count)))
    out_same = jnp.stack(chip_copies(order.after(out_pair)))

    cut = (pictures + 1) // 2
    groups = [(0, cut), (cut, pictures)] if pictures > 1 else [(0, pictures)]
    held, o_parts, got_parts = [], [], []
    for n, (lo, hi) in enumerate(groups):
        *held, o_part = order.run(
            lambda x, v, w, *h: attend(x, v, w, lo, hi, h), x, vectors, qkv_w, *held
        )
        o_parts.append(o_part)
        got_parts.append(hop(o_part, "tensor", 1))
        if n == 0:
            out_same = order.wait(out_same)
            out_flip = hop(out_same, "expert", 1)
    a_rows, qkv, o_rows, lse = held
    (out_w,) = order.run(lambda *v: assemble(*v, (D,)), out_same, out_flip)
    rows_next = hop(order.after(rows_lane), "expert", 1)
    cot_next = hop(order.after(cot_here), "expert", 1)
    rows_next, cot_next = order.wait((rows_next, cot_next))
    in_other = order.wait(in_other)
    back_other = hop(order.after(back_own), "dp", 1)
    w1h, w1t = jnp.where(same, in_own, in_other), jnp.where(same, in_other, in_own)
    held, h_parts, h_next = [], [], []
    for n, (lo, hi) in enumerate(groups):
        *held, h_part = order.run(
            lambda x, o, g, v, w, r, i, *h: route(which, x, o, g, v, w, r, i, count, lo, hi, h),
            x, o_parts[n], got_parts[n], vectors, out_w, router_pad, ids_pad, *held,
        )
        h_parts.append(h_part.reshape(-1, D))
        h_next.append(hop(h_parts[-1], "expert", 1))
    y, probs, gates = held
    probs = probs.reshape(rows_all, LANES)[:, :count]
    gates_lane = jnp.transpose(gates.reshape(rows_all, LANES)[:, :2])
    gates_next = hop(gates_lane, "expert", 1)

    lanes_of = lambda value: [value[:, lo * ROWS : hi * ROWS] for lo, hi in groups]
    own = (lanes_of(rows_lane), h_parts)
    other = (lanes_of(rows_next), h_next)
    far = list(range(1, chips))
    outgoing = order.run(lambda *v: send_rows(*v, capacity, far, False), own, other)
    arrived = [None] + [hop(o, "expert", 2 * c) for o, c in zip(outgoing, far)]
    (arrived[0],) = order.run(lambda *v: send_rows(*v, capacity, [0], False), own, other)
    own = ([rows_lane], [cot_here], [gates_lane])
    other = ([rows_next], [cot_next], [gates_next])
    grad_outgoing = order.run(lambda *v: send_rows(*v, capacity, far, True), own, other)
    grad_arrived = [None] + [hop(o, "expert", 2 * c) for o, c in zip(grad_outgoing, far)]
    (grad_arrived[0],) = order.run(lambda *v: send_rows(*v, capacity, [0], True), own, other)
    w2h, w2t = jnp.where(same, back_own, back_other), jnp.where(same, back_other, back_own)

    hidden, slopes, grads, came_back, grad_home = [], [], [], [], []

    def return_rows(away, near, c):
        value = (near + hop(away, "tensor", 1).astype(F32)).astype(BF)
        return hop(value, "expert", 2 * c) if c else value

    for c in range(chips):
        g, s, zt, zh = order.run(expert_forward, arrived[c], w1h, w1t, w2h, w2t)
        hidden.append(g)
        slopes.append(s)
        came_back.append(return_rows(zt, zh, c))
    for c in range(chips):
        u, mt, mh = order.run(
            expert_backward, grad_arrived[c], slopes[c], w1h, w1t, w2h, w2t
        )
        grads.append(u)
        grad_home.append(return_rows(mt, mh, c))
    send_half = jnp.where(same, 1, 0).astype(jnp.int32).reshape(1)
    back_send = order.run(lambda h, g: outer(send_half, h, g, True), hidden, grad_arrived)
    back_got = hop(back_send, "dp", 1)
    in_send = order.run(lambda g, a: outer(send_half, g, a, False), grads, arrived)
    in_got = hop(follow(in_send, back_got), "dp", 1)

    def settle(parts):
        mine = jnp.stack([p[0] for p in parts])
        return mine, hop(jnp.stack([p[1] for p in parts]), "expert", 1)

    out_half, dgate = order.run(
        lambda *v: bring_home(which, *v), rows, y, cot, gates, *settle(came_back)
    )
    out_other = hop(out_half, "tensor", 1)
    dgate = jnp.transpose(dgate.reshape(rows_all, LANES)[:, :2])
    dgate = jnp.transpose(dgate + hop(dgate, "tensor", 1))
    ids_flat = ids_pad.reshape(rows_all, 2)
    lanes = jnp.arange(count, dtype=jnp.int32)[None, :]
    grad_probs = sum(
        jnp.where(ids_flat[:, c : c + 1] == lanes, dgate[:, c : c + 1], 0.0) for c in range(2)
    )
    grad_logits = probs * (grad_probs - jnp.sum(probs * grad_probs, axis=-1, keepdims=True))
    grad_rout = jnp.dot(grad_logits, jnp.transpose(router_w.astype(F32)), precision=HIGH)
    grad_rout = grad_rout.reshape(pictures, ROWS, D)

    back = settle(grad_home)
    near_parts = []
    for lo, hi in groups:
        near = order.run(lambda *v: sum_home(*v, lo, hi), rows, *back)
        near_parts.append((near, hop(near, "tensor", 1)))
    held, parts, sums, got = [], [], [], []
    for n, (lo, hi) in enumerate(groups):
        *held, part, sums2, sums1 = order.run(
            lambda *v: attend_back(which, *v[:11], lo, hi, v[11:]),
            x, y, *near_parts[n], grad_rout, cot, vectors, out_w, qkv, lse, qkv_w, *held,
        )
        parts.append(part)
        got.append(hop(part, "tensor", 1))
        sums.append(jnp.concatenate([sums1[:2], 0.5 * sums2[:2]], axis=0))
    dy, dyb, dqkv = held
    out_other = order.wait(out_other)

    flat = lambda value: value.reshape(rows_all, -1)
    grad_outw = dot_tn(flat(dyb), flat(o_rows))
    grad_wqkv = dot_tn(flat(a_rows), flat(dqkv))
    shards, leaving = scatter_sum(jnp.concatenate([grad_wqkv, grad_outw], axis=1), BF)
    grad_router = sum(
        jnp.dot(part, h.astype(F32), precision=HIGH)
        for part, h in zip(lanes_of(jnp.transpose(grad_logits)), h_parts)
    )
    grad_router = jnp.where(
        here_t == 0,
        grad_router,
        jnp.concatenate([grad_router[:, HALF:], grad_router[:, :HALF]], axis=1),
    )
    tiny = jnp.concatenate([0.5 * grad_router, sum(sums)], axis=0)
    tiny = tiny + hop(tiny, "tensor", 1)
    for offset in [1 << b for b in range(count.bit_length() - 1)]:
        tiny = tiny + hop(tiny, "expert", offset)
    tiny = tiny + hop(tiny, "dp", 1)
    tiny = tiny.reshape(tiny.shape[0], 2 * count, -1)
    tiny = lax.dynamic_index_in_dim(tiny, here_dp * count + here, 1, False)

    grad_tokens = []
    for n, (lo, hi) in enumerate(groups):
        if n == len(groups) - 1:
            leaving = order.wait(leaving)
            shards = shards + hop(leaving, "dp", 1).astype(F32)
        grad_tokens = [
            order.run(
                lambda *v: token_back(*v[:5], lo, hi, v[5:]),
                x, parts[n], got[n], dy, vectors, *grad_tokens,
            )
        ]
    grad_tokens = grad_tokens[0][:, :SEQ].reshape(tok, D)
    block_out = jnp.where(
        here_t == 0,
        jnp.concatenate([out_half, out_other], axis=2),
        jnp.concatenate([out_other, out_half], axis=2),
    )
    block_out = block_out[:, :SEQ].reshape(tok, D)

    keep_half = 1 - send_half
    grad_back = order.run(lambda h, g, b: outer(keep_half, h, g, True, b), hidden, grad_arrived, back_got)[None]
    grad_in = order.run(lambda g, a, b: outer(keep_half, g, a, False, b), grads, arrived, in_got)[None]
    return (
        block_out,
        grad_tokens,
        tiny[count],
        tiny[count + 1],
        tiny[count + 2],
        tiny[count + 3],
        shards[:, :HALF],
        shards[:, HALF : 2 * HALF],
        shards[:, 2 * HALF : 3 * HALF],
        jnp.transpose(shards[:, 3 * HALF :]),
        jnp.transpose(tiny[:count]),
        grad_in,
        grad_back,
    )


def solution(mesh):
    rows = ("dp", "expert")
    in_specs = (
        P(rows, None),
        P(rows, None),
        P(rows),
        P(rows),
        P(rows),
        P(rows),
        P(rows, "tensor"),
        P(rows, "tensor"),
        P(rows, "tensor"),
        P("tensor", rows),
        P(rows, None),
        P("expert", "dp", "tensor"),
        P("expert", "tensor", "dp"),
        P(rows, None),
    )
    out_specs = (
        P(rows, None),
        P(rows, None),
        P(rows),
        P(rows),
        P(rows),
        P(rows),
        P(rows, "tensor"),
        P(rows, "tensor"),
        P(rows, "tensor"),
        P("tensor", rows),
        P(rows, None),
        P("expert", "dp", "tensor"),
        P("expert", "tensor", "dp"),
    )
    return jax.shard_map(
        on_device, mesh=mesh, in_specs=in_specs, out_specs=out_specs, check_vma=False
    )
```

time: 699 us -> 630 us (0.901)
  Pallas kernels: 34 us -> 246 us
  matrix products: 139 us -> 10.3 us
  waiting for transfers between devices: 286 us -> 205 us
  local copies, waits for them, and re-layouts: 96.8 us -> 49.6 us
  starting transfers between devices: 86.7 us -> 61.6 us
    pallas_call x4 -> x29, Pallas kernels: 34 us -> 246 us  [the longest x4 52.2 us: expert_forward(): pl.pallas_call(forward_kernel, grid=(hidden // TILE,), in_specs=[whole(ro...]
    dot_general x24 -> x4, matrix products: 135 us -> 6.53 us  [the longest x2 5.49 us: dot_tn(): lax.dot_general(a, b, (((0,), (0,)), ((), ())), preferred_element_type=F32)]
    ppermute x70 -> x60, waiting for transfers between devices: 286 us -> 205 us  [hop(): return lax.ppermute(value, axis, [(i, i ^ offset) for i in range(count)])]
    ppermute x70 -> x60, starting transfers between devices: 86.7 us -> 61.6 us  [hop(): return lax.ppermute(value, axis, [(i, i ^ offset) for i in range(count)])]
    reshape x18 -> x10, local copies, waits for them, and re-layouts: 35.6 us -> 11.2 us  [the longest x6 4.01 us: images_of(): value = value.reshape(-1, SEQ, value.shape[-1])]
    unnamed x205 -> x118, local copies, waits for them, and re-layouts: 28.3 us -> 12.9 us
    slice x7 -> x21, local copies, waits for them, and re-layouts: 3.37 us -> 12.3 us  [the longest x8 5.25 us: settle(): return (mine, hop(jnp.stack([p[1] for p in parts]), 'expert', 1))]
    reduce_sum x10 -> x1, other arithmetic: 7.81 us -> 0.8 us  [on_device(): jnp.sum(probs * grad_probs, axis=-1, keepdims=True)]
  transfers between devices with their start and end apart: 70 -> 60, of which waited for: 30 -> 23; matrix products, arithmetic and copies ran while one was open for 34% -> 13% of each run, Pallas kernels for 5% -> 37%
where the time goes in v2:
time: 630 us; the launch traced here: 620 us
  Pallas kernels  246 us (39%)
  waiting for transfers between devices  205 us (33%)
  starting transfers between devices  61.6 us (10%)
  local copies, waits for them, and re-layouts  49.6 us (8%)
  other arithmetic  44.3 us (7%)
  matrix products  10.3 us (2%)
    ppermute x60, waiting for transfers between devices, hop(): return lax.ppermute(value, axis, [(i, i ^ offset) for i in range(count)])  205 us
    ppermute x60, starting transfers between devices, hop(): return lax.ppermute(value, axis, [(i, i ^ offset) for i in range(count)])  61.6 us
    pallas_call x4, Pallas kernels, expert_forward(): pl.pallas_call(forward_kernel, grid=(hidden // TILE,), in_specs=[whole(ro...  52.2 us
    pallas_call x4, Pallas kernels, expert_backward(): pl.pallas_call(backward_kernel, grid=(hidden // TILE,), in_specs=[whole(r...  39.6 us
    pallas_call x4, Pallas kernels, outer(): pl.pallas_call(functools.partial(outer_kernel, chunks=len(wides), hidden_...  38.6 us
    pallas_call x2, Pallas kernels, attend_back(): pl.pallas_call(attend_back_kernel, grid_spec=pltpu.PrefetchScalarGridSpec...  28.8 us
    pallas_call x4, Pallas kernels, send_rows(): pl.pallas_call(functools.partial(send_kernel, parts=len(own[0]), chips=ch...  23.5 us
    pallas_call x2, Pallas kernels, attend(): pl.pallas_call(attend_kernel, grid=(hi - lo,), in_specs=[image(D, lo), wh...  14.8 us
  transfers between devices with their start and end apart: 60, of which 23 were waited for; matrix products, arithmetic and copies ran while one was open for 13% of the time, Pallas kernels for 37%

profile of v2, /device:TPU:0, one launch (start us, length us, event | category | flops | bytes accessed | tf_op | source)
XLA Modules:
  0.0 619.7 jit_solution(9801773446831969078)
XLA Ops:
  5.1 4.1 collective-permute-start
  25.0 3.0 reshape.182
  30.6 3.5 collective-permute-done.3
  35.9 6.6 %collective-permute-done.5 = bf16[48,768]{1,0:T(8,128)(2,1)S(1)} collective-permute-done((bf16[48,768]{1,0:T(8,128)(2,1)S(1)}, bf16[48,768]{1,0:T(8,128)(2,1)S(1)}, u32[]{:S(2)}, u32[]{:S(2)}) %collective-permute-start.5) | collective-permute-done | bytes 73760 | tf_op jit(solution)/shard_map/ppermute | solution.py:40
  43.5 3.0 assemble.2
  51.6 8.3 %attend.2 = (bf16[5,208,768]{2,1,0:T(8,128)(2,1)}, bf16[5,208,1152]{2,1,0:T(8,128)(2,1)}, bf16[5,208,384]{2,1,0:T(8,128)(2,1)}, f32[5,208,128]{2,1,0:T(8,128)}, bf16[3,208,384]{2,1,0:T(8,128)(2,1)}) custom-call(bf16[5,208,768]{2,1,0:T(8,128)(2,1)} %pad.34.x_ref, f32[8,768]{1,0:T(8,128)} %pad_convert_fusion.1.vec_ref, bf16[768,1152]{1,0:T(8,128)(2,1)} %get-tuple-element.747.w_ref), custom_call_target="tpu_custom_call" | custom-call | flops 1000 | bytes 1000 | tf_op jit(solution)/shard_map/attend/pallas_call | solution.py:195
  60.2 6.4 %attend.3 = (bf16[5,208,768]{2,1,0:T(8,128)(2,1)}, bf16[5,208,1152]{2,1,0:T(8,128)(2,1)}, bf16[5,208,384]{2,1,0:T(8,128)(2,1)}, f32[5,208,128]{2,1,0:T(8,128)}, bf16[2,208,384]{2,1,0:T(8,128)(2,1)}) custom-call(bf16[5,208,768]{2,1,0:T(8,128)(2,1)} %pad.34.x_ref, ...), custom_call_target="tpu_custom_call", output_to_operand_aliasing={{0}: (3, {}), {1}: (4, {}), {2}: (5, {}), {3}: (6, {})} | custom-call | flops 1000 | bytes 1000 | tf_op jit(solution)/shard_map/attend/pallas_call | solution.py:195
  75.6 49.4 %collective-permute-done.13 = bf16[384,1536]{1,0:T(8,128)(2,1)S(1)} collective-permute-done((bf16[384,1536]{1,0:T(8,128)(2,1)S(1)}, bf16[384,1536]{1,0:T(8,128)(2,1)S(1)}, u32[]{:S(2)}, u32[]{:S(2)}) %collective-permute-start.13) | collective-permute-done | bytes 1179680 | tf_op jit(solution)/shard_map/ppermute | solution.py:40
  130.5 6.4 %route.2 = (f32[5,208,768]{2,1,0:T(8,128)}, f32[5,208,128]{2,1,0:T(8,128)}, f32[5,208,128]{2,1,0:T(8,128)}, bf16[3,208,768]{2,1,0:T(8,128)(2,1)}) custom-call(s32[1]{0:T(128)} %bitcast.30.which_ref, bf16[5,208,768]{2,1,0:T(8,128)(2,1)} %pad.34.x_ref, bf16[3,208,384]{2,1,0:T(8,128)(2,1)} %get-tuple-element.480.own_ref, ...), custom_call_target="tpu_custom_call" | custom-call | flops 1000 | bytes 1000 | tf_op jit(solution)/shard_map/route/pallas_call | solution.py:240
  138.2 20.8 %collective-permute-done.15.got_ref = bf16[2,208,384]{2,1,0:T(8,128)(2,1)} collective-permute-done((bf16[2,208,384]{2,1,0:T(8,128)(2,1)}, bf16[2,208,384]{2,1,0:T(8,128)(2,1)}, u32[]{:S(2)}, u32[]{:S(2)}) %collective-permute-start.15) | collective-permute-done | bytes 319520 | tf_op jit(solution)/shard_map/ppermute | solution.py:40
  159.0 5.6 route.3
  166.4 2.8 broadcast_select_fusion.2
  171.5 6.9 %send_rows.2 = (bf16[2,312,768]{2,1,0:T(8,128)(2,1)}, bf16[2,312,768]{2,1,0:T(8,128)(2,1)}, bf16[2,312,768]{2,1,0:T(8,128)(2,1)}) custom-call(s32[2,624]{1,0:T(2,128)} %slice.173.refs_0_, s32[2,416]{1,0:T(2,128)} %slice.174.refs_1_, bf16[624,768]{1,0:T(8,128)(2,1)} %bitcast.147, bf16[416,768]{1,0:T(8,128)(2,1)} %bitcast.154, s32[2,624]{1,0:T(2,128)} %slice.175.refs_4_, ...), custom_call_target="tpu_custom_call" | custom-call | flops 1000 | bytes 1000 | tf_op jit(solution)/shard_map/send_rows/pallas_call | solution.py:297
  178.4 4.4 send_rows.3.m_ref.refs_4_
  185.0 7.3 %send_gated.2 = (bf16[2,312,768]{2,1,0:T(8,128)(2,1)}, bf16[2,312,768]{2,1,0:T(8,128)(2,1)}, bf16[2,312,768]{2,1,0:T(8,128)(2,1)}) custom-call(s32[2,1040]{1,0:T(2,128)} %bitcast.171, bf16[1040,768]{1,0:T(8,128)(2,1)} %copy-done.3, f32[2,1040]{1,0:T(2,128)} %bitcast.178, s32[2,1040]{1,0:T(2,128)} %copy-done.51, bf16[1040,768]{1,0:T(8,128)(2,1)} %copy-done.13, ...), custom_call_target="tpu_custom_call" | custom-call | flops 1000 | bytes 1000 | tf_op jit(solution)/shard_map/send_gated/pallas_call | solution.py:297
  192.3 4.9 send_gated.3.z_ref.refs_4_
  197.2 3.0 broadcast_select_fusion
  200.2 13.1 %expert_forward.4 = (bf16[2,312,1536]{2,1,0:T(8,128)(2,1)}, bf16[2,312,1536]{2,1,0:T(8,128)(2,1)}, bf16[2,312,384]{2,1,0:T(8,128)(2,1)}, f32[2,312,384]{2,1,0:T(8,128)}) custom-call(bf16[2,312,768]{2,1,0:T(8,128)(2,1)} %send_rows.3.m_ref.refs_4_, bf16[384,1536]{1,0:T(8,128)(2,1)} %get-tuple-element.641.w1h, bf16[384,1536]{1,0:T(8,128)(2,1)} %get-tuple-element.642.w1t, ...), custom_call_target="tpu_custom_call" | custom-call | flops 1000 | bytes 1000 | tf_op jit(solution)/shard_map/expert_forward/pallas_call | solution.py:416
  218.8 8.0 %collective-permute-done.26 = bf16[2,312,384]{2,1,0:T(8,128)(2,1)S(1)} collective-permute-done((bf16[2,312,384]{2,1,0:T(8,128)(2,1)}, bf16[2,312,384]{2,1,0:T(8,128)(2,1)S(1)}, u32[]{:S(2)}, u32[]{:S(2)}) %collective-permute-start.26) | collective-permute-done | bytes 479264 | tf_op jit(solution)/shard_map/ppermute | solution.py:40
  229.6 13.0 %expert_forward.5 = (bf16[2,312,1536]{2,1,0:T(8,128)(2,1)}, bf16[2,312,1536]{2,1,0:T(8,128)(2,1)}, bf16[2,312,384]{2,1,0:T(8,128)(2,1)}, f32[2,312,384]{2,1,0:T(8,128)}) custom-call(bf16[2,312,768]{2,1,0:T(8,128)(2,1)} %copy-done.10, bf16[384,1536]{1,0:T(8,128)(2,1)} %get-tuple-element.641.w1h, bf16[384,1536]{1,0:T(8,128)(2,1)} %get-tuple-element.642.w1t, ...), custom_call_target="tpu_custom_call" | custom-call | flops 1000 | bytes 1000 | tf_op jit(solution)/shard_map/expert_forward/pallas_call | solution.py:416
  245.6 13.0 %expert_forward.6 = (bf16[2,312,1536]{2,1,0:T(8,128)(2,1)}, bf16[2,312,1536]{2,1,0:T(8,128)(2,1)}, bf16[2,312,384]{2,1,0:T(8,128)(2,1)}, f32[2,312,384]{2,1,0:T(8,128)}) custom-call(bf16[2,312,768]{2,1,0:T(8,128)(2,1)} %collective-permute-done.21.m_ref.refs_6_, bf16[384,1536]{1,0:T(8,128)(2,1)} %get-tuple-element.641.w1h, ...), custom_call_target="tpu_custom_call" | custom-call | flops 1000 | bytes 1000 | tf_op jit(solution)/shard_map/expert_forward/pallas_call | solution.py:416
  259.7 13.0 %expert_forward.7 = (bf16[2,312,1536]{2,1,0:T(8,128)(2,1)}, bf16[2,312,1536]{2,1,0:T(8,128)(2,1)}, bf16[2,312,384]{2,1,0:T(8,128)(2,1)}, f32[2,312,384]{2,1,0:T(8,128)}) custom-call(bf16[2,312,768]{2,1,0:T(8,128)(2,1)} %copy-done.11, bf16[384,1536]{1,0:T(8,128)(2,1)} %get-tuple-element.641.w1h, bf16[384,1536]{1,0:T(8,128)(2,1)} %get-tuple-element.642.w1t, ...), custom_call_target="tpu_custom_call" | custom-call | flops 1000 | bytes 1000 | tf_op jit(solution)/shard_map/expert_forward/pallas_call | solution.py:416
  272.7 10.2 %expert_backward.4 = (bf16[2,312,1536]{2,1,0:T(8,128)(2,1)}, bf16[2,312,384]{2,1,0:T(8,128)(2,1)}, f32[2,312,384]{2,1,0:T(8,128)}) custom-call(bf16[2,312,768]{2,1,0:T(8,128)(2,1)} %send_gated.3.z_ref.refs_4_, bf16[2,312,1536]{2,1,0:T(8,128)(2,1)} %get-tuple-element.604.s_ref, bf16[384,1536]{1,0:T(8,128)(2,1)} %get-tuple-element.641.w1h, ...), custom_call_target="tpu_custom_call" | custom-call | flops 1000 | bytes 1000 | tf_op jit(solution)/shard_map/expert_backward/pallas_call | solution.py:460
  284.7 9.8 %expert_backward.5 = (bf16[2,312,1536]{2,1,0:T(8,128)(2,1)}, bf16[2,312,384]{2,1,0:T(8,128)(2,1)}, f32[2,312,384]{2,1,0:T(8,128)}) custom-call(bf16[2,312,768]{2,1,0:T(8,128)(2,1)} %collective-permute-done.23.z_ref.refs_5_, bf16[2,312,1536]{2,1,0:T(8,128)(2,1)} %get-tuple-element.616.s_ref, bf16[384,1536]{1,0:T(8,128)(2,1)} %get-tuple-element.641.w1h, ...), custom_call_target="tpu_custom_call" | custom-call | flops 1000 | bytes 1000 | tf_op jit(solution)/shard_map/expert_backward/pallas_call | solution.py:460
  294.8 9.8 %expert_backward.6 = (bf16[2,312,1536]{2,1,0:T(8,128)(2,1)}, bf16[2,312,384]{2,1,0:T(8,128)(2,1)}, f32[2,312,384]{2,1,0:T(8,128)}) custom-call(bf16[2,312,768]{2,1,0:T(8,128)(2,1)} %collective-permute-done.24.z_ref.refs_6_, bf16[2,312,1536]{2,1,0:T(8,128)(2,1)} %get-tuple-element.628.s_ref, bf16[384,1536]{1,0:T(8,128)(2,1)} %get-tuple-element.641.w1h, ...), custom_call_target="tpu_custom_call" | custom-call | flops 1000 | bytes 1000 | tf_op jit(solution)/shard_map/expert_backward/pallas_call | solution.py:460
  306.4 9.8 %expert_backward.7 = (bf16[2,312,1536]{2,1,0:T(8,128)(2,1)}, bf16[2,312,384]{2,1,0:T(8,128)(2,1)}, f32[2,312,384]{2,1,0:T(8,128)}) custom-call(bf16[2,312,768]{2,1,0:T(8,128)(2,1)} %collective-permute-done.25.z_ref.refs_7_, bf16[2,312,1536]{2,1,0:T(8,128)(2,1)} %get-tuple-element.640.s_ref, bf16[384,1536]{1,0:T(8,128)(2,1)} %get-tuple-element.641.w1h, ...), custom_call_target="tpu_custom_call" | custom-call | flops 1000 | bytes 1000 | tf_op jit(solution)/shard_map/expert_backward/pallas_call | solution.py:460
  331.3 5.0 collective-permute-done.37
  346.1 9.1 %collective-permute-done.36 = bf16[2,312,384]{2,1,0:T(8,128)(2,1)S(1)} collective-permute-done((bf16[2,312,384]{2,1,0:T(8,128)(2,1)S(1)}, bf16[2,312,384]{2,1,0:T(8,128)(2,1)S(1)}, u32[]{:S(2)}, u32[]{:S(2)}) %collective-permute-start.36) | collective-permute-done | bytes 479264 | tf_op jit(solution)/shard_map/ppermute | solution.py:40
  355.9 5.3 collective-permute-done.40
  365.1 9.7 %outer_send.2 = bf16[1536,384]{1,0:T(8,128)(2,1)} custom-call(s32[1]{0:T(128)} %bitcast.36.which_ref, bf16[2,312,1536]{2,1,0:T(8,128)(2,1)} %get-tuple-element.789.refs_0_, bf16[2,312,1536]{2,1,0:T(8,128)(2,1)} %get-tuple-element.790.refs_1_, bf16[2,312,1536]{2,1,0:T(8,128)(2,1)} %get-tuple-element.791.refs_2_, ...), custom_call_target="tpu_custom_call" | custom-call | flops 1000 | bytes 1000 | tf_op jit(solution)/shard_map/outer_send/pallas_call | solution.py:500
  374.7 9.0 %outer_send.3 = bf16[384,1536]{1,0:T(8,128)(2,1)} custom-call(s32[1]{0:T(128)} %bitcast.36.which_ref, bf16[2,312,1536]{2,1,0:T(8,128)(2,1)} %get-tuple-element.802.refs_0_, bf16[2,312,1536]{2,1,0:T(8,128)(2,1)} %get-tuple-element.803.refs_1_, bf16[2,312,1536]{2,1,0:T(8,128)(2,1)} %get-tuple-element.804.refs_2_, ...), custom_call_target="tpu_custom_call" | custom-call | flops 1000 | bytes 1000 | tf_op jit(solution)/shard_map/outer_send/pallas_call | solution.py:500
  385.8 13.3 %bring_home.1 = (bf16[5,208,384]{2,1,0:T(8,128)(2,1)}, f32[5,208,128]{2,1,0:T(8,128)}) custom-call(s32[1]{0:T(128)} %bitcast.30.which_ref, s32[5,208,2]{2,1,0:T(8,128)} %copy-done.5, f32[5,208,768]{2,1,0:T(8,128)} %get-tuple-element.738.middle_ref.y_ref, bf16[5,208,768]{2,1,0:T(8,128)(2,1)} %copy-done, f32[5,208,128]{2,1,0:T(8,128)} %get-tuple-element.687.gates_ref, ...), custom_call_target="tpu_custom_call" | custom-call | flops 1000 | bytes 1000 | tf_op jit(solution)/shard_map/bring_home/pallas_call | solution.py:332
  403.2 5.6 sum_home.2.near_ref
  408.8 4.6 sum_home.3.near_ref
  418.3 3.8 fusion.10
  422.1 11.5 %collective-permute-done.42.away_ref = bf16[3,208,384]{2,1,0:T(8,128)(2,1)S(1)} collective-permute-done((bf16[3,208,384]{2,1,0:T(8,128)(2,1)S(1)}, bf16[3,208,384]{2,1,0:T(8,128)(2,1)S(1)}, u32[]{:S(2)}, u32[]{:S(2)}) %collective-permute-start.42) | collective-permute-done | bytes 479264 | tf_op jit(solution)/shard_map/ppermute | solution.py:40
  434.3 16.3 %attend_back.2 = (f32[5,208,768]{2,1,0:T(8,128)}, bf16[5,208,768]{2,1,0:T(8,128)(2,1)}, bf16[5,208,1152]{2,1,0:T(8,128)(2,1)}, bf16[3,208,768]{2,1,0:T(8,128)(2,1)}, f32[8,768]{1,0:T(8,128)}, /*index=5*/f32[8,768]{1,0:T(8,128)}) custom-call(s32[1]{0:T(128)} %bitcast.30.which_ref, bf16[5,208,768]{2,1,0:T(8,128)(2,1)} %pad.34.x_ref, ...), custom_call_target="tpu_custom_call" | custom-call | flops 1000 | bytes 1000 | tf_op jit(solution)/shard_map/attend_back/pallas_call | solution.py:589
  451.4 12.5 %attend_back.3 = (f32[5,208,768]{2,1,0:T(8,128)}, bf16[5,208,768]{2,1,0:T(8,128)(2,1)}, bf16[5,208,1152]{2,1,0:T(8,128)(2,1)}, bf16[2,208,768]{2,1,0:T(8,128)(2,1)}, f32[8,768]{1,0:T(8,128)}, /*index=5*/f32[8,768]{1,0:T(8,128)}) custom-call(s32[1]{0:T(128)} %bitcast.30.which_ref, ...), custom_call_target="tpu_custom_call", output_to_operand_aliasing={{0}: (12, {}), {1}: (13, {}), {2}: (14, {})} | custom-call | flops 1000 | bytes 1000 | tf_op jit(solution)/shard_map/attend_back/pallas_call | solution.py:589
  481.9 3.2 collective-permute-done.54
  494.1 37.7 %collective-permute-done.58.refs_8_ = bf16[1536,384]{1,0:T(8,128)(2,1)} collective-permute-done((bf16[1536,384]{1,0:T(8,128)(2,1)}, bf16[1536,384]{1,0:T(8,128)(2,1)}, u32[]{:S(2)}, u32[]{:S(2)}) %collective-permute-start.58) | collective-permute-done | bytes 1179680 | tf_op jit(solution)/shard_map/ppermute | solution.py:40
  533.1 9.4 %collective-permute-done.56 = f32[12,768]{1,0:T(8,128)S(1)} collective-permute-done((f32[12,768]{1,0:T(8,128)S(1)}, f32[12,768]{1,0:T(8,128)S(1)}, u32[]{:S(2)}, u32[]{:S(2)}) %collective-permute-start.56) | collective-permute-done | bytes 36896 | tf_op jit(solution)/shard_map/ppermute | solution.py:40
  543.6 3.4 collective-permute-start.59
  553.2 5.1 token_back.2.refs_0_
  566.1 21.0 %collective-permute-done.51.got_ref = bf16[2,208,768]{2,1,0:T(8,128)(2,1)} collective-permute-done((bf16[2,208,768]{2,1,0:T(8,128)(2,1)}, bf16[2,208,768]{2,1,0:T(8,128)(2,1)}, u32[]{:S(2)}, u32[]{:S(2)}) %collective-permute-start.51) | collective-permute-done | bytes 639008 | tf_op jit(solution)/shard_map/ppermute | solution.py:40
  587.2 3.2 token_back.3
  590.4 10.4 %outer_keep.2 = f32[1536,384]{1,0:T(8,128)} custom-call(s32[1]{0:T(128)S(6)} %sub.25.which_ref, bf16[2,312,1536]{2,1,0:T(8,128)(2,1)} %get-tuple-element.789.refs_0_, bf16[2,312,1536]{2,1,0:T(8,128)(2,1)} %get-tuple-element.790.refs_1_, bf16[2,312,1536]{2,1,0:T(8,128)(2,1)} %get-tuple-element.791.refs_2_, bf16[2,312,1536]{2,1,0:T(8,128)(2,1)} %get-tuple-element.792.refs_3_, ...), custom_call_target="tpu_custom_call" | custom-call | flops 1000 | bytes 1000 | tf_op jit(solution)/shard_map/outer_keep/pallas_call | solution.py:500
  602.3 9.5 %outer_keep.3 = f32[384,1536]{1,0:T(8,128)} custom-call(s32[1]{0:T(128)S(6)} %sub.25.which_ref, bf16[2,312,1536]{2,1,0:T(8,128)(2,1)} %get-tuple-element.802.refs_0_, bf16[2,312,1536]{2,1,0:T(8,128)(2,1)} %get-tuple-element.803.refs_1_, bf16[2,312,1536]{2,1,0:T(8,128)(2,1)} %get-tuple-element.804.refs_2_, bf16[2,312,1536]{2,1,0:T(8,128)(2,1)} %get-tuple-element.805.refs_3_, ...), custom_call_target="tpu_custom_call" | custom-call | flops 1000 | bytes 1000 | tf_op jit(solution)/shard_map/outer_keep/pallas_call | solution.py:500
  613.7 3.9 reshape.203
  (330 shorter events, 158.8 us)
Async XLA Ops:
  5.1 15.6 %collective-permute-start = (bf16[48,1280]{1,0:T(8,128)(2,1)S(1)}, bf16[48,1280]{1,0:T(8,128)(2,1)S(1)}, u32[]{:S(2)}, u32[]{:S(2)}) collective-permute-start(bf16[48,1280]{1,0:T(8,128)(2,1)S(1)} %pad_maximum_fusion.9), channel_id=1, source_target_pairs={{0,16},{16,0},{1,17},{17,1},{2,18},{18,2},{3,19},{19,3},{4,20},{20... | collective-permute-start | bytes 368648 | tf_op jit(solution)/shard_map/ppermute | solution.py:40
  23.2 10.9 %collective-permute-start.3 = (bf16[2,48,1280]{2,1,0:T(8,128)(2,1)S(1)}, bf16[2,48,1280]{2,1,0:T(8,128)(2,1)S(1)}, u32[]{:S(2)}, u32[]{:S(2)}) collective-permute-start(bf16[2,48,1280]{2,1,0:T(8,128)(2,1)S(1)} %maximum_select_fusion.1), channel_id=1, source_target_pairs={{0,8},{2,10},{4,12},{6,14},{8,0},{10,2},{12,4},{14,6},{1,9},{3,11}... | collective-permute-start | bytes 737288 | tf_op jit(solution)/shard_map/ppermute | solution.py:40
  23.7 10.6 %collective-permute-start.2 = (bf16[2,48,1280]{2,1,0:T(8,128)(2,1)S(1)}, bf16[2,48,1280]{2,1,0:T(8,128)(2,1)}, u32[]{:S(2)}, u32[]{:S(2)}) collective-permute-start(bf16[2,48,1280]{2,1,0:T(8,128)(2,1)S(1)} %maximum_select_fusion.1), channel_id=1, source_target_pairs={{0,4},{2,6},{4,0},{6,2},{8,12},{10,14},{12,8},{14,10},{1,5},{3,7},... | collective-permute-start | bytes 737288 | tf_op jit(solution)/shard_map/ppermute | solution.py:40
  46.4 13.5 %collective-permute-start.9 = (bf16[2,48,768]{2,1,0:T(8,128)(2,1)S(1)}, bf16[2,48,768]{2,1,0:T(8,128)(2,1)S(1)}, u32[]{:S(2)}, u32[]{:S(2)}) collective-permute-start(bf16[2,48,768]{2,1,0:T(8,128)(2,1)S(1)} %maximum_select_fusion.2), channel_id=1, source_target_pairs={{0,12},{2,14},{4,8},{6,10},{8,4},{10,6},{12,0},{14,2},{1,13},{3,15... | collective-permute-start | bytes 442376 | tf_op jit(solution)/shard_map/ppermute | solution.py:40
  48.0 12.0 %collective-permute-start.8 = (bf16[2,48,768]{2,1,0:T(8,128)(2,1)S(1)}, bf16[2,48,768]{2,1,0:T(8,128)(2,1)S(1)}, u32[]{:S(2)}, u32[]{:S(2)}) collective-permute-start(bf16[2,48,768]{2,1,0:T(8,128)(2,1)S(1)} %maximum_select_fusion.2), channel_id=1, source_target_pairs={{0,8},{2,10},{4,12},{6,14},{8,0},{10,2},{12,4},{14,6},{1,9},{3,11}... | collective-permute-start | bytes 442376 | tf_op jit(solution)/shard_map/ppermute | solution.py:40
  49.4 10.6 %collective-permute-start.7 = (bf16[2,48,768]{2,1,0:T(8,128)(2,1)S(1)}, bf16[2,48,768]{2,1,0:T(8,128)(2,1)S(1)}, u32[]{:S(2)}, u32[]{:S(2)}) collective-permute-start(bf16[2,48,768]{2,1,0:T(8,128)(2,1)S(1)} %maximum_select_fusion.2), channel_id=1, source_target_pairs={{0,4},{2,6},{4,0},{6,2},{8,12},{10,14},{12,8},{14,10},{1,5},{3,7},... | collective-permute-start | bytes 442376 | tf_op jit(solution)/shard_map/ppermute | solution.py:40
  72.3 52.7 %collective-permute-start.13 = (bf16[384,1536]{1,0:T(8,128)(2,1)S(1)}, bf16[384,1536]{1,0:T(8,128)(2,1)S(1)}, u32[]{:S(2)}, u32[]{:S(2)}) collective-permute-start(bf16[384,1536]{1,0:T(8,128)(2,1)S(1)} %convert_bitcast_fusion.1), channel_id=1, source_target_pairs={{0,16},{16,0},{1,17},{17,1},{2,18},{18,2},{3,19},{19,3},{4,20},{20... | collective-permute-start | bytes 3538952 | tf_op jit(solution)/shard_map/ppermute | solution.py:40
  72.4 58.1 %collective-permute-start.14 = (bf16[3,208,384]{2,1,0:T(8,128)(2,1)S(1)}, bf16[3,208,384]{2,1,0:T(8,128)(2,1)}, u32[]{:S(2)}, u32[]{:S(2)}) collective-permute-start(bf16[3,208,384]{2,1,0:T(8,128)(2,1)S(1)} %copy-done.45), channel_id=1, source_target_pairs={{0,1},{1,0},{2,3},{3,2},{4,5},{5,4},{6,7},{7,6},{8,9},{9,8},{10,11... | collective-permute-start | bytes 1437704 | tf_op jit(solution)/shard_map/ppermute | solution.py:40
  126.1 71.2 %collective-permute-start.19 = (bf16[1536,384]{1,0:T(8,128)(2,1)}, bf16[1536,384]{1,0:T(8,128)(2,1)}, u32[]{:S(2)}, u32[]{:S(2)}) collective-permute-start(bf16[1536,384]{1,0:T(8,128)(2,1)} %convert_bitcast_fusion), channel_id=1, source_target_pairs={{0,16},{16,0},{1,17},{17,1},{2,18},{18,2},{3,19},{19,3},{4,20},{20... | collective-permute-start | bytes 3538952 | tf_op jit(solution)/shard_map/ppermute | solution.py:40
  126.1 32.9 %collective-permute-start.15 = (bf16[2,208,384]{2,1,0:T(8,128)(2,1)}, bf16[2,208,384]{2,1,0:T(8,128)(2,1)}, u32[]{:S(2)}, u32[]{:S(2)}) collective-permute-start(bf16[2,208,384]{2,1,0:T(8,128)(2,1)} %get-tuple-element.496.own_ref), channel_id=1, source_target_pairs={{0,1},{1,0},{2,3},{3,2},{4,5},{5,4},{6,7},{7,6},{8,9},{9,8},{10,11... | collective-permute-start | bytes 958472 | tf_op jit(solution)/shard_map/ppermute | solution.py:40
  136.9 33.6 %collective-permute-start.16 = (bf16[624,768]{1,0:T(8,128)(2,1)}, bf16[624,768]{1,0:T(8,128)(2,1)S(1)}, u32[]{:S(2)}, u32[]{:S(2)}) collective-permute-start(bf16[624,768]{1,0:T(8,128)(2,1)} %bitcast.146), channel_id=1, source_target_pairs={{0,2},{2,0},{4,6},{6,4},{8,10},{10,8},{12,14},{14,12},{1,3},{3,1},... | collective-permute-start | bytes 2875400 | tf_op jit(solution)/shard_map/ppermute | solution.py:40
  165.8 17.0 %collective-permute-start.18 = (f32[2,1040]{1,0:T(2,128)S(1)}, f32[2,1040]{1,0:T(2,128)S(1)}, u32[]{:S(2)}, u32[]{:S(2)}) collective-permute-start(f32[2,1040]{1,0:T(2,128)S(1)} %bitcast.177), channel_id=1, source_target_pairs={{0,2},{2,0},{4,6},{6,4},{8,10},{10,8},{12,14},{14,12},{1,3},{3,1},... | collective-permute-start | bytes 24968 | tf_op jit(solution)/shard_map/ppermute | solution.py:40
  182.8 45.4 %collective-permute-start.20 = (bf16[2,312,768]{2,1,0:T(8,128)(2,1)}, bf16[2,312,768]{2,1,0:T(8,128)(2,1)S(1)}, u32[]{:S(2)}, u32[]{:S(2)}) collective-permute-start(bf16[2,312,768]{2,1,0:T(8,128)(2,1)} %get-tuple-element.568), channel_id=1, source_target_pairs={{0,4},{2,6},{4,0},{6,2},{8,12},{10,14},{12,8},{14,10},{1,5},{3,7},... | collective-permute-start | bytes 2875400 | tf_op jit(solution)/shard_map/ppermute | solution.py:40
  184.4 58.3 %collective-permute-start.21 = (bf16[2,312,768]{2,1,0:T(8,128)(2,1)}, bf16[2,312,768]{2,1,0:T(8,128)(2,1)}, u32[]{:S(2)}, u32[]{:S(2)}) collective-permute-start(bf16[2,312,768]{2,1,0:T(8,128)(2,1)} %get-tuple-element.579), channel_id=1, source_target_pairs={{0,8},{2,10},{4,12},{6,14},{8,0},{10,2},{12,4},{14,6},{1,9},{3,11}... | collective-permute-start | bytes 2875400 | tf_op jit(solution)/shard_map/ppermute | solution.py:40
  213.4 13.4 %collective-permute-start.26 = (bf16[2,312,384]{2,1,0:T(8,128)(2,1)}, bf16[2,312,384]{2,1,0:T(8,128)(2,1)S(1)}, u32[]{:S(2)}, u32[]{:S(2)}) collective-permute-start(bf16[2,312,384]{2,1,0:T(8,128)(2,1)} %get-tuple-element.677), channel_id=1, source_target_pairs={{0,1},{1,0},{2,3},{3,2},{4,5},{5,4},{6,7},{7,6},{8,9},{9,8},{10,11... | collective-permute-start | bytes 1437704 | tf_op jit(solution)/shard_map/ppermute | solution.py:40
  216.0 42.6 %collective-permute-start.22 = (bf16[2,312,768]{2,1,0:T(8,128)(2,1)}, bf16[2,312,768]{2,1,0:T(8,128)(2,1)S(1)}, u32[]{:S(2)}, u32[]{:S(2)}) collective-permute-start(bf16[2,312,768]{2,1,0:T(8,128)(2,1)} %get-tuple-element.590), channel_id=1, source_target_pairs={{0,12},{2,14},{4,8},{6,10},{8,4},{10,6},{12,0},{14,2},{1,13},{3,15... | collective-permute-start | bytes 2875400 | tf_op jit(solution)/shard_map/ppermute | solution.py:40
  217.3 65.5 %collective-permute-start.23 = (bf16[2,312,768]{2,1,0:T(8,128)(2,1)}, bf16[2,312,768]{2,1,0:T(8,128)(2,1)}, u32[]{:S(2)}, u32[]{:S(2)}) collective-permute-start(bf16[2,312,768]{2,1,0:T(8,128)(2,1)} %get-tuple-element.613), channel_id=1, source_target_pairs={{0,4},{2,6},{4,0},{6,2},{8,12},{10,14},{12,8},{14,10},{1,5},{3,7},... | collective-permute-start | bytes 2875400 | tf_op jit(solution)/shard_map/ppermute | solution.py:40
  226.8 67.6 %collective-permute-start.24 = (bf16[2,312,768]{2,1,0:T(8,128)(2,1)}, bf16[2,312,768]{2,1,0:T(8,128)(2,1)}, u32[]{:S(2)}, u32[]{:S(2)}) collective-permute-start(bf16[2,312,768]{2,1,0:T(8,128)(2,1)} %get-tuple-element.625), channel_id=1, source_target_pairs={{0,8},{2,10},{4,12},{6,14},{8,0},{10,2},{12,4},{14,6},{1,9},{3,11}... | collective-permute-start | bytes 2875400 | tf_op jit(solution)/shard_map/ppermute | solution.py:40
  228.2 76.4 %collective-permute-start.25 = (bf16[2,312,768]{2,1,0:T(8,128)(2,1)}, bf16[2,312,768]{2,1,0:T(8,128)(2,1)}, u32[]{:S(2)}, u32[]{:S(2)}) collective-permute-start(bf16[2,312,768]{2,1,0:T(8,128)(2,1)} %get-tuple-element.637), channel_id=1, source_target_pairs={{0,12},{2,14},{4,8},{6,10},{8,4},{10,6},{12,0},{14,2},{1,13},{3,15... | collective-permute-start | bytes 2875400 | tf_op jit(solution)/shard_map/ppermute | solution.py:40
  242.6 73.6 %collective-permute-start.27 = (bf16[2,312,384]{2,1,0:T(8,128)(2,1)}, bf16[2,312,384]{2,1,0:T(8,128)(2,1)}, u32[]{:S(2)}, u32[]{:S(2)}) collective-permute-start(bf16[2,312,384]{2,1,0:T(8,128)(2,1)} %get-tuple-element.679), channel_id=1, source_target_pairs={{0,1},{1,0},{2,3},{3,2},{4,5},{5,4},{6,7},{7,6},{8,9},{9,8},{10,11... | collective-permute-start | bytes 1437704 | tf_op jit(solution)/shard_map/ppermute | solution.py:40
  258.6 59.3 %collective-permute-start.29 = (bf16[2,312,384]{2,1,0:T(8,128)(2,1)}, bf16[2,312,384]{2,1,0:T(8,128)(2,1)}, u32[]{:S(2)}, u32[]{:S(2)}) collective-permute-start(bf16[2,312,384]{2,1,0:T(8,128)(2,1)} %get-tuple-element.681), channel_id=1, source_target_pairs={{0,1},{1,0},{2,3},{3,2},{4,5},{5,4},{6,7},{7,6},{8,9},{9,8},{10,11... | collective-permute-start | bytes 1437704 | tf_op jit(solution)/shard_map/ppermute | solution.py:40
  282.9 37.9 %collective-permute-start.31 = (bf16[2,312,384]{2,1,0:T(8,128)(2,1)}, bf16[2,312,384]{2,1,0:T(8,128)(2,1)}, u32[]{:S(2)}, u32[]{:S(2)}) collective-permute-start(bf16[2,312,384]{2,1,0:T(8,128)(2,1)} %get-tuple-element.683), channel_id=1, source_target_pairs={{0,1},{1,0},{2,3},{3,2},{4,5},{5,4},{6,7},{7,6},{8,9},{9,8},{10,11... | collective-permute-start | bytes 1437704 | tf_op jit(solution)/shard_map/ppermute | solution.py:40
  294.4 28.4 %collective-permute-start.34 = (bf16[2,312,384]{2,1,0:T(8,128)(2,1)}, bf16[2,312,384]{2,1,0:T(8,128)(2,1)}, u32[]{:S(2)}, u32[]{:S(2)}) collective-permute-start(bf16[2,312,384]{2,1,0:T(8,128)(2,1)} %get-tuple-element.695), channel_id=1, source_target_pairs={{0,1},{1,0},{2,3},{3,2},{4,5},{5,4},{6,7},{7,6},{8,9},{9,8},{10,11... | collective-permute-start | bytes 1437704 | tf_op jit(solution)/shard_map/ppermute | solution.py:40
  304.6 20.7 %collective-permute-start.35 = (bf16[2,312,384]{2,1,0:T(8,128)(2,1)}, bf16[2,312,384]{2,1,0:T(8,128)(2,1)}, u32[]{:S(2)}, u32[]{:S(2)}) collective-permute-start(bf16[2,312,384]{2,1,0:T(8,128)(2,1)} %get-tuple-element.697), channel_id=1, source_target_pairs={{0,1},{1,0},{2,3},{3,2},{4,5},{5,4},{6,7},{7,6},{8,9},{9,8},{10,11... | collective-permute-start | bytes 1437704 | tf_op jit(solution)/shard_map/ppermute | solution.py:40
  316.3 14.1 %collective-permute-start.39 = (bf16[2,312,384]{2,1,0:T(8,128)(2,1)}, bf16[2,312,384]{2,1,0:T(8,128)(2,1)S(1)}, u32[]{:S(2)}, u32[]{:S(2)}) collective-permute-start(bf16[2,312,384]{2,1,0:T(8,128)(2,1)} %get-tuple-element.701), channel_id=1, source_target_pairs={{0,1},{1,0},{2,3},{3,2},{4,5},{5,4},{6,7},{7,6},{8,9},{9,8},{10,11... | collective-permute-start | bytes 1437704 | tf_op jit(solution)/shard_map/ppermute | solution.py:40
  318.0 18.4 %collective-permute-start.37 = (bf16[2,312,384]{2,1,0:T(8,128)(2,1)S(1)}, bf16[2,312,384]{2,1,0:T(8,128)(2,1)S(1)}, u32[]{:S(2)}, u32[]{:S(2)}) collective-permute-start(bf16[2,312,384]{2,1,0:T(8,128)(2,1)S(1)} %copy-done.56), channel_id=1, source_target_pairs={{0,1},{1,0},{2,3},{3,2},{4,5},{5,4},{6,7},{7,6},{8,9},{9,8},{10,11... | collective-permute-start | bytes 1437704 | tf_op jit(solution)/shard_map/ppermute | solution.py:40
  320.7 17.5 %collective-permute-start.28 = (bf16[2,312,384]{2,1,0:T(8,128)(2,1)S(1)}, bf16[2,312,384]{2,1,0:T(8,128)(2,1)S(1)}, u32[]{:S(2)}, u32[]{:S(2)}) collective-permute-start(bf16[2,312,384]{2,1,0:T(8,128)(2,1)S(1)} %add_convert_fusion.6), channel_id=1, source_target_pairs={{0,4},{2,6},{4,0},{6,2},{8,12},{10,14},{12,8},{14,10},{1,5},{3,7},... | collective-permute-start | bytes 1437704 | tf_op jit(solution)/shard_map/ppermute | solution.py:40
  322.8 19.2 %collective-permute-start.30 = (bf16[2,312,384]{2,1,0:T(8,128)(2,1)S(1)}, bf16[2,312,384]{2,1,0:T(8,128)(2,1)S(1)}, u32[]{:S(2)}, u32[]{:S(2)}) collective-permute-start(bf16[2,312,384]{2,1,0:T(8,128)(2,1)S(1)} %add_convert_fusion.5), channel_id=1, source_target_pairs={{0,8},{2,10},{4,12},{6,14},{8,0},{10,2},{12,4},{14,6},{1,9},{3,11}... | collective-permute-start | bytes 1437704 | tf_op jit(solution)/shard_map/ppermute | solution.py:40
  325.4 19.7 %collective-permute-start.32 = (bf16[2,312,384]{2,1,0:T(8,128)(2,1)S(1)}, bf16[2,312,384]{2,1,0:T(8,128)(2,1)S(1)}, u32[]{:S(2)}, u32[]{:S(2)}) collective-permute-start(bf16[2,312,384]{2,1,0:T(8,128)(2,1)S(1)} %add_convert_fusion.4), channel_id=1, source_target_pairs={{0,12},{2,14},{4,8},{6,10},{8,4},{10,6},{12,0},{14,2},{1,13},{3,15... | collective-permute-start | bytes 1437704 | tf_op jit(solution)/shard_map/ppermute | solution.py:40
  330.4 24.8 %collective-permute-start.36 = (bf16[2,312,384]{2,1,0:T(8,128)(2,1)S(1)}, bf16[2,312,384]{2,1,0:T(8,128)(2,1)S(1)}, u32[]{:S(2)}, u32[]{:S(2)}) collective-permute-start(bf16[2,312,384]{2,1,0:T(8,128)(2,1)S(1)} %add_convert_fusion.2), channel_id=1, source_target_pairs={{0,4},{2,6},{4,0},{6,2},{8,12},{10,14},{12,8},{14,10},{1,5},{3,7},... | collective-permute-start | bytes 1437704 | tf_op jit(solution)/shard_map/ppermute | solution.py:40
  336.4 24.8 %collective-permute-start.40 = (bf16[2,312,384]{2,1,0:T(8,128)(2,1)S(1)}, bf16[2,312,384]{2,1,0:T(8,128)(2,1)S(1)}, u32[]{:S(2)}, u32[]{:S(2)}) collective-permute-start(bf16[2,312,384]{2,1,0:T(8,128)(2,1)S(1)} %add_convert_fusion), channel_id=1, source_target_pairs={{0,12},{2,14},{4,8},{6,10},{8,4},{10,6},{12,0},{14,2},{1,13},{3,15... | collective-permute-start | bytes 1437704 | tf_op jit(solution)/shard_map/ppermute | solution.py:40
  338.2 24.5 %collective-permute-start.38 = (bf16[2,312,384]{2,1,0:T(8,128)(2,1)S(1)}, bf16[2,312,384]{2,1,0:T(8,128)(2,1)S(1)}, u32[]{:S(2)}, u32[]{:S(2)}) collective-permute-start(bf16[2,312,384]{2,1,0:T(8,128)(2,1)S(1)} %add_convert_fusion.1), channel_id=1, source_target_pairs={{0,8},{2,10},{4,12},{6,14},{8,0},{10,2},{12,4},{14,6},{1,9},{3,11}... | collective-permute-start | bytes 1437704 | tf_op jit(solution)/shard_map/ppermute | solution.py:40
  346.0 39.8 %collective-permute-start.33 = (bf16[4,312,384]{2,1,0:T(8,128)(2,1)S(1)}, bf16[4,312,384]{2,1,0:T(8,128)(2,1)}, u32[]{:S(2)}, u32[]{:S(2)}) collective-permute-start(bf16[4,312,384]{2,1,0:T(8,128)(2,1)S(1)} %pad_maximum_fusion.5), channel_id=1, source_target_pairs={{0,2},{2,0},{4,6},{6,4},{8,10},{10,8},{12,14},{14,12},{1,3},{3,1},... | collective-permute-start | bytes 2875400 | tf_op jit(solution)/shard_map/ppermute | solution.py:40
  364.5 37.7 %collective-permute-start.41 = (bf16[4,312,384]{2,1,0:T(8,128)(2,1)}, bf16[4,312,384]{2,1,0:T(8,128)(2,1)S(1)}, u32[]{:S(2)}, u32[]{:S(2)}) collective-permute-start(bf16[4,312,384]{2,1,0:T(8,128)(2,1)} %pad_maximum_fusion.7), channel_id=1, source_target_pairs={{0,2},{2,0},{4,6},{6,4},{8,10},{10,8},{12,14},{14,12},{1,3},{3,1},... | collective-permute-start | bytes 2875400 | tf_op jit(solution)/shard_map/ppermute | solution.py:40
  400.3 15.1 %collective-permute-start.43 = (f32[2,1040]{1,0:T(2,128)S(1)}, f32[2,1040]{1,0:T(2,128)S(1)}, u32[]{:S(2)}, u32[]{:S(2)}) collective-permute-start(f32[2,1040]{1,0:T(2,128)S(1)} %bitcast.182), channel_id=1, source_target_pairs={{0,1},{1,0},{2,3},{3,2},{4,5},{5,4},{6,7},{7,6},{8,9},{9,8},{10,11... | collective-permute-start | bytes 24968 | tf_op jit(solution)/shard_map/ppermute | solution.py:40
  413.4 37.2 %collective-permute-start.44 = (bf16[2,208,384]{2,1,0:T(8,128)(2,1)}, bf16[2,208,384]{2,1,0:T(8,128)(2,1)S(1)}, u32[]{:S(2)}, u32[]{:S(2)}) collective-permute-start(bf16[2,208,384]{2,1,0:T(8,128)(2,1)} %sum_home.3.near_ref), channel_id=1, source_target_pairs={{0,1},{1,0},{2,3},{3,2},{4,5},{5,4},{6,7},{7,6},{8,9},{9,8},{10,11... | collective-permute-start | bytes 958472 | tf_op jit(solution)/shard_map/ppermute | solution.py:40
  414.7 18.9 %collective-permute-start.42 = (bf16[3,208,384]{2,1,0:T(8,128)(2,1)S(1)}, bf16[3,208,384]{2,1,0:T(8,128)(2,1)S(1)}, u32[]{:S(2)}, u32[]{:S(2)}) collective-permute-start(bf16[3,208,384]{2,1,0:T(8,128)(2,1)S(1)} %copy-done.20), channel_id=1, source_target_pairs={{0,1},{1,0},{2,3},{3,2},{4,5},{5,4},{6,7},{7,6},{8,9},{9,8},{10,11... | collective-permute-start | bytes 1437704 | tf_op jit(solution)/shard_map/ppermute | solution.py:40
  472.4 17.8 %collective-permute-start.47 = (bf16[2,4,48,1536]{3,2,0,1:T(8,128)(2,1)S(1)}, bf16[2,4,48,1536]{3,2,0,1:T(8,128)(2,1)S(1)}, u32[]{:S(2)}, u32[]{:S(2)}) collective-permute-start(bf16[2,4,48,1536]{3,2,0,1:T(8,128)(2,1)S(1)} %fusion.1), channel_id=1, source_target_pairs={{0,2},{2,0},{4,6},{6,4},{8,10},{10,8},{12,14},{14,12},{1,3},{3,1},... | collective-permute-start | bytes 3538952 | tf_op jit(solution)/shard_map/ppermute | solution.py:40
  476.8 55.0 %collective-permute-start.58 = (bf16[1536,384]{1,0:T(8,128)(2,1)}, bf16[1536,384]{1,0:T(8,128)(2,1)}, u32[]{:S(2)}, u32[]{:S(2)}) collective-permute-start(bf16[1536,384]{1,0:T(8,128)(2,1)} %outer_send.2), channel_id=1, source_target_pairs={{0,16},{16,0},{1,17},{17,1},{2,18},{18,2},{3,19},{19,3},{4,20},{20... | collective-permute-start | bytes 3538952 | tf_op jit(solution)/shard_map/ppermute | solution.py:40
  486.3 57.3 %collective-permute-start.45 = (bf16[5,208,384]{2,1,0:T(8,128)(2,1)}, bf16[5,208,384]{2,1,0:T(8,128)(2,1)}, u32[]{:S(2)}, u32[]{:S(2)}) collective-permute-start(bf16[5,208,384]{2,1,0:T(8,128)(2,1)} %get-tuple-element.692), channel_id=1, source_target_pairs={{0,1},{1,0},{2,3},{3,2},{4,5},{5,4},{6,7},{7,6},{8,9},{9,8},{10,11... | collective-permute-start | bytes 2396168 | tf_op jit(solution)/shard_map/ppermute | solution.py:40
  488.0 65.1 %collective-permute-start.46 = (bf16[3,208,768]{2,1,0:T(8,128)(2,1)}, bf16[3,208,768]{2,1,0:T(8,128)(2,1)}, u32[]{:S(2)}, u32[]{:S(2)}) collective-permute-start(bf16[3,208,768]{2,1,0:T(8,128)(2,1)} %get-tuple-element.763.own_ref), channel_id=1, source_target_pairs={{0,1},{1,0},{2,3},{3,2},{4,5},{5,4},{6,7},{7,6},{8,9},{9,8},{10,11... | collective-permute-start | bytes 2875400 | tf_op jit(solution)/shard_map/ppermute | solution.py:40
  489.3 53.2 %collective-permute-start.56 = (f32[12,768]{1,0:T(8,128)S(1)}, f32[12,768]{1,0:T(8,128)S(1)}, u32[]{:S(2)}, u32[]{:S(2)}) collective-permute-start(f32[12,768]{1,0:T(8,128)S(1)} %add.146), channel_id=1, source_target_pairs={{0,16},{16,0},{1,17},{17,1},{2,18},{18,2},{3,19},{19,3},{4,20},{20... | collective-permute-start | bytes 110600 | tf_op jit(solution)/shard_map/ppermute | solution.py:40
  493.2 65.0 %collective-permute-start.48 = (bf16[2,48,1536]{2,1,0:T(8,128)(2,1)}, bf16[2,48,1536]{2,1,0:T(8,128)(2,1)}, u32[]{:S(2)}, u32[]{:S(2)}) collective-permute-start(bf16[2,48,1536]{2,1,0:T(8,128)(2,1)} %get-tuple-element.817), channel_id=1, source_target_pairs={{0,4},{2,6},{4,0},{6,2},{8,12},{10,14},{12,8},{14,10},{1,5},{3,7},... | collective-permute-start | bytes 884744 | tf_op jit(solution)/shard_map/ppermute | solution.py:40
  531.8 26.4 %collective-permute-start.50 = (bf16[2,48,1536]{2,1,0:T(8,128)(2,1)}, bf16[2,48,1536]{2,1,0:T(8,128)(2,1)}, u32[]{:S(2)}, u32[]{:S(2)}) collective-permute-start(bf16[2,48,1536]{2,1,0:T(8,128)(2,1)} %get-tuple-element.818), channel_id=1, source_target_pairs={{0,12},{2,14},{4,8},{6,10},{8,4},{10,6},{12,0},{14,2},{1,13},{3,15... | collective-permute-start | bytes 884744 | tf_op jit(solution)/shard_map/ppermute | solution.py:40
  542.5 15.7 %collective-permute-start.49 = (bf16[2,48,1536]{2,1,0:T(8,128)(2,1)}, bf16[2,48,1536]{2,1,0:T(8,128)(2,1)}, u32[]{:S(2)}, u32[]{:S(2)}) collective-permute-start(bf16[2,48,1536]{2,1,0:T(8,128)(2,1)} %get-tuple-element.819), channel_id=1, source_target_pairs={{0,8},{2,10},{4,12},{6,14},{8,0},{10,2},{12,4},{14,6},{1,9},{3,11}... | collective-permute-start | bytes 884744 | tf_op jit(solution)/shard_map/ppermute | solution.py:40
  543.6 58.7 %collective-permute-start.59 = (bf16[384,1536]{1,0:T(8,128)(2,1)S(1)}, bf16[384,1536]{1,0:T(8,128)(2,1)}, u32[]{:S(2)}, u32[]{:S(2)}) collective-permute-start(bf16[384,1536]{1,0:T(8,128)(2,1)S(1)} %copy-done.26), channel_id=1, source_target_pairs={{0,16},{16,0},{1,17},{17,1},{2,18},{18,2},{3,19},{19,3},{4,20},{20... | collective-permute-start | bytes 3538952 | tf_op jit(solution)/shard_map/ppermute | solution.py:40
  553.1 34.0 %collective-permute-start.51 = (bf16[2,208,768]{2,1,0:T(8,128)(2,1)}, bf16[2,208,768]{2,1,0:T(8,128)(2,1)}, u32[]{:S(2)}, u32[]{:S(2)}) collective-permute-start(bf16[2,208,768]{2,1,0:T(8,128)(2,1)} %get-tuple-element.776.own_ref), channel_id=1, source_target_pairs={{0,1},{1,0},{2,3},{3,2},{4,5},{5,4},{6,7},{7,6},{8,9},{9,8},{10,11... | collective-permute-start | bytes 1916936 | tf_op jit(solution)/shard_map/ppermute | solution.py:40
  560.4 57.2 %collective-permute-start.57 = (bf16[48,1536]{1,0:T(8,128)(2,1)}, bf16[48,1536]{1,0:T(8,128)(2,1)}, u32[]{:S(2)}, u32[]{:S(2)}) collective-permute-start(bf16[48,1536]{1,0:T(8,128)(2,1)} %fusion.18), channel_id=1, source_target_pairs={{0,16},{16,0},{1,17},{17,1},{2,18},{18,2},{3,19},{19,3},{4,20},{20... | collective-permute-start | bytes 442376 | tf_op jit(solution)/shard_map/ppermute | solution.py:40
  (69 other events, 740.8 us)

commit v3 on v2

--- a/solution.py
+++ b/solution.py
@@ -92,10 +92,104 @@
     return pl.BlockSpec(shape, lambda *_: zeros)
 
 
+def flag(value):
+    return value.astype(jnp.int32).reshape(1)
+
+
+def cross_kernel(here_ref, own_ref, across_ref, out_ref):
+    first = here_ref[0] == 0
+    out_ref[0] = jnp.where(first, own_ref[...], across_ref[...])
+    out_ref[1] = jnp.where(first, across_ref[...], own_ref[...])
+
+
 def cross(shard):
     across = hop(shard, "dp", 1)
-    mine = lax.axis_index("dp") == 0
-    return jnp.where(mine, jnp.stack([shard, across]), jnp.stack([across, shard]))
+    return pl.pallas_call(
+        cross_kernel,
+        grid_spec=pltpu.PrefetchScalarGridSpec(
+            num_scalar_prefetch=1,
+            grid=(1,),
+            in_specs=[whole(shard.shape)] * 2,
+            out_specs=whole((2,) + shard.shape),
+        ),
+        out_shape=jax.ShapeDtypeStruct((2,) + shard.shape, shard.dtype),
+        name="cross",
+        cost_estimate=cost(),
+    )(flag(lax.axis_index("dp")), shard, across)
+
+
+def stack_kernel(*refs):
+    for n, ref in enumerate(refs[:-1]):
+        refs[-1][n] = ref[...]
+
+
+def stacked(parts):
+    shape = (len(parts),) + parts[0].shape
+    return pl.pallas_call(
+        stack_kernel,
+        grid=(1,),
+        in_specs=[whole(p.shape) for p in parts],
+        out_specs=whole(shape),
+        out_shape=jax.ShapeDtypeStruct(shape, parts[0].dtype),
+        name="stacked",
+        cost_estimate=cost(),
+    )(*parts)
+
+
+def sort_kernel(*refs):
+    parts, (mine_ref, away_ref) = refs[:-2], refs[-2:]
+    for n, ref in enumerate(parts):
+        mine_ref[n] = ref[0]
+        away_ref[n] = ref[1]
+
+
+def sort_groups(parts):
+    shape = (len(parts),) + parts[0].shape[1:]
+    return pl.pallas_call(
+        sort_kernel,
+        grid=(1,),
+        in_specs=[whole(p.shape) for p in parts],
+        out_specs=[whole(shape)] * 2,
+        out_shape=[jax.ShapeDtypeStruct(shape, parts[0].dtype)] * 2,
+        name="sort_groups",
+        cost_estimate=cost(),
+    )(*parts)
+
+
+def add_kernel(near_ref, away_ref, out_ref):
+    out_ref[...] = (near_ref[...] + away_ref[...].astype(F32)).astype(BF)
+
+
+def add_halves(near, away):
+    part = pl.BlockSpec((1,) + near.shape[1:], lambda i: (i, 0, 0))
+    return pl.pallas_call(
+        add_kernel,
+        grid=(near.shape[0],),
+        in_specs=[part, part],
+        out_specs=part,
+        out_shape=jax.ShapeDtypeStruct(near.shape, BF),
+        name="add_halves",
+        cost_estimate=cost(),
+    )(near, away)
+
+
+def vector_kernel(narrow_ref, out_ref, *, start):
+    row = lax.broadcasted_iota(jnp.int32, (8, LANES), 0)
+    lane = lax.broadcasted_iota(jnp.int32, (8, LANES), 1)
+    wanted = jnp.where((lane == row + start) & (row < 4), 1.0, 0.0).astype(BF)
+    out_ref[...] = dot_nt(wanted, narrow_ref[...])
+
+
+def vectors_of(narrow, start):
+    return pl.pallas_call(
+        functools.partial(vector_kernel, start=start),
+        grid=(1,),
+        in_specs=[whole(narrow.shape)],
+        out_specs=whole((8, D)),
+        out_shape=jax.ShapeDtypeStruct((8, D), F32),
+        name="vectors",
+        cost_estimate=cost(),
+    )(narrow)
 
 
 def assemble_kernel(here_ref, same_ref, flip_ref, *out_refs):
@@ -141,19 +235,24 @@
     return [pair] + [hop(pair, "expert", k) for k in range(2, count, 2)]
 
 
-def scatter_sum(grad, wide):
+def pick(array, index, axis):
+    return lax.dynamic_index_in_dim(array, index, axis, False)
+
+
+def core_sum(grad, wide):
     count = lax.axis_size("expert")
-    here_dp = lax.axis_index("dp")
-    here = lax.axis_index("expert")
-    core = here & 1
-    chip = here >> 1
+    core = lax.axis_index("expert") & 1
     blocks = grad.reshape((2, count // 2, 2, -1) + grad.shape[1:])
-    pick = lambda array, index, axis: lax.dynamic_index_in_dim(array, index, axis, False)
-    total = pick(blocks, core, 2) + hop(
+    return pick(blocks, core, 2) + hop(
         pick(blocks, 1 - core, 2).astype(wide), "expert", 1
     ).astype(F32)
+
+
+def chip_sum(total, wide):
+    here_dp = lax.axis_index("dp")
+    chip = lax.axis_index("expert") >> 1
     summed = pick(total, chip, 1)
-    for k in range(1, count // 2):
+    for k in range(1, total.shape[1]):
         summed = summed + hop(pick(total, chip ^ k, 1).astype(wide), "expert", 2 * k).astype(F32)
     return pick(summed, here_dp, 0), pick(summed, 1 - here_dp, 0).astype(wide)
 
@@ -211,11 +310,11 @@
 
 
 def route_kernel(
-    which_ref, x_ref, own_ref, got_ref, vec_ref, out_w_ref, router_ref, ids_ref, *refs, count
+    which_ref, x_ref, own_ref, got_ref, vec_ref, here_ref, there_ref, router_ref, ids_ref, *refs, count
 ):
     y_ref, r_ref, g_ref, h_ref = refs[-4:]
     y = x_ref[0].astype(F32) + (
-        dot_nt(own_ref[0], out_w_ref[:, :HALF]) + dot_nt(got_ref[0], out_w_ref[:, HALF:])
+        dot_nt(own_ref[0], here_ref[...]) + dot_nt(got_ref[0], there_ref[...])
     )
     y_ref[0] = y
     hat, _ = normed(y)
@@ -235,7 +334,7 @@
     g_ref[0] = gates
 
 
-def route(which, x, own, got, vectors, out_w, router, ids, count, lo, hi, held):
+def route(which, x, own, got, vectors, out_here, out_there, router, ids, count, lo, hi, held):
     total = x.shape[0]
     return pl.pallas_call(
         functools.partial(route_kernel, count=count),
@@ -247,7 +346,8 @@
                 image(HALF),
                 image(HALF),
                 whole(vectors.shape),
-                whole(out_w.shape),
+                whole(out_here.shape),
+                whole(out_there.shape),
                 whole(router.shape),
                 image(2, lo),
             ]
@@ -260,10 +360,10 @@
             images(total, LANES, F32),
             images(hi - lo, D, BF),
         ],
-        input_output_aliases={8 + n: n for n in range(len(held))},
+        input_output_aliases={9 + n: n for n in range(len(held))},
         name="route",
         cost_estimate=cost(),
-    )(which, x, own, got, vectors, out_w, router, ids, *held)
+    )(which, x, own, got, vectors, out_here, out_there, router, ids, *held)
 
 
 def send_kernel(*refs, parts, chips, gated):
@@ -305,6 +405,23 @@
     )(*operands)
 
 
+def first_lanes():
+    row = lax.broadcasted_iota(jnp.int32, (8, LANES), 0)
+    return jnp.where(row == lax.broadcasted_iota(jnp.int32, (8, LANES), 1), 1.0, 0.0)
+
+
+def turn(columns):
+    return lax.dot_general(
+        first_lanes(), columns, (((1,), (1,)), ((), ())), precision=HIGH, preferred_element_type=F32
+    )
+
+
+def turn_back(rows):
+    return lax.dot_general(
+        rows, first_lanes(), (((0,), (0,)), ((), ())), precision=HIGH, preferred_element_type=F32
+    )
+
+
 def home_kernel(which_ref, rows_ref, middle_ref, grad_ref, gates_ref, own_ref, other_ref, out_ref, dgate_ref):
     value = middle_ref[0]
     grad = grad_ref[0].astype(F32)
@@ -323,7 +440,7 @@
         dgate = jnp.sum(picked * grad, axis=1, keepdims=True)
         found = jnp.where(lane == c, dgate, found)
     out_ref[0] = value.astype(BF)
-    dgate_ref[0] = found
+    dgate_ref[0] = turn(found)
 
 
 def bring_home(which, rows, middle, grad, gates, own, other):
@@ -335,9 +452,9 @@
             num_scalar_prefetch=1,
             grid=(total,),
             in_specs=[image(2), part, part, image(LANES), whole(own.shape), whole(other.shape)],
-            out_specs=[image(HALF), image(LANES)],
+            out_specs=[image(HALF), pl.BlockSpec((1, 8, ROWS), lambda i, s: (i, 0, 0))],
         ),
-        out_shape=[images(total, HALF, BF), images(total, LANES, F32)],
+        out_shape=[images(total, HALF, BF), jax.ShapeDtypeStruct((total, 8, ROWS), F32)],
         name="bring_home",
         cost_estimate=cost(),
     )(which, rows, middle, grad, gates, own, other)
@@ -379,17 +496,24 @@
     return u * normal, normal + u * (DENSITY * bell)
 
 
-def forward_kernel(m_ref, w1h, w1t, w2h, w2t, g_ref, s_ref, zt_ref, zh_ref, acc):
+def in_order(same_ref, in_own, in_other, back_own, back_other):
+    same = same_ref[0] == 1
+    choose = lambda a, b: (jnp.where(same, a[...], b[...]), jnp.where(same, b[...], a[...]))
+    return choose(in_own, in_other) + choose(back_own, back_other)
+
+
+def forward_kernel(same_ref, m_ref, in_own, in_other, back_own, back_other, g_ref, s_ref, zt_ref, zh_ref, acc):
+    w1h, w1t, w2h, w2t = in_order(same_ref, in_own, in_other, back_own, back_other)
     step = pl.program_id(0)
     last = pl.num_programs(0) - 1
     for b in range(m_ref.shape[0]):
-        u = dot_nn(m_ref[b, :, :HALF], w1h[...]) + dot_nn(m_ref[b, :, HALF:], w1t[...])
+        u = dot_nn(m_ref[b, :, :HALF], w1h) + dot_nn(m_ref[b, :, HALF:], w1t)
         g, slope = gelu_parts(u)
         g = g.astype(BF)
         g_ref[b] = g
         s_ref[b] = slope.astype(BF)
-        away = dot_nn(g, w2t[...])
-        near = dot_nn(g, w2h[...])
+        away = dot_nn(g, w2t)
+        near = dot_nn(g, w2h)
 
         @pl.when(step == 0)
         def _():
@@ -406,34 +530,38 @@
             zt_ref[b] = acc[b].astype(BF)
 
 
-def expert_forward(rows, w1h, w1t, w2h, w2t):
+def expert_forward(same, rows, *weights):
     blocks, capacity, _ = rows.shape
-    hidden = w1h.shape[1]
-    across = pl.BlockSpec((HALF, TILE), lambda i: (0, i))
-    down = pl.BlockSpec((TILE, HALF), lambda i: (i, 0))
-    wide = pl.BlockSpec((blocks, capacity, TILE), lambda i: (0, 0, i))
+    hidden = weights[0].shape[1]
+    across = pl.BlockSpec((HALF, TILE), lambda i, s: (0, i))
+    down = pl.BlockSpec((TILE, HALF), lambda i, s: (i, 0))
+    wide = pl.BlockSpec((blocks, capacity, TILE), lambda i, s: (0, 0, i))
     make = lambda w, t: jax.ShapeDtypeStruct((blocks, capacity, w), t)
     return pl.pallas_call(
         forward_kernel,
-        grid=(hidden // TILE,),
-        in_specs=[whole(rows.shape), across, across, down, down],
-        out_specs=[wide, wide] + [whole((blocks, capacity, HALF))] * 2,
+        grid_spec=pltpu.PrefetchScalarGridSpec(
+            num_scalar_prefetch=1,
+            grid=(hidden // TILE,),
+            in_specs=[whole(rows.shape), across, across, down, down],
+            out_specs=[wide, wide] + [whole((blocks, capacity, HALF))] * 2,
+            scratch_shapes=[pltpu.VMEM((blocks, capacity, HALF), F32)],
+        ),
         out_shape=[make(hidden, BF), make(hidden, BF), make(HALF, BF), make(HALF, F32)],
-        scratch_shapes=[pltpu.VMEM((blocks, capacity, HALF), F32)],
         name="expert_forward",
         cost_estimate=cost(),
-    )(rows, w1h, w1t, w2h, w2t)
-
-
-def backward_kernel(z_ref, s_ref, w1h, w1t, w2h, w2t, u_ref, mt_ref, mh_ref, acc):
+    )(same, rows, *weights)
+
+
+def backward_kernel(same_ref, z_ref, s_ref, in_own, in_other, back_own, back_other, u_ref, mt_ref, mh_ref, acc):
+    w1h, w1t, w2h, w2t = in_order(same_ref, in_own, in_other, back_own, back_other)
     step = pl.program_id(0)
     last = pl.num_programs(0) - 1
     for b in range(z_ref.shape[0]):
-        grad = dot_nt(z_ref[b, :, :HALF], w2h[...]) + dot_nt(z_ref[b, :, HALF:], w2t[...])
+        grad = dot_nt(z_ref[b, :, :HALF], w2h) + dot_nt(z_ref[b, :, HALF:], w2t)
         grad = (grad * s_ref[b].astype(F32)).astype(BF)
         u_ref[b] = grad
-        away = dot_nt(grad, w1t[...])
-        near = dot_nt(grad, w1h[...])
+        away = dot_nt(grad, w1t)
+        near = dot_nt(grad, w1h)
 
         @pl.when(step == 0)
         def _():
@@ -450,23 +578,26 @@
             mt_ref[b] = acc[b].astype(BF)
 
 
-def expert_backward(rows, slope, w1h, w1t, w2h, w2t):
+def expert_backward(same, rows, slope, *weights):
     blocks, capacity, _ = rows.shape
-    hidden = w1h.shape[1]
-    across = pl.BlockSpec((HALF, TILE), lambda i: (0, i))
-    down = pl.BlockSpec((TILE, HALF), lambda i: (i, 0))
-    wide = pl.BlockSpec((blocks, capacity, TILE), lambda i: (0, 0, i))
+    hidden = weights[0].shape[1]
+    across = pl.BlockSpec((HALF, TILE), lambda i, s: (0, i))
+    down = pl.BlockSpec((TILE, HALF), lambda i, s: (i, 0))
+    wide = pl.BlockSpec((blocks, capacity, TILE), lambda i, s: (0, 0, i))
     make = lambda w, t: jax.ShapeDtypeStruct((blocks, capacity, w), t)
     return pl.pallas_call(
         backward_kernel,
-        grid=(hidden // TILE,),
-        in_specs=[whole(rows.shape), wide, across, across, down, down],
-        out_specs=[wide] + [whole((blocks, capacity, HALF))] * 2,
+        grid_spec=pltpu.PrefetchScalarGridSpec(
+            num_scalar_prefetch=1,
+            grid=(hidden // TILE,),
+            in_specs=[whole(rows.shape), wide, across, across, down, down],
+            out_specs=[wide] + [whole((blocks, capacity, HALF))] * 2,
+            scratch_shapes=[pltpu.VMEM((blocks, capacity, HALF), F32)],
+        ),
         out_shape=[make(hidden, BF), make(HALF, BF), make(HALF, F32)],
-        scratch_shapes=[pltpu.VMEM((blocks, capacity, HALF), F32)],
         name="expert_backward",
         cost_estimate=cost(),
-    )(rows, slope, w1h, w1t, w2h, w2t)
+    )(same, rows, slope, *weights)
 
 
 def outer_kernel(which_ref, *refs, chunks, hidden_first, added):
@@ -539,7 +670,11 @@
     y_ref,
     near_ref,
     away_ref,
-    rout_ref,
+    dgate_ref,
+    dgate2_ref,
+    probs_ref,
+    ids_ref,
+    narrow_ref,
     cot_ref,
     vec_ref,
     out_w_ref,
@@ -548,21 +683,45 @@
     w_ref,
     *refs,
 ):
-    dy_ref, dyb_ref, dqkv_ref, part_ref, sums2_ref, sums1_ref, att_ref = refs[-7:]
+    dy_ref, dyb_ref, dqkv_ref, part_ref, sums2_ref, sums1_ref, router_ref, att_ref = refs[-8:]
     first = which_ref[0] == 0
     start = pl.program_id(0) == 0
     near = near_ref[0].astype(F32)
     away = away_ref[0].astype(F32)
-    grad = rout_ref[0] + jnp.concatenate(
+    dgate = turn_back(dgate_ref[0] + dgate2_ref[0])
+    lane = lax.broadcasted_iota(jnp.int32, (ROWS, LANES), 1)
+    probs = probs_ref[0]
+    grad_probs = sum(
+        jnp.where(lane == ids_ref[0, :, c : c + 1], dgate[:, c : c + 1], 0.0) for c in range(2)
+    )
+    grad_logits = probs * (grad_probs - jnp.sum(probs * grad_probs, axis=1, keepdims=True))
+    grad = lax.dot_general(
+        grad_logits, narrow_ref[...].astype(F32), (((1,), (1,)), ((), ())),
+        precision=HIGH, preferred_element_type=F32,
+    ) + jnp.concatenate(
         [jnp.where(first, near, away), jnp.where(first, away, near)], axis=1
     )
     hat, scale = normed(y_ref[0])
+    h = (hat * vec_ref[2:3, :] + vec_ref[3:4, :]).astype(BF)
+    grad_router = lax.dot_general(
+        grad_logits, h.astype(F32), (((0,), (0,)), ((), ())),
+        precision=HIGH, preferred_element_type=F32,
+    )
+
+    @pl.when(start)
+    def _():
+        router_ref[...] = grad_router
+
+    @pl.when(jnp.logical_not(start))
+    def _():
+        router_ref[...] += grad_router
+
     add_sums(sums2_ref, grad, hat, start)
     dy = cot_ref[0].astype(F32) + norm_back(grad, hat, scale, vec_ref[2:3, :])
     dy_ref[0] = dy
     dyb = dy.astype(BF)
     dyb_ref[0] = dyb
-    att_ref[...] = dot_nn(dyb, out_w_ref[:, :HALF]).astype(BF)
+    att_ref[...] = dot_nn(dyb, out_w_ref[...]).astype(BF)
     keys_in = lax.broadcasted_iota(jnp.int32, (ROWS, ROWS), 1) < SEQ
     for h in range(HALF // HEAD):
         at = h * HEAD
@@ -584,8 +743,9 @@
     add_sums(sums1_ref, part, hat, start)
 
 
-def attend_back(which, x, y, near, away, rout, cot, vectors, out_w, qkv, lse, weight, lo, hi, held):
+def attend_back(which, x, y, near, away, dgate, dgate2, probs, ids, narrow, cot, vectors, out_w, qkv, lse, weight, lo, hi, held):
     total = y.shape[0]
+    turned = pl.BlockSpec((1, 8, ROWS), lambda i, s: (i + lo, 0, 0))
     return pl.pallas_call(
         attend_back_kernel,
         grid_spec=pltpu.PrefetchScalarGridSpec(
@@ -596,7 +756,11 @@
                 image(D, lo),
                 image(HALF),
                 image(HALF),
-                image(D, lo),
+                turned,
+                turned,
+                image(LANES, lo),
+                image(2, lo),
+                whole(narrow.shape),
                 image(D, lo),
                 whole(vectors.shape),
                 whole(out_w.shape),
@@ -612,6 +776,7 @@
                 image(D),
                 whole((8, D)),
                 whole((8, D)),
+                whole((LANES, D)),
             ],
             scratch_shapes=[pltpu.VMEM((ROWS, HALF), BF)],
         ),
@@ -622,11 +787,12 @@
             images(hi - lo, D, BF),
             jax.ShapeDtypeStruct((8, D), F32),
             jax.ShapeDtypeStruct((8, D), F32),
+            jax.ShapeDtypeStruct((LANES, D), F32),
         ],
-        input_output_aliases={12 + n: n for n in range(len(held))},
+        input_output_aliases={16 + n: n for n in range(len(held))},
         name="attend_back",
         cost_estimate=cost(),
-    )(which, x, y, near, away, rout, cot, vectors, out_w, qkv, lse, weight, *held)
+    )(which, x, y, near, away, dgate, dgate2, probs, ids, narrow, cot, vectors, out_w, qkv, lse, weight, *held)
 
 
 def token_kernel(x_ref, own_ref, got_ref, dy_ref, vec_ref, *refs):
@@ -697,43 +863,45 @@
     order = Order()
 
     small = jnp.stack([ln1_gain, ln1_bias, ln2_gain, ln2_bias], axis=1)
-    narrow = jnp.concatenate([small, w_router], axis=1)
+    narrow = jnp.concatenate([w_router, small], axis=1)
     narrow = jnp.pad(narrow, ((0, 0), (0, LANES - narrow.shape[1])))
-    first_pack = jnp.concatenate([w_query, w_key, w_value, narrow], axis=1).astype(BF)
-    out_own = jnp.transpose(w_out).astype(BF)
+    first_pack = jnp.concatenate(
+        [w_query, w_key, w_value, narrow, jnp.transpose(w_out)], axis=1
+    ).astype(BF)
     pair = cross(first_pack)
-    out_both = jnp.concatenate([out_own, hop(follow(out_own, first_pack), "tensor", 1)], axis=1)
-
-    slots = slot_table(follow(expert_ids, out_own), count)
-    rows = images_of(jnp.transpose((jnp.transpose(expert_ids) ^ here) * capacity + slots), -1)
+    in_own = follow(w_in, first_pack)[0].astype(BF)
+    back_own = follow(w_back, first_pack)[0].astype(BF)
+    ids_pad = images_of(follow(expert_ids, first_pack), -1)
+    pair, in_own, back_own, ids_pad = order.wait((pair, in_own, back_own, ids_pad))
+
+    same_chips = stacked(chip_copies(order.after(pair)))
+    in_other = hop(order.after(in_own), "dp", 1)
+
+    routes = order.after(expert_ids)
+    slots = slot_table(routes, count)
+    rows = images_of(jnp.transpose((jnp.transpose(routes) ^ here) * capacity + slots), -1)
     rows_lane = jnp.transpose(rows.reshape(-1, 2))
-    ids_pad = images_of(expert_ids, -1)
-    x = images_of(follow(tokens, out_own))
-    cot = images_of(follow(cotangent, out_own))
+    x = images_of(order.after(tokens))
+    cot = images_of(order.after(cotangent))
     cot_flat = cot.reshape(rows_all, D)
     cot_here = jnp.where(
         here_t == 0, cot_flat, jnp.concatenate([cot_flat[:, HALF:], cot_flat[:, :HALF]], axis=1)
     )
-    in_own = follow(w_in, out_own)[0].astype(BF)
-    back_own = follow(w_back, out_own)[0].astype(BF)
-
-    pair, out_both = order.wait((pair, out_both))
-    out_pair = cross(out_both)
-    same_chips = jnp.stack(chip_copies(pair))
-    same_chips, x, rows_lane, cot_here = order.wait((same_chips, x, rows_lane, cot_here))
-    flipped = hop(same_chips, "expert", 1)
-    out_pair = order.wait(out_pair)
-    in_other = hop(order.after(in_own), "dp", 1)
-    qkv_w, narrow_all = order.run(
-        lambda *v: assemble(*v, (3 * HALF, LANES)), same_chips, flipped
-    )
-    vectors = jnp.pad(jnp.transpose(narrow_all[:, :4]).astype(F32), ((0, 4), (0, 0)))
-    router_w = narrow_all[:, 4 : 4 + count]
-    router_pad = jnp.pad(router_w, ((0, 0), (0, LANES - count)))
-    out_same = jnp.stack(chip_copies(order.after(out_pair)))
-
     cut = (pictures + 1) // 2
     groups = [(0, cut), (cut, pictures)] if pictures > 1 else [(0, pictures)]
+    lanes_of = lambda value: [value[:, lo * ROWS : hi * ROWS] for lo, hi in groups]
+    same_chips, x, rows, rows_lane, cot, cot_here, own_lanes = order.wait(
+        (same_chips, x, rows, rows_lane, cot, cot_here, lanes_of(rows_lane))
+    )
+    flipped = order.wait(hop(order.after(same_chips), "expert", 1))
+    qkv_w, narrow_all, out_here = order.run(
+        lambda *v: assemble(*v, (3 * HALF, LANES, HALF)), same_chips, flipped
+    )
+    out_there = hop(order.after(out_here), "tensor", 1)
+    vectors = order.run(lambda v: vectors_of(v, count), narrow_all)
+    rows_next = hop(order.after(rows_lane), "expert", 1)
+    cot_next = hop(order.after(cot_here), "expert", 1)
+
     held, o_parts, got_parts = [], [], []
     for n, (lo, hi) in enumerate(groups):
         *held, o_part = order.run(
@@ -742,32 +910,29 @@
         o_parts.append(o_part)
         got_parts.append(hop(o_part, "tensor", 1))
         if n == 0:
-            out_same = order.wait(out_same)
-            out_flip = hop(out_same, "expert", 1)
+            rows_next, cot_next = order.wait((rows_next, cot_next))
     a_rows, qkv, o_rows, lse = held
-    (out_w,) = order.run(lambda *v: assemble(*v, (D,)), out_same, out_flip)
-    rows_next = hop(order.after(rows_lane), "expert", 1)
-    cot_next = hop(order.after(cot_here), "expert", 1)
-    rows_next, cot_next = order.wait((rows_next, cot_next))
-    in_other = order.wait(in_other)
-    back_other = hop(order.after(back_own), "dp", 1)
-    w1h, w1t = jnp.where(same, in_own, in_other), jnp.where(same, in_other, in_own)
+    out_there = order.wait(out_there)
+    got_parts = list(order.wait(tuple(got_parts)))
+    next_lanes = order.wait(lanes_of(rows_next))
     held, h_parts, h_next = [], [], []
     for n, (lo, hi) in enumerate(groups):
         *held, h_part = order.run(
-            lambda x, o, g, v, w, r, i, *h: route(which, x, o, g, v, w, r, i, count, lo, hi, h),
-            x, o_parts[n], got_parts[n], vectors, out_w, router_pad, ids_pad, *held,
+            lambda x, o, g, v, w, t, r, i, *h: route(which, x, o, g, v, w, t, r, i, count, lo, hi, h),
+            x, o_parts[n], got_parts[n], vectors, out_here, out_there, narrow_all, ids_pad, *held,
         )
         h_parts.append(h_part.reshape(-1, D))
         h_next.append(hop(h_parts[-1], "expert", 1))
+        if n == 0:
+            in_other = order.wait(in_other)
+            back_other = hop(order.after(back_own), "dp", 1)
     y, probs, gates = held
-    probs = probs.reshape(rows_all, LANES)[:, :count]
     gates_lane = jnp.transpose(gates.reshape(rows_all, LANES)[:, :2])
     gates_next = hop(gates_lane, "expert", 1)
 
-    lanes_of = lambda value: [value[:, lo * ROWS : hi * ROWS] for lo, hi in groups]
-    own = (lanes_of(rows_lane), h_parts)
-    other = (lanes_of(rows_next), h_next)
+    gates_next = order.wait(gates_next)
+    own = (own_lanes, h_parts)
+    other = (next_lanes, h_next)
     far = list(range(1, chips))
     outgoing = order.run(lambda *v: send_rows(*v, capacity, far, False), own, other)
     arrived = [None] + [hop(o, "expert", 2 * c) for o, c in zip(outgoing, far)]
@@ -775,101 +940,122 @@
     own = ([rows_lane], [cot_here], [gates_lane])
     other = ([rows_next], [cot_next], [gates_next])
     grad_outgoing = order.run(lambda *v: send_rows(*v, capacity, far, True), own, other)
-    grad_arrived = [None] + [hop(o, "expert", 2 * c) for o, c in zip(grad_outgoing, far)]
+    grad_arrived = [None] * chips
     (grad_arrived[0],) = order.run(lambda *v: send_rows(*v, capacity, [0], True), own, other)
-    w2h, w2t = jnp.where(same, back_own, back_other), jnp.where(same, back_other, back_own)
-
-    hidden, slopes, grads, came_back, grad_home = [], [], [], [], []
-
-    def return_rows(away, near, c):
-        value = (near + hop(away, "tensor", 1).astype(F32)).astype(BF)
-        return hop(value, "expert", 2 * c) if c else value
-
+    back_other = order.wait(back_other)
+    weights = (in_own, in_other, back_own, back_other)
+    same = flag(same)
+
+    hidden, slopes, grads = [], [], []
+    came_back, grad_home = [None] * chips, [None] * chips
+
+    def back_to(chip, waiting):
+        value = order.run(add_halves, *waiting)
+        return hop(value, "expert", 2 * chip) if chip else value
+
+    pending = None
     for c in range(chips):
-        g, s, zt, zh = order.run(expert_forward, arrived[c], w1h, w1t, w2h, w2t)
+        if c == 1:
+            arrived[1:] = order.wait(arrived[1:])
+            if chips <= 4:
+                grad_arrived[1:] = [
+                    hop(order.after(o), "expert", 2 * k) for o, k in zip(grad_outgoing, far)
+                ]
+        if c and chips > 4:
+            grad_arrived[c] = hop(order.after(grad_outgoing[c - 1]), "expert", 2 * c)
+        if c == chips - 1 and chips <= 4:
+            grad_arrived[1:] = order.wait(grad_arrived[1:])
+        g, s, zt, zh = order.run(lambda *v: expert_forward(same, *v), arrived[c], *weights)
         hidden.append(g)
         slopes.append(s)
-        came_back.append(return_rows(zt, zh, c))
+        if pending is not None:
+            came_back[c - 1] = back_to(c - 1, pending)
+        pending = (zh, hop(order.after(zt), "tensor", 1))
     for c in range(chips):
+        if c and chips > 4:
+            grad_arrived[c] = order.wait(grad_arrived[c])
         u, mt, mh = order.run(
-            expert_backward, grad_arrived[c], slopes[c], w1h, w1t, w2h, w2t
+            lambda *v: expert_backward(same, *v), grad_arrived[c], slopes[c], *weights
         )
         grads.append(u)
-        grad_home.append(return_rows(mt, mh, c))
-    send_half = jnp.where(same, 1, 0).astype(jnp.int32).reshape(1)
+        if c:
+            grad_home[c - 1] = back_to(c - 1, pending)
+        else:
+            came_back[1] = order.wait(came_back[1])
+            came_back[chips - 1] = back_to(chips - 1, pending)
+        if c >= chips // 2:
+            step = (chips - 2) * 2 // chips
+            for k in range(2 + (c - chips // 2) * step, 2 + (c - chips // 2 + 1) * step):
+                came_back[k] = order.wait(came_back[k])
+        pending = (mh, hop(order.after(mt), "tensor", 1))
+    z_here, z_there = order.run(lambda *v: sort_groups(v), *order.wait(tuple(came_back)))
+    z_there = hop(z_there, "expert", 1)
+    send_half = same
     back_send = order.run(lambda h, g: outer(send_half, h, g, True), hidden, grad_arrived)
-    back_got = hop(back_send, "dp", 1)
+    grad_home[chips - 1] = back_to(chips - 1, pending)
+    back_got = hop(order.after(back_send), "dp", 1)
     in_send = order.run(lambda g, a: outer(send_half, g, a, False), grads, arrived)
-    in_got = hop(follow(in_send, back_got), "dp", 1)
-
-    def settle(parts):
-        mine = jnp.stack([p[0] for p in parts])
-        return mine, hop(jnp.stack([p[1] for p in parts]), "expert", 1)
+    grad_home = list(order.wait(tuple(grad_home)))
+    m_here, m_there = order.run(lambda *v: sort_groups(v), *grad_home)
+    m_there = hop(m_there, "expert", 1)
 
     out_half, dgate = order.run(
-        lambda *v: bring_home(which, *v), rows, y, cot, gates, *settle(came_back)
-    )
-    out_other = hop(out_half, "tensor", 1)
-    dgate = jnp.transpose(dgate.reshape(rows_all, LANES)[:, :2])
-    dgate = jnp.transpose(dgate + hop(dgate, "tensor", 1))
-    ids_flat = ids_pad.reshape(rows_all, 2)
-    lanes = jnp.arange(count, dtype=jnp.int32)[None, :]
-    grad_probs = sum(
-        jnp.where(ids_flat[:, c : c + 1] == lanes, dgate[:, c : c + 1], 0.0) for c in range(2)
-    )
-    grad_logits = probs * (grad_probs - jnp.sum(probs * grad_probs, axis=-1, keepdims=True))
-    grad_rout = jnp.dot(grad_logits, jnp.transpose(router_w.astype(F32)), precision=HIGH)
-    grad_rout = grad_rout.reshape(pictures, ROWS, D)
-
-    back = settle(grad_home)
+        lambda *v: bring_home(which, *v), rows, y, cot, gates, z_here, z_there
+    )
+    dgate_next = hop(dgate, "tensor", 1)
+    m_there = order.wait(m_there)
     near_parts = []
-    for lo, hi in groups:
-        near = order.run(lambda *v: sum_home(*v, lo, hi), rows, *back)
+    for n, (lo, hi) in enumerate(groups):
+        near = order.run(lambda *v: sum_home(*v, lo, hi), rows, m_here, m_there)
         near_parts.append((near, hop(near, "tensor", 1)))
+    dgate_next = order.wait(dgate_next)
     held, parts, sums, got = [], [], [], []
     for n, (lo, hi) in enumerate(groups):
-        *held, part, sums2, sums1 = order.run(
-            lambda *v: attend_back(which, *v[:11], lo, hi, v[11:]),
-            x, y, *near_parts[n], grad_rout, cot, vectors, out_w, qkv, lse, qkv_w, *held,
+        if n == len(groups) - 1:
+            near_parts[n], back_got = order.wait((near_parts[n], back_got))
+            in_got = hop(order.after(in_send), "dp", 1)
+        *held, part, sums2, sums1, grad_router = order.run(
+            lambda *v: attend_back(which, *v[:15], lo, hi, v[15:]),
+            x, y, *near_parts[n], dgate, dgate_next, probs, ids_pad, narrow_all, cot, vectors, out_here, qkv, lse, qkv_w, *held,
         )
         parts.append(part)
         got.append(hop(part, "tensor", 1))
-        sums.append(jnp.concatenate([sums1[:2], 0.5 * sums2[:2]], axis=0))
+        sums.append(
+            jnp.concatenate([0.5 * grad_router[:count], sums1[:2], 0.5 * sums2[:2]], axis=0)
+        )
     dy, dyb, dqkv = held
-    out_other = order.wait(out_other)
 
     flat = lambda value: value.reshape(rows_all, -1)
     grad_outw = dot_tn(flat(dyb), flat(o_rows))
     grad_wqkv = dot_tn(flat(a_rows), flat(dqkv))
-    shards, leaving = scatter_sum(jnp.concatenate([grad_wqkv, grad_outw], axis=1), BF)
-    grad_router = sum(
-        jnp.dot(part, h.astype(F32), precision=HIGH)
-        for part, h in zip(lanes_of(jnp.transpose(grad_logits)), h_parts)
-    )
-    grad_router = jnp.where(
-        here_t == 0,
-        grad_router,
-        jnp.concatenate([grad_router[:, HALF:], grad_router[:, :HALF]], axis=1),
-    )
-    tiny = jnp.concatenate([0.5 * grad_router, sum(sums)], axis=0)
-    tiny = tiny + hop(tiny, "tensor", 1)
-    for offset in [1 << b for b in range(count.bit_length() - 1)]:
-        tiny = tiny + hop(tiny, "expert", offset)
-    tiny = tiny + hop(tiny, "dp", 1)
-    tiny = tiny.reshape(tiny.shape[0], 2 * count, -1)
-    tiny = lax.dynamic_index_in_dim(tiny, here_dp * count + here, 1, False)
-
+    tiny = jnp.transpose(sum(sums))
+    tiny = jnp.pad(tiny, ((0, 0), (0, -tiny.shape[1] % LANES)))
+    all_grads = jnp.concatenate([grad_wqkv, grad_outw, tiny], axis=1)
+    keep_half = 1 - send_half
+    total = core_sum(order.after(all_grads), BF)
+    grad_back = order.run(
+        lambda h, g, b: outer(keep_half, h, g, True, b), hidden, grad_arrived, back_got
+    )[None]
+    shards, leaving = chip_sum(order.wait(total), BF)
     grad_tokens = []
     for n, (lo, hi) in enumerate(groups):
-        if n == len(groups) - 1:
-            leaving = order.wait(leaving)
-            shards = shards + hop(leaving, "dp", 1).astype(F32)
         grad_tokens = [
             order.run(
                 lambda *v: token_back(*v[:5], lo, hi, v[5:]),
                 x, parts[n], got[n], dy, vectors, *grad_tokens,
             )
         ]
+        if n == 0:
+            shards, leaving = order.wait((shards, leaving))
+            entering = hop(leaving, "dp", 1)
+    out_other = hop(order.after(out_half), "tensor", 1)
+    shards = order.wait(shards + entering.astype(F32))
+    tiny = shards[:, 4 * HALF :]
+    tiny_next = hop(tiny, "tensor", 1)
+    grad_in = order.run(
+        lambda g, a, b: outer(keep_half, g, a, False, b), grads, arrived, in_got
+    )[None]
+    tiny = tiny + tiny_next
     grad_tokens = grad_tokens[0][:, :SEQ].reshape(tok, D)
     block_out = jnp.where(
         here_t == 0,
@@ -877,22 +1063,18 @@
         jnp.concatenate([out_other, out_half], axis=2),
     )
     block_out = block_out[:, :SEQ].reshape(tok, D)
-
-    keep_half = 1 - send_half
-    grad_back = order.run(lambda h, g, b: outer(keep_half, h, g, True, b), hidden, grad_arrived, back_got)[None]
-    grad_in = order.run(lambda g, a, b: outer(keep_half, g, a, False, b), grads, arrived, in_got)[None]
     return (
         block_out,
         grad_tokens,
-        tiny[count],
-        tiny[count + 1],
-        tiny[count + 2],
-        tiny[count + 3],
+        tiny[:, count],
+        tiny[:, count + 1],
+        tiny[:, count + 2],
+        tiny[:, count + 3],
         shards[:, :HALF],
         shards[:, HALF : 2 * HALF],
         shards[:, 2 * HALF : 3 * HALF],
-        jnp.transpose(shards[:, 3 * HALF :]),
-        jnp.transpose(tiny[:count]),
+        jnp.transpose(shards[:, 3 * HALF : 4 * HALF]),
+        tiny[:, :count],
         grad_in,
         grad_back,
     )

time: 630 us -> 607 us (0.963)
  Pallas kernels: 246 us -> 283 us
  other arithmetic: 44.3 us -> 20.7 us
  waiting for transfers between devices: 205 us -> 184 us
    pallas_call x8 -> x21, Pallas kernels: 91.7 us -> 121 us  [the longest x4 52.9 us: expert_forward(): pl.pallas_call(forward_kernel, grid_spec=pltpu.PrefetchScalarGridSpec(num...]
    ppermute x60 -> x51, waiting for transfers between devices: 205 us -> 184 us  [hop(): return lax.ppermute(value, axis, [(i, i ^ offset) for i in range(count)])]
    convert_element_type x11 -> x2, other arithmetic: 11.3 us -> 1.92 us  [the longest x1 1.79 us: on_device(): back_own = follow(w_back, first_pack)[0].astype(BF)]
    unnamed x118 -> x120, local copies, waits for them, and re-layouts: 12.9 us -> 21.4 us
    pallas_call x2, Pallas kernels: 28.8 us -> 36.5 us  [attend_back(): pl.pallas_call(attend_back_kernel, grid_spec=pltpu.PrefetchScalarGridSpec...]
    slice x16 -> x5, local copies, waits for them, and re-layouts: 9.06 us -> 2.51 us  [the longest x2 1.48 us: on_device(): sums1[:2]]
    ppermute x60 -> x51, starting transfers between devices: 61.6 us -> 55.5 us  [hop(): return lax.ppermute(value, axis, [(i, i ^ offset) for i in range(count)])]
  transfers between devices with their start and end apart: 60 -> 51, of which waited for: 23 -> 18; matrix products, arithmetic and copies ran while one was open for 13% -> 6% of each run, Pallas kernels for 37% -> 42%
where the time goes in v3:
time: 607 us; the launch traced here: 598 us
  Pallas kernels  283 us (47%)
  waiting for transfers between devices  184 us (30%)
  starting transfers between devices  55.5 us (9%)
  local copies, waits for them, and re-layouts  47.8 us (8%)
  other arithmetic  20.7 us (3%)
    ppermute x51, waiting for transfers between devices, hop(): return lax.ppermute(value, axis, [(i, i ^ offset) for i in range(count)])  184 us
    ppermute x51, starting transfers between devices, hop(): return lax.ppermute(value, axis, [(i, i ^ offset) for i in range(count)])  55.5 us
    pallas_call x4, Pallas kernels, expert_forward(): pl.pallas_call(forward_kernel, grid_spec=pltpu.PrefetchScalarGridSpec(num...  52.9 us
    pallas_call x4, Pallas kernels, expert_backward(): pl.pallas_call(backward_kernel, grid_spec=pltpu.PrefetchScalarGridSpec(nu...  39.5 us
    pallas_call x4, Pallas kernels, outer(): pl.pallas_call(functools.partial(outer_kernel, chunks=len(wides), hidden_...  38.1 us
    pallas_call x2, Pallas kernels, attend_back(): pl.pallas_call(attend_back_kernel, grid_spec=pltpu.PrefetchScalarGridSpec...  36.5 us
    pallas_call x4, Pallas kernels, send_rows(): pl.pallas_call(functools.partial(send_kernel, parts=len(own[0]), chips=ch...  23.4 us
    unnamed x120, local copies, waits for them, and re-layouts  21.4 us
  transfers between devices with their start and end apart: 51, of which 18 were waited for; matrix products, arithmetic and copies ran while one was open for 6% of the time, Pallas kernels for 42%

profile of v3, /device:TPU:0, one launch (start us, length us, event | category | flops | bytes accessed | tf_op | source)
XLA Modules:
  0.0 598.2 jit_solution(3634546335958544931)
XLA Ops:
  6.6 4.1 collective-permute-start
  14.4 3.8 collective-permute-done.across_ref
  29.2 2.9 reshape.110
  35.8 2.9 reshape.104
  38.8 2.8 pad.29.x_ref
  45.6 3.3 collective-permute-done.4.flip_ref
  49.0 3.4 assemble.1
  54.2 4.1 collective-permute-start.7
  58.3 8.3 %attend.2 = (bf16[5,208,768]{2,1,0:T(8,128)(2,1)}, bf16[5,208,1152]{2,1,0:T(8,128)(2,1)}, bf16[5,208,384]{2,1,0:T(8,128)(2,1)}, f32[5,208,128]{2,1,0:T(8,128)}, bf16[3,208,384]{2,1,0:T(8,128)(2,1)}) custom-call(bf16[5,208,768]{2,1,0:T(8,128)(2,1)} %pad.29.x_ref, f32[8,768]{1,0:T(8,128)} %vectors.1.vec_ref, bf16[768,1152]{1,0:T(8,128)(2,1)} %get-tuple-element.980.w_ref), custom_call_target="tpu_custom_call" | custom-call | flops 1000 | bytes 1000 | tf_op jit(solution)/shard_map/attend/pallas_call | solution.py:294
  68.5 6.4 %attend.3 = (bf16[5,208,768]{2,1,0:T(8,128)(2,1)}, bf16[5,208,1152]{2,1,0:T(8,128)(2,1)}, bf16[5,208,384]{2,1,0:T(8,128)(2,1)}, f32[5,208,128]{2,1,0:T(8,128)}, bf16[2,208,384]{2,1,0:T(8,128)(2,1)}) custom-call(bf16[5,208,768]{2,1,0:T(8,128)(2,1)} %pad.29.x_ref, ...), custom_call_target="tpu_custom_call", output_to_operand_aliasing={{0}: (3, {}), {1}: (4, {}), {2}: (5, {}), {3}: (6, {})} | custom-call | flops 1000 | bytes 1000 | tf_op jit(solution)/shard_map/attend/pallas_call | solution.py:294
  78.1 15.3 %collective-permute-done.7.there_ref = bf16[768,384]{1,0:T(8,128)(2,1)} collective-permute-done((bf16[768,384]{1,0:T(8,128)(2,1)}, bf16[768,384]{1,0:T(8,128)(2,1)}, u32[]{:S(2)}, u32[]{:S(2)}) %collective-permute-start.7) | collective-permute-done | bytes 589856 | tf_op jit(solution)/shard_map/ppermute | solution.py:40
  93.4 10.3 %collective-permute-done.8.got_ref = bf16[3,208,384]{2,1,0:T(8,128)(2,1)} collective-permute-done((bf16[3,208,384]{2,1,0:T(8,128)(2,1)}, bf16[3,208,384]{2,1,0:T(8,128)(2,1)}, u32[]{:S(2)}, u32[]{:S(2)}) %collective-permute-start.8) | collective-permute-done | bytes 479264 | tf_op jit(solution)/shard_map/ppermute | solution.py:40
  103.7 10.0 %collective-permute-done.9.got_ref = bf16[2,208,384]{2,1,0:T(8,128)(2,1)} collective-permute-done((bf16[2,208,384]{2,1,0:T(8,128)(2,1)}, bf16[2,208,384]{2,1,0:T(8,128)(2,1)}, u32[]{:S(2)}, u32[]{:S(2)}) %collective-permute-start.9) | collective-permute-done | bytes 319520 | tf_op jit(solution)/shard_map/ppermute | solution.py:40
  113.6 6.7 %route.2 = (f32[5,208,768]{2,1,0:T(8,128)}, f32[5,208,128]{2,1,0:T(8,128)}, f32[5,208,128]{2,1,0:T(8,128)}, bf16[3,208,768]{2,1,0:T(8,128)(2,1)}) custom-call(s32[1]{0:T(128)} %bitcast.15.which_ref, bf16[5,208,768]{2,1,0:T(8,128)(2,1)} %pad.29.x_ref, bf16[3,208,384]{2,1,0:T(8,128)(2,1)} %get-tuple-element.605.own_ref, ...), custom_call_target="tpu_custom_call" | custom-call | flops 1000 | bytes 1000 | tf_op jit(solution)/shard_map/route/pallas_call | solution.py:339
  121.6 5.4 route.3
  130.7 7.0 %send_rows.2 = (bf16[2,312,768]{2,1,0:T(8,128)(2,1)}, bf16[2,312,768]{2,1,0:T(8,128)(2,1)}, bf16[2,312,768]{2,1,0:T(8,128)(2,1)}) custom-call(s32[2,624]{1,0:T(2,128)} %slice.116.refs_0_, s32[2,416]{1,0:T(2,128)} %slice.117.refs_1_, bf16[624,768]{1,0:T(8,128)(2,1)} %bitcast.95, bf16[416,768]{1,0:T(8,128)(2,1)} %bitcast.98, s32[2,624]{1,0:T(2,128)} %slice.91.refs_4_, ...), custom_call_target="tpu_custom_call" | custom-call | flops 1000 | bytes 1000 | tf_op jit(solution)/shard_map/send_rows/pallas_call | solution.py:397
  141.1 4.4 send_rows.3.m_ref.refs_4_
  145.5 7.4 %send_gated.2 = (bf16[2,312,768]{2,1,0:T(8,128)(2,1)}, bf16[2,312,768]{2,1,0:T(8,128)(2,1)}, bf16[2,312,768]{2,1,0:T(8,128)(2,1)}) custom-call(s32[2,1040]{1,0:T(2,128)} %bitcast.108, bf16[1040,768]{1,0:T(8,128)(2,1)} %maximum_select_fusion.refs_1_, f32[2,1040]{1,0:T(2,128)} %bitcast.111, s32[2,1040]{1,0:T(2,128)} %copy-done.47, ...), custom_call_target="tpu_custom_call" | custom-call | flops 1000 | bytes 1000 | tf_op jit(solution)/shard_map/send_gated/pallas_call | solution.py:397
  152.9 4.7 send_gated.3.z_ref.refs_4_
  157.6 17.3 %collective-permute-done.14.back_other = bf16[1536,384]{1,0:T(8,128)(2,1)S(1)} collective-permute-done((bf16[1536,384]{1,0:T(8,128)(2,1)S(1)}, bf16[1536,384]{1,0:T(8,128)(2,1)S(1)}, u32[]{:S(2)}, u32[]{:S(2)}) %collective-permute-start.14) | collective-permute-done | bytes 1179680 | tf_op jit(solution)/shard_map/ppermute | solution.py:40
  175.9 13.3 %expert_forward.4 = (bf16[2,312,1536]{2,1,0:T(8,128)(2,1)}, bf16[2,312,1536]{2,1,0:T(8,128)(2,1)}, bf16[2,312,384]{2,1,0:T(8,128)(2,1)}, f32[2,312,384]{2,1,0:T(8,128)}) custom-call(s32[1]{0:T(128)} %bitcast.20.same_ref.which_ref, bf16[2,312,768]{2,1,0:T(8,128)(2,1)} %send_rows.3.m_ref.refs_4_, bf16[384,1536]{1,0:T(8,128)(2,1)} %copy-done.1, ...), custom_call_target="tpu_custom_call" | custom-call | flops 1000 | bytes 1000 | tf_op jit(solution)/shard_map/expert_forward/pallas_call | solution.py:540
  190.2 13.1 %expert_forward.5 = (bf16[2,312,1536]{2,1,0:T(8,128)(2,1)}, bf16[2,312,1536]{2,1,0:T(8,128)(2,1)}, bf16[2,312,384]{2,1,0:T(8,128)(2,1)}, f32[2,312,384]{2,1,0:T(8,128)}) custom-call(s32[1]{0:T(128)} %bitcast.20.same_ref.which_ref, bf16[2,312,768]{2,1,0:T(8,128)(2,1)} %copy-done.11, bf16[384,1536]{1,0:T(8,128)(2,1)} %copy-done.1, ...), custom_call_target="tpu_custom_call" | custom-call | flops 1000 | bytes 1000 | tf_op jit(solution)/shard_map/expert_forward/pallas_call | solution.py:540
  211.7 13.1 %expert_forward.6 = (bf16[2,312,1536]{2,1,0:T(8,128)(2,1)}, bf16[2,312,1536]{2,1,0:T(8,128)(2,1)}, bf16[2,312,384]{2,1,0:T(8,128)(2,1)}, f32[2,312,384]{2,1,0:T(8,128)}) custom-call(s32[1]{0:T(128)} %bitcast.20.same_ref.which_ref, bf16[2,312,768]{2,1,0:T(8,128)(2,1)} %collective-permute-done.16.m_ref.refs_6_, bf16[384,1536]{1,0:T(8,128)(2,1)} %copy-done.1, ...), custom_call_target="tpu_custom_call" | custom-call | flops 1000 | bytes 1000 | tf_op jit(solution)/shard_map/expert_forward/pallas_call | solution.py:540
  231.5 19.7 %collective-permute-done.21.z_ref.refs_6_ = bf16[2,312,768]{2,1,0:T(8,128)(2,1)S(1)} collective-permute-done((bf16[2,312,768]{2,1,0:T(8,128)(2,1)}, bf16[2,312,768]{2,1,0:T(8,128)(2,1)S(1)}, u32[]{:S(2)}, u32[]{:S(2)}) %collective-permute-start.21) | collective-permute-done | bytes 958496 | tf_op jit(solution)/shard_map/ppermute | solution.py:40
  252.1 13.4 %expert_forward.7 = (bf16[2,312,1536]{2,1,0:T(8,128)(2,1)}, bf16[2,312,1536]{2,1,0:T(8,128)(2,1)}, bf16[2,312,384]{2,1,0:T(8,128)(2,1)}, f32[2,312,384]{2,1,0:T(8,128)}) custom-call(s32[1]{0:T(128)} %bitcast.20.same_ref.which_ref, bf16[2,312,768]{2,1,0:T(8,128)(2,1)} %collective-permute-done.17.m_ref.refs_7_, bf16[384,1536]{1,0:T(8,128)(2,1)} %copy-done.1, ...), custom_call_target="tpu_custom_call" | custom-call | flops 1000 | bytes 1000 | tf_op jit(solution)/shard_map/expert_forward/pallas_call | solution.py:540
  269.6 10.2 %expert_backward.4 = (bf16[2,312,1536]{2,1,0:T(8,128)(2,1)}, bf16[2,312,384]{2,1,0:T(8,128)(2,1)}, f32[2,312,384]{2,1,0:T(8,128)}) custom-call(s32[1]{0:T(128)} %bitcast.20.same_ref.which_ref, bf16[2,312,768]{2,1,0:T(8,128)(2,1)} %send_gated.3.z_ref.refs_4_, bf16[2,312,1536]{2,1,0:T(8,128)(2,1)} %get-tuple-element.769.s_ref, bf16[384,1536]{1,0:T(8,128)(2,1)} %copy-done.1, ...), custom_call_target="tpu_custom_call" | custom-call | flops 1000 | bytes 1000 | tf_op jit(solution)/shard_map/expert_backward/pallas_call | solution.py:588
  284.6 9.8 %expert_backward.5 = (bf16[2,312,1536]{2,1,0:T(8,128)(2,1)}, bf16[2,312,384]{2,1,0:T(8,128)(2,1)}, f32[2,312,384]{2,1,0:T(8,128)}) custom-call(s32[1]{0:T(128)} %bitcast.20.same_ref.which_ref, bf16[2,312,768]{2,1,0:T(8,128)(2,1)} %copy-done.10, bf16[2,312,1536]{2,1,0:T(8,128)(2,1)} %get-tuple-element.789.s_ref, bf16[384,1536]{1,0:T(8,128)(2,1)} %copy-done.1, ...), custom_call_target="tpu_custom_call" | custom-call | flops 1000 | bytes 1000 | tf_op jit(solution)/shard_map/expert_backward/pallas_call | solution.py:588
  301.0 9.8 %expert_backward.6 = (bf16[2,312,1536]{2,1,0:T(8,128)(2,1)}, bf16[2,312,384]{2,1,0:T(8,128)(2,1)}, f32[2,312,384]{2,1,0:T(8,128)}) custom-call(s32[1]{0:T(128)} %bitcast.20.same_ref.which_ref, bf16[2,312,768]{2,1,0:T(8,128)(2,1)} %copy-done.9, bf16[2,312,1536]{2,1,0:T(8,128)(2,1)} %get-tuple-element.807.s_ref, bf16[384,1536]{1,0:T(8,128)(2,1)} %copy-done.1, ...), custom_call_target="tpu_custom_call" | custom-call | flops 1000 | bytes 1000 | tf_op jit(solution)/shard_map/expert_backward/pallas_call | solution.py:588
  315.2 9.7 %expert_backward.7 = (bf16[2,312,1536]{2,1,0:T(8,128)(2,1)}, bf16[2,312,384]{2,1,0:T(8,128)(2,1)}, f32[2,312,384]{2,1,0:T(8,128)}) custom-call(s32[1]{0:T(128)} %bitcast.20.same_ref.which_ref, bf16[2,312,768]{2,1,0:T(8,128)(2,1)} %copy-done.8, bf16[2,312,1536]{2,1,0:T(8,128)(2,1)} %get-tuple-element.827.s_ref, bf16[384,1536]{1,0:T(8,128)(2,1)} %copy-done.1, ...), custom_call_target="tpu_custom_call" | custom-call | flops 1000 | bytes 1000 | tf_op jit(solution)/shard_map/expert_backward/pallas_call | solution.py:588
  330.1 2.9 sort_groups.2
  333.0 9.7 %outer_send.2 = bf16[1536,384]{1,0:T(8,128)(2,1)} custom-call(s32[1]{0:T(128)} %bitcast.20.same_ref.which_ref, bf16[2,312,1536]{2,1,0:T(8,128)(2,1)} %get-tuple-element.993.refs_0_, bf16[2,312,1536]{2,1,0:T(8,128)(2,1)} %get-tuple-element.994.refs_1_, bf16[2,312,1536]{2,1,0:T(8,128)(2,1)} %get-tuple-element.995.refs_2_, ...), custom_call_target="tpu_custom_call" | custom-call | flops 1000 | bytes 1000 | tf_op jit(solution)/shard_map/outer_send/pallas_call | solution.py:631
  348.3 8.8 %outer_send.3 = bf16[384,1536]{1,0:T(8,128)(2,1)} custom-call(s32[1]{0:T(128)} %bitcast.20.same_ref.which_ref, bf16[2,312,1536]{2,1,0:T(8,128)(2,1)} %get-tuple-element.1042.refs_0_, bf16[2,312,1536]{2,1,0:T(8,128)(2,1)} %get-tuple-element.1043.refs_1_, bf16[2,312,1536]{2,1,0:T(8,128)(2,1)} %get-tuple-element.1044.refs_2_, ...), custom_call_target="tpu_custom_call" | custom-call | flops 1000 | bytes 1000 | tf_op jit(solution)/shard_map/outer_send/pallas_call | solution.py:631
  357.1 5.7 collective-permute-done.33.refs_2_
  364.4 2.9 sort_groups.3
  369.7 15.1 %bring_home.1 = (bf16[5,208,384]{2,1,0:T(8,128)(2,1)}, f32[5,8,208]{2,1,0:T(8,128)}) custom-call(s32[1]{0:T(128)} %bitcast.15.which_ref, s32[5,208,2]{2,1,0:T(8,128)} %copy-done.7, f32[5,208,768]{2,1,0:T(8,128)} %get-tuple-element.967.middle_ref.y_ref, bf16[5,208,768]{2,1,0:T(8,128)(2,1)} %copy-done.4, f32[5,208,128]{2,1,0:T(8,128)} %get-tuple-element.908.gates_ref, ...), custom_call_target="tpu_custom_call" | custom-call | flops 1000 | bytes 1000 | tf_op jit(solution)/shard_map/bring_home/pallas_call | solution.py:449
  385.7 5.6 sum_home.2.near_ref
  392.7 4.5 sum_home.3.near_ref
  399.2 38.2 %collective-permute-done.37.dgate2_ref = f32[5,8,208]{2,1,0:T(8,128)S(1)} collective-permute-done((f32[5,8,208]{2,1,0:T(8,128)S(1)}, f32[5,8,208]{2,1,0:T(8,128)S(1)}, u32[]{:S(2)}, u32[]{:S(2)}) %collective-permute-start.37) | collective-permute-done | bytes 33312 | tf_op jit(solution)/shard_map/ppermute | solution.py:40
  438.8 20.9 %attend_back.2 = (f32[5,208,768]{2,1,0:T(8,128)}, bf16[5,208,768]{2,1,0:T(8,128)(2,1)}, bf16[5,208,1152]{2,1,0:T(8,128)(2,1)}, bf16[3,208,768]{2,1,0:T(8,128)(2,...) custom-call(s32[1]{0:T(128)} %bitcast.15.which_ref, bf16[5,208,768]{2,1,0:T(8,128)(2,1)} %pad.29.x_ref, ...), custom_call_target="tpu_custom_call" | custom-call | flops 1000 | bytes 1000 | tf_op jit(solution)/shard_map/attend_back/pallas_call | solution.py:749
  460.5 15.6 %attend_back.3 = (f32[5,208,768]{2,1,0:T(8,128)}, bf16[5,208,768]{2,1,0:T(8,128)(2,1)}, bf16[5,208,1152]{2,1,0:T(8,128)(2,1)}, bf16[2,208,768]{2,1,0:T(8,128)(2,...) custom-call(s32[1]{0:T(128)} %bitcast.15.which_ref, ...), custom_call_target="tpu_custom_call", output_to_operand_aliasing={{0}: (16, {}), {1}: (17, {}), {2}: (18, {})} | custom-call | flops 1000 | bytes 1000 | tf_op jit(solution)/shard_map/attend_back/pallas_call | solution.py:749
  480.8 4.5 convolution_bitcast_fusion
  489.5 10.2 %outer_keep.2 = f32[1536,384]{1,0:T(8,128)} custom-call(s32[1]{0:T(128)S(6)} %sub.13.which_ref, bf16[2,312,1536]{2,1,0:T(8,128)(2,1)} %get-tuple-element.993.refs_0_, bf16[2,312,1536]{2,1,0:T(8,128)(2,1)} %get-tuple-element.994.refs_1_, bf16[2,312,1536]{2,1,0:T(8,128)(2,1)} %get-tuple-element.995.refs_2_, bf16[2,312,1536]{2,1,0:T(8,128)(2,1)} %get-tuple-element.996.refs_3_, ...), custom_call_target="tpu_custom_call" | custom-call | flops 1000 | bytes 1000 | tf_op jit(solution)/shard_map/outer_keep/pallas_call | solution.py:631
  508.8 28.1 %collective-permute-done.42.got_ref = bf16[3,208,768]{2,1,0:T(8,128)(2,1)} collective-permute-done((bf16[3,208,768]{2,1,0:T(8,128)(2,1)S(1)}, bf16[3,208,768]{2,1,0:T(8,128)(2,1)}, u32[]{:S(2)}, u32[]{:S(2)}) %collective-permute-start.42) | collective-permute-done | bytes 958496 | tf_op jit(solution)/shard_map/ppermute | solution.py:40
  536.9 5.4 token_back.2.refs_0_
  547.0 21.3 %collective-permute-done.46.got_ref = bf16[2,208,768]{2,1,0:T(8,128)(2,1)} collective-permute-done((bf16[2,208,768]{2,1,0:T(8,128)(2,1)}, bf16[2,208,768]{2,1,0:T(8,128)(2,1)}, u32[]{:S(2)}, u32[]{:S(2)}) %collective-permute-start.46) | collective-permute-done | bytes 639008 | tf_op jit(solution)/shard_map/ppermute | solution.py:40
  568.4 3.2 token_back.3
  578.5 9.5 %outer_keep.3 = f32[384,1536]{1,0:T(8,128)} custom-call(s32[1]{0:T(128)S(6)} %sub.13.which_ref, bf16[2,312,1536]{2,1,0:T(8,128)(2,1)} %get-tuple-element.1042.refs_0_, bf16[2,312,1536]{2,1,0:T(8,128)(2,1)} %get-tuple-element.1043.refs_1_, bf16[2,312,1536]{2,1,0:T(8,128)(2,1)} %get-tuple-element.1044.refs_2_, ...), custom_call_target="tpu_custom_call" | custom-call | flops 1000 | bytes 1000 | tf_op jit(solution)/shard_map/outer_keep/pallas_call | solution.py:631
  588.0 5.3 collective-permute-done.49
  (278 shorter events, 136.4 us)
Async XLA Ops:
  6.6 11.7 %collective-permute-start = (bf16[48,1664]{1,0:T(8,128)(2,1)S(1)}, bf16[48,1664]{1,0:T(8,128)(2,1)S(1)}, u32[]{:S(2)}, u32[]{:S(2)}) collective-permute-start(bf16[48,1664]{1,0:T(8,128)(2,1)S(1)} %bitcast_dynamic-update-slice_fusion.own_ref), channel_id=1, source_target_pairs={{0,16},{16,0},{1,17},{17,1},{2,18},{18,2},{3,19},{19,3},{4,20},{20... | collective-permute-start | bytes 479240 | tf_op jit(solution)/shard_map/ppermute | solution.py:40
  20.7 22.5 %collective-permute-start.1 = (bf16[2,48,1664]{2,1,0:T(8,128)(2,1)}, bf16[2,48,1664]{2,1,0:T(8,128)(2,1)}, u32[]{:S(2)}, u32[]{:S(2)}) collective-permute-start(bf16[2,48,1664]{2,1,0:T(8,128)(2,1)} %cross.1.refs_0_), channel_id=1, source_target_pairs={{0,4},{2,6},{4,0},{6,2},{8,12},{10,14},{12,8},{14,10},{1,5},{3,7},... | collective-permute-start | bytes 958472 | tf_op jit(solution)/shard_map/ppermute | solution.py:40
  22.2 21.0 %collective-permute-start.2 = (bf16[2,48,1664]{2,1,0:T(8,128)(2,1)}, bf16[2,48,1664]{2,1,0:T(8,128)(2,1)}, u32[]{:S(2)}, u32[]{:S(2)}) collective-permute-start(bf16[2,48,1664]{2,1,0:T(8,128)(2,1)} %cross.1.refs_0_), channel_id=1, source_target_pairs={{0,8},{2,10},{4,12},{6,14},{8,0},{10,2},{12,4},{14,6},{1,9},{3,11}... | collective-permute-start | bytes 958472 | tf_op jit(solution)/shard_map/ppermute | solution.py:40
  23.7 19.5 %collective-permute-start.3 = (bf16[2,48,1664]{2,1,0:T(8,128)(2,1)}, bf16[2,48,1664]{2,1,0:T(8,128)(2,1)}, u32[]{:S(2)}, u32[]{:S(2)}) collective-permute-start(bf16[2,48,1664]{2,1,0:T(8,128)(2,1)} %cross.1.refs_0_), channel_id=1, source_target_pairs={{0,12},{2,14},{4,8},{6,10},{8,4},{10,6},{12,0},{14,2},{1,13},{3,15... | collective-permute-start | bytes 958472 | tf_op jit(solution)/shard_map/ppermute | solution.py:40
  45.6 3.3 collective-permute-start.4
  54.1 14.4 %collective-permute-start.6 = (bf16[1040,768]{1,0:T(8,128)(2,1)}, bf16[1040,768]{1,0:T(8,128)(2,1)}, u32[]{:S(2)}, u32[]{:S(2)}) collective-permute-start(bf16[1040,768]{1,0:T(8,128)(2,1)} %maximum_select_fusion.refs_1_), channel_id=1, source_target_pairs={{0,2},{2,0},{4,6},{6,4},{8,10},{10,8},{12,14},{14,12},{1,3},{3,1},... | collective-permute-start | bytes 4792328 | tf_op jit(solution)/shard_map/ppermute | solution.py:40
  54.2 66.2 %collective-permute-start.10 = (bf16[384,1536]{1,0:T(8,128)(2,1)S(1)}, bf16[384,1536]{1,0:T(8,128)(2,1)S(1)}, u32[]{:S(2)}, u32[]{:S(2)}) collective-permute-start(bf16[384,1536]{1,0:T(8,128)(2,1)S(1)} %convert_bitcast_fusion.1.in_own), channel_id=1, source_target_pairs={{0,16},{16,0},{1,17},{17,1},{2,18},{18,2},{3,19},{19,3},{4,20},{20... | collective-permute-start | bytes 3538952 | tf_op jit(solution)/shard_map/ppermute | solution.py:40
  54.2 39.1 %collective-permute-start.7 = (bf16[768,384]{1,0:T(8,128)(2,1)}, bf16[768,384]{1,0:T(8,128)(2,1)}, u32[]{:S(2)}, u32[]{:S(2)}) collective-permute-start(bf16[768,384]{1,0:T(8,128)(2,1)} %get-tuple-element.977.here_ref.out_w_ref), channel_id=1, source_target_pairs={{0,1},{1,0},{2,3},{3,2},{4,5},{5,4},{6,7},{7,6},{8,9},{9,8},{10,11... | collective-permute-start | bytes 1769480 | tf_op jit(solution)/shard_map/ppermute | solution.py:40
  66.6 37.0 %collective-permute-start.8 = (bf16[3,208,384]{2,1,0:T(8,128)(2,1)}, bf16[3,208,384]{2,1,0:T(8,128)(2,1)}, u32[]{:S(2)}, u32[]{:S(2)}) collective-permute-start(bf16[3,208,384]{2,1,0:T(8,128)(2,1)} %get-tuple-element.605.own_ref), channel_id=1, source_target_pairs={{0,1},{1,0},{2,3},{3,2},{4,5},{5,4},{6,7},{7,6},{8,9},{9,8},{10,11... | collective-permute-start | bytes 1437704 | tf_op jit(solution)/shard_map/ppermute | solution.py:40
  74.9 38.7 %collective-permute-start.9 = (bf16[2,208,384]{2,1,0:T(8,128)(2,1)}, bf16[2,208,384]{2,1,0:T(8,128)(2,1)}, u32[]{:S(2)}, u32[]{:S(2)}) collective-permute-start(bf16[2,208,384]{2,1,0:T(8,128)(2,1)} %get-tuple-element.625.own_ref), channel_id=1, source_target_pairs={{0,1},{1,0},{2,3},{3,2},{4,5},{5,4},{6,7},{7,6},{8,9},{9,8},{10,11... | collective-permute-start | bytes 958472 | tf_op jit(solution)/shard_map/ppermute | solution.py:40
  120.3 9.5 %collective-permute-start.12 = (bf16[624,768]{1,0:T(8,128)(2,1)}, bf16[624,768]{1,0:T(8,128)(2,1)}, u32[]{:S(2)}, u32[]{:S(2)}) collective-permute-start(bf16[624,768]{1,0:T(8,128)(2,1)} %bitcast.94), channel_id=1, source_target_pairs={{0,2},{2,0},{4,6},{6,4},{8,10},{10,8},{12,14},{14,12},{1,3},{3,1},... | collective-permute-start | bytes 2875400 | tf_op jit(solution)/shard_map/ppermute | solution.py:40
  120.4 54.4 %collective-permute-start.14 = (bf16[1536,384]{1,0:T(8,128)(2,1)S(1)}, bf16[1536,384]{1,0:T(8,128)(2,1)S(1)}, u32[]{:S(2)}, u32[]{:S(2)}) collective-permute-start(bf16[1536,384]{1,0:T(8,128)(2,1)S(1)} %convert_bitcast_fusion.back_own), channel_id=1, source_target_pairs={{0,16},{16,0},{1,17},{17,1},{2,18},{18,2},{3,19},{19,3},{4,20},{20... | collective-permute-start | bytes 3538952 | tf_op jit(solution)/shard_map/ppermute | solution.py:40
  137.6 51.6 %collective-permute-start.15 = (bf16[2,312,768]{2,1,0:T(8,128)(2,1)}, bf16[2,312,768]{2,1,0:T(8,128)(2,1)S(1)}, u32[]{:S(2)}, u32[]{:S(2)}) collective-permute-start(bf16[2,312,768]{2,1,0:T(8,128)(2,1)} %get-tuple-element.704), channel_id=1, source_target_pairs={{0,4},{2,6},{4,0},{6,2},{8,12},{10,14},{12,8},{14,10},{1,5},{3,7},... | collective-permute-start | bytes 2875400 | tf_op jit(solution)/shard_map/ppermute | solution.py:40
  139.1 50.1 %collective-permute-start.16 = (bf16[2,312,768]{2,1,0:T(8,128)(2,1)}, bf16[2,312,768]{2,1,0:T(8,128)(2,1)}, u32[]{:S(2)}, u32[]{:S(2)}) collective-permute-start(bf16[2,312,768]{2,1,0:T(8,128)(2,1)} %get-tuple-element.705), channel_id=1, source_target_pairs={{0,8},{2,10},{4,12},{6,14},{8,0},{10,2},{12,4},{14,6},{1,9},{3,11}... | collective-permute-start | bytes 2875400 | tf_op jit(solution)/shard_map/ppermute | solution.py:40
  140.6 48.6 %collective-permute-start.17 = (bf16[2,312,768]{2,1,0:T(8,128)(2,1)}, bf16[2,312,768]{2,1,0:T(8,128)(2,1)}, u32[]{:S(2)}, u32[]{:S(2)}) collective-permute-start(bf16[2,312,768]{2,1,0:T(8,128)(2,1)} %get-tuple-element.706), channel_id=1, source_target_pairs={{0,12},{2,14},{4,8},{6,10},{8,4},{10,6},{12,0},{14,2},{1,13},{3,15... | collective-permute-start | bytes 2875400 | tf_op jit(solution)/shard_map/ppermute | solution.py:40
  189.1 14.2 %collective-permute-start.18 = (bf16[2,312,384]{2,1,0:T(8,128)(2,1)}, bf16[2,312,384]{2,1,0:T(8,128)(2,1)S(1)}, u32[]{:S(2)}, u32[]{:S(2)}) collective-permute-start(bf16[2,312,384]{2,1,0:T(8,128)(2,1)} %get-tuple-element.721), channel_id=1, source_target_pairs={{0,1},{1,0},{2,3},{3,2},{4,5},{5,4},{6,7},{7,6},{8,9},{9,8},{10,11... | collective-permute-start | bytes 1437704 | tf_op jit(solution)/shard_map/ppermute | solution.py:40
  206.2 25.3 %collective-permute-start.22 = (bf16[2,312,768]{2,1,0:T(8,128)(2,1)}, bf16[2,312,768]{2,1,0:T(8,128)(2,1)S(1)}, u32[]{:S(2)}, u32[]{:S(2)}) collective-permute-start(bf16[2,312,768]{2,1,0:T(8,128)(2,1)} %get-tuple-element.747), channel_id=1, source_target_pairs={{0,12},{2,14},{4,8},{6,10},{8,4},{10,6},{12,0},{14,2},{1,13},{3,15... | collective-permute-start | bytes 2875400 | tf_op jit(solution)/shard_map/ppermute | solution.py:40
  208.7 42.5 %collective-permute-start.21 = (bf16[2,312,768]{2,1,0:T(8,128)(2,1)}, bf16[2,312,768]{2,1,0:T(8,128)(2,1)S(1)}, u32[]{:S(2)}, u32[]{:S(2)}) collective-permute-start(bf16[2,312,768]{2,1,0:T(8,128)(2,1)} %get-tuple-element.745), channel_id=1, source_target_pairs={{0,8},{2,10},{4,12},{6,14},{8,0},{10,2},{12,4},{14,6},{1,9},{3,11}... | collective-permute-start | bytes 2875400 | tf_op jit(solution)/shard_map/ppermute | solution.py:40
  209.2 42.9 %collective-permute-start.20 = (bf16[2,312,768]{2,1,0:T(8,128)(2,1)}, bf16[2,312,768]{2,1,0:T(8,128)(2,1)S(1)}, u32[]{:S(2)}, u32[]{:S(2)}) collective-permute-start(bf16[2,312,768]{2,1,0:T(8,128)(2,1)} %get-tuple-element.743), channel_id=1, source_target_pairs={{0,4},{2,6},{4,0},{6,2},{8,12},{10,14},{12,8},{14,10},{1,5},{3,7},... | collective-permute-start | bytes 2875400 | tf_op jit(solution)/shard_map/ppermute | solution.py:40
  209.7 15.1 %collective-permute-start.19 = (bf16[2,312,384]{2,1,0:T(8,128)(2,1)}, bf16[2,312,384]{2,1,0:T(8,128)(2,1)S(1)}, u32[]{:S(2)}, u32[]{:S(2)}) collective-permute-start(bf16[2,312,384]{2,1,0:T(8,128)(2,1)} %get-tuple-element.738), channel_id=1, source_target_pairs={{0,1},{1,0},{2,3},{3,2},{4,5},{5,4},{6,7},{7,6},{8,9},{9,8},{10,11... | collective-permute-start | bytes 1437704 | tf_op jit(solution)/shard_map/ppermute | solution.py:40
  227.7 37.8 %collective-permute-start.23 = (bf16[2,312,384]{2,1,0:T(8,128)(2,1)}, bf16[2,312,384]{2,1,0:T(8,128)(2,1)}, u32[]{:S(2)}, u32[]{:S(2)}) collective-permute-start(bf16[2,312,384]{2,1,0:T(8,128)(2,1)} %get-tuple-element.762), channel_id=1, source_target_pairs={{0,1},{1,0},{2,3},{3,2},{4,5},{5,4},{6,7},{7,6},{8,9},{9,8},{10,11... | collective-permute-start | bytes 1437704 | tf_op jit(solution)/shard_map/ppermute | solution.py:40
  227.7 52.1 %collective-permute-start.24 = (bf16[2,312,384]{2,1,0:T(8,128)(2,1)}, bf16[2,312,384]{2,1,0:T(8,128)(2,1)S(1)}, u32[]{:S(2)}, u32[]{:S(2)}) collective-permute-start(bf16[2,312,384]{2,1,0:T(8,128)(2,1)} %add_halves.9), channel_id=1, source_target_pairs={{0,4},{2,6},{4,0},{6,2},{8,12},{10,14},{12,8},{14,10},{1,5},{3,7},... | collective-permute-start | bytes 1437704 | tf_op jit(solution)/shard_map/ppermute | solution.py:40
  267.6 12.4 %collective-permute-start.25 = (bf16[2,312,384]{2,1,0:T(8,128)(2,1)S(1)}, bf16[2,312,384]{2,1,0:T(8,128)(2,1)S(1)}, u32[]{:S(2)}, u32[]{:S(2)}) collective-permute-start(bf16[2,312,384]{2,1,0:T(8,128)(2,1)S(1)} %copy-done.54), channel_id=1, source_target_pairs={{0,1},{1,0},{2,3},{3,2},{4,5},{5,4},{6,7},{7,6},{8,9},{9,8},{10,11... | collective-permute-start | bytes 1437704 | tf_op jit(solution)/shard_map/ppermute | solution.py:40
  282.9 11.7 %collective-permute-start.26 = (bf16[2,312,384]{2,1,0:T(8,128)(2,1)S(1)}, bf16[2,312,384]{2,1,0:T(8,128)(2,1)S(1)}, u32[]{:S(2)}, u32[]{:S(2)}) collective-permute-start(bf16[2,312,384]{2,1,0:T(8,128)(2,1)S(1)} %copy-done.55), channel_id=1, source_target_pairs={{0,1},{1,0},{2,3},{3,2},{4,5},{5,4},{6,7},{7,6},{8,9},{9,8},{10,11... | collective-permute-start | bytes 1437704 | tf_op jit(solution)/shard_map/ppermute | solution.py:40
  297.4 13.4 %collective-permute-start.27 = (bf16[2,312,384]{2,1,0:T(8,128)(2,1)S(1)}, bf16[2,312,384]{2,1,0:T(8,128)(2,1)S(1)}, u32[]{:S(2)}, u32[]{:S(2)}) collective-permute-start(bf16[2,312,384]{2,1,0:T(8,128)(2,1)S(1)} %copy-done.56), channel_id=1, source_target_pairs={{0,1},{1,0},{2,3},{3,2},{4,5},{5,4},{6,7},{7,6},{8,9},{9,8},{10,11... | collective-permute-start | bytes 1437704 | tf_op jit(solution)/shard_map/ppermute | solution.py:40
  298.7 15.0 %collective-permute-start.28 = (bf16[2,312,384]{2,1,0:T(8,128)(2,1)S(1)}, bf16[2,312,384]{2,1,0:T(8,128)(2,1)S(1)}, u32[]{:S(2)}, u32[]{:S(2)}) collective-permute-start(bf16[2,312,384]{2,1,0:T(8,128)(2,1)S(1)} %copy-done.26), channel_id=1, source_target_pairs={{0,8},{2,10},{4,12},{6,14},{8,0},{10,2},{12,4},{14,6},{1,9},{3,11}... | collective-permute-start | bytes 1437704 | tf_op jit(solution)/shard_map/ppermute | solution.py:40
  313.8 11.2 %collective-permute-start.29 = (bf16[2,312,384]{2,1,0:T(8,128)(2,1)S(1)}, bf16[2,312,384]{2,1,0:T(8,128)(2,1)S(1)}, u32[]{:S(2)}, u32[]{:S(2)}) collective-permute-start(bf16[2,312,384]{2,1,0:T(8,128)(2,1)S(1)} %copy-done.53), channel_id=1, source_target_pairs={{0,1},{1,0},{2,3},{3,2},{4,5},{5,4},{6,7},{7,6},{8,9},{9,8},{10,11... | collective-permute-start | bytes 1437704 | tf_op jit(solution)/shard_map/ppermute | solution.py:40
  314.1 13.7 %collective-permute-start.30 = (bf16[2,312,384]{2,1,0:T(8,128)(2,1)S(1)}, bf16[2,312,384]{2,1,0:T(8,128)(2,1)S(1)}, u32[]{:S(2)}, u32[]{:S(2)}) collective-permute-start(bf16[2,312,384]{2,1,0:T(8,128)(2,1)S(1)} %copy-done.25), channel_id=1, source_target_pairs={{0,12},{2,14},{4,8},{6,10},{8,4},{10,6},{12,0},{14,2},{1,13},{3,15... | collective-permute-start | bytes 1437704 | tf_op jit(solution)/shard_map/ppermute | solution.py:40
  327.9 16.8 %collective-permute-start.31 = (bf16[2,312,384]{2,1,0:T(8,128)(2,1)S(1)}, bf16[2,312,384]{2,1,0:T(8,128)(2,1)S(1)}, u32[]{:S(2)}, u32[]{:S(2)}) collective-permute-start(bf16[2,312,384]{2,1,0:T(8,128)(2,1)S(1)} %copy-done.52), channel_id=1, source_target_pairs={{0,1},{1,0},{2,3},{3,2},{4,5},{5,4},{6,7},{7,6},{8,9},{9,8},{10,11... | collective-permute-start | bytes 1437704 | tf_op jit(solution)/shard_map/ppermute | solution.py:40
  329.3 27.8 %collective-permute-start.32 = (bf16[2,312,384]{2,1,0:T(8,128)(2,1)S(1)}, bf16[2,312,384]{2,1,0:T(8,128)(2,1)S(1)}, u32[]{:S(2)}, u32[]{:S(2)}) collective-permute-start(bf16[2,312,384]{2,1,0:T(8,128)(2,1)S(1)} %copy-done.24), channel_id=1, source_target_pairs={{0,4},{2,6},{4,0},{6,2},{8,12},{10,14},{12,8},{14,10},{1,5},{3,7},... | collective-permute-start | bytes 1437704 | tf_op jit(solution)/shard_map/ppermute | solution.py:40
  342.7 20.1 %collective-permute-start.33 = (bf16[2,312,384]{2,1,0:T(8,128)(2,1)S(1)}, bf16[2,312,384]{2,1,0:T(8,128)(2,1)S(1)}, u32[]{:S(2)}, u32[]{:S(2)}) collective-permute-start(bf16[2,312,384]{2,1,0:T(8,128)(2,1)S(1)} %copy-done.28), channel_id=1, source_target_pairs={{0,8},{2,10},{4,12},{6,14},{8,0},{10,2},{12,4},{14,6},{1,9},{3,11}... | collective-permute-start | bytes 1437704 | tf_op jit(solution)/shard_map/ppermute | solution.py:40
  347.6 15.2 %collective-permute-start.34 = (bf16[2,312,384]{2,1,0:T(8,128)(2,1)}, bf16[2,312,384]{2,1,0:T(8,128)(2,1)S(1)}, u32[]{:S(2)}, u32[]{:S(2)}) collective-permute-start(bf16[2,312,384]{2,1,0:T(8,128)(2,1)} %add_halves.15), channel_id=1, source_target_pairs={{0,12},{2,14},{4,8},{6,10},{8,4},{10,6},{12,0},{14,2},{1,13},{3,15... | collective-permute-start | bytes 1437704 | tf_op jit(solution)/shard_map/ppermute | solution.py:40
  348.3 20.5 %collective-permute-start.35 = (bf16[4,312,384]{2,1,0:T(8,128)(2,1)}, bf16[4,312,384]{2,1,0:T(8,128)(2,1)S(1)}, u32[]{:S(2)}, u32[]{:S(2)}) collective-permute-start(bf16[4,312,384]{2,1,0:T(8,128)(2,1)} %get-tuple-element.904), channel_id=1, source_target_pairs={{0,2},{2,0},{4,6},{6,4},{8,10},{10,8},{12,14},{14,12},{1,3},{3,1},... | collective-permute-start | bytes 2875400 | tf_op jit(solution)/shard_map/ppermute | solution.py:40
  367.3 17.5 %collective-permute-start.36 = (bf16[4,312,384]{2,1,0:T(8,128)(2,1)}, bf16[4,312,384]{2,1,0:T(8,128)(2,1)S(1)}, u32[]{:S(2)}, u32[]{:S(2)}) collective-permute-start(bf16[4,312,384]{2,1,0:T(8,128)(2,1)} %get-tuple-element.915), channel_id=1, source_target_pairs={{0,2},{2,0},{4,6},{6,4},{8,10},{10,8},{12,14},{14,12},{1,3},{3,1},... | collective-permute-start | bytes 2875400 | tf_op jit(solution)/shard_map/ppermute | solution.py:40
  367.3 92.5 %collective-permute-start.40 = (bf16[1536,384]{1,0:T(8,128)(2,1)}, bf16[1536,384]{1,0:T(8,128)(2,1)S(1)}, u32[]{:S(2)}, u32[]{:S(2)}) collective-permute-start(bf16[1536,384]{1,0:T(8,128)(2,1)} %outer_send.2), channel_id=1, source_target_pairs={{0,16},{16,0},{1,17},{17,1},{2,18},{18,2},{3,19},{19,3},{4,20},{20... | collective-permute-start | bytes 3538952 | tf_op jit(solution)/shard_map/ppermute | solution.py:40
  391.4 46.1 %collective-permute-start.38 = (bf16[3,208,384]{2,1,0:T(8,128)(2,1)}, bf16[3,208,384]{2,1,0:T(8,128)(2,1)S(1)}, u32[]{:S(2)}, u32[]{:S(2)}) collective-permute-start(bf16[3,208,384]{2,1,0:T(8,128)(2,1)} %sum_home.2.near_ref), channel_id=1, source_target_pairs={{0,1},{1,0},{2,3},{3,2},{4,5},{5,4},{6,7},{7,6},{8,9},{9,8},{10,11... | collective-permute-start | bytes 1437704 | tf_op jit(solution)/shard_map/ppermute | solution.py:40
  397.1 62.6 %collective-permute-start.39 = (bf16[2,208,384]{2,1,0:T(8,128)(2,1)}, bf16[2,208,384]{2,1,0:T(8,128)(2,1)S(1)}, u32[]{:S(2)}, u32[]{:S(2)}) collective-permute-start(bf16[2,208,384]{2,1,0:T(8,128)(2,1)} %sum_home.3.near_ref), channel_id=1, source_target_pairs={{0,1},{1,0},{2,3},{3,2},{4,5},{5,4},{6,7},{7,6},{8,9},{9,8},{10,11... | collective-permute-start | bytes 958472 | tf_op jit(solution)/shard_map/ppermute | solution.py:40
  397.9 39.6 %collective-permute-start.37 = (f32[5,8,208]{2,1,0:T(8,128)S(1)}, f32[5,8,208]{2,1,0:T(8,128)S(1)}, u32[]{:S(2)}, u32[]{:S(2)}) collective-permute-start(f32[5,8,208]{2,1,0:T(8,128)S(1)} %copy-done.43), channel_id=1, source_target_pairs={{0,1},{1,0},{2,3},{3,2},{4,5},{5,4},{6,7},{7,6},{8,9},{9,8},{10,11... | collective-permute-start | bytes 99848 | tf_op jit(solution)/shard_map/ppermute | solution.py:40
  489.4 10.4 %collective-permute-start.41 = (bf16[2,4,48,1664]{3,2,1,0:T(8,128)(2,1)S(1)}, bf16[2,4,48,1664]{3,2,1,0:T(8,128)(2,1)}, u32[]{:S(2)}, u32[]{:S(2)}) collective-permute-start(bf16[2,4,48,1664]{3,2,1,0:T(8,128)(2,1)S(1)} %fusion.1), channel_id=1, source_target_pairs={{0,2},{2,0},{4,6},{6,4},{8,10},{10,8},{12,14},{14,12},{1,3},{3,1},... | collective-permute-start | bytes 3833864 | tf_op jit(solution)/shard_map/ppermute | solution.py:40
  499.7 37.2 %collective-permute-start.42 = (bf16[3,208,768]{2,1,0:T(8,128)(2,1)S(1)}, bf16[3,208,768]{2,1,0:T(8,128)(2,1)}, u32[]{:S(2)}, u32[]{:S(2)}) collective-permute-start(bf16[3,208,768]{2,1,0:T(8,128)(2,1)S(1)} %copy-done.19), channel_id=1, source_target_pairs={{0,1},{1,0},{2,3},{3,2},{4,5},{5,4},{6,7},{7,6},{8,9},{9,8},{10,11... | collective-permute-start | bytes 2875400 | tf_op jit(solution)/shard_map/ppermute | solution.py:40
  503.1 39.1 %collective-permute-start.43 = (bf16[2,48,1664]{2,1,0:T(8,128)(2,1)}, bf16[2,48,1664]{2,1,0:T(8,128)(2,1)}, u32[]{:S(2)}, u32[]{:S(2)}) collective-permute-start(bf16[2,48,1664]{2,1,0:T(8,128)(2,1)} %get-tuple-element.1109), channel_id=1, source_target_pairs={{0,4},{2,6},{4,0},{6,2},{8,12},{10,14},{12,8},{14,10},{1,5},{3,7},... | collective-permute-start | bytes 958472 | tf_op jit(solution)/shard_map/ppermute | solution.py:40
  503.7 38.6 %collective-permute-start.44 = (bf16[2,48,1664]{2,1,0:T(8,128)(2,1)}, bf16[2,48,1664]{2,1,0:T(8,128)(2,1)}, u32[]{:S(2)}, u32[]{:S(2)}) collective-permute-start(bf16[2,48,1664]{2,1,0:T(8,128)(2,1)} %get-tuple-element.1111), channel_id=1, source_target_pairs={{0,8},{2,10},{4,12},{6,14},{8,0},{10,2},{12,4},{14,6},{1,9},{3,11}... | collective-permute-start | bytes 958472 | tf_op jit(solution)/shard_map/ppermute | solution.py:40
  505.1 37.1 %collective-permute-start.45 = (bf16[2,48,1664]{2,1,0:T(8,128)(2,1)}, bf16[2,48,1664]{2,1,0:T(8,128)(2,1)}, u32[]{:S(2)}, u32[]{:S(2)}) collective-permute-start(bf16[2,48,1664]{2,1,0:T(8,128)(2,1)} %get-tuple-element.1110), channel_id=1, source_target_pairs={{0,12},{2,14},{4,8},{6,10},{8,4},{10,6},{12,0},{14,2},{1,13},{3,15... | collective-permute-start | bytes 958472 | tf_op jit(solution)/shard_map/ppermute | solution.py:40
  506.6 71.9 %collective-permute-start.50 = (bf16[384,1536]{1,0:T(8,128)(2,1)}, bf16[384,1536]{1,0:T(8,128)(2,1)}, u32[]{:S(2)}, u32[]{:S(2)}) collective-permute-start(bf16[384,1536]{1,0:T(8,128)(2,1)} %outer_send.3), channel_id=1, source_target_pairs={{0,16},{16,0},{1,17},{17,1},{2,18},{18,2},{3,19},{19,3},{4,20},{20... | collective-permute-start | bytes 3538952 | tf_op jit(solution)/shard_map/ppermute | solution.py:40
  536.9 31.5 %collective-permute-start.46 = (bf16[2,208,768]{2,1,0:T(8,128)(2,1)}, bf16[2,208,768]{2,1,0:T(8,128)(2,1)}, u32[]{:S(2)}, u32[]{:S(2)}) collective-permute-start(bf16[2,208,768]{2,1,0:T(8,128)(2,1)} %get-tuple-element.1028.own_ref), channel_id=1, source_target_pairs={{0,1},{1,0},{2,3},{3,2},{4,5},{5,4},{6,7},{7,6},{8,9},{9,8},{10,11... | collective-permute-start | bytes 1916936 | tf_op jit(solution)/shard_map/ppermute | solution.py:40
  544.3 31.4 %collective-permute-start.48 = (bf16[48,1664]{1,0:T(8,128)(2,1)}, bf16[48,1664]{1,0:T(8,128)(2,1)S(1)}, u32[]{:S(2)}, u32[]{:S(2)}) collective-permute-start(bf16[48,1664]{1,0:T(8,128)(2,1)} %fusion.7), channel_id=1, source_target_pairs={{0,16},{16,0},{1,17},{17,1},{2,18},{18,2},{3,19},{19,3},{4,20},{20... | collective-permute-start | bytes 479240 | tf_op jit(solution)/shard_map/ppermute | solution.py:40
  575.6 19.0 %collective-permute-start.47 = (bf16[5,208,384]{2,1,0:T(8,128)(2,1)}, bf16[5,208,384]{2,1,0:T(8,128)(2,1)}, u32[]{:S(2)}, u32[]{:S(2)}) collective-permute-start(bf16[5,208,384]{2,1,0:T(8,128)(2,1)} %get-tuple-element.1034), channel_id=1, source_target_pairs={{0,1},{1,0},{2,3},{3,2},{4,5},{5,4},{6,7},{7,6},{8,9},{9,8},{10,11... | collective-permute-start | bytes 2396168 | tf_op jit(solution)/shard_map/ppermute | solution.py:40
  575.7 17.5 %collective-permute-start.49 = (f32[48,128]{1,0:T(8,128)S(1)}, f32[48,128]{1,0:T(8,128)S(1)}, u32[]{:S(2)}, u32[]{:S(2)}) collective-permute-start(f32[48,128]{1,0:T(8,128)S(1)} %slice.102), channel_id=1, source_target_pairs={{0,1},{1,0},{2,3},{3,2},{4,5},{5,4},{6,7},{7,6},{8,9},{9,8},{10,11... | collective-permute-start | bytes 73736 | tf_op jit(solution)/shard_map/ppermute | solution.py:40
  (60 other events, 496.4 us)

commit v4 on v3

--- a/solution.py
+++ b/solution.py
@@ -20,7 +20,8 @@
 F32 = jnp.float32
 LANES = 128
 TILE = 512
-CHUNKS = 4
+IN_CUTS = ((0, 112), (112, 176), (176, 384))
+BACK_CUTS = ((0, 128), (128, 384))
 TAIL_RATE = 0.305
 TAIL = (
     0.12163973686996697,
@@ -237,15 +238,6 @@
 
 def pick(array, index, axis):
     return lax.dynamic_index_in_dim(array, index, axis, False)
-
-
-def core_sum(grad, wide):
-    count = lax.axis_size("expert")
-    core = lax.axis_index("expert") & 1
-    blocks = grad.reshape((2, count // 2, 2, -1) + grad.shape[1:])
-    return pick(blocks, core, 2) + hop(
-        pick(blocks, 1 - core, 2).astype(wide), "expert", 1
-    ).astype(F32)
 
 
 def chip_sum(total, wide):
@@ -496,14 +488,26 @@
     return u * normal, normal + u * (DENSITY * bell)
 
 
-def in_order(same_ref, in_own, in_other, back_own, back_other):
+def in_order(same_ref, refs):
     same = same_ref[0] == 1
-    choose = lambda a, b: (jnp.where(same, a[...], b[...]), jnp.where(same, b[...], a[...]))
-    return choose(in_own, in_other) + choose(back_own, back_other)
-
-
-def forward_kernel(same_ref, m_ref, in_own, in_other, back_own, back_other, g_ref, s_ref, zt_ref, zh_ref, acc):
-    w1h, w1t, w2h, w2t = in_order(same_ref, in_own, in_other, back_own, back_other)
+    n, m = len(IN_CUTS), len(BACK_CUTS)
+    join = lambda refs, axis: jnp.concatenate([ref[...] for ref in refs], axis=axis)
+    pairs = [
+        (join(refs[:n], 0), join(refs[n : 2 * n], 0)),
+        (join(refs[2 * n : 2 * n + m], 1), join(refs[2 * n + m :], 1)),
+    ]
+    return [v for a, b in pairs for v in (jnp.where(same, a, b), jnp.where(same, b, a))]
+
+
+def weight_specs():
+    across = [pl.BlockSpec((hi - lo, TILE), lambda i, s: (0, i)) for lo, hi in IN_CUTS]
+    down = [pl.BlockSpec((TILE, hi - lo), lambda i, s: (i, 0)) for lo, hi in BACK_CUTS]
+    return across * 2 + down * 2
+
+
+def forward_kernel(same_ref, m_ref, *refs):
+    *weights, g_ref, s_ref, zt_ref, zh_ref, acc = refs
+    w1h, w1t, w2h, w2t = in_order(same_ref, weights)
     step = pl.program_id(0)
     last = pl.num_programs(0) - 1
     for b in range(m_ref.shape[0]):
@@ -533,8 +537,6 @@
 def expert_forward(same, rows, *weights):
     blocks, capacity, _ = rows.shape
     hidden = weights[0].shape[1]
-    across = pl.BlockSpec((HALF, TILE), lambda i, s: (0, i))
-    down = pl.BlockSpec((TILE, HALF), lambda i, s: (i, 0))
     wide = pl.BlockSpec((blocks, capacity, TILE), lambda i, s: (0, 0, i))
     make = lambda w, t: jax.ShapeDtypeStruct((blocks, capacity, w), t)
     return pl.pallas_call(
@@ -542,7 +544,7 @@
         grid_spec=pltpu.PrefetchScalarGridSpec(
             num_scalar_prefetch=1,
             grid=(hidden // TILE,),
-            in_specs=[whole(rows.shape), across, across, down, down],
+            in_specs=[whole(rows.shape)] + weight_specs(),
             out_specs=[wide, wide] + [whole((blocks, capacity, HALF))] * 2,
             scratch_shapes=[pltpu.VMEM((blocks, capacity, HALF), F32)],
         ),
@@ -552,8 +554,9 @@
     )(same, rows, *weights)
 
 
-def backward_kernel(same_ref, z_ref, s_ref, in_own, in_other, back_own, back_other, u_ref, mt_ref, mh_ref, acc):
-    w1h, w1t, w2h, w2t = in_order(same_ref, in_own, in_other, back_own, back_other)
+def backward_kernel(same_ref, z_ref, s_ref, *refs):
+    *weights, u_ref, mt_ref, mh_ref, acc = refs
+    w1h, w1t, w2h, w2t = in_order(same_ref, weights)
     step = pl.program_id(0)
     last = pl.num_programs(0) - 1
     for b in range(z_ref.shape[0]):
@@ -581,8 +584,6 @@
 def expert_backward(same, rows, slope, *weights):
     blocks, capacity, _ = rows.shape
     hidden = weights[0].shape[1]
-    across = pl.BlockSpec((HALF, TILE), lambda i, s: (0, i))
-    down = pl.BlockSpec((TILE, HALF), lambda i, s: (i, 0))
     wide = pl.BlockSpec((blocks, capacity, TILE), lambda i, s: (0, 0, i))
     make = lambda w, t: jax.ShapeDtypeStruct((blocks, capacity, w), t)
     return pl.pallas_call(
@@ -590,7 +591,7 @@
         grid_spec=pltpu.PrefetchScalarGridSpec(
             num_scalar_prefetch=1,
             grid=(hidden // TILE,),
-            in_specs=[whole(rows.shape), wide, across, across, down, down],
+            in_specs=[whole(rows.shape), wide] + weight_specs(),
             out_specs=[wide] + [whole((blocks, capacity, HALF))] * 2,
             scratch_shapes=[pltpu.VMEM((blocks, capacity, HALF), F32)],
         ),
@@ -695,18 +696,15 @@
         jnp.where(lane == ids_ref[0, :, c : c + 1], dgate[:, c : c + 1], 0.0) for c in range(2)
     )
     grad_logits = probs * (grad_probs - jnp.sum(probs * grad_probs, axis=1, keepdims=True))
-    grad = lax.dot_general(
-        grad_logits, narrow_ref[...].astype(F32), (((1,), (1,)), ((), ())),
-        precision=HIGH, preferred_element_type=F32,
-    ) + jnp.concatenate(
+    high = grad_logits.astype(BF)
+    low = (grad_logits - high.astype(F32)).astype(BF)
+    narrow = narrow_ref[...]
+    grad = (dot_nt(high, narrow) + dot_nt(low, narrow)) + jnp.concatenate(
         [jnp.where(first, near, away), jnp.where(first, away, near)], axis=1
     )
     hat, scale = normed(y_ref[0])
     h = (hat * vec_ref[2:3, :] + vec_ref[3:4, :]).astype(BF)
-    grad_router = lax.dot_general(
-        grad_logits, h.astype(F32), (((0,), (0,)), ((), ())),
-        precision=HIGH, preferred_element_type=F32,
-    )
+    grad_router = dot_tn(high, h) + dot_tn(low, h)
 
     @pl.when(start)
     def _():
@@ -817,19 +815,157 @@
     )(x, own, got, dy, vectors, *held)
 
 
-def slot_table(routes, expert_count):
-    total = routes.shape[0]
-    sequence = jnp.transpose(routes).reshape(-1)
-    onehot = (sequence[:, None] == jnp.arange(expert_count, dtype=jnp.int32)[None, :]).astype(
-        jnp.int32
-    )
-    before = jnp.cumsum(onehot, axis=0) - onehot
-    return jnp.sum(before * onehot, axis=1).reshape(2, total)
-
-
-def images_of(value, fill=0):
-    value = value.reshape(-1, SEQ, value.shape[-1])
-    return jnp.pad(value, ((0, 0), (0, ROWS - SEQ), (0, 0)), constant_values=fill)
+def exact(a, b, contract):
+    return lax.dot_general(
+        a, b, ((contract[:1], contract[1:]), ((), ())), precision=HIGH, preferred_element_type=F32
+    )
+
+
+def of_image(i, tok):
+    row = lax.broadcasted_iota(jnp.int32, (ROWS, tok), 0)
+    token = lax.broadcasted_iota(jnp.int32, (ROWS, tok), 1)
+    return jnp.where((token == row + i * SEQ) & (row < SEQ), 1.0, 0.0)
+
+
+def image_kernel(which_ref, tok_ref, cot_ref, x_ref, cot_out_ref, here_ref):
+    mine = of_image(pl.program_id(0), tok_ref.shape[0]).astype(BF)
+    x_ref[0] = dot_nn(mine, tok_ref[...]).astype(BF)
+    cot = dot_nn(mine, cot_ref[...]).astype(BF)
+    cot_out_ref[0] = cot
+    first = which_ref[0] == 0
+    here_ref[0, :, :HALF] = jnp.where(first, cot[:, :HALF], cot[:, HALF:])
+    here_ref[0, :, HALF:] = jnp.where(first, cot[:, HALF:], cot[:, :HALF])
+
+
+def image_rows(which, tokens, cotangent):
+    pictures = tokens.shape[0] // SEQ
+    return pl.pallas_call(
+        image_kernel,
+        grid_spec=pltpu.PrefetchScalarGridSpec(
+            num_scalar_prefetch=1,
+            grid=(pictures,),
+            in_specs=[whole(tokens.shape)] * 2,
+            out_specs=[image(D)] * 3,
+        ),
+        out_shape=[images(pictures, D, BF)] * 3,
+        name="image_rows",
+        cost_estimate=cost(),
+    )(which, tokens, cotangent)
+
+
+def slot_kernel(here_ref, ids_ref, rows_ref, lanes_ref, ids_out_ref, *, capacity):
+    tok = ids_ref.shape[0]
+    lane = lax.broadcasted_iota(jnp.int32, (tok, LANES), 1)
+    earlier = jnp.where(
+        lax.broadcasted_iota(jnp.int32, (tok, tok), 1) < lax.broadcasted_iota(jnp.int32, (tok, tok), 0),
+        1.0, 0.0,
+    ).astype(BF)
+    ids = [ids_ref[:, c : c + 1] for c in range(2)]
+    taken = jnp.zeros((1, LANES), F32)
+    table = jnp.zeros((tok, LANES), F32)
+    for c in range(2):
+        onehot = jnp.where(lane == ids[c], 1.0, 0.0)
+        before = dot_nn(earlier, onehot.astype(BF)) + taken
+        slot = jnp.sum(before * onehot, axis=1, keepdims=True)
+        taken = taken + jnp.sum(onehot, axis=0, keepdims=True)
+        place = ((ids[c] ^ here_ref[0]) * capacity).astype(F32) + slot + 1.0
+        table = jnp.where(lane == c, place, table)
+        table = jnp.where(lane == 2 + c, ids[c].astype(F32) + 1.0, table)
+    for i in range(rows_ref.shape[0]):
+        part = exact(of_image(i, tok), table, (1, 0)) - 1.0
+        whole_part = part.astype(jnp.int32)
+        rows_ref[i] = whole_part[:, 0:2]
+        ids_out_ref[i] = whole_part[:, 2:4]
+        lanes_ref[:, i * ROWS : (i + 1) * ROWS] = exact(first_lanes(), part, (1, 1)).astype(jnp.int32)
+
+
+def slot_rows(here, expert_ids, capacity):
+    tok = expert_ids.shape[0]
+    pictures = tok // SEQ
+    shapes = [(pictures, ROWS, 2), (8, pictures * ROWS), (pictures, ROWS, 2)]
+    rows, lanes, ids = pl.pallas_call(
+        functools.partial(slot_kernel, capacity=capacity),
+        grid_spec=pltpu.PrefetchScalarGridSpec(
+            num_scalar_prefetch=1,
+            grid=(1,),
+            in_specs=[whole(expert_ids.shape)],
+            out_specs=[whole(shape) for shape in shapes],
+        ),
+        out_shape=[jax.ShapeDtypeStruct(shape, jnp.int32) for shape in shapes],
+        name="slot_rows",
+        cost_estimate=cost(),
+    )(flag(here), expert_ids)
+    return rows, lanes[:2], ids
+
+
+def projection_kernel(core_ref, *refs, parts, split):
+    a_ref, dqkv_ref, dyb_ref, o_ref = refs[:4]
+    routers, ones, twos = (refs[4 + n * parts : 4 + (n + 1) * parts] for n in range(3))
+    out_ref = refs[-1]
+    step = pl.program_id(0)
+    last = pl.num_programs(0) - 1
+    qkv = dot_tn(a_ref[0], dqkv_ref[0])
+    out = dot_tn(dyb_ref[0], o_ref[0])
+
+    @pl.when(step == 0)
+    def _():
+        out_ref[:, : 3 * HALF] = qkv
+        out_ref[:, 3 * HALF : 4 * HALF] = out
+        total = 0.5 * sum(r[...] for r in routers)
+        sums = jnp.concatenate(
+            [sum(r[0:2, :] for r in ones), 0.5 * sum(r[0:2, :] for r in twos), jnp.zeros((4, D), F32)],
+            axis=0,
+        )
+        out_ref[:, 4 * HALF :] = jnp.transpose(
+            jnp.concatenate([total[: LANES - 8], sums], axis=0)
+        )
+
+    @pl.when(step > 0)
+    def _():
+        out_ref[:, : 3 * HALF] += qkv
+        out_ref[:, 3 * HALF : 4 * HALF] += out
+
+    if split:
+
+        @pl.when(step == last)
+        def _():
+            near_ref, away_ref = refs[-3:-1]
+            dps, chips, rows, _ = near_ref.shape
+            for d in range(dps):
+                for chip in range(chips):
+                    at = (2 * (d * chips + chip) + core_ref[0]) * rows
+                    near_ref[d, chip] = out_ref[pl.ds(pl.multiple_of(at, 16), rows), :]
+                    at = (2 * (d * chips + chip) + 1 - core_ref[0]) * rows
+                    away = out_ref[pl.ds(pl.multiple_of(at, 16), rows), :]
+                    away_ref[d, chip] = away.astype(BF)
+
+
+def projection_grads(a_rows, dqkv, dyb, o_rows, *small):
+    count = lax.axis_size("expert")
+    core = lax.axis_index("expert") & 1
+    rows = D // (2 * count)
+    split = rows % 16 == 0
+    shape = (D, 4 * HALF + LANES)
+    shares = (2, count // 2, rows, shape[1])
+    kinds = [(shares, F32), (shares, BF)] if split else [(shape, F32)]
+    out = pl.pallas_call(
+        functools.partial(projection_kernel, parts=len(small) // 3, split=split),
+        grid_spec=pltpu.PrefetchScalarGridSpec(
+            num_scalar_prefetch=1,
+            grid=(a_rows.shape[0],),
+            in_specs=[image(D), image(3 * HALF), image(D), image(HALF)]
+            + [whole(v.shape) for v in small],
+            out_specs=[whole(k) for k, _ in kinds],
+            scratch_shapes=[pltpu.VMEM(shape, F32)] if split else [],
+        ),
+        out_shape=[jax.ShapeDtypeStruct(*kind) for kind in kinds],
+        name="projection_grads",
+        cost_estimate=cost(),
+    )(flag(core), a_rows, dqkv, dyb, o_rows, *small)
+    if split:
+        return out
+    blocks = out[0].reshape((2, count // 2, 2, rows, -1))
+    return pick(blocks, core, 2), pick(blocks, 1 - core, 2).astype(BF)
 
 
 def on_device(
@@ -854,6 +990,9 @@
     capacity = (10 * tok + 32 * count - 1) // (32 * count) * 8
     pictures = tok // SEQ
     rows_all = pictures * ROWS
+    cut = (pictures + 1) // 2
+    groups = [(0, cut), (cut, pictures)] if pictures > 1 else [(0, pictures)]
+    lanes_of = lambda value: [value[:, lo * ROWS : hi * ROWS] for lo, hi in groups]
     here = lax.axis_index("expert")
     here_dp = lax.axis_index("dp")
     here_t = lax.axis_index("tensor")
@@ -869,36 +1008,28 @@
         [w_query, w_key, w_value, narrow, jnp.transpose(w_out)], axis=1
     ).astype(BF)
     pair = cross(first_pack)
-    in_own = follow(w_in, first_pack)[0].astype(BF)
-    back_own = follow(w_back, first_pack)[0].astype(BF)
-    ids_pad = images_of(follow(expert_ids, first_pack), -1)
-    pair, in_own, back_own, ids_pad = order.wait((pair, in_own, back_own, ids_pad))
+    in_own = [follow(w_in, first_pack)[0, lo:hi].astype(BF) for lo, hi in IN_CUTS]
+    back_own = [follow(w_back, first_pack)[0, :, lo:hi].astype(BF) for lo, hi in BACK_CUTS]
+    rows, rows_lane, ids_pad = slot_rows(here, follow(expert_ids, first_pack), capacity)
+    own_lanes = lanes_of(rows_lane)
+    pair, in_own, back_own, rows, rows_lane, ids_pad, own_lanes = order.wait(
+        (pair, in_own, back_own, rows, rows_lane, ids_pad, own_lanes)
+    )
 
     same_chips = stacked(chip_copies(order.after(pair)))
-    in_other = hop(order.after(in_own), "dp", 1)
-
-    routes = order.after(expert_ids)
-    slots = slot_table(routes, count)
-    rows = images_of(jnp.transpose((jnp.transpose(routes) ^ here) * capacity + slots), -1)
-    rows_lane = jnp.transpose(rows.reshape(-1, 2))
-    x = images_of(order.after(tokens))
-    cot = images_of(order.after(cotangent))
-    cot_flat = cot.reshape(rows_all, D)
-    cot_here = jnp.where(
-        here_t == 0, cot_flat, jnp.concatenate([cot_flat[:, HALF:], cot_flat[:, :HALF]], axis=1)
-    )
-    cut = (pictures + 1) // 2
-    groups = [(0, cut), (cut, pictures)] if pictures > 1 else [(0, pictures)]
-    lanes_of = lambda value: [value[:, lo * ROWS : hi * ROWS] for lo, hi in groups]
-    same_chips, x, rows, rows_lane, cot, cot_here, own_lanes = order.wait(
-        (same_chips, x, rows, rows_lane, cot, cot_here, lanes_of(rows_lane))
-    )
+    in_other = [hop(order.after(in_own[0]), "dp", 1)]
+    x, cot, cot_here = order.run(lambda *v: image_rows(which, *v), tokens, cotangent)
+    cot_here = cot_here.reshape(rows_all, D)
+    same_chips, in_other[0] = order.wait((same_chips, in_other[0]))
+    in_other.append(hop(order.after(in_own[1]), "dp", 1))
     flipped = order.wait(hop(order.after(same_chips), "expert", 1))
     qkv_w, narrow_all, out_here = order.run(
         lambda *v: assemble(*v, (3 * HALF, LANES, HALF)), same_chips, flipped
     )
     out_there = hop(order.after(out_here), "tensor", 1)
     vectors = order.run(lambda v: vectors_of(v, count), narrow_all)
+    in_other[1] = order.wait(in_other[1])
+    in_other.append(hop(order.after(in_own[2]), "dp", 1))
     rows_next = hop(order.after(rows_lane), "expert", 1)
     cot_next = hop(order.after(cot_here), "expert", 1)
 
@@ -913,7 +1044,8 @@
             rows_next, cot_next = order.wait((rows_next, cot_next))
     a_rows, qkv, o_rows, lse = held
     out_there = order.wait(out_there)
-    got_parts = list(order.wait(tuple(got_parts)))
+    got_parts, in_other[2] = order.wait((got_parts, in_other[2]))
+    back_other = [hop(order.after(back_own[0]), "dp", 1)]
     next_lanes = order.wait(lanes_of(rows_next))
     held, h_parts, h_next = [], [], []
     for n, (lo, hi) in enumerate(groups):
@@ -922,28 +1054,29 @@
             x, o_parts[n], got_parts[n], vectors, out_here, out_there, narrow_all, ids_pad, *held,
         )
         h_parts.append(h_part.reshape(-1, D))
+        if n == len(groups) - 1:
+            gates_lane = jnp.transpose(held[2].reshape(rows_all, LANES)[:, :2])
+            back_other[0], gates_lane = order.wait((back_other[0], gates_lane))
+            h_parts[-1] = order.after(h_parts[-1])
+            back_other.append(hop(order.after(back_own[1]), "dp", 1))
         h_next.append(hop(h_parts[-1], "expert", 1))
-        if n == 0:
-            in_other = order.wait(in_other)
-            back_other = hop(order.after(back_own), "dp", 1)
     y, probs, gates = held
-    gates_lane = jnp.transpose(gates.reshape(rows_all, LANES)[:, :2])
-    gates_next = hop(gates_lane, "expert", 1)
-
-    gates_next = order.wait(gates_next)
+    gates_next = hop(order.after(gates_lane), "expert", 1)
+
     own = (own_lanes, h_parts)
     other = (next_lanes, h_next)
     far = list(range(1, chips))
     outgoing = order.run(lambda *v: send_rows(*v, capacity, far, False), own, other)
     arrived = [None] + [hop(o, "expert", 2 * c) for o, c in zip(outgoing, far)]
     (arrived[0],) = order.run(lambda *v: send_rows(*v, capacity, [0], False), own, other)
+    gates_next = order.wait(gates_next)
     own = ([rows_lane], [cot_here], [gates_lane])
     other = ([rows_next], [cot_next], [gates_next])
     grad_outgoing = order.run(lambda *v: send_rows(*v, capacity, far, True), own, other)
     grad_arrived = [None] * chips
+    back_other[1] = order.wait(back_other[1])
     (grad_arrived[0],) = order.run(lambda *v: send_rows(*v, capacity, [0], True), own, other)
-    back_other = order.wait(back_other)
-    weights = (in_own, in_other, back_own, back_other)
+    weights = (*in_own, *in_other, *back_own, *back_other)
     same = flag(same)
 
     hidden, slopes, grads = [], [], []
@@ -953,7 +1086,12 @@
         value = order.run(add_halves, *waiting)
         return hop(value, "expert", 2 * chip) if chip else value
 
-    pending = None
+    leaving = []
+
+    def settle_oldest():
+        home, chip, waiting = leaving.pop(0)
+        home[chip] = back_to(chip, waiting)
+
     for c in range(chips):
         if c == 1:
             arrived[1:] = order.wait(arrived[1:])
@@ -968,9 +1106,9 @@
         g, s, zt, zh = order.run(lambda *v: expert_forward(same, *v), arrived[c], *weights)
         hidden.append(g)
         slopes.append(s)
-        if pending is not None:
-            came_back[c - 1] = back_to(c - 1, pending)
-        pending = (zh, hop(order.after(zt), "tensor", 1))
+        if len(leaving) > 1:
+            settle_oldest()
+        leaving.append((came_back, c, (zh, hop(order.after(zt), "tensor", 1))))
     for c in range(chips):
         if c and chips > 4:
             grad_arrived[c] = order.wait(grad_arrived[c])
@@ -978,21 +1116,18 @@
             lambda *v: expert_backward(same, *v), grad_arrived[c], slopes[c], *weights
         )
         grads.append(u)
-        if c:
-            grad_home[c - 1] = back_to(c - 1, pending)
-        else:
-            came_back[1] = order.wait(came_back[1])
-            came_back[chips - 1] = back_to(chips - 1, pending)
+        settle_oldest()
+        leaving.append((grad_home, c, (mh, hop(order.after(mt), "tensor", 1))))
         if c >= chips // 2:
-            step = (chips - 2) * 2 // chips
-            for k in range(2 + (c - chips // 2) * step, 2 + (c - chips // 2 + 1) * step):
+            step = 2 * (chips - 1) // chips
+            for k in range(1 + (c - chips // 2) * step, 1 + (c - chips // 2 + 1) * step):
                 came_back[k] = order.wait(came_back[k])
-        pending = (mh, hop(order.after(mt), "tensor", 1))
     z_here, z_there = order.run(lambda *v: sort_groups(v), *order.wait(tuple(came_back)))
     z_there = hop(z_there, "expert", 1)
     send_half = same
+    settle_oldest()
     back_send = order.run(lambda h, g: outer(send_half, h, g, True), hidden, grad_arrived)
-    grad_home[chips - 1] = back_to(chips - 1, pending)
+    settle_oldest()
     back_got = hop(order.after(back_send), "dp", 1)
     in_send = order.run(lambda g, a: outer(send_half, g, a, False), grads, arrived)
     grad_home = list(order.wait(tuple(grad_home)))
@@ -1008,11 +1143,12 @@
     for n, (lo, hi) in enumerate(groups):
         near = order.run(lambda *v: sum_home(*v, lo, hi), rows, m_here, m_there)
         near_parts.append((near, hop(near, "tensor", 1)))
-    dgate_next = order.wait(dgate_next)
+        if n == 0:
+            back_got, dgate_next = order.wait((back_got, dgate_next))
     held, parts, sums, got = [], [], [], []
     for n, (lo, hi) in enumerate(groups):
         if n == len(groups) - 1:
-            near_parts[n], back_got = order.wait((near_parts[n], back_got))
+            near_parts[n] = order.wait(near_parts[n])
             in_got = hop(order.after(in_send), "dp", 1)
         *held, part, sums2, sums1, grad_router = order.run(
             lambda *v: attend_back(which, *v[:15], lo, hi, v[15:]),
@@ -1020,23 +1156,27 @@
         )
         parts.append(part)
         got.append(hop(part, "tensor", 1))
-        sums.append(
-            jnp.concatenate([0.5 * grad_router[:count], sums1[:2], 0.5 * sums2[:2]], axis=0)
-        )
+        sums.append((grad_router, sums1, sums2))
     dy, dyb, dqkv = held
 
-    flat = lambda value: value.reshape(rows_all, -1)
-    grad_outw = dot_tn(flat(dyb), flat(o_rows))
-    grad_wqkv = dot_tn(flat(a_rows), flat(dqkv))
-    tiny = jnp.transpose(sum(sums))
-    tiny = jnp.pad(tiny, ((0, 0), (0, -tiny.shape[1] % LANES)))
-    all_grads = jnp.concatenate([grad_wqkv, grad_outw, tiny], axis=1)
+    routers, ones, twos = zip(*sums)
+    total, total_away = order.run(
+        projection_grads, a_rows, dqkv, dyb, o_rows, *routers, *ones, *twos
+    )
     keep_half = 1 - send_half
-    total = core_sum(order.after(all_grads), BF)
     grad_back = order.run(
         lambda h, g, b: outer(keep_half, h, g, True, b), hidden, grad_arrived, back_got
     )[None]
-    shards, leaving = chip_sum(order.wait(total), BF)
+    in_got, got[0] = order.wait((in_got, got[0]))
+    total_got = hop(order.after(total_away), "expert", 1)
+    grad_in = order.run(
+        lambda g, a, b: outer(keep_half, g, a, False, b), grads, arrived, in_got
+    )[None]
+    total_got = order.wait(total_got)
+    shards, leaving = chip_sum(order.wait(total + total_got.astype(F32)), BF)
+    shards, leaving, got = order.wait((shards, leaving, got))
+    entering = hop(leaving, "dp", 1)
+    out_other = hop(order.after(out_half), "tensor", 1)
     grad_tokens = []
     for n, (lo, hi) in enumerate(groups):
         grad_tokens = [
@@ -1045,17 +1185,9 @@
                 x, parts[n], got[n], dy, vectors, *grad_tokens,
             )
         ]
-        if n == 0:
-            shards, leaving = order.wait((shards, leaving))
-            entering = hop(leaving, "dp", 1)
-    out_other = hop(order.after(out_half), "tensor", 1)
     shards = order.wait(shards + entering.astype(F32))
     tiny = shards[:, 4 * HALF :]
-    tiny_next = hop(tiny, "tensor", 1)
-    grad_in = order.run(
-        lambda g, a, b: outer(keep_half, g, a, False, b), grads, arrived, in_got
-    )[None]
-    tiny = tiny + tiny_next
+    tiny = tiny + hop(tiny, "tensor", 1)
     grad_tokens = grad_tokens[0][:, :SEQ].reshape(tok, D)
     block_out = jnp.where(
         here_t == 0,
@@ -1066,10 +1198,10 @@
     return (
         block_out,
         grad_tokens,
-        tiny[:, count],
-        tiny[:, count + 1],
-        tiny[:, count + 2],
-        tiny[:, count + 3],
+        tiny[:, LANES - 8],
+        tiny[:, LANES - 7],
+        tiny[:, LANES - 6],
+        tiny[:, LANES - 5],
         shards[:, :HALF],
         shards[:, HALF : 2 * HALF],
         shards[:, 2 * HALF : 3 * HALF],

time: 607 us -> 566 us (0.932)
  waiting for transfers between devices: 184 us -> 149 us
  Pallas kernels: 283 us -> 311 us
  other arithmetic: 20.7 us -> 9.84 us
  local copies, waits for them, and re-layouts: 47.8 us -> 37.1 us
    ppermute x51 -> x54, waiting for transfers between devices: 184 us -> 149 us  [hop(): return lax.ppermute(value, axis, [(i, i ^ offset) for i in range(count)])]
    pallas_call x0 -> x3, Pallas kernels: none -> 28.1 us  [the longest x1 11.1 us: projection_grads(): pl.pallas_call(functools.partial(projection_kernel, parts=len(small) // 3...]
    convert_element_type x1 -> x5, local copies, waits for them, and re-layouts: 0.14 us -> 6.98 us  [the longest x3 4.09 us: on_device(): follow(w_in, first_pack)[0, lo:hi].astype(BF)]
    reshape x8 -> x0, local copies, waits for them, and re-layouts: 6.77 us -> none  [the longest x6 6.5 us: images_of(): value = value.reshape(-1, SEQ, value.shape[-1])]
    unnamed x120 -> x107, local copies, waits for them, and re-layouts: 21.4 us -> 14.8 us
    ppermute x51 -> x54, starting transfers between devices: 55.5 us -> 49.9 us  [hop(): return lax.ppermute(value, axis, [(i, i ^ offset) for i in range(count)])]
  transfers between devices with their start and end apart: 51 -> 54, of which waited for: 18 -> 21; matrix products, arithmetic and copies ran while one was open for 6% -> 4% of each run, Pallas kernels for 42% -> 54%
where the time goes in v4:
time: 566 us; the launch traced here: 559 us
  Pallas kernels  311 us (55%)
  waiting for transfers between devices  149 us (26%)
  starting transfers between devices  49.9 us (9%)
  local copies, waits for them, and re-layouts  37.1 us (7%)
  other arithmetic  9.84 us (2%)
    ppermute x54, waiting for transfers between devices, hop(): return lax.ppermute(value, axis, [(i, i ^ offset) for i in range(count)])  149 us
    pallas_call x4, Pallas kernels, expert_forward(): pl.pallas_call(forward_kernel, grid_spec=pltpu.PrefetchScalarGridSpec(num...  53.8 us
    ppermute x54, starting transfers between devices, hop(): return lax.ppermute(value, axis, [(i, i ^ offset) for i in range(count)])  49.9 us
    pallas_call x4, Pallas kernels, expert_backward(): pl.pallas_call(backward_kernel, grid_spec=pltpu.PrefetchScalarGridSpec(nu...  39.7 us
    pallas_call x4, Pallas kernels, outer(): pl.pallas_call(functools.partial(outer_kernel, chunks=len(wides), hidden_...  37.9 us
    pallas_call x2, Pallas kernels, attend_back(): pl.pallas_call(attend_back_kernel, grid_spec=pltpu.PrefetchScalarGridSpec...  34.6 us
    pallas_call x4, Pallas kernels, send_rows(): pl.pallas_call(functools.partial(send_kernel, parts=len(own[0]), chips=ch...  23.7 us
    pallas_call x8, Pallas kernels, add_halves(): pl.pallas_call(add_kernel, grid=(near.shape[0],), in_specs=[part, part],...  16.8 us
  transfers between devices with their start and end apart: 54, of which 21 were waited for; matrix products, arithmetic and copies ran while one was open for 4% of the time, Pallas kernels for 54%

profile of v4, /device:TPU:0, one launch (start us, length us, event | category | flops | bytes accessed | tf_op | source)
XLA Modules:
  0.0 558.7 jit_solution(14583363094455665136)
XLA Ops:
  6.4 4.1 collective-permute-start
  18.7 9.9 %slot_rows.1 = (s32[5,208,2]{2,1,0:T(8,128)}, s32[8,1040]{1,0:T(8,128)}, s32[5,208,2]{2,1,0:T(8,128)}) custom-call(s32[1]{0:T(128)} %bitcast.11.here_ref, s32[985,2]{1,0:T(8,128)} %copy.59.ids_ref), custom_call_target="tpu_custom_call" | custom-call | flops 1000 | bytes 1000 | tf_op jit(solution)/shard_map/slot_rows/pallas_call | solution.py:886
  38.0 7.1 %image_rows.1 = (bf16[5,208,768]{2,1,0:T(8,128)(2,1)}, bf16[5,208,768]{2,1,0:T(8,128)(2,1)}, bf16[5,208,768]{2,1,0:T(8,128)(2,1)}) custom-call(s32[1]{0:T(128)} %bitcast.12.which_ref, bf16[985,768]{1,0:T(8,128)(2,1)} %tok_ref, bf16[985,768]{1,0:T(8,128)(2,1)} %cot_ref), custom_call_target="tpu_custom_call" | custom-call | flops 1000 | bytes 1000 | tf_op jit(solution)/shard_map/image_rows/pallas_call | solution.py:842
  45.1 6.7 %collective-permute-done.2.refs_2_ = bf16[2,48,1664]{2,1,0:T(8,128)(2,1)S(1)} collective-permute-done((bf16[2,48,1664]{2,1,0:T(8,128)(2,1)}, bf16[2,48,1664]{2,1,0:T(8,128)(2,1)S(1)}, u32[]{:S(2)}, u32[]{:S(2)}) %collective-permute-start.2) | collective-permute-done | bytes 319520 | tf_op jit(solution)/shard_map/ppermute | solution.py:41
  58.2 3.4 assemble.1
  63.4 4.0 collective-permute-done.6.refs_4_
  68.0 4.1 collective-permute-start.9
  72.2 8.3 %attend.2 = (bf16[5,208,768]{2,1,0:T(8,128)(2,1)}, bf16[5,208,1152]{2,1,0:T(8,128)(2,1)}, bf16[5,208,384]{2,1,0:T(8,128)(2,1)}, f32[5,208,128]{2,1,0:T(8,128)}, bf16[3,208,384]{2,1,0:T(8,128)(2,1)}) custom-call(bf16[5,208,768]{2,1,0:T(8,128)(2,1)} %get-tuple-element.1226.x_ref, f32[8,768]{1,0:T(8,128)} %vectors.1.vec_ref, ...), custom_call_target="tpu_custom_call" | custom-call | flops 1000 | bytes 1000 | tf_op jit(solution)/shard_map/attend/pallas_call | solution.py:286
  81.8 6.3 %attend.3 = (bf16[5,208,768]{2,1,0:T(8,128)(2,1)}, bf16[5,208,1152]{2,1,0:T(8,128)(2,1)}, bf16[5,208,384]{2,1,0:T(8,128)(2,1)}, f32[5,208,128]{2,1,0:T(8,128)}, bf16[2,208,384]{2,1,0:T(8,128)(2,1)}) custom-call(bf16[5,208,768]{2,1,0:T(8,128)(2,1)} %get-tuple-element.1226.x_ref, ...), custom_call_target="tpu_custom_call", output_to_operand_aliasing={{0}: (3, {}), {1}: (4, {}), {2}: (5, {}), {3}: (6, {})} | custom-call | flops 1000 | bytes 1000 | tf_op jit(solution)/shard_map/attend/pallas_call | solution.py:286
  90.1 5.5 collective-permute-done.9.there_ref
  95.6 14.0 %collective-permute-done.10.got_ref = bf16[3,208,384]{2,1,0:T(8,128)(2,1)S(1)} collective-permute-done((bf16[3,208,384]{2,1,0:T(8,128)(2,1)}, bf16[3,208,384]{2,1,0:T(8,128)(2,1)S(1)}, u32[]{:S(2)}, u32[]{:S(2)}) %collective-permute-start.10) | collective-permute-done | bytes 479264 | tf_op jit(solution)/shard_map/ppermute | solution.py:41
  109.6 6.3 %collective-permute-done.11.got_ref = bf16[2,208,384]{2,1,0:T(8,128)(2,1)S(1)} collective-permute-done((bf16[2,208,384]{2,1,0:T(8,128)(2,1)}, bf16[2,208,384]{2,1,0:T(8,128)(2,1)S(1)}, u32[]{:S(2)}, u32[]{:S(2)}) %collective-permute-start.11) | collective-permute-done | bytes 319520 | tf_op jit(solution)/shard_map/ppermute | solution.py:41
  118.2 6.7 %route.2 = (f32[5,208,768]{2,1,0:T(8,128)}, f32[5,208,128]{2,1,0:T(8,128)}, f32[5,208,128]{2,1,0:T(8,128)}, bf16[3,208,768]{2,1,0:T(8,128)(2,1)}) custom-call(s32[1]{0:T(128)} %bitcast.12.which_ref, bf16[5,208,768]{2,1,0:T(8,128)(2,1)} %get-tuple-element.1226.x_ref, bf16[3,208,384]{2,1,0:T(8,128)(2,1)} %get-tuple-element.717.own_ref, ...), custom_call_target="tpu_custom_call" | custom-call | flops 1000 | bytes 1000 | tf_op jit(solution)/shard_map/route/pallas_call | solution.py:331
  125.0 5.5 route.3
  131.8 3.8 collective-permute-done.13.refs_8_
  138.8 6.9 %send_rows.2 = (bf16[2,312,768]{2,1,0:T(8,128)(2,1)}, bf16[2,312,768]{2,1,0:T(8,128)(2,1)}, bf16[2,312,768]{2,1,0:T(8,128)(2,1)}) custom-call(s32[2,624]{1,0:T(2,128)} %slice.82.refs_0_, s32[2,416]{1,0:T(2,128)} %slice.83.refs_1_, bf16[624,768]{1,0:T(8,128)(2,1)} %bitcast.57, bf16[416,768]{1,0:T(8,128)(2,1)} %bitcast.60, s32[2,624]{1,0:T(2,128)} %slice.84.refs_4_, ...), custom_call_target="tpu_custom_call" | custom-call | flops 1000 | bytes 1000 | tf_op jit(solution)/shard_map/send_rows/pallas_call | solution.py:389
  149.1 4.4 send_rows.3.m_ref.refs_4_
  154.2 7.4 %send_gated.2 = (bf16[2,312,768]{2,1,0:T(8,128)(2,1)}, bf16[2,312,768]{2,1,0:T(8,128)(2,1)}, bf16[2,312,768]{2,1,0:T(8,128)(2,1)}) custom-call(s32[2,1040]{1,0:T(2,128)} %copy-done.45, bf16[1040,768]{1,0:T(8,128)(2,1)} %bitcast.53, f32[2,1040]{1,0:T(2,128)} %bitcast.66, s32[2,1040]{1,0:T(2,128)} %copy-done.46, ...), custom_call_target="tpu_custom_call" | custom-call | flops 1000 | bytes 1000 | tf_op jit(solution)/shard_map/send_gated/pallas_call | solution.py:389
  161.6 23.9 %collective-permute-done.17.refs_9_ = bf16[1536,256]{1,0:T(8,128)(2,1)S(1)} collective-permute-done((bf16[1536,256]{1,0:T(8,128)(2,1)S(1)}, bf16[1536,256]{1,0:T(8,128)(2,1)S(1)}, u32[]{:S(2)}, u32[]{:S(2)}) %collective-permute-start.17) | collective-permute-done | bytes 786464 | tf_op jit(solution)/shard_map/ppermute | solution.py:41
  185.5 5.0 send_gated.3.z_ref.refs_4_
  190.5 13.6 %expert_forward.4 = (bf16[2,312,1536]{2,1,0:T(8,128)(2,1)}, bf16[2,312,1536]{2,1,0:T(8,128)(2,1)}, bf16[2,312,384]{2,1,0:T(8,128)(2,1)}, f32[2,312,384]{2,1,0:T(8,128)}) custom-call(s32[1]{0:T(128)} %bitcast.18.same_ref.which_ref, bf16[2,312,768]{2,1,0:T(8,128)(2,1)} %send_rows.3.m_ref.refs_4_, bf16[112,1536]{1,0:T(8,128)(2,1)} %copy-done.5, ...), custom_call_target="tpu_custom_call" | custom-call | flops 1000 | bytes 1000 | tf_op jit(solution)/shard_map/expert_forward/pallas_call | solution.py:542
  207.7 13.2 %expert_forward.5 = (bf16[2,312,1536]{2,1,0:T(8,128)(2,1)}, bf16[2,312,1536]{2,1,0:T(8,128)(2,1)}, bf16[2,312,384]{2,1,0:T(8,128)(2,1)}, f32[2,312,384]{2,1,0:T(8,128)}) custom-call(s32[1]{0:T(128)} %bitcast.18.same_ref.which_ref, bf16[2,312,768]{2,1,0:T(8,128)(2,1)} %copy-done.13, bf16[112,1536]{1,0:T(8,128)(2,1)} %copy-done.5, bf16[64,1536]{1,0:T(8,128)(2,1)} %copy-done.8, ...), custom_call_target="tpu_custom_call" | custom-call | flops 1000 | bytes 1000 | tf_op jit(solution)/shard_map/expert_forward/pallas_call | solution.py:542
  223.0 13.2 %expert_forward.6 = (bf16[2,312,1536]{2,1,0:T(8,128)(2,1)}, bf16[2,312,1536]{2,1,0:T(8,128)(2,1)}, bf16[2,312,384]{2,1,0:T(8,128)(2,1)}, f32[2,312,384]{2,1,0:T(8,128)}) custom-call(s32[1]{0:T(128)} %bitcast.18.same_ref.which_ref, bf16[2,312,768]{2,1,0:T(8,128)(2,1)} %collective-permute-done.19.m_ref.refs_6_, bf16[112,1536]{1,0:T(8,128)(2,1)} %copy-done.5, ...), custom_call_target="tpu_custom_call" | custom-call | flops 1000 | bytes 1000 | tf_op jit(solution)/shard_map/expert_forward/pallas_call | solution.py:542
  238.4 10.7 %collective-permute-done.23.z_ref.refs_6_ = bf16[2,312,768]{2,1,0:T(8,128)(2,1)S(1)} collective-permute-done((bf16[2,312,768]{2,1,0:T(8,128)(2,1)}, bf16[2,312,768]{2,1,0:T(8,128)(2,1)S(1)}, u32[]{:S(2)}, u32[]{:S(2)}) %collective-permute-start.23) | collective-permute-done | bytes 958496 | tf_op jit(solution)/shard_map/ppermute | solution.py:41
  249.2 13.8 %expert_forward.7 = (bf16[2,312,1536]{2,1,0:T(8,128)(2,1)}, bf16[2,312,1536]{2,1,0:T(8,128)(2,1)}, bf16[2,312,384]{2,1,0:T(8,128)(2,1)}, f32[2,312,384]{2,1,0:T(8,128)}) custom-call(s32[1]{0:T(128)} %bitcast.18.same_ref.which_ref, bf16[2,312,768]{2,1,0:T(8,128)(2,1)} %collective-permute-done.20.m_ref.refs_7_, bf16[112,1536]{1,0:T(8,128)(2,1)} %copy-done.5, ...), custom_call_target="tpu_custom_call" | custom-call | flops 1000 | bytes 1000 | tf_op jit(solution)/shard_map/expert_forward/pallas_call | solution.py:542
  265.9 10.1 %expert_backward.4 = (bf16[2,312,1536]{2,1,0:T(8,128)(2,1)}, bf16[2,312,384]{2,1,0:T(8,128)(2,1)}, f32[2,312,384]{2,1,0:T(8,128)}) custom-call(s32[1]{0:T(128)} %bitcast.18.same_ref.which_ref, bf16[2,312,768]{2,1,0:T(8,128)(2,1)} %send_gated.3.z_ref.refs_4_, bf16[2,312,1536]{2,1,0:T(8,128)(2,1)} %get-tuple-element.905.s_ref, bf16[112,1536]{1,0:T(8,128)(2,1)} %copy-done.5, ...), custom_call_target="tpu_custom_call" | custom-call | flops 1000 | bytes 1000 | tf_op jit(solution)/shard_map/expert_backward/pallas_call | solution.py:589
  280.8 9.9 %expert_backward.5 = (bf16[2,312,1536]{2,1,0:T(8,128)(2,1)}, bf16[2,312,384]{2,1,0:T(8,128)(2,1)}, f32[2,312,384]{2,1,0:T(8,128)}) custom-call(s32[1]{0:T(128)} %bitcast.18.same_ref.which_ref, bf16[2,312,768]{2,1,0:T(8,128)(2,1)} %copy-done.12, bf16[2,312,1536]{2,1,0:T(8,128)(2,1)} %get-tuple-element.929.s_ref, bf16[112,1536]{1,0:T(8,128)(2,1)} %copy-done.5, ...), custom_call_target="tpu_custom_call" | custom-call | flops 1000 | bytes 1000 | tf_op jit(solution)/shard_map/expert_backward/pallas_call | solution.py:589
  295.0 9.9 %expert_backward.6 = (bf16[2,312,1536]{2,1,0:T(8,128)(2,1)}, bf16[2,312,384]{2,1,0:T(8,128)(2,1)}, f32[2,312,384]{2,1,0:T(8,128)}) custom-call(s32[1]{0:T(128)} %bitcast.18.same_ref.which_ref, bf16[2,312,768]{2,1,0:T(8,128)(2,1)} %copy-done.11, bf16[2,312,1536]{2,1,0:T(8,128)(2,1)} %get-tuple-element.953.s_ref, bf16[112,1536]{1,0:T(8,128)(2,1)} %copy-done.5, ...), custom_call_target="tpu_custom_call" | custom-call | flops 1000 | bytes 1000 | tf_op jit(solution)/shard_map/expert_backward/pallas_call | solution.py:589
  310.5 9.9 %expert_backward.7 = (bf16[2,312,1536]{2,1,0:T(8,128)(2,1)}, bf16[2,312,384]{2,1,0:T(8,128)(2,1)}, f32[2,312,384]{2,1,0:T(8,128)}) custom-call(s32[1]{0:T(128)} %bitcast.18.same_ref.which_ref, bf16[2,312,768]{2,1,0:T(8,128)(2,1)} %copy-done.10, bf16[2,312,1536]{2,1,0:T(8,128)(2,1)} %get-tuple-element.979.s_ref, bf16[112,1536]{1,0:T(8,128)(2,1)} %copy-done.5, ...), custom_call_target="tpu_custom_call" | custom-call | flops 1000 | bytes 1000 | tf_op jit(solution)/shard_map/expert_backward/pallas_call | solution.py:589
  330.8 9.7 %outer_send.2 = bf16[1536,384]{1,0:T(8,128)(2,1)} custom-call(s32[1]{0:T(128)} %bitcast.18.same_ref.which_ref, bf16[2,312,1536]{2,1,0:T(8,128)(2,1)} %get-tuple-element.1180.refs_0_, bf16[2,312,1536]{2,1,0:T(8,128)(2,1)} %get-tuple-element.1181.refs_1_, bf16[2,312,1536]{2,1,0:T(8,128)(2,1)} %get-tuple-element.1182.refs_2_, ...), custom_call_target="tpu_custom_call" | custom-call | flops 1000 | bytes 1000 | tf_op jit(solution)/shard_map/outer_send/pallas_call | solution.py:632
  348.6 8.8 %outer_send.3 = bf16[384,1536]{1,0:T(8,128)(2,1)} custom-call(s32[1]{0:T(128)} %bitcast.18.same_ref.which_ref, bf16[2,312,1536]{2,1,0:T(8,128)(2,1)} %get-tuple-element.1195.refs_0_, bf16[2,312,1536]{2,1,0:T(8,128)(2,1)} %get-tuple-element.1196.refs_1_, bf16[2,312,1536]{2,1,0:T(8,128)(2,1)} %get-tuple-element.1197.refs_2_, ...), custom_call_target="tpu_custom_call" | custom-call | flops 1000 | bytes 1000 | tf_op jit(solution)/shard_map/outer_send/pallas_call | solution.py:632
  357.4 5.7 %collective-permute-done.37.refs_3_ = bf16[2,312,384]{2,1,0:T(8,128)(2,1)} collective-permute-done((bf16[2,312,384]{2,1,0:T(8,128)(2,1)}, bf16[2,312,384]{2,1,0:T(8,128)(2,1)}, u32[]{:S(2)}, u32[]{:S(2)}) %collective-permute-start.37) | collective-permute-done | bytes 479264 | tf_op jit(solution)/shard_map/ppermute | solution.py:41
  366.9 15.2 %bring_home.1 = (bf16[5,208,384]{2,1,0:T(8,128)(2,1)}, f32[5,8,208]{2,1,0:T(8,128)}) custom-call(s32[1]{0:T(128)} %bitcast.12.which_ref, s32[5,208,2]{2,1,0:T(8,128)} %get-tuple-element.1091.rows_ref, f32[5,208,768]{2,1,0:T(8,128)} %get-tuple-element.1131.middle_ref.y_ref, bf16[5,208,768]{2,1,0:T(8,128)(2,1)} %get-tuple-element.1139.grad_ref.cot_ref, ...), custom_call_target="tpu_custom_call" | custom-call | flops 1000 | bytes 1000 | tf_op jit(solution)/shard_map/bring_home/pallas_call | solution.py:441
  383.0 5.6 %sum_home.2.near_ref = bf16[3,208,384]{2,1,0:T(8,128)(2,1)} custom-call(s32[5,208,2]{2,1,0:T(8,128)} %get-tuple-element.1091.rows_ref, bf16[4,312,384]{2,1,0:T(8,128)(2,1)} %get-tuple-element.1092.own_ref, bf16[4,312,384]{2,1,0:T(8,128)(2,1)} %copy-done.14), custom_call_target="tpu_custom_call" | custom-call | flops 1000 | bytes 1000 | tf_op jit(solution)/shard_map/sum_home/pallas_call | solution.py:468
  390.7 18.9 %collective-permute-done.41.dgate2_ref = f32[5,8,208]{2,1,0:T(8,128)S(1)} collective-permute-done((f32[5,8,208]{2,1,0:T(8,128)S(1)}, f32[5,8,208]{2,1,0:T(8,128)S(1)}, u32[]{:S(2)}, u32[]{:S(2)}) %collective-permute-start.41) | collective-permute-done | bytes 33312 | tf_op jit(solution)/shard_map/ppermute | solution.py:41
  409.6 4.9 sum_home.3.near_ref
  415.3 19.8 %attend_back.2 = (f32[5,208,768]{2,1,0:T(8,128)}, bf16[5,208,768]{2,1,0:T(8,128)(2,1)}, bf16[5,208,1152]{2,1,0:T(8,128)(2,1)}, bf16[3,208,768]{2,1,0:T(8,128)(2,...) custom-call(s32[1]{0:T(128)} %bitcast.12.which_ref, bf16[5,208,768]{2,1,0:T(8,128)(2,1)} %get-tuple-element.1226.x_ref, ...), custom_call_target="tpu_custom_call" | custom-call | flops 1000 | bytes 1000 | tf_op jit(solution)/shard_map/attend_back/pallas_call | solution.py:747
  437.3 14.9 %attend_back.3 = (f32[5,208,768]{2,1,0:T(8,128)}, bf16[5,208,768]{2,1,0:T(8,128)(2,1)}, bf16[5,208,1152]{2,1,0:T(8,128)(2,1)}, bf16[2,208,768]{2,1,0:T(8,128)(2,...) custom-call(s32[1]{0:T(128)} %bitcast.12.which_ref, ...), custom_call_target="tpu_custom_call", output_to_operand_aliasing={{0}: (16, {}), {1}: (17, {}), {2}: (18, {})} | custom-call | flops 1000 | bytes 1000 | tf_op jit(solution)/shard_map/attend_back/pallas_call | solution.py:747
  452.2 11.1 %projection_grads.1 = (f32[2,4,48,1664]{3,2,1,0:T(8,128)}, bf16[2,4,48,1664]{3,2,1,0:T(8,128)(2,1)}) custom-call(s32[1]{0:T(128)} %bitcast.19.core_ref, bf16[5,208,768]{2,1,0:T(8,128)(2,1)} %get-tuple-element.1166.refs_0_, bf16[5,208,1152]{2,1,0:T(8,128)(2,1)} %get-tuple-element.1167.refs_1_, bf16[5,208,768]{2,1,0:T(8,128)(2,1)} %get-tuple-element.1168.refs_2_, ...), custom_call_target="tpu_custom_call" | custom-call | flops 1000 | bytes 1000 | tf_op jit(solution)/shard_map/projection_grads/pallas_call | solution.py:951
  463.3 10.1 %outer_keep.2 = f32[1536,384]{1,0:T(8,128)} custom-call(s32[1]{0:T(128)S(6)} %sub.6.which_ref, bf16[2,312,1536]{2,1,0:T(8,128)(2,1)} %get-tuple-element.1180.refs_0_, bf16[2,312,1536]{2,1,0:T(8,128)(2,1)} %get-tuple-element.1181.refs_1_, bf16[2,312,1536]{2,1,0:T(8,128)(2,1)} %get-tuple-element.1182.refs_2_, ...), custom_call_target="tpu_custom_call" | custom-call | flops 1000 | bytes 1000 | tf_op jit(solution)/shard_map/outer_keep/pallas_call | solution.py:632
  473.4 9.6 %collective-permute-done.45.got_ref = bf16[3,208,768]{2,1,0:T(8,128)(2,1)S(1)} collective-permute-done((bf16[3,208,768]{2,1,0:T(8,128)(2,1)}, bf16[3,208,768]{2,1,0:T(8,128)(2,1)S(1)}, u32[]{:S(2)}, u32[]{:S(2)}) %collective-permute-start.45) | collective-permute-done | bytes 958496 | tf_op jit(solution)/shard_map/ppermute | solution.py:41
  483.0 6.3 %collective-permute-done.44.refs_8_ = bf16[384,1536]{1,0:T(8,128)(2,1)S(1)} collective-permute-done((bf16[384,1536]{1,0:T(8,128)(2,1)S(1)}, bf16[384,1536]{1,0:T(8,128)(2,1)S(1)}, u32[]{:S(2)}, u32[]{:S(2)}) %collective-permute-start.44) | collective-permute-done | bytes 1179680 | tf_op jit(solution)/shard_map/ppermute | solution.py:41
  490.4 9.4 %outer_keep.3 = f32[384,1536]{1,0:T(8,128)} custom-call(s32[1]{0:T(128)S(6)} %sub.6.which_ref, bf16[2,312,1536]{2,1,0:T(8,128)(2,1)} %get-tuple-element.1195.refs_0_, bf16[2,312,1536]{2,1,0:T(8,128)(2,1)} %get-tuple-element.1196.refs_1_, bf16[2,312,1536]{2,1,0:T(8,128)(2,1)} %get-tuple-element.1197.refs_2_, ...), custom_call_target="tpu_custom_call" | custom-call | flops 1000 | bytes 1000 | tf_op jit(solution)/shard_map/outer_keep/pallas_call | solution.py:632
  507.2 6.4 %collective-permute-done.47 = bf16[2,48,1664]{2,1,0:T(8,128)(2,1)S(1)} collective-permute-done((bf16[2,48,1664]{2,1,0:T(8,128)(2,1)}, bf16[2,48,1664]{2,1,0:T(8,128)(2,1)S(1)}, u32[]{:S(2)}, u32[]{:S(2)}) %collective-permute-start.47) | collective-permute-done | bytes 319520 | tf_op jit(solution)/shard_map/ppermute | solution.py:41
  513.6 4.8 collective-permute-done.48
  522.8 5.1 token_back.2.refs_0_
  527.9 3.3 token_back.3
  538.1 15.4 %collective-permute-done.53 = f32[48,128]{1,0:T(8,128)S(1)} collective-permute-done((f32[48,128]{1,0:T(8,128)S(1)}, f32[48,128]{1,0:T(8,128)S(1)}, u32[]{:S(2)}, u32[]{:S(2)}) %collective-permute-start.53) | collective-permute-done | bytes 24608 | tf_op jit(solution)/shard_map/ppermute | solution.py:41
  (246 shorter events, 124.5 us)
Async XLA Ops:
  6.4 25.6 %collective-permute-start = (bf16[48,1664]{1,0:T(8,128)(2,1)S(1)}, bf16[48,1664]{1,0:T(8,128)(2,1)S(1)}, u32[]{:S(2)}, u32[]{:S(2)}) collective-permute-start(bf16[48,1664]{1,0:T(8,128)(2,1)S(1)} %bitcast_dynamic-update-slice_fusion.own_ref), channel_id=1, source_target_pairs={{0,16},{16,0},{1,17},{17,1},{2,18},{18,2},{3,19},{19,3},{4,20},{20... | collective-permute-start | bytes 479240 | tf_op jit(solution)/shard_map/ppermute | solution.py:41
  34.5 20.5 %collective-permute-start.4 = (bf16[112,1536]{1,0:T(8,128)(2,1)S(1)}, bf16[112,1536]{1,0:T(8,128)(2,1)S(1)}, u32[]{:S(2)}, u32[]{:S(2)}) collective-permute-start(bf16[112,1536]{1,0:T(8,128)(2,1)S(1)} %fusion.6.refs_0_), channel_id=1, source_target_pairs={{0,16},{16,0},{1,17},{17,1},{2,18},{18,2},{3,19},{19,3},{4,20},{20... | collective-permute-start | bytes 1032200 | tf_op jit(solution)/shard_map/ppermute | solution.py:41
  36.3 15.5 %collective-permute-start.2 = (bf16[2,48,1664]{2,1,0:T(8,128)(2,1)}, bf16[2,48,1664]{2,1,0:T(8,128)(2,1)S(1)}, u32[]{:S(2)}, u32[]{:S(2)}) collective-permute-start(bf16[2,48,1664]{2,1,0:T(8,128)(2,1)} %cross.1.refs_0_), channel_id=1, source_target_pairs={{0,8},{2,10},{4,12},{6,14},{8,0},{10,2},{12,4},{14,6},{1,9},{3,11}... | collective-permute-start | bytes 958472 | tf_op jit(solution)/shard_map/ppermute | solution.py:41
  37.8 14.0 %collective-permute-start.3 = (bf16[2,48,1664]{2,1,0:T(8,128)(2,1)}, bf16[2,48,1664]{2,1,0:T(8,128)(2,1)}, u32[]{:S(2)}, u32[]{:S(2)}) collective-permute-start(bf16[2,48,1664]{2,1,0:T(8,128)(2,1)} %cross.1.refs_0_), channel_id=1, source_target_pairs={{0,12},{2,14},{4,8},{6,10},{8,4},{10,6},{12,0},{14,2},{1,13},{3,15... | collective-permute-start | bytes 958472 | tf_op jit(solution)/shard_map/ppermute | solution.py:41
  54.9 12.4 %collective-permute-start.6 = (bf16[64,1536]{1,0:T(8,128)(2,1)S(1)}, bf16[64,1536]{1,0:T(8,128)(2,1)S(1)}, u32[]{:S(2)}, u32[]{:S(2)}) collective-permute-start(bf16[64,1536]{1,0:T(8,128)(2,1)S(1)} %fusion.10.refs_1_), channel_id=1, source_target_pairs={{0,16},{16,0},{1,17},{17,1},{2,18},{18,2},{3,19},{19,3},{4,20},{20... | collective-permute-start | bytes 589832 | tf_op jit(solution)/shard_map/ppermute | solution.py:41
  68.0 13.8 %collective-permute-start.8 = (bf16[1040,768]{1,0:T(8,128)(2,1)}, bf16[1040,768]{1,0:T(8,128)(2,1)}, u32[]{:S(2)}, u32[]{:S(2)}) collective-permute-start(bf16[1040,768]{1,0:T(8,128)(2,1)} %bitcast.52), channel_id=1, source_target_pairs={{0,2},{2,0},{4,6},{6,4},{8,10},{10,8},{12,14},{14,12},{1,3},{3,1},... | collective-permute-start | bytes 4792328 | tf_op jit(solution)/shard_map/ppermute | solution.py:41
  68.0 41.5 %collective-permute-start.12 = (bf16[208,1536]{1,0:T(8,128)(2,1)S(1)}, bf16[208,1536]{1,0:T(8,128)(2,1)S(1)}, u32[]{:S(2)}, u32[]{:S(2)}) collective-permute-start(bf16[208,1536]{1,0:T(8,128)(2,1)S(1)} %fusion.2.refs_2_), channel_id=1, source_target_pairs={{0,16},{16,0},{1,17},{17,1},{2,18},{18,2},{3,19},{19,3},{4,20},{20... | collective-permute-start | bytes 1916936 | tf_op jit(solution)/shard_map/ppermute | solution.py:41
  68.0 27.6 %collective-permute-start.9 = (bf16[768,384]{1,0:T(8,128)(2,1)}, bf16[768,384]{1,0:T(8,128)(2,1)}, u32[]{:S(2)}, u32[]{:S(2)}) collective-permute-start(bf16[768,384]{1,0:T(8,128)(2,1)} %get-tuple-element.1141.here_ref.out_w_ref), channel_id=1, source_target_pairs={{0,1},{1,0},{2,3},{3,2},{4,5},{5,4},{6,7},{7,6},{8,9},{9,8},{10,11... | collective-permute-start | bytes 1769480 | tf_op jit(solution)/shard_map/ppermute | solution.py:41
  80.5 29.1 %collective-permute-start.10 = (bf16[3,208,384]{2,1,0:T(8,128)(2,1)}, bf16[3,208,384]{2,1,0:T(8,128)(2,1)S(1)}, u32[]{:S(2)}, u32[]{:S(2)}) collective-permute-start(bf16[3,208,384]{2,1,0:T(8,128)(2,1)} %get-tuple-element.717.own_ref), channel_id=1, source_target_pairs={{0,1},{1,0},{2,3},{3,2},{4,5},{5,4},{6,7},{7,6},{8,9},{9,8},{10,11... | collective-permute-start | bytes 1437704 | tf_op jit(solution)/shard_map/ppermute | solution.py:41
  88.1 27.7 %collective-permute-start.11 = (bf16[2,208,384]{2,1,0:T(8,128)(2,1)}, bf16[2,208,384]{2,1,0:T(8,128)(2,1)S(1)}, u32[]{:S(2)}, u32[]{:S(2)}) collective-permute-start(bf16[2,208,384]{2,1,0:T(8,128)(2,1)} %get-tuple-element.734.own_ref), channel_id=1, source_target_pairs={{0,1},{1,0},{2,3},{3,2},{4,5},{5,4},{6,7},{7,6},{8,9},{9,8},{10,11... | collective-permute-start | bytes 958472 | tf_op jit(solution)/shard_map/ppermute | solution.py:41
  115.9 19.7 %collective-permute-start.13 = (bf16[1536,128]{1,0:T(8,128)(2,1)S(1)}, bf16[1536,128]{1,0:T(8,128)(2,1)S(1)}, u32[]{:S(2)}, u32[]{:S(2)}) collective-permute-start(bf16[1536,128]{1,0:T(8,128)(2,1)S(1)} %fusion.5.refs_6_), channel_id=1, source_target_pairs={{0,16},{16,0},{1,17},{17,1},{2,18},{18,2},{3,19},{19,3},{4,20},{20... | collective-permute-start | bytes 1179656 | tf_op jit(solution)/shard_map/ppermute | solution.py:41
  125.0 10.7 %collective-permute-start.14 = (bf16[624,768]{1,0:T(8,128)(2,1)}, bf16[624,768]{1,0:T(8,128)(2,1)S(1)}, u32[]{:S(2)}, u32[]{:S(2)}) collective-permute-start(bf16[624,768]{1,0:T(8,128)(2,1)} %bitcast.56), channel_id=1, source_target_pairs={{0,2},{2,0},{4,6},{6,4},{8,10},{10,8},{12,14},{14,12},{1,3},{3,1},... | collective-permute-start | bytes 2875400 | tf_op jit(solution)/shard_map/ppermute | solution.py:41
  145.6 58.4 %collective-permute-start.18 = (bf16[2,312,768]{2,1,0:T(8,128)(2,1)}, bf16[2,312,768]{2,1,0:T(8,128)(2,1)S(1)}, u32[]{:S(2)}, u32[]{:S(2)}) collective-permute-start(bf16[2,312,768]{2,1,0:T(8,128)(2,1)} %get-tuple-element.828), channel_id=1, source_target_pairs={{0,4},{2,6},{4,0},{6,2},{8,12},{10,14},{12,8},{14,10},{1,5},{3,7},... | collective-permute-start | bytes 2875400 | tf_op jit(solution)/shard_map/ppermute | solution.py:41
  146.2 57.8 %collective-permute-start.19 = (bf16[2,312,768]{2,1,0:T(8,128)(2,1)}, bf16[2,312,768]{2,1,0:T(8,128)(2,1)}, u32[]{:S(2)}, u32[]{:S(2)}) collective-permute-start(bf16[2,312,768]{2,1,0:T(8,128)(2,1)} %get-tuple-element.829), channel_id=1, source_target_pairs={{0,8},{2,10},{4,12},{6,14},{8,0},{10,2},{12,4},{14,6},{1,9},{3,11}... | collective-permute-start | bytes 2875400 | tf_op jit(solution)/shard_map/ppermute | solution.py:41
  147.7 56.4 %collective-permute-start.20 = (bf16[2,312,768]{2,1,0:T(8,128)(2,1)}, bf16[2,312,768]{2,1,0:T(8,128)(2,1)}, u32[]{:S(2)}, u32[]{:S(2)}) collective-permute-start(bf16[2,312,768]{2,1,0:T(8,128)(2,1)} %get-tuple-element.830), channel_id=1, source_target_pairs={{0,12},{2,14},{4,8},{6,10},{8,4},{10,6},{12,0},{14,2},{1,13},{3,15... | collective-permute-start | bytes 2875400 | tf_op jit(solution)/shard_map/ppermute | solution.py:41
  149.1 36.3 %collective-permute-start.17 = (bf16[1536,256]{1,0:T(8,128)(2,1)S(1)}, bf16[1536,256]{1,0:T(8,128)(2,1)S(1)}, u32[]{:S(2)}, u32[]{:S(2)}) collective-permute-start(bf16[1536,256]{1,0:T(8,128)(2,1)S(1)} %fusion.1.refs_7_), channel_id=1, source_target_pairs={{0,16},{16,0},{1,17},{17,1},{2,18},{18,2},{3,19},{19,3},{4,20},{20... | collective-permute-start | bytes 2359304 | tf_op jit(solution)/shard_map/ppermute | solution.py:41
  204.1 34.3 %collective-permute-start.24 = (bf16[2,312,768]{2,1,0:T(8,128)(2,1)}, bf16[2,312,768]{2,1,0:T(8,128)(2,1)S(1)}, u32[]{:S(2)}, u32[]{:S(2)}) collective-permute-start(bf16[2,312,768]{2,1,0:T(8,128)(2,1)} %get-tuple-element.877), channel_id=1, source_target_pairs={{0,12},{2,14},{4,8},{6,10},{8,4},{10,6},{12,0},{14,2},{1,13},{3,15... | collective-permute-start | bytes 2875400 | tf_op jit(solution)/shard_map/ppermute | solution.py:41
  205.7 43.4 %collective-permute-start.23 = (bf16[2,312,768]{2,1,0:T(8,128)(2,1)}, bf16[2,312,768]{2,1,0:T(8,128)(2,1)S(1)}, u32[]{:S(2)}, u32[]{:S(2)}) collective-permute-start(bf16[2,312,768]{2,1,0:T(8,128)(2,1)} %get-tuple-element.875), channel_id=1, source_target_pairs={{0,8},{2,10},{4,12},{6,14},{8,0},{10,2},{12,4},{14,6},{1,9},{3,11}... | collective-permute-start | bytes 2875400 | tf_op jit(solution)/shard_map/ppermute | solution.py:41
  206.5 42.6 %collective-permute-start.22 = (bf16[2,312,768]{2,1,0:T(8,128)(2,1)}, bf16[2,312,768]{2,1,0:T(8,128)(2,1)S(1)}, u32[]{:S(2)}, u32[]{:S(2)}) collective-permute-start(bf16[2,312,768]{2,1,0:T(8,128)(2,1)} %get-tuple-element.873), channel_id=1, source_target_pairs={{0,4},{2,6},{4,0},{6,2},{8,12},{10,14},{12,8},{14,10},{1,5},{3,7},... | collective-permute-start | bytes 2875400 | tf_op jit(solution)/shard_map/ppermute | solution.py:41
  207.7 28.6 %collective-permute-start.21 = (bf16[2,312,384]{2,1,0:T(8,128)(2,1)}, bf16[2,312,384]{2,1,0:T(8,128)(2,1)}, u32[]{:S(2)}, u32[]{:S(2)}) collective-permute-start(bf16[2,312,384]{2,1,0:T(8,128)(2,1)} %get-tuple-element.868), channel_id=1, source_target_pairs={{0,1},{1,0},{2,3},{3,2},{4,5},{5,4},{6,7},{7,6},{8,9},{9,8},{10,11... | collective-permute-start | bytes 1437704 | tf_op jit(solution)/shard_map/ppermute | solution.py:41
  220.9 42.1 %collective-permute-start.25 = (bf16[2,312,384]{2,1,0:T(8,128)(2,1)}, bf16[2,312,384]{2,1,0:T(8,128)(2,1)S(1)}, u32[]{:S(2)}, u32[]{:S(2)}) collective-permute-start(bf16[2,312,384]{2,1,0:T(8,128)(2,1)} %get-tuple-element.898), channel_id=1, source_target_pairs={{0,1},{1,0},{2,3},{3,2},{4,5},{5,4},{6,7},{7,6},{8,9},{9,8},{10,11... | collective-permute-start | bytes 1437704 | tf_op jit(solution)/shard_map/ppermute | solution.py:41
  238.3 37.6 %collective-permute-start.26 = (bf16[2,312,384]{2,1,0:T(8,128)(2,1)}, bf16[2,312,384]{2,1,0:T(8,128)(2,1)}, u32[]{:S(2)}, u32[]{:S(2)}) collective-permute-start(bf16[2,312,384]{2,1,0:T(8,128)(2,1)} %get-tuple-element.922), channel_id=1, source_target_pairs={{0,1},{1,0},{2,3},{3,2},{4,5},{5,4},{6,7},{7,6},{8,9},{9,8},{10,11... | collective-permute-start | bytes 1437704 | tf_op jit(solution)/shard_map/ppermute | solution.py:41
  265.9 24.8 %collective-permute-start.27 = (bf16[2,312,384]{2,1,0:T(8,128)(2,1)S(1)}, bf16[2,312,384]{2,1,0:T(8,128)(2,1)S(1)}, u32[]{:S(2)}, u32[]{:S(2)}) collective-permute-start(bf16[2,312,384]{2,1,0:T(8,128)(2,1)S(1)} %copy-done.51), channel_id=1, source_target_pairs={{0,1},{1,0},{2,3},{3,2},{4,5},{5,4},{6,7},{7,6},{8,9},{9,8},{10,11... | collective-permute-start | bytes 1437704 | tf_op jit(solution)/shard_map/ppermute | solution.py:41
  278.1 26.8 %collective-permute-start.28 = (bf16[2,312,384]{2,1,0:T(8,128)(2,1)S(1)}, bf16[2,312,384]{2,1,0:T(8,128)(2,1)}, u32[]{:S(2)}, u32[]{:S(2)}) collective-permute-start(bf16[2,312,384]{2,1,0:T(8,128)(2,1)S(1)} %copy-done.50), channel_id=1, source_target_pairs={{0,1},{1,0},{2,3},{3,2},{4,5},{5,4},{6,7},{7,6},{8,9},{9,8},{10,11... | collective-permute-start | bytes 1437704 | tf_op jit(solution)/shard_map/ppermute | solution.py:41
  280.1 28.4 %collective-permute-start.29 = (bf16[2,312,384]{2,1,0:T(8,128)(2,1)S(1)}, bf16[2,312,384]{2,1,0:T(8,128)(2,1)S(1)}, u32[]{:S(2)}, u32[]{:S(2)}) collective-permute-start(bf16[2,312,384]{2,1,0:T(8,128)(2,1)S(1)} %copy-done.26), channel_id=1, source_target_pairs={{0,4},{2,6},{4,0},{6,2},{8,12},{10,14},{12,8},{14,10},{1,5},{3,7},... | collective-permute-start | bytes 1437704 | tf_op jit(solution)/shard_map/ppermute | solution.py:41
  293.5 26.9 %collective-permute-start.30 = (bf16[2,312,384]{2,1,0:T(8,128)(2,1)}, bf16[2,312,384]{2,1,0:T(8,128)(2,1)S(1)}, u32[]{:S(2)}, u32[]{:S(2)}) collective-permute-start(bf16[2,312,384]{2,1,0:T(8,128)(2,1)} %get-tuple-element.996), channel_id=1, source_target_pairs={{0,1},{1,0},{2,3},{3,2},{4,5},{5,4},{6,7},{7,6},{8,9},{9,8},{10,11... | collective-permute-start | bytes 1437704 | tf_op jit(solution)/shard_map/ppermute | solution.py:41
  293.6 29.9 %collective-permute-start.31 = (bf16[2,312,384]{2,1,0:T(8,128)(2,1)S(1)}, bf16[2,312,384]{2,1,0:T(8,128)(2,1)S(1)}, u32[]{:S(2)}, u32[]{:S(2)}) collective-permute-start(bf16[2,312,384]{2,1,0:T(8,128)(2,1)S(1)} %copy-done.24), channel_id=1, source_target_pairs={{0,8},{2,10},{4,12},{6,14},{8,0},{10,2},{12,4},{14,6},{1,9},{3,11}... | collective-permute-start | bytes 1437704 | tf_op jit(solution)/shard_map/ppermute | solution.py:41
  304.9 18.5 %collective-permute-start.32 = (bf16[2,312,384]{2,1,0:T(8,128)(2,1)S(1)}, bf16[2,312,384]{2,1,0:T(8,128)(2,1)S(1)}, u32[]{:S(2)}, u32[]{:S(2)}) collective-permute-start(bf16[2,312,384]{2,1,0:T(8,128)(2,1)S(1)} %copy-done.25), channel_id=1, source_target_pairs={{0,12},{2,14},{4,8},{6,10},{8,4},{10,6},{12,0},{14,2},{1,13},{3,15... | collective-permute-start | bytes 1437704 | tf_op jit(solution)/shard_map/ppermute | solution.py:41
  308.5 19.4 %collective-permute-start.33 = (bf16[2,312,384]{2,1,0:T(8,128)(2,1)}, bf16[2,312,384]{2,1,0:T(8,128)(2,1)S(1)}, u32[]{:S(2)}, u32[]{:S(2)}) collective-permute-start(bf16[2,312,384]{2,1,0:T(8,128)(2,1)} %get-tuple-element.1016), channel_id=1, source_target_pairs={{0,1},{1,0},{2,3},{3,2},{4,5},{5,4},{6,7},{7,6},{8,9},{9,8},{10,11... | collective-permute-start | bytes 1437704 | tf_op jit(solution)/shard_map/ppermute | solution.py:41
  323.4 19.2 %collective-permute-start.34 = (bf16[2,312,384]{2,1,0:T(8,128)(2,1)}, bf16[2,312,384]{2,1,0:T(8,128)(2,1)S(1)}, u32[]{:S(2)}, u32[]{:S(2)}) collective-permute-start(bf16[2,312,384]{2,1,0:T(8,128)(2,1)} %get-tuple-element.1035), channel_id=1, source_target_pairs={{0,1},{1,0},{2,3},{3,2},{4,5},{5,4},{6,7},{7,6},{8,9},{9,8},{10,11... | collective-permute-start | bytes 1437704 | tf_op jit(solution)/shard_map/ppermute | solution.py:41
  340.5 16.9 %collective-permute-start.36 = (bf16[2,312,384]{2,1,0:T(8,128)(2,1)}, bf16[2,312,384]{2,1,0:T(8,128)(2,1)S(1)}, u32[]{:S(2)}, u32[]{:S(2)}) collective-permute-start(bf16[2,312,384]{2,1,0:T(8,128)(2,1)} %add_halves.14), channel_id=1, source_target_pairs={{0,8},{2,10},{4,12},{6,14},{8,0},{10,2},{12,4},{14,6},{1,9},{3,11}... | collective-permute-start | bytes 1437704 | tf_op jit(solution)/shard_map/ppermute | solution.py:41
  341.9 15.5 %collective-permute-start.35 = (bf16[2,312,384]{2,1,0:T(8,128)(2,1)S(1)}, bf16[2,312,384]{2,1,0:T(8,128)(2,1)}, u32[]{:S(2)}, u32[]{:S(2)}) collective-permute-start(bf16[2,312,384]{2,1,0:T(8,128)(2,1)S(1)} %copy-done.28), channel_id=1, source_target_pairs={{0,4},{2,6},{4,0},{6,2},{8,12},{10,14},{12,8},{14,10},{1,5},{3,7},... | collective-permute-start | bytes 1437704 | tf_op jit(solution)/shard_map/ppermute | solution.py:41
  345.4 17.7 %collective-permute-start.37 = (bf16[2,312,384]{2,1,0:T(8,128)(2,1)}, bf16[2,312,384]{2,1,0:T(8,128)(2,1)}, u32[]{:S(2)}, u32[]{:S(2)}) collective-permute-start(bf16[2,312,384]{2,1,0:T(8,128)(2,1)} %add_halves.15), channel_id=1, source_target_pairs={{0,12},{2,14},{4,8},{6,10},{8,4},{10,6},{12,0},{14,2},{1,13},{3,15... | collective-permute-start | bytes 1437704 | tf_op jit(solution)/shard_map/ppermute | solution.py:41
  346.8 62.8 %collective-permute-start.40 = (bf16[1536,384]{1,0:T(8,128)(2,1)}, bf16[1536,384]{1,0:T(8,128)(2,1)S(1)}, u32[]{:S(2)}, u32[]{:S(2)}) collective-permute-start(bf16[1536,384]{1,0:T(8,128)(2,1)} %outer_send.2), channel_id=1, source_target_pairs={{0,16},{16,0},{1,17},{17,1},{2,18},{18,2},{3,19},{19,3},{4,20},{20... | collective-permute-start | bytes 3538952 | tf_op jit(solution)/shard_map/ppermute | solution.py:41
  348.6 17.4 %collective-permute-start.38 = (bf16[4,312,384]{2,1,0:T(8,128)(2,1)}, bf16[4,312,384]{2,1,0:T(8,128)(2,1)S(1)}, u32[]{:S(2)}, u32[]{:S(2)}) collective-permute-start(bf16[4,312,384]{2,1,0:T(8,128)(2,1)} %get-tuple-element.1068), channel_id=1, source_target_pairs={{0,2},{2,0},{4,6},{6,4},{8,10},{10,8},{12,14},{14,12},{1,3},{3,1},... | collective-permute-start | bytes 2875400 | tf_op jit(solution)/shard_map/ppermute | solution.py:41
  366.0 16.1 %collective-permute-start.39 = (bf16[4,312,384]{2,1,0:T(8,128)(2,1)}, bf16[4,312,384]{2,1,0:T(8,128)(2,1)S(1)}, u32[]{:S(2)}, u32[]{:S(2)}) collective-permute-start(bf16[4,312,384]{2,1,0:T(8,128)(2,1)} %get-tuple-element.1079), channel_id=1, source_target_pairs={{0,2},{2,0},{4,6},{6,4},{8,10},{10,8},{12,14},{14,12},{1,3},{3,1},... | collective-permute-start | bytes 2875400 | tf_op jit(solution)/shard_map/ppermute | solution.py:41
  388.7 25.8 %collective-permute-start.42 = (bf16[3,208,384]{2,1,0:T(8,128)(2,1)}, bf16[3,208,384]{2,1,0:T(8,128)(2,1)S(1)}, u32[]{:S(2)}, u32[]{:S(2)}) collective-permute-start(bf16[3,208,384]{2,1,0:T(8,128)(2,1)} %sum_home.2.near_ref), channel_id=1, source_target_pairs={{0,1},{1,0},{2,3},{3,2},{4,5},{5,4},{6,7},{7,6},{8,9},{9,8},{10,11... | collective-permute-start | bytes 1437704 | tf_op jit(solution)/shard_map/ppermute | solution.py:41
  390.3 19.3 %collective-permute-start.41 = (f32[5,8,208]{2,1,0:T(8,128)S(1)}, f32[5,8,208]{2,1,0:T(8,128)S(1)}, u32[]{:S(2)}, u32[]{:S(2)}) collective-permute-start(f32[5,8,208]{2,1,0:T(8,128)S(1)} %copy-done.42), channel_id=1, source_target_pairs={{0,1},{1,0},{2,3},{3,2},{4,5},{5,4},{6,7},{7,6},{8,9},{9,8},{10,11... | collective-permute-start | bytes 99848 | tf_op jit(solution)/shard_map/ppermute | solution.py:41
  414.5 20.6 %collective-permute-start.43 = (bf16[2,208,384]{2,1,0:T(8,128)(2,1)}, bf16[2,208,384]{2,1,0:T(8,128)(2,1)}, u32[]{:S(2)}, u32[]{:S(2)}) collective-permute-start(bf16[2,208,384]{2,1,0:T(8,128)(2,1)} %sum_home.3.near_ref), channel_id=1, source_target_pairs={{0,1},{1,0},{2,3},{3,2},{4,5},{5,4},{6,7},{7,6},{8,9},{9,8},{10,11... | collective-permute-start | bytes 958472 | tf_op jit(solution)/shard_map/ppermute | solution.py:41
  435.2 54.2 %collective-permute-start.44 = (bf16[384,1536]{1,0:T(8,128)(2,1)S(1)}, bf16[384,1536]{1,0:T(8,128)(2,1)S(1)}, u32[]{:S(2)}, u32[]{:S(2)}) collective-permute-start(bf16[384,1536]{1,0:T(8,128)(2,1)S(1)} %copy-done.18), channel_id=1, source_target_pairs={{0,16},{16,0},{1,17},{17,1},{2,18},{18,2},{3,19},{19,3},{4,20},{20... | collective-permute-start | bytes 3538952 | tf_op jit(solution)/shard_map/ppermute | solution.py:41
  437.1 45.9 %collective-permute-start.45 = (bf16[3,208,768]{2,1,0:T(8,128)(2,1)}, bf16[3,208,768]{2,1,0:T(8,128)(2,1)S(1)}, u32[]{:S(2)}, u32[]{:S(2)}) collective-permute-start(bf16[3,208,768]{2,1,0:T(8,128)(2,1)} %get-tuple-element.1219.own_ref), channel_id=1, source_target_pairs={{0,1},{1,0},{2,3},{3,2},{4,5},{5,4},{6,7},{7,6},{8,9},{9,8},{10,11... | collective-permute-start | bytes 2875400 | tf_op jit(solution)/shard_map/ppermute | solution.py:41
  503.0 10.6 %collective-permute-start.47 = (bf16[2,48,1664]{2,1,0:T(8,128)(2,1)}, bf16[2,48,1664]{2,1,0:T(8,128)(2,1)S(1)}, u32[]{:S(2)}, u32[]{:S(2)}) collective-permute-start(bf16[2,48,1664]{2,1,0:T(8,128)(2,1)} %get-tuple-element.1282), channel_id=1, source_target_pairs={{0,4},{2,6},{4,0},{6,2},{8,12},{10,14},{12,8},{14,10},{1,5},{3,7},... | collective-permute-start | bytes 958472 | tf_op jit(solution)/shard_map/ppermute | solution.py:41
  503.6 14.8 %collective-permute-start.48 = (bf16[2,48,1664]{2,1,0:T(8,128)(2,1)}, bf16[2,48,1664]{2,1,0:T(8,128)(2,1)S(1)}, u32[]{:S(2)}, u32[]{:S(2)}) collective-permute-start(bf16[2,48,1664]{2,1,0:T(8,128)(2,1)} %get-tuple-element.1283), channel_id=1, source_target_pairs={{0,8},{2,10},{4,12},{6,14},{8,0},{10,2},{12,4},{14,6},{1,9},{3,11}... | collective-permute-start | bytes 958472 | tf_op jit(solution)/shard_map/ppermute | solution.py:41
  505.8 14.1 %collective-permute-start.49 = (bf16[2,48,1664]{2,1,0:T(8,128)(2,1)}, bf16[2,48,1664]{2,1,0:T(8,128)(2,1)S(1)}, u32[]{:S(2)}, u32[]{:S(2)}) collective-permute-start(bf16[2,48,1664]{2,1,0:T(8,128)(2,1)} %fusion.9), channel_id=1, source_target_pairs={{0,12},{2,14},{4,8},{6,10},{8,4},{10,6},{12,0},{14,2},{1,13},{3,15... | collective-permute-start | bytes 958472 | tf_op jit(solution)/shard_map/ppermute | solution.py:41
  507.2 15.3 %collective-permute-start.50 = (bf16[2,208,768]{2,1,0:T(8,128)(2,1)}, bf16[2,208,768]{2,1,0:T(8,128)(2,1)}, u32[]{:S(2)}, u32[]{:S(2)}) collective-permute-start(bf16[2,208,768]{2,1,0:T(8,128)(2,1)} %get-tuple-element.1227.own_ref), channel_id=1, source_target_pairs={{0,1},{1,0},{2,3},{3,2},{4,5},{5,4},{6,7},{7,6},{8,9},{9,8},{10,11... | collective-permute-start | bytes 1916936 | tf_op jit(solution)/shard_map/ppermute | solution.py:41
  522.5 14.5 %collective-permute-start.52 = (bf16[48,1664]{1,0:T(8,128)(2,1)}, bf16[48,1664]{1,0:T(8,128)(2,1)S(1)}, u32[]{:S(2)}, u32[]{:S(2)}) collective-permute-start(bf16[48,1664]{1,0:T(8,128)(2,1)} %fusion.11), channel_id=1, source_target_pairs={{0,16},{16,0},{1,17},{17,1},{2,18},{18,2},{3,19},{19,3},{4,20},{20... | collective-permute-start | bytes 479240 | tf_op jit(solution)/shard_map/ppermute | solution.py:41
  535.3 19.7 %collective-permute-start.51 = (bf16[5,208,384]{2,1,0:T(8,128)(2,1)}, bf16[5,208,384]{2,1,0:T(8,128)(2,1)}, u32[]{:S(2)}, u32[]{:S(2)}) collective-permute-start(bf16[5,208,384]{2,1,0:T(8,128)(2,1)} %get-tuple-element.1215), channel_id=1, source_target_pairs={{0,1},{1,0},{2,3},{3,2},{4,5},{5,4},{6,7},{7,6},{8,9},{9,8},{10,11... | collective-permute-start | bytes 2396168 | tf_op jit(solution)/shard_map/ppermute | solution.py:41
  537.0 16.5 %collective-permute-start.53 = (f32[48,128]{1,0:T(8,128)S(1)}, f32[48,128]{1,0:T(8,128)S(1)}, u32[]{:S(2)}, u32[]{:S(2)}) collective-permute-start(f32[48,128]{1,0:T(8,128)S(1)} %slice.89), channel_id=1, source_target_pairs={{0,1},{1,0},{2,3},{3,2},{4,5},{5,4},{6,7},{7,6},{8,9},{9,8},{10,11... | collective-permute-start | bytes 73736 | tf_op jit(solution)/shard_map/ppermute | solution.py:41
  (58 other events, 819.9 us)

commit v5 on v4

--- a/solution.py
+++ b/solution.py
@@ -21,7 +21,7 @@
 LANES = 128
 TILE = 512
 IN_CUTS = ((0, 112), (112, 176), (176, 384))
-BACK_CUTS = ((0, 128), (128, 384))
+BACK_CUTS = ((0, 128), (128, 256), (256, 384))
 TAIL_RATE = 0.305
 TAIL = (
     0.12163973686996697,
@@ -602,6 +602,7 @@
 
 
 def outer_kernel(which_ref, *refs, chunks, hidden_first, added):
+    step = pl.program_id(0)
     wides = refs[:chunks]
     narrows = refs[chunks : 2 * chunks]
     out_ref = refs[-1]
@@ -611,8 +612,10 @@
             slim = slim_ref[b]
             term = dot_tn(wide_ref[b], slim) if hidden_first else dot_tn(slim, wide_ref[b])
             total = term if total is None else total + term
-    if added:
+    if added == 1:
         total = total + refs[-2][...].astype(F32)
+    elif added == 2:
+        total = total + jnp.where(step == 0, refs[-3][...], refs[-2][...]).astype(F32)
     out_ref[...] = total.astype(out_ref.dtype)
 
 
@@ -626,21 +629,25 @@
     specs = [pl.BlockSpec((per, capacity, TILE), lambda i, s: (0, 0, i))] * len(wides)
     specs += [slim] * len(narrows)
     operands = list(wides) + list(narrows)
-    if extra is not None:
+    extra = [] if extra is None else list(extra)
+    if len(extra) == 1:
         specs.append(out)
-        operands.append(extra)
+    elif len(extra) == 2:
+        specs.append(pl.BlockSpec((TILE, HALF), lambda i, s: (0, 0)))
+        specs.append(pl.BlockSpec((TILE, HALF), lambda i, s: (jnp.maximum(i - 1, 0), 0)))
+    operands += extra
     return pl.pallas_call(
         functools.partial(
             outer_kernel,
             chunks=len(wides),
             hidden_first=hidden_first,
-            added=extra is not None,
+            added=len(extra),
         ),
         grid_spec=pltpu.PrefetchScalarGridSpec(
             num_scalar_prefetch=1, grid=(hidden // TILE,), in_specs=specs, out_specs=out
         ),
-        out_shape=jax.ShapeDtypeStruct(shape, BF if extra is None else F32),
-        name="outer_send" if extra is None else "outer_keep",
+        out_shape=jax.ShapeDtypeStruct(shape, F32 if extra else BF),
+        name="outer_keep" if extra else "outer_send",
         cost_estimate=cost(),
     )(which, *operands)
 
@@ -752,8 +759,8 @@
             in_specs=[
                 image(D, lo),
                 image(D, lo),
-                image(HALF),
-                image(HALF),
+                image(HALF, lo),
+                image(HALF, lo),
                 turned,
                 turned,
                 image(LANES, lo),
@@ -895,7 +902,7 @@
         name="slot_rows",
         cost_estimate=cost(),
     )(flag(here), expert_ids)
-    return rows, lanes[:2], ids
+    return rows, lanes, ids
 
 
 def projection_kernel(core_ref, *refs, parts, split):
@@ -1010,18 +1017,18 @@
     pair = cross(first_pack)
     in_own = [follow(w_in, first_pack)[0, lo:hi].astype(BF) for lo, hi in IN_CUTS]
     back_own = [follow(w_back, first_pack)[0, :, lo:hi].astype(BF) for lo, hi in BACK_CUTS]
-    rows, rows_lane, ids_pad = slot_rows(here, follow(expert_ids, first_pack), capacity)
-    own_lanes = lanes_of(rows_lane)
-    pair, in_own, back_own, rows, rows_lane, ids_pad, own_lanes = order.wait(
-        (pair, in_own, back_own, rows, rows_lane, ids_pad, own_lanes)
-    )
+    pair, in_own, back_own = order.wait((pair, in_own, back_own))
 
     same_chips = stacked(chip_copies(order.after(pair)))
     in_other = [hop(order.after(in_own[0]), "dp", 1)]
     x, cot, cot_here = order.run(lambda *v: image_rows(which, *v), tokens, cotangent)
     cot_here = cot_here.reshape(rows_all, D)
+    rows, rows_lanes, ids_pad = order.run(lambda v: slot_rows(here, v, capacity), expert_ids)
     same_chips, in_other[0] = order.wait((same_chips, in_other[0]))
+    rows_lane = order.wait(rows_lanes[:2])
     in_other.append(hop(order.after(in_own[1]), "dp", 1))
+    rows_next = hop(order.after(rows_lane), "expert", 1)
+    cot_next = hop(order.after(cot_here), "expert", 1)
     flipped = order.wait(hop(order.after(same_chips), "expert", 1))
     qkv_w, narrow_all, out_here = order.run(
         lambda *v: assemble(*v, (3 * HALF, LANES, HALF)), same_chips, flipped
@@ -1030,8 +1037,9 @@
     vectors = order.run(lambda v: vectors_of(v, count), narrow_all)
     in_other[1] = order.wait(in_other[1])
     in_other.append(hop(order.after(in_own[2]), "dp", 1))
-    rows_next = hop(order.after(rows_lane), "expert", 1)
-    cot_next = hop(order.after(cot_here), "expert", 1)
+    back_other = [hop(order.after(back_own[0]), "dp", 1)]
+    rows_next, cot_next = order.wait((rows_next, cot_next))
+    own_lanes, next_lanes = order.wait((lanes_of(rows_lane), lanes_of(rows_next)))
 
     held, o_parts, got_parts = [], [], []
     for n, (lo, hi) in enumerate(groups):
@@ -1040,13 +1048,10 @@
         )
         o_parts.append(o_part)
         got_parts.append(hop(o_part, "tensor", 1))
-        if n == 0:
-            rows_next, cot_next = order.wait((rows_next, cot_next))
     a_rows, qkv, o_rows, lse = held
     out_there = order.wait(out_there)
-    got_parts, in_other[2] = order.wait((got_parts, in_other[2]))
-    back_other = [hop(order.after(back_own[0]), "dp", 1)]
-    next_lanes = order.wait(lanes_of(rows_next))
+    got_parts, in_other[2], back_other[0] = order.wait((got_parts, in_other[2], back_other[0]))
+    back_other.append(hop(order.after(back_own[1]), "dp", 1))
     held, h_parts, h_next = [], [], []
     for n, (lo, hi) in enumerate(groups):
         *held, h_part = order.run(
@@ -1056,9 +1061,9 @@
         h_parts.append(h_part.reshape(-1, D))
         if n == len(groups) - 1:
             gates_lane = jnp.transpose(held[2].reshape(rows_all, LANES)[:, :2])
-            back_other[0], gates_lane = order.wait((back_other[0], gates_lane))
+            back_other[1], gates_lane = order.wait((back_other[1], gates_lane))
             h_parts[-1] = order.after(h_parts[-1])
-            back_other.append(hop(order.after(back_own[1]), "dp", 1))
+            back_other.append(hop(order.after(back_own[2]), "dp", 1))
         h_next.append(hop(h_parts[-1], "expert", 1))
     y, probs, gates = held
     gates_next = hop(order.after(gates_lane), "expert", 1)
@@ -1067,14 +1072,14 @@
     other = (next_lanes, h_next)
     far = list(range(1, chips))
     outgoing = order.run(lambda *v: send_rows(*v, capacity, far, False), own, other)
-    arrived = [None] + [hop(o, "expert", 2 * c) for o, c in zip(outgoing, far)]
+    back_other[2] = order.wait(back_other[2])
+    arrived = [None] + [hop(order.after(o), "expert", 2 * c) for o, c in zip(outgoing, far)]
     (arrived[0],) = order.run(lambda *v: send_rows(*v, capacity, [0], False), own, other)
     gates_next = order.wait(gates_next)
     own = ([rows_lane], [cot_here], [gates_lane])
     other = ([rows_next], [cot_next], [gates_next])
     grad_outgoing = order.run(lambda *v: send_rows(*v, capacity, far, True), own, other)
     grad_arrived = [None] * chips
-    back_other[1] = order.wait(back_other[1])
     (grad_arrived[0],) = order.run(lambda *v: send_rows(*v, capacity, [0], True), own, other)
     weights = (*in_own, *in_other, *back_own, *back_other)
     same = flag(same)
@@ -1127,32 +1132,31 @@
     send_half = same
     settle_oldest()
     back_send = order.run(lambda h, g: outer(send_half, h, g, True), hidden, grad_arrived)
+    back_send = order.wait([back_send[:TILE], back_send[TILE:]])
     settle_oldest()
-    back_got = hop(order.after(back_send), "dp", 1)
+    back_got = [hop(order.after(back_send[0]), "dp", 1)]
     in_send = order.run(lambda g, a: outer(send_half, g, a, False), grads, arrived)
     grad_home = list(order.wait(tuple(grad_home)))
     m_here, m_there = order.run(lambda *v: sort_groups(v), *grad_home)
-    m_there = hop(m_there, "expert", 1)
+    back_got[0] = order.wait(back_got[0])
+    back_got.append(hop(order.after(back_send[1]), "dp", 1))
+    m_there = hop(order.after(m_there), "expert", 1)
 
     out_half, dgate = order.run(
         lambda *v: bring_home(which, *v), rows, y, cot, gates, z_here, z_there
     )
     dgate_next = hop(dgate, "tensor", 1)
     m_there = order.wait(m_there)
-    near_parts = []
-    for n, (lo, hi) in enumerate(groups):
-        near = order.run(lambda *v: sum_home(*v, lo, hi), rows, m_here, m_there)
-        near_parts.append((near, hop(near, "tensor", 1)))
-        if n == 0:
-            back_got, dgate_next = order.wait((back_got, dgate_next))
+    near = order.run(lambda *v: sum_home(*v, 0, pictures), rows, m_here, m_there)
+    away = hop(near, "tensor", 1)
+    back_got, dgate_next = order.wait((back_got, dgate_next))
+    in_got = hop(order.after(in_send), "dp", 1)
+    away = order.wait(away)
     held, parts, sums, got = [], [], [], []
     for n, (lo, hi) in enumerate(groups):
-        if n == len(groups) - 1:
-            near_parts[n] = order.wait(near_parts[n])
-            in_got = hop(order.after(in_send), "dp", 1)
         *held, part, sums2, sums1, grad_router = order.run(
             lambda *v: attend_back(which, *v[:15], lo, hi, v[15:]),
-            x, y, *near_parts[n], dgate, dgate_next, probs, ids_pad, narrow_all, cot, vectors, out_here, qkv, lse, qkv_w, *held,
+            x, y, near, away, dgate, dgate_next, probs, ids_pad, narrow_all, cot, vectors, out_here, qkv, lse, qkv_w, *held,
         )
         parts.append(part)
         got.append(hop(part, "tensor", 1))
@@ -1170,7 +1174,7 @@
     in_got, got[0] = order.wait((in_got, got[0]))
     total_got = hop(order.after(total_away), "expert", 1)
     grad_in = order.run(
-        lambda g, a, b: outer(keep_half, g, a, False, b), grads, arrived, in_got
+        lambda g, a, b: outer(keep_half, g, a, False, [b]), grads, arrived, in_got
     )[None]
     total_got = order.wait(total_got)
     shards, leaving = chip_sum(order.wait(total + total_got.astype(F32)), BF)
@@ -1185,7 +1189,7 @@
                 x, parts[n], got[n], dy, vectors, *grad_tokens,
             )
         ]
-    shards = order.wait(shards + entering.astype(F32))
+    shards, out_other = order.wait((shards + entering.astype(F32), out_other))
     tiny = shards[:, 4 * HALF :]
     tiny = tiny + hop(tiny, "tensor", 1)
     grad_tokens = grad_tokens[0][:, :SEQ].reshape(tok, D)

time: 566 us -> 563 us (level)
  waiting for transfers between devices: 149 us -> 132 us
    ppermute x54 -> x55, waiting for transfers between devices: 149 us -> 132 us  [hop(): return lax.ppermute(value, axis, [(i, i ^ offset) for i in range(count)])]
    pallas_call x4, Pallas kernels: 53.8 us -> 62.4 us  [expert_forward(): pl.pallas_call(forward_kernel, grid_spec=pltpu.PrefetchScalarGridSpec(num...]
    ppermute x54 -> x55, starting transfers between devices: 49.9 us -> 54.3 us  [hop(): return lax.ppermute(value, axis, [(i, i ^ offset) for i in range(count)])]
    unnamed x107 -> x109, local copies, waits for them, and re-layouts: 14.8 us -> 14.5 us
  transfers between devices with their start and end apart: 54 -> 55, of which waited for: 21 -> 19; matrix products, arithmetic and copies ran while one was open for 4% -> 5% of each run, Pallas kernels for 54% -> 57%
where the time goes in v5:
time: 563 us; the launch traced here: 553 us
  Pallas kernels  315 us (56%)
  waiting for transfers between devices  132 us (23%)
  starting transfers between devices  54.3 us (10%)
  local copies, waits for them, and re-layouts  40.1 us (7%)
  other arithmetic  9.88 us (2%)
    ppermute x55, waiting for transfers between devices, hop(): return lax.ppermute(value, axis, [(i, i ^ offset) for i in range(count)])  132 us
    pallas_call x4, Pallas kernels, expert_forward(): pl.pallas_call(forward_kernel, grid_spec=pltpu.PrefetchScalarGridSpec(num...  62.4 us
    ppermute x55, starting transfers between devices, hop(): return lax.ppermute(value, axis, [(i, i ^ offset) for i in range(count)])  54.3 us
    pallas_call x4, Pallas kernels, expert_backward(): pl.pallas_call(backward_kernel, grid_spec=pltpu.PrefetchScalarGridSpec(nu...  39 us
    pallas_call x4, Pallas kernels, outer(): pl.pallas_call(functools.partial(outer_kernel, chunks=len(wides), hidden_...  38.1 us
    pallas_call x2, Pallas kernels, attend_back(): pl.pallas_call(attend_back_kernel, grid_spec=pltpu.PrefetchScalarGridSpec...  34.6 us
    pallas_call x4, Pallas kernels, send_rows(): pl.pallas_call(functools.partial(send_kernel, parts=len(own[0]), chips=ch...  23.4 us
    pallas_call x8, Pallas kernels, add_halves(): pl.pallas_call(add_kernel, grid=(near.shape[0],), in_specs=[part, part],...  16.7 us
  transfers between devices with their start and end apart: 55, of which 19 were waited for; matrix products, arithmetic and copies ran while one was open for 5% of the time, Pallas kernels for 57%

profile of v5, /device:TPU:0, one launch (start us, length us, event | category | flops | bytes accessed | tf_op | source)
XLA Modules:
  0.0 553.5 jit_solution(12067991657726866442)
XLA Ops:
  6.4 4.1 collective-permute-start
  24.4 6.9 %image_rows.1 = (bf16[5,208,768]{2,1,0:T(8,128)(2,1)}, bf16[5,208,768]{2,1,0:T(8,128)(2,1)}, bf16[5,208,768]{2,1,0:T(8,128)(2,1)}) custom-call(s32[1]{0:T(128)} %bitcast.12.which_ref, bf16[985,768]{1,0:T(8,128)(2,1)} %tok_ref, bf16[985,768]{1,0:T(8,128)(2,1)} %cot_ref), custom_call_target="tpu_custom_call" | custom-call | flops 1000 | bytes 1000 | tf_op jit(solution)/shard_map/image_rows/pallas_call | solution.py:849
  32.4 9.9 %slot_rows.1 = (s32[5,208,2]{2,1,0:T(8,128)}, s32[8,1040]{1,0:T(8,128)}, s32[5,208,2]{2,1,0:T(8,128)}) custom-call(s32[1]{0:T(128)} %bitcast.13.here_ref, s32[985,2]{1,0:T(8,128)} %copy.59.ids_ref), custom_call_target="tpu_custom_call" | custom-call | flops 1000 | bytes 1000 | tf_op jit(solution)/shard_map/slot_rows/pallas_call | solution.py:893
  46.8 2.9 collective-permute-start.6
  51.9 3.4 assemble.1
  60.0 3.3 collective-permute-start.9
  65.8 8.3 %attend.2 = (bf16[5,208,768]{2,1,0:T(8,128)(2,1)}, bf16[5,208,1152]{2,1,0:T(8,128)(2,1)}, bf16[5,208,384]{2,1,0:T(8,128)(2,1)}, f32[5,208,128]{2,1,0:T(8,128)}, bf16[3,208,384]{2,1,0:T(8,128)(2,1)}) custom-call(bf16[5,208,768]{2,1,0:T(8,128)(2,1)} %get-tuple-element.1284.x_ref, f32[8,768]{1,0:T(8,128)} %vectors.1.vec_ref, ...), custom_call_target="tpu_custom_call" | custom-call | flops 1000 | bytes 1000 | tf_op jit(solution)/shard_map/attend/pallas_call | solution.py:286
  75.0 6.6 %attend.3 = (bf16[5,208,768]{2,1,0:T(8,128)(2,1)}, bf16[5,208,1152]{2,1,0:T(8,128)(2,1)}, bf16[5,208,384]{2,1,0:T(8,128)(2,1)}, f32[5,208,128]{2,1,0:T(8,128)}, bf16[2,208,384]{2,1,0:T(8,128)(2,1)}) custom-call(bf16[5,208,768]{2,1,0:T(8,128)(2,1)} %get-tuple-element.1284.x_ref, ...), custom_call_target="tpu_custom_call", output_to_operand_aliasing={{0}: (3, {}), {1}: (4, {}), {2}: (5, {}), {3}: (6, {})} | custom-call | flops 1000 | bytes 1000 | tf_op jit(solution)/shard_map/attend/pallas_call | solution.py:286
  83.2 4.3 collective-permute-done.9.there_ref
  87.5 18.6 %collective-permute-done.13.refs_9_ = bf16[1536,128]{1,0:T(8,128)(2,1)S(1)} collective-permute-done((bf16[1536,128]{1,0:T(8,128)(2,1)S(1)}, bf16[1536,128]{1,0:T(8,128)(2,1)S(1)}, u32[]{:S(2)}, u32[]{:S(2)}) %collective-permute-start.13) | collective-permute-done | bytes 393248 | tf_op jit(solution)/shard_map/ppermute | solution.py:41
  106.1 8.5 %collective-permute-done.11.got_ref = bf16[2,208,384]{2,1,0:T(8,128)(2,1)S(1)} collective-permute-done((bf16[2,208,384]{2,1,0:T(8,128)(2,1)}, bf16[2,208,384]{2,1,0:T(8,128)(2,1)S(1)}, u32[]{:S(2)}, u32[]{:S(2)}) %collective-permute-start.11) | collective-permute-done | bytes 319520 | tf_op jit(solution)/shard_map/ppermute | solution.py:41
  116.4 6.7 %route.2 = (f32[5,208,768]{2,1,0:T(8,128)}, f32[5,208,128]{2,1,0:T(8,128)}, f32[5,208,128]{2,1,0:T(8,128)}, bf16[3,208,768]{2,1,0:T(8,128)(2,1)}) custom-call(s32[1]{0:T(128)} %bitcast.12.which_ref, bf16[5,208,768]{2,1,0:T(8,128)(2,1)} %get-tuple-element.1284.x_ref, bf16[3,208,384]{2,1,0:T(8,128)(2,1)} %get-tuple-element.753.own_ref, ...), custom_call_target="tpu_custom_call" | custom-call | flops 1000 | bytes 1000 | tf_op jit(solution)/shard_map/route/pallas_call | solution.py:331
  123.2 5.3 route.3
  129.7 4.9 collective-permute-done.14.refs_10_
  137.8 6.9 %send_rows.2 = (bf16[2,312,768]{2,1,0:T(8,128)(2,1)}, bf16[2,312,768]{2,1,0:T(8,128)(2,1)}, bf16[2,312,768]{2,1,0:T(8,128)(2,1)}) custom-call(s32[2,624]{1,0:T(2,128)} %slice.91.refs_0_, s32[2,416]{1,0:T(2,128)} %slice.92.refs_1_, bf16[624,768]{1,0:T(8,128)(2,1)} %bitcast.59, bf16[416,768]{1,0:T(8,128)(2,1)} %bitcast.62, s32[2,624]{1,0:T(2,128)} %slice.93.refs_4_, ...), custom_call_target="tpu_custom_call" | custom-call | flops 1000 | bytes 1000 | tf_op jit(solution)/shard_map/send_rows/pallas_call | solution.py:389
  144.7 10.4 %collective-permute-done.17.refs_11_ = bf16[1536,128]{1,0:T(8,128)(2,1)S(1)} collective-permute-done((bf16[1536,128]{1,0:T(8,128)(2,1)S(1)}, bf16[1536,128]{1,0:T(8,128)(2,1)S(1)}, u32[]{:S(2)}, u32[]{:S(2)}) %collective-permute-start.17) | collective-permute-done | bytes 393248 | tf_op jit(solution)/shard_map/ppermute | solution.py:41
  155.1 2.4 collective-permute-start.21
  158.6 4.4 send_rows.3.m_ref.refs_4_
  163.6 7.4 %send_gated.2 = (bf16[2,312,768]{2,1,0:T(8,128)(2,1)}, bf16[2,312,768]{2,1,0:T(8,128)(2,1)}, bf16[2,312,768]{2,1,0:T(8,128)(2,1)}) custom-call(s32[2,1040]{1,0:T(2,128)} %copy-done.47, bf16[1040,768]{1,0:T(8,128)(2,1)} %bitcast.55, f32[2,1040]{1,0:T(2,128)} %bitcast.68, s32[2,1040]{1,0:T(2,128)} %copy-done.48, ...), custom_call_target="tpu_custom_call" | custom-call | flops 1000 | bytes 1000 | tf_op jit(solution)/shard_map/send_gated/pallas_call | solution.py:389
  171.0 4.7 send_gated.3.z_ref.refs_4_
  175.7 21.9 %expert_forward.4 = (bf16[2,312,1536]{2,1,0:T(8,128)(2,1)}, bf16[2,312,1536]{2,1,0:T(8,128)(2,1)}, bf16[2,312,384]{2,1,0:T(8,128)(2,1)}, f32[2,312,384]{2,1,0:T(8,128)}) custom-call(s32[1]{0:T(128)} %bitcast.19.same_ref.which_ref, bf16[2,312,768]{2,1,0:T(8,128)(2,1)} %send_rows.3.m_ref.refs_4_, bf16[112,1536]{1,0:T(8,128)(2,1)} %copy-done.5, ...), custom_call_target="tpu_custom_call" | custom-call | flops 1000 | bytes 1000 | tf_op jit(solution)/shard_map/expert_forward/pallas_call | solution.py:542
  203.7 13.3 %expert_forward.5 = (bf16[2,312,1536]{2,1,0:T(8,128)(2,1)}, bf16[2,312,1536]{2,1,0:T(8,128)(2,1)}, bf16[2,312,384]{2,1,0:T(8,128)(2,1)}, f32[2,312,384]{2,1,0:T(8,128)}) custom-call(s32[1]{0:T(128)} %bitcast.19.same_ref.which_ref, bf16[2,312,768]{2,1,0:T(8,128)(2,1)} %collective-permute-done.19.m_ref.refs_5_, bf16[112,1536]{1,0:T(8,128)(2,1)} %copy-done.5, ...), custom_call_target="tpu_custom_call" | custom-call | flops 1000 | bytes 1000 | tf_op jit(solution)/shard_map/expert_forward/pallas_call | solution.py:542
  219.1 13.3 %expert_forward.6 = (bf16[2,312,1536]{2,1,0:T(8,128)(2,1)}, bf16[2,312,1536]{2,1,0:T(8,128)(2,1)}, bf16[2,312,384]{2,1,0:T(8,128)(2,1)}, f32[2,312,384]{2,1,0:T(8,128)}) custom-call(s32[1]{0:T(128)} %bitcast.19.same_ref.which_ref, bf16[2,312,768]{2,1,0:T(8,128)(2,1)} %copy-done.15, bf16[112,1536]{1,0:T(8,128)(2,1)} %copy-done.5, ...), custom_call_target="tpu_custom_call" | custom-call | flops 1000 | bytes 1000 | tf_op jit(solution)/shard_map/expert_forward/pallas_call | solution.py:542
  234.5 10.4 %collective-permute-done.24.z_ref.refs_6_ = bf16[2,312,768]{2,1,0:T(8,128)(2,1)S(1)} collective-permute-done((bf16[2,312,768]{2,1,0:T(8,128)(2,1)}, bf16[2,312,768]{2,1,0:T(8,128)(2,1)S(1)}, u32[]{:S(2)}, u32[]{:S(2)}) %collective-permute-start.24) | collective-permute-done | bytes 958496 | tf_op jit(solution)/shard_map/ppermute | solution.py:41
  244.9 13.9 %expert_forward.7 = (bf16[2,312,1536]{2,1,0:T(8,128)(2,1)}, bf16[2,312,1536]{2,1,0:T(8,128)(2,1)}, bf16[2,312,384]{2,1,0:T(8,128)(2,1)}, f32[2,312,384]{2,1,0:T(8,128)}) custom-call(s32[1]{0:T(128)} %bitcast.19.same_ref.which_ref, bf16[2,312,768]{2,1,0:T(8,128)(2,1)} %copy-done.14, bf16[112,1536]{1,0:T(8,128)(2,1)} %copy-done.5, ...), custom_call_target="tpu_custom_call" | custom-call | flops 1000 | bytes 1000 | tf_op jit(solution)/shard_map/expert_forward/pallas_call | solution.py:542
  261.8 9.9 %expert_backward.4 = (bf16[2,312,1536]{2,1,0:T(8,128)(2,1)}, bf16[2,312,384]{2,1,0:T(8,128)(2,1)}, f32[2,312,384]{2,1,0:T(8,128)}) custom-call(s32[1]{0:T(128)} %bitcast.19.same_ref.which_ref, bf16[2,312,768]{2,1,0:T(8,128)(2,1)} %send_gated.3.z_ref.refs_4_, bf16[2,312,1536]{2,1,0:T(8,128)(2,1)} %get-tuple-element.953.s_ref, bf16[112,1536]{1,0:T(8,128)(2,1)} %copy-done.5, ...), custom_call_target="tpu_custom_call" | custom-call | flops 1000 | bytes 1000 | tf_op jit(solution)/shard_map/expert_backward/pallas_call | solution.py:589
  277.4 9.7 %expert_backward.5 = (bf16[2,312,1536]{2,1,0:T(8,128)(2,1)}, bf16[2,312,384]{2,1,0:T(8,128)(2,1)}, f32[2,312,384]{2,1,0:T(8,128)}) custom-call(s32[1]{0:T(128)} %bitcast.19.same_ref.which_ref, bf16[2,312,768]{2,1,0:T(8,128)(2,1)} %copy-done.13, bf16[2,312,1536]{2,1,0:T(8,128)(2,1)} %get-tuple-element.979.s_ref, bf16[112,1536]{1,0:T(8,128)(2,1)} %copy-done.5, ...), custom_call_target="tpu_custom_call" | custom-call | flops 1000 | bytes 1000 | tf_op jit(solution)/shard_map/expert_backward/pallas_call | solution.py:589
  290.4 9.7 %expert_backward.6 = (bf16[2,312,1536]{2,1,0:T(8,128)(2,1)}, bf16[2,312,384]{2,1,0:T(8,128)(2,1)}, f32[2,312,384]{2,1,0:T(8,128)}) custom-call(s32[1]{0:T(128)} %bitcast.19.same_ref.which_ref, bf16[2,312,768]{2,1,0:T(8,128)(2,1)} %copy-done.12, bf16[2,312,1536]{2,1,0:T(8,128)(2,1)} %get-tuple-element.1005.s_ref, bf16[112,1536]{1,0:T(8,128)(2,1)} %copy-done.5, ...), custom_call_target="tpu_custom_call" | custom-call | flops 1000 | bytes 1000 | tf_op jit(solution)/shard_map/expert_backward/pallas_call | solution.py:589
  305.8 9.7 %expert_backward.7 = (bf16[2,312,1536]{2,1,0:T(8,128)(2,1)}, bf16[2,312,384]{2,1,0:T(8,128)(2,1)}, f32[2,312,384]{2,1,0:T(8,128)}) custom-call(s32[1]{0:T(128)} %bitcast.19.same_ref.which_ref, bf16[2,312,768]{2,1,0:T(8,128)(2,1)} %copy-done.11, bf16[2,312,1536]{2,1,0:T(8,128)(2,1)} %get-tuple-element.1033.s_ref, bf16[112,1536]{1,0:T(8,128)(2,1)} %copy-done.5, ...), custom_call_target="tpu_custom_call" | custom-call | flops 1000 | bytes 1000 | tf_op jit(solution)/shard_map/expert_backward/pallas_call | solution.py:589
  320.1 2.9 sort_groups.2
  325.8 9.6 %outer_send.2 = bf16[1536,384]{1,0:T(8,128)(2,1)} custom-call(s32[1]{0:T(128)} %bitcast.19.same_ref.which_ref, bf16[2,312,1536]{2,1,0:T(8,128)(2,1)} %get-tuple-element.1238.refs_0_, bf16[2,312,1536]{2,1,0:T(8,128)(2,1)} %get-tuple-element.1239.refs_1_, bf16[2,312,1536]{2,1,0:T(8,128)(2,1)} %get-tuple-element.1240.refs_2_, ...), custom_call_target="tpu_custom_call" | custom-call | flops 1000 | bytes 1000 | tf_op jit(solution)/shard_map/outer_send/pallas_call | solution.py:639
  347.9 8.8 %outer_send.3 = bf16[384,1536]{1,0:T(8,128)(2,1)} custom-call(s32[1]{0:T(128)} %bitcast.19.same_ref.which_ref, bf16[2,312,1536]{2,1,0:T(8,128)(2,1)} %get-tuple-element.1254.refs_0_, bf16[2,312,1536]{2,1,0:T(8,128)(2,1)} %get-tuple-element.1255.refs_1_, bf16[2,312,1536]{2,1,0:T(8,128)(2,1)} %get-tuple-element.1256.refs_2_, ...), custom_call_target="tpu_custom_call" | custom-call | flops 1000 | bytes 1000 | tf_op jit(solution)/shard_map/outer_send/pallas_call | solution.py:639
  356.7 5.2 collective-permute-done.38.refs_3_
  362.7 2.9 sort_groups.3
  368.4 15.3 %bring_home.1 = (bf16[5,208,384]{2,1,0:T(8,128)(2,1)}, f32[5,8,208]{2,1,0:T(8,128)}) custom-call(s32[1]{0:T(128)} %bitcast.12.which_ref, s32[5,208,2]{2,1,0:T(8,128)} %get-tuple-element.1145.rows_ref, f32[5,208,768]{2,1,0:T(8,128)} %get-tuple-element.1188.middle_ref.y_ref, bf16[5,208,768]{2,1,0:T(8,128)(2,1)} %get-tuple-element.1196.grad_ref.cot_ref, ...), custom_call_target="tpu_custom_call" | custom-call | flops 1000 | bytes 1000 | tf_op jit(solution)/shard_map/bring_home/pallas_call | solution.py:441
  384.7 7.9 %sum_home.1.near_ref = bf16[5,208,384]{2,1,0:T(8,128)(2,1)} custom-call(s32[5,208,2]{2,1,0:T(8,128)} %get-tuple-element.1145.rows_ref, bf16[4,312,384]{2,1,0:T(8,128)(2,1)} %get-tuple-element.1146.own_ref, bf16[4,312,384]{2,1,0:T(8,128)(2,1)} %copy-done.21), custom_call_target="tpu_custom_call" | custom-call | flops 1000 | bytes 1000 | tf_op jit(solution)/shard_map/sum_home/pallas_call | solution.py:468
  394.6 26.9 %collective-permute-done.43.dgate2_ref = f32[5,8,208]{2,1,0:T(8,128)S(1)} collective-permute-done((f32[5,8,208]{2,1,0:T(8,128)S(1)}, f32[5,8,208]{2,1,0:T(8,128)S(1)}, u32[]{:S(2)}, u32[]{:S(2)}) %collective-permute-start.43) | collective-permute-done | bytes 33312 | tf_op jit(solution)/shard_map/ppermute | solution.py:41
  423.0 19.8 %attend_back.2 = (f32[5,208,768]{2,1,0:T(8,128)}, bf16[5,208,768]{2,1,0:T(8,128)(2,1)}, bf16[5,208,1152]{2,1,0:T(8,128)(2,1)}, bf16[3,208,768]{2,1,0:T(8,128)(2,...) custom-call(s32[1]{0:T(128)} %bitcast.12.which_ref, bf16[5,208,768]{2,1,0:T(8,128)(2,1)} %get-tuple-element.1284.x_ref, ...), custom_call_target="tpu_custom_call" | custom-call | flops 1000 | bytes 1000 | tf_op jit(solution)/shard_map/attend_back/pallas_call | solution.py:754
  444.5 14.8 %attend_back.3 = (f32[5,208,768]{2,1,0:T(8,128)}, bf16[5,208,768]{2,1,0:T(8,128)(2,1)}, bf16[5,208,1152]{2,1,0:T(8,128)(2,1)}, bf16[2,208,768]{2,1,0:T(8,128)(2,...) custom-call(s32[1]{0:T(128)} %bitcast.12.which_ref, ...), custom_call_target="tpu_custom_call", output_to_operand_aliasing={{0}: (16, {}), {1}: (17, {}), {2}: (18, {})} | custom-call | flops 1000 | bytes 1000 | tf_op jit(solution)/shard_map/attend_back/pallas_call | solution.py:754
  459.3 11.1 %projection_grads.1 = (f32[2,4,48,1664]{3,2,1,0:T(8,128)}, bf16[2,4,48,1664]{3,2,1,0:T(8,128)(2,1)}) custom-call(s32[1]{0:T(128)} %bitcast.20.core_ref, bf16[5,208,768]{2,1,0:T(8,128)(2,1)} %get-tuple-element.1223.refs_0_, bf16[5,208,1152]{2,1,0:T(8,128)(2,1)} %get-tuple-element.1224.refs_1_, bf16[5,208,768]{2,1,0:T(8,128)(2,1)} %get-tuple-element.1225.refs_2_, ...), custom_call_target="tpu_custom_call" | custom-call | flops 1000 | bytes 1000 | tf_op jit(solution)/shard_map/projection_grads/pallas_call | solution.py:958
  470.4 10.3 %outer_keep.2 = f32[1536,384]{1,0:T(8,128)} custom-call(s32[1]{0:T(128)S(6)} %sub.6.which_ref, bf16[2,312,1536]{2,1,0:T(8,128)(2,1)} %get-tuple-element.1238.refs_0_, bf16[2,312,1536]{2,1,0:T(8,128)(2,1)} %get-tuple-element.1239.refs_1_, bf16[2,312,1536]{2,1,0:T(8,128)(2,1)} %get-tuple-element.1240.refs_2_, ...), custom_call_target="tpu_custom_call" | custom-call | flops 1000 | bytes 1000 | tf_op jit(solution)/shard_map/outer_keep/pallas_call | solution.py:639
  480.7 10.9 %collective-permute-done.46.got_ref = bf16[3,208,768]{2,1,0:T(8,128)(2,1)} collective-permute-done((bf16[3,208,768]{2,1,0:T(8,128)(2,1)}, bf16[3,208,768]{2,1,0:T(8,128)(2,1)}, u32[]{:S(2)}, u32[]{:S(2)}) %collective-permute-start.46) | collective-permute-done | bytes 958496 | tf_op jit(solution)/shard_map/ppermute | solution.py:41
  491.5 9.4 %outer_keep.3 = f32[384,1536]{1,0:T(8,128)} custom-call(s32[1]{0:T(128)S(6)} %sub.6.which_ref, bf16[2,312,1536]{2,1,0:T(8,128)(2,1)} %get-tuple-element.1254.refs_0_, bf16[2,312,1536]{2,1,0:T(8,128)(2,1)} %get-tuple-element.1255.refs_1_, bf16[2,312,1536]{2,1,0:T(8,128)(2,1)} %get-tuple-element.1256.refs_2_, ...), custom_call_target="tpu_custom_call" | custom-call | flops 1000 | bytes 1000 | tf_op jit(solution)/shard_map/outer_keep/pallas_call | solution.py:639
  508.4 6.4 %collective-permute-done.48 = bf16[2,48,1664]{2,1,0:T(8,128)(2,1)S(1)} collective-permute-done((bf16[2,48,1664]{2,1,0:T(8,128)(2,1)}, bf16[2,48,1664]{2,1,0:T(8,128)(2,1)S(1)}, u32[]{:S(2)}, u32[]{:S(2)}) %collective-permute-start.48) | collective-permute-done | bytes 319520 | tf_op jit(solution)/shard_map/ppermute | solution.py:41
  514.8 7.6 %collective-permute-done.49 = bf16[2,48,1664]{2,1,0:T(8,128)(2,1)S(1)} collective-permute-done((bf16[2,48,1664]{2,1,0:T(8,128)(2,1)}, bf16[2,48,1664]{2,1,0:T(8,128)(2,1)S(1)}, u32[]{:S(2)}, u32[]{:S(2)}) %collective-permute-start.49) | collective-permute-done | bytes 319520 | tf_op jit(solution)/shard_map/ppermute | solution.py:41
  527.1 5.1 token_back.2.refs_0_
  532.1 3.2 token_back.3
  539.5 5.6 %collective-permute-done.52 = bf16[48,1664]{1,0:T(8,128)(2,1)S(1)} collective-permute-done((bf16[48,1664]{1,0:T(8,128)(2,1)}, bf16[48,1664]{1,0:T(8,128)(2,1)S(1)}, u32[]{:S(2)}, u32[]{:S(2)}) %collective-permute-start.52) | collective-permute-done | bytes 159776 | tf_op jit(solution)/shard_map/ppermute | solution.py:41
  (252 shorter events, 126.5 us)
Async XLA Ops:
  6.4 12.1 %collective-permute-start = (bf16[48,1664]{1,0:T(8,128)(2,1)S(1)}, bf16[48,1664]{1,0:T(8,128)(2,1)S(1)}, u32[]{:S(2)}, u32[]{:S(2)}) collective-permute-start(bf16[48,1664]{1,0:T(8,128)(2,1)S(1)} %bitcast_dynamic-update-slice_fusion.own_ref), channel_id=1, source_target_pairs={{0,16},{16,0},{1,17},{17,1},{2,18},{18,2},{3,19},{19,3},{4,20},{20... | collective-permute-start | bytes 479240 | tf_op jit(solution)/shard_map/ppermute | solution.py:41
  20.9 25.4 %collective-permute-start.4 = (bf16[112,1536]{1,0:T(8,128)(2,1)S(1)}, bf16[112,1536]{1,0:T(8,128)(2,1)S(1)}, u32[]{:S(2)}, u32[]{:S(2)}) collective-permute-start(bf16[112,1536]{1,0:T(8,128)(2,1)S(1)} %fusion.7.refs_0_), channel_id=1, source_target_pairs={{0,16},{16,0},{1,17},{17,1},{2,18},{18,2},{3,19},{19,3},{4,20},{20... | collective-permute-start | bytes 1032200 | tf_op jit(solution)/shard_map/ppermute | solution.py:41
  21.0 22.1 %collective-permute-start.1 = (bf16[2,48,1664]{2,1,0:T(8,128)(2,1)}, bf16[2,48,1664]{2,1,0:T(8,128)(2,1)S(1)}, u32[]{:S(2)}, u32[]{:S(2)}) collective-permute-start(bf16[2,48,1664]{2,1,0:T(8,128)(2,1)} %cross.1.refs_0_), channel_id=1, source_target_pairs={{0,4},{2,6},{4,0},{6,2},{8,12},{10,14},{12,8},{14,10},{1,5},{3,7},... | collective-permute-start | bytes 958472 | tf_op jit(solution)/shard_map/ppermute | solution.py:41
  22.8 20.3 %collective-permute-start.2 = (bf16[2,48,1664]{2,1,0:T(8,128)(2,1)}, bf16[2,48,1664]{2,1,0:T(8,128)(2,1)S(1)}, u32[]{:S(2)}, u32[]{:S(2)}) collective-permute-start(bf16[2,48,1664]{2,1,0:T(8,128)(2,1)} %cross.1.refs_0_), channel_id=1, source_target_pairs={{0,8},{2,10},{4,12},{6,14},{8,0},{10,2},{12,4},{14,6},{1,9},{3,11}... | collective-permute-start | bytes 958472 | tf_op jit(solution)/shard_map/ppermute | solution.py:41
  24.3 18.8 %collective-permute-start.3 = (bf16[2,48,1664]{2,1,0:T(8,128)(2,1)}, bf16[2,48,1664]{2,1,0:T(8,128)(2,1)}, u32[]{:S(2)}, u32[]{:S(2)}) collective-permute-start(bf16[2,48,1664]{2,1,0:T(8,128)(2,1)} %cross.1.refs_0_), channel_id=1, source_target_pairs={{0,12},{2,14},{4,8},{6,10},{8,4},{10,6},{12,0},{14,2},{1,13},{3,15... | collective-permute-start | bytes 958472 | tf_op jit(solution)/shard_map/ppermute | solution.py:41
  46.3 18.3 %collective-permute-start.8 = (bf16[1040,768]{1,0:T(8,128)(2,1)}, bf16[1040,768]{1,0:T(8,128)(2,1)}, u32[]{:S(2)}, u32[]{:S(2)}) collective-permute-start(bf16[1040,768]{1,0:T(8,128)(2,1)} %bitcast.54), channel_id=1, source_target_pairs={{0,2},{2,0},{4,6},{6,4},{8,10},{10,8},{12,14},{14,12},{1,3},{3,1},... | collective-permute-start | bytes 4792328 | tf_op jit(solution)/shard_map/ppermute | solution.py:41
  46.8 12.4 %collective-permute-start.6 = (bf16[64,1536]{1,0:T(8,128)(2,1)S(1)}, bf16[64,1536]{1,0:T(8,128)(2,1)}, u32[]{:S(2)}, u32[]{:S(2)}) collective-permute-start(bf16[64,1536]{1,0:T(8,128)(2,1)S(1)} %fusion.11.refs_1_), channel_id=1, source_target_pairs={{0,16},{16,0},{1,17},{17,1},{2,18},{18,2},{3,19},{19,3},{4,20},{20... | collective-permute-start | bytes 589832 | tf_op jit(solution)/shard_map/ppermute | solution.py:41
  59.2 55.5 %collective-permute-start.12 = (bf16[208,1536]{1,0:T(8,128)(2,1)S(1)}, bf16[208,1536]{1,0:T(8,128)(2,1)S(1)}, u32[]{:S(2)}, u32[]{:S(2)}) collective-permute-start(bf16[208,1536]{1,0:T(8,128)(2,1)S(1)} %fusion.1.refs_2_), channel_id=1, source_target_pairs={{0,16},{16,0},{1,17},{17,1},{2,18},{18,2},{3,19},{19,3},{4,20},{20... | collective-permute-start | bytes 1916936 | tf_op jit(solution)/shard_map/ppermute | solution.py:41
  60.0 27.6 %collective-permute-start.9 = (bf16[768,384]{1,0:T(8,128)(2,1)}, bf16[768,384]{1,0:T(8,128)(2,1)}, u32[]{:S(2)}, u32[]{:S(2)}) collective-permute-start(bf16[768,384]{1,0:T(8,128)(2,1)} %get-tuple-element.1198.here_ref.out_w_ref), channel_id=1, source_target_pairs={{0,1},{1,0},{2,3},{3,2},{4,5},{5,4},{6,7},{7,6},{8,9},{9,8},{10,11... | collective-permute-start | bytes 1769480 | tf_op jit(solution)/shard_map/ppermute | solution.py:41
  74.1 40.6 %collective-permute-start.10 = (bf16[3,208,384]{2,1,0:T(8,128)(2,1)}, bf16[3,208,384]{2,1,0:T(8,128)(2,1)}, u32[]{:S(2)}, u32[]{:S(2)}) collective-permute-start(bf16[3,208,384]{2,1,0:T(8,128)(2,1)} %get-tuple-element.753.own_ref), channel_id=1, source_target_pairs={{0,1},{1,0},{2,3},{3,2},{4,5},{5,4},{6,7},{7,6},{8,9},{9,8},{10,11... | collective-permute-start | bytes 1437704 | tf_op jit(solution)/shard_map/ppermute | solution.py:41
  74.2 31.9 %collective-permute-start.13 = (bf16[1536,128]{1,0:T(8,128)(2,1)S(1)}, bf16[1536,128]{1,0:T(8,128)(2,1)S(1)}, u32[]{:S(2)}, u32[]{:S(2)}) collective-permute-start(bf16[1536,128]{1,0:T(8,128)(2,1)S(1)} %fusion.4.refs_6_), channel_id=1, source_target_pairs={{0,16},{16,0},{1,17},{17,1},{2,18},{18,2},{3,19},{19,3},{4,20},{20... | collective-permute-start | bytes 1179656 | tf_op jit(solution)/shard_map/ppermute | solution.py:41
  81.6 33.1 %collective-permute-start.11 = (bf16[2,208,384]{2,1,0:T(8,128)(2,1)}, bf16[2,208,384]{2,1,0:T(8,128)(2,1)S(1)}, u32[]{:S(2)}, u32[]{:S(2)}) collective-permute-start(bf16[2,208,384]{2,1,0:T(8,128)(2,1)} %get-tuple-element.770.own_ref), channel_id=1, source_target_pairs={{0,1},{1,0},{2,3},{3,2},{4,5},{5,4},{6,7},{7,6},{8,9},{9,8},{10,11... | collective-permute-start | bytes 958472 | tf_op jit(solution)/shard_map/ppermute | solution.py:41
  114.7 20.0 %collective-permute-start.14 = (bf16[1536,128]{1,0:T(8,128)(2,1)S(1)}, bf16[1536,128]{1,0:T(8,128)(2,1)S(1)}, u32[]{:S(2)}, u32[]{:S(2)}) collective-permute-start(bf16[1536,128]{1,0:T(8,128)(2,1)S(1)} %fusion.5.refs_7_), channel_id=1, source_target_pairs={{0,16},{16,0},{1,17},{17,1},{2,18},{18,2},{3,19},{19,3},{4,20},{20... | collective-permute-start | bytes 1179656 | tf_op jit(solution)/shard_map/ppermute | solution.py:41
  123.1 11.7 %collective-permute-start.15 = (bf16[624,768]{1,0:T(8,128)(2,1)}, bf16[624,768]{1,0:T(8,128)(2,1)S(1)}, u32[]{:S(2)}, u32[]{:S(2)}) collective-permute-start(bf16[624,768]{1,0:T(8,128)(2,1)} %bitcast.58), channel_id=1, source_target_pairs={{0,2},{2,0},{4,6},{6,4},{8,10},{10,8},{12,14},{14,12},{1,3},{3,1},... | collective-permute-start | bytes 2875400 | tf_op jit(solution)/shard_map/ppermute | solution.py:41
  134.7 20.4 %collective-permute-start.17 = (bf16[1536,128]{1,0:T(8,128)(2,1)S(1)}, bf16[1536,128]{1,0:T(8,128)(2,1)S(1)}, u32[]{:S(2)}, u32[]{:S(2)}) collective-permute-start(bf16[1536,128]{1,0:T(8,128)(2,1)S(1)} %fusion.6.refs_8_), channel_id=1, source_target_pairs={{0,16},{16,0},{1,17},{17,1},{2,18},{18,2},{3,19},{19,3},{4,20},{20... | collective-permute-start | bytes 1179656 | tf_op jit(solution)/shard_map/ppermute | solution.py:41
  155.1 42.5 %collective-permute-start.21 = (bf16[2,312,768]{2,1,0:T(8,128)(2,1)}, bf16[2,312,768]{2,1,0:T(8,128)(2,1)S(1)}, u32[]{:S(2)}, u32[]{:S(2)}) collective-permute-start(bf16[2,312,768]{2,1,0:T(8,128)(2,1)} %get-tuple-element.872), channel_id=1, source_target_pairs={{0,12},{2,14},{4,8},{6,10},{8,4},{10,6},{12,0},{14,2},{1,13},{3,15... | collective-permute-start | bytes 2875400 | tf_op jit(solution)/shard_map/ppermute | solution.py:41
  157.5 42.4 %collective-permute-start.20 = (bf16[2,312,768]{2,1,0:T(8,128)(2,1)}, bf16[2,312,768]{2,1,0:T(8,128)(2,1)S(1)}, u32[]{:S(2)}, u32[]{:S(2)}) collective-permute-start(bf16[2,312,768]{2,1,0:T(8,128)(2,1)} %get-tuple-element.870), channel_id=1, source_target_pairs={{0,8},{2,10},{4,12},{6,14},{8,0},{10,2},{12,4},{14,6},{1,9},{3,11}... | collective-permute-start | bytes 2875400 | tf_op jit(solution)/shard_map/ppermute | solution.py:41
  158.1 42.1 %collective-permute-start.19 = (bf16[2,312,768]{2,1,0:T(8,128)(2,1)}, bf16[2,312,768]{2,1,0:T(8,128)(2,1)}, u32[]{:S(2)}, u32[]{:S(2)}) collective-permute-start(bf16[2,312,768]{2,1,0:T(8,128)(2,1)} %get-tuple-element.868), channel_id=1, source_target_pairs={{0,4},{2,6},{4,0},{6,2},{8,12},{10,14},{12,8},{14,10},{1,5},{3,7},... | collective-permute-start | bytes 2875400 | tf_op jit(solution)/shard_map/ppermute | solution.py:41
  200.2 34.3 %collective-permute-start.25 = (bf16[2,312,768]{2,1,0:T(8,128)(2,1)}, bf16[2,312,768]{2,1,0:T(8,128)(2,1)S(1)}, u32[]{:S(2)}, u32[]{:S(2)}) collective-permute-start(bf16[2,312,768]{2,1,0:T(8,128)(2,1)} %get-tuple-element.923), channel_id=1, source_target_pairs={{0,12},{2,14},{4,8},{6,10},{8,4},{10,6},{12,0},{14,2},{1,13},{3,15... | collective-permute-start | bytes 2875400 | tf_op jit(solution)/shard_map/ppermute | solution.py:41
  201.8 43.2 %collective-permute-start.24 = (bf16[2,312,768]{2,1,0:T(8,128)(2,1)}, bf16[2,312,768]{2,1,0:T(8,128)(2,1)S(1)}, u32[]{:S(2)}, u32[]{:S(2)}) collective-permute-start(bf16[2,312,768]{2,1,0:T(8,128)(2,1)} %get-tuple-element.921), channel_id=1, source_target_pairs={{0,8},{2,10},{4,12},{6,14},{8,0},{10,2},{12,4},{14,6},{1,9},{3,11}... | collective-permute-start | bytes 2875400 | tf_op jit(solution)/shard_map/ppermute | solution.py:41
  203.1 41.8 %collective-permute-start.23 = (bf16[2,312,768]{2,1,0:T(8,128)(2,1)}, bf16[2,312,768]{2,1,0:T(8,128)(2,1)S(1)}, u32[]{:S(2)}, u32[]{:S(2)}) collective-permute-start(bf16[2,312,768]{2,1,0:T(8,128)(2,1)} %get-tuple-element.919), channel_id=1, source_target_pairs={{0,4},{2,6},{4,0},{6,2},{8,12},{10,14},{12,8},{14,10},{1,5},{3,7},... | collective-permute-start | bytes 2875400 | tf_op jit(solution)/shard_map/ppermute | solution.py:41
  203.7 28.7 %collective-permute-start.22 = (bf16[2,312,384]{2,1,0:T(8,128)(2,1)}, bf16[2,312,384]{2,1,0:T(8,128)(2,1)}, u32[]{:S(2)}, u32[]{:S(2)}) collective-permute-start(bf16[2,312,384]{2,1,0:T(8,128)(2,1)} %get-tuple-element.914), channel_id=1, source_target_pairs={{0,1},{1,0},{2,3},{3,2},{4,5},{5,4},{6,7},{7,6},{8,9},{9,8},{10,11... | collective-permute-start | bytes 1437704 | tf_op jit(solution)/shard_map/ppermute | solution.py:41
  217.0 41.9 %collective-permute-start.26 = (bf16[2,312,384]{2,1,0:T(8,128)(2,1)}, bf16[2,312,384]{2,1,0:T(8,128)(2,1)S(1)}, u32[]{:S(2)}, u32[]{:S(2)}) collective-permute-start(bf16[2,312,384]{2,1,0:T(8,128)(2,1)} %get-tuple-element.946), channel_id=1, source_target_pairs={{0,1},{1,0},{2,3},{3,2},{4,5},{5,4},{6,7},{7,6},{8,9},{9,8},{10,11... | collective-permute-start | bytes 1437704 | tf_op jit(solution)/shard_map/ppermute | solution.py:41
  234.5 37.3 %collective-permute-start.27 = (bf16[2,312,384]{2,1,0:T(8,128)(2,1)}, bf16[2,312,384]{2,1,0:T(8,128)(2,1)}, u32[]{:S(2)}, u32[]{:S(2)}) collective-permute-start(bf16[2,312,384]{2,1,0:T(8,128)(2,1)} %get-tuple-element.972), channel_id=1, source_target_pairs={{0,1},{1,0},{2,3},{3,2},{4,5},{5,4},{6,7},{7,6},{8,9},{9,8},{10,11... | collective-permute-start | bytes 1437704 | tf_op jit(solution)/shard_map/ppermute | solution.py:41
  261.8 25.3 %collective-permute-start.28 = (bf16[2,312,384]{2,1,0:T(8,128)(2,1)S(1)}, bf16[2,312,384]{2,1,0:T(8,128)(2,1)S(1)}, u32[]{:S(2)}, u32[]{:S(2)}) collective-permute-start(bf16[2,312,384]{2,1,0:T(8,128)(2,1)S(1)} %copy-done.52), channel_id=1, source_target_pairs={{0,1},{1,0},{2,3},{3,2},{4,5},{5,4},{6,7},{7,6},{8,9},{9,8},{10,11... | collective-permute-start | bytes 1437704 | tf_op jit(solution)/shard_map/ppermute | solution.py:41
  273.9 27.9 %collective-permute-start.29 = (bf16[2,312,384]{2,1,0:T(8,128)(2,1)}, bf16[2,312,384]{2,1,0:T(8,128)(2,1)}, u32[]{:S(2)}, u32[]{:S(2)}) collective-permute-start(bf16[2,312,384]{2,1,0:T(8,128)(2,1)} %get-tuple-element.1024), channel_id=1, source_target_pairs={{0,1},{1,0},{2,3},{3,2},{4,5},{5,4},{6,7},{7,6},{8,9},{9,8},{10,11... | collective-permute-start | bytes 1437704 | tf_op jit(solution)/shard_map/ppermute | solution.py:41
  275.9 28.0 %collective-permute-start.30 = (bf16[2,312,384]{2,1,0:T(8,128)(2,1)S(1)}, bf16[2,312,384]{2,1,0:T(8,128)(2,1)S(1)}, u32[]{:S(2)}, u32[]{:S(2)}) collective-permute-start(bf16[2,312,384]{2,1,0:T(8,128)(2,1)S(1)} %copy-done.28), channel_id=1, source_target_pairs={{0,4},{2,6},{4,0},{6,2},{8,12},{10,14},{12,8},{14,10},{1,5},{3,7},... | collective-permute-start | bytes 1437704 | tf_op jit(solution)/shard_map/ppermute | solution.py:41
  289.9 25.7 %collective-permute-start.31 = (bf16[2,312,384]{2,1,0:T(8,128)(2,1)}, bf16[2,312,384]{2,1,0:T(8,128)(2,1)S(1)}, u32[]{:S(2)}, u32[]{:S(2)}) collective-permute-start(bf16[2,312,384]{2,1,0:T(8,128)(2,1)} %get-tuple-element.1052), channel_id=1, source_target_pairs={{0,1},{1,0},{2,3},{3,2},{4,5},{5,4},{6,7},{7,6},{8,9},{9,8},{10,11... | collective-permute-start | bytes 1437704 | tf_op jit(solution)/shard_map/ppermute | solution.py:41
  290.0 28.6 %collective-permute-start.32 = (bf16[2,312,384]{2,1,0:T(8,128)(2,1)S(1)}, bf16[2,312,384]{2,1,0:T(8,128)(2,1)S(1)}, u32[]{:S(2)}, u32[]{:S(2)}) collective-permute-start(bf16[2,312,384]{2,1,0:T(8,128)(2,1)S(1)} %copy-done.25), channel_id=1, source_target_pairs={{0,8},{2,10},{4,12},{6,14},{8,0},{10,2},{12,4},{14,6},{1,9},{3,11}... | collective-permute-start | bytes 1437704 | tf_op jit(solution)/shard_map/ppermute | solution.py:41
  300.1 18.5 %collective-permute-start.33 = (bf16[2,312,384]{2,1,0:T(8,128)(2,1)S(1)}, bf16[2,312,384]{2,1,0:T(8,128)(2,1)S(1)}, u32[]{:S(2)}, u32[]{:S(2)}) collective-permute-start(bf16[2,312,384]{2,1,0:T(8,128)(2,1)S(1)} %copy-done.26), channel_id=1, source_target_pairs={{0,12},{2,14},{4,8},{6,10},{8,4},{10,6},{12,0},{14,2},{1,13},{3,15... | collective-permute-start | bytes 1437704 | tf_op jit(solution)/shard_map/ppermute | solution.py:41
  303.8 19.1 %collective-permute-start.34 = (bf16[2,312,384]{2,1,0:T(8,128)(2,1)}, bf16[2,312,384]{2,1,0:T(8,128)(2,1)S(1)}, u32[]{:S(2)}, u32[]{:S(2)}) collective-permute-start(bf16[2,312,384]{2,1,0:T(8,128)(2,1)} %get-tuple-element.1072), channel_id=1, source_target_pairs={{0,1},{1,0},{2,3},{3,2},{4,5},{5,4},{6,7},{7,6},{8,9},{9,8},{10,11... | collective-permute-start | bytes 1437704 | tf_op jit(solution)/shard_map/ppermute | solution.py:41
  318.5 22.9 %collective-permute-start.35 = (bf16[2,312,384]{2,1,0:T(8,128)(2,1)}, bf16[2,312,384]{2,1,0:T(8,128)(2,1)S(1)}, u32[]{:S(2)}, u32[]{:S(2)}) collective-permute-start(bf16[2,312,384]{2,1,0:T(8,128)(2,1)} %get-tuple-element.1093), channel_id=1, source_target_pairs={{0,1},{1,0},{2,3},{3,2},{4,5},{5,4},{6,7},{7,6},{8,9},{9,8},{10,11... | collective-permute-start | bytes 1437704 | tf_op jit(solution)/shard_map/ppermute | solution.py:41
  339.4 17.2 %collective-permute-start.37 = (bf16[2,312,384]{2,1,0:T(8,128)(2,1)S(1)}, bf16[2,312,384]{2,1,0:T(8,128)(2,1)S(1)}, u32[]{:S(2)}, u32[]{:S(2)}) collective-permute-start(bf16[2,312,384]{2,1,0:T(8,128)(2,1)S(1)} %copy-done.37), channel_id=1, source_target_pairs={{0,8},{2,10},{4,12},{6,14},{8,0},{10,2},{12,4},{14,6},{1,9},{3,11}... | collective-permute-start | bytes 1437704 | tf_op jit(solution)/shard_map/ppermute | solution.py:41
  340.8 15.8 %collective-permute-start.36 = (bf16[2,312,384]{2,1,0:T(8,128)(2,1)S(1)}, bf16[2,312,384]{2,1,0:T(8,128)(2,1)S(1)}, u32[]{:S(2)}, u32[]{:S(2)}) collective-permute-start(bf16[2,312,384]{2,1,0:T(8,128)(2,1)S(1)} %copy-done.29), channel_id=1, source_target_pairs={{0,4},{2,6},{4,0},{6,2},{8,12},{10,14},{12,8},{14,10},{1,5},{3,7},... | collective-permute-start | bytes 1437704 | tf_op jit(solution)/shard_map/ppermute | solution.py:41
  344.2 17.7 %collective-permute-start.38 = (bf16[2,312,384]{2,1,0:T(8,128)(2,1)}, bf16[2,312,384]{2,1,0:T(8,128)(2,1)S(1)}, u32[]{:S(2)}, u32[]{:S(2)}) collective-permute-start(bf16[2,312,384]{2,1,0:T(8,128)(2,1)} %add_halves.15), channel_id=1, source_target_pairs={{0,12},{2,14},{4,8},{6,10},{8,4},{10,6},{12,0},{14,2},{1,13},{3,15... | collective-permute-start | bytes 1437704 | tf_op jit(solution)/shard_map/ppermute | solution.py:41
  345.8 19.8 %collective-permute-start.39 = (bf16[512,384]{1,0:T(8,128)(2,1)}, bf16[512,384]{1,0:T(8,128)(2,1)}, u32[]{:S(2)}, u32[]{:S(2)}) collective-permute-start(bf16[512,384]{1,0:T(8,128)(2,1)} %slice.96), channel_id=1, source_target_pairs={{0,16},{16,0},{1,17},{17,1},{2,18},{18,2},{3,19},{19,3},{4,20},{20... | collective-permute-start | bytes 1179656 | tf_op jit(solution)/shard_map/ppermute | solution.py:41
  347.9 19.6 %collective-permute-start.40 = (bf16[4,312,384]{2,1,0:T(8,128)(2,1)}, bf16[4,312,384]{2,1,0:T(8,128)(2,1)S(1)}, u32[]{:S(2)}, u32[]{:S(2)}) collective-permute-start(bf16[4,312,384]{2,1,0:T(8,128)(2,1)} %get-tuple-element.1129), channel_id=1, source_target_pairs={{0,2},{2,0},{4,6},{6,4},{8,10},{10,8},{12,14},{14,12},{1,3},{3,1},... | collective-permute-start | bytes 2875400 | tf_op jit(solution)/shard_map/ppermute | solution.py:41
  365.6 18.2 %collective-permute-start.41 = (bf16[4,312,384]{2,1,0:T(8,128)(2,1)}, bf16[4,312,384]{2,1,0:T(8,128)(2,1)S(1)}, u32[]{:S(2)}, u32[]{:S(2)}) collective-permute-start(bf16[4,312,384]{2,1,0:T(8,128)(2,1)} %get-tuple-element.1141), channel_id=1, source_target_pairs={{0,2},{2,0},{4,6},{6,4},{8,10},{10,8},{12,14},{14,12},{1,3},{3,1},... | collective-permute-start | bytes 2875400 | tf_op jit(solution)/shard_map/ppermute | solution.py:41
  365.6 55.9 %collective-permute-start.42 = (bf16[1024,384]{1,0:T(8,128)(2,1)}, bf16[1024,384]{1,0:T(8,128)(2,1)}, u32[]{:S(2)}, u32[]{:S(2)}) collective-permute-start(bf16[1024,384]{1,0:T(8,128)(2,1)} %slice.97), channel_id=1, source_target_pairs={{0,16},{16,0},{1,17},{17,1},{2,18},{18,2},{3,19},{19,3},{4,20},{20... | collective-permute-start | bytes 2359304 | tf_op jit(solution)/shard_map/ppermute | solution.py:41
  392.6 29.0 %collective-permute-start.44 = (bf16[5,208,384]{2,1,0:T(8,128)(2,1)}, bf16[5,208,384]{2,1,0:T(8,128)(2,1)S(1)}, u32[]{:S(2)}, u32[]{:S(2)}) collective-permute-start(bf16[5,208,384]{2,1,0:T(8,128)(2,1)} %sum_home.1.near_ref), channel_id=1, source_target_pairs={{0,1},{1,0},{2,3},{3,2},{4,5},{5,4},{6,7},{7,6},{8,9},{9,8},{10,11... | collective-permute-start | bytes 2396168 | tf_op jit(solution)/shard_map/ppermute | solution.py:41
  393.0 28.5 %collective-permute-start.43 = (f32[5,8,208]{2,1,0:T(8,128)S(1)}, f32[5,8,208]{2,1,0:T(8,128)S(1)}, u32[]{:S(2)}, u32[]{:S(2)}) collective-permute-start(f32[5,8,208]{2,1,0:T(8,128)S(1)} %copy-done.44), channel_id=1, source_target_pairs={{0,1},{1,0},{2,3},{3,2},{4,5},{5,4},{6,7},{7,6},{8,9},{9,8},{10,11... | collective-permute-start | bytes 99848 | tf_op jit(solution)/shard_map/ppermute | solution.py:41
  421.5 59.1 %collective-permute-start.45 = (bf16[384,1536]{1,0:T(8,128)(2,1)S(1)}, bf16[384,1536]{1,0:T(8,128)(2,1)S(1)}, u32[]{:S(2)}, u32[]{:S(2)}) collective-permute-start(bf16[384,1536]{1,0:T(8,128)(2,1)S(1)} %copy-done.19), channel_id=1, source_target_pairs={{0,16},{16,0},{1,17},{17,1},{2,18},{18,2},{3,19},{19,3},{4,20},{20... | collective-permute-start | bytes 3538952 | tf_op jit(solution)/shard_map/ppermute | solution.py:41
  442.8 48.7 %collective-permute-start.46 = (bf16[3,208,768]{2,1,0:T(8,128)(2,1)}, bf16[3,208,768]{2,1,0:T(8,128)(2,1)}, u32[]{:S(2)}, u32[]{:S(2)}) collective-permute-start(bf16[3,208,768]{2,1,0:T(8,128)(2,1)} %get-tuple-element.1277.own_ref), channel_id=1, source_target_pairs={{0,1},{1,0},{2,3},{3,2},{4,5},{5,4},{6,7},{7,6},{8,9},{9,8},{10,11... | collective-permute-start | bytes 2875400 | tf_op jit(solution)/shard_map/ppermute | solution.py:41
  505.6 16.7 %collective-permute-start.49 = (bf16[2,48,1664]{2,1,0:T(8,128)(2,1)}, bf16[2,48,1664]{2,1,0:T(8,128)(2,1)S(1)}, u32[]{:S(2)}, u32[]{:S(2)}) collective-permute-start(bf16[2,48,1664]{2,1,0:T(8,128)(2,1)} %get-tuple-element.1343), channel_id=1, source_target_pairs={{0,8},{2,10},{4,12},{6,14},{8,0},{10,2},{12,4},{14,6},{1,9},{3,11}... | collective-permute-start | bytes 958472 | tf_op jit(solution)/shard_map/ppermute | solution.py:41
  506.9 15.5 %collective-permute-start.50 = (bf16[2,48,1664]{2,1,0:T(8,128)(2,1)}, bf16[2,48,1664]{2,1,0:T(8,128)(2,1)S(1)}, u32[]{:S(2)}, u32[]{:S(2)}) collective-permute-start(bf16[2,48,1664]{2,1,0:T(8,128)(2,1)} %fusion.10), channel_id=1, source_target_pairs={{0,12},{2,14},{4,8},{6,10},{8,4},{10,6},{12,0},{14,2},{1,13},{3,15... | collective-permute-start | bytes 958472 | tf_op jit(solution)/shard_map/ppermute | solution.py:41
  508.4 16.3 %collective-permute-start.51 = (bf16[2,208,768]{2,1,0:T(8,128)(2,1)}, bf16[2,208,768]{2,1,0:T(8,128)(2,1)}, u32[]{:S(2)}, u32[]{:S(2)}) collective-permute-start(bf16[2,208,768]{2,1,0:T(8,128)(2,1)} %get-tuple-element.1285.own_ref), channel_id=1, source_target_pairs={{0,1},{1,0},{2,3},{3,2},{4,5},{5,4},{6,7},{7,6},{8,9},{9,8},{10,11... | collective-permute-start | bytes 1916936 | tf_op jit(solution)/shard_map/ppermute | solution.py:41
  524.7 22.3 %collective-permute-start.53 = (bf16[5,208,384]{2,1,0:T(8,128)(2,1)}, bf16[5,208,384]{2,1,0:T(8,128)(2,1)}, u32[]{:S(2)}, u32[]{:S(2)}) collective-permute-start(bf16[5,208,384]{2,1,0:T(8,128)(2,1)} %get-tuple-element.1293), channel_id=1, source_target_pairs={{0,1},{1,0},{2,3},{3,2},{4,5},{5,4},{6,7},{7,6},{8,9},{9,8},{10,11... | collective-permute-start | bytes 2396168 | tf_op jit(solution)/shard_map/ppermute | solution.py:41
  525.0 20.1 %collective-permute-start.52 = (bf16[48,1664]{1,0:T(8,128)(2,1)}, bf16[48,1664]{1,0:T(8,128)(2,1)S(1)}, u32[]{:S(2)}, u32[]{:S(2)}) collective-permute-start(bf16[48,1664]{1,0:T(8,128)(2,1)} %fusion.12), channel_id=1, source_target_pairs={{0,16},{16,0},{1,17},{17,1},{2,18},{18,2},{3,19},{19,3},{4,20},{20... | collective-permute-start | bytes 479240 | tf_op jit(solution)/shard_map/ppermute | solution.py:41
  (60 other events, 808.0 us)

commit v6 on v5

--- a/solution.py
+++ b/solution.py
@@ -20,7 +20,7 @@
 F32 = jnp.float32
 LANES = 128
 TILE = 512
-IN_CUTS = ((0, 112), (112, 176), (176, 384))
+IN_CUTS = ((0, 176), (176, 240), (240, 384))
 BACK_CUTS = ((0, 128), (128, 256), (256, 384))
 TAIL_RATE = 0.305
 TAIL = (
@@ -614,6 +614,8 @@
             total = term if total is None else total + term
     if added == 1:
         total = total + refs[-2][...].astype(F32)
+    elif added == 2 and not hidden_first:
+        total = total + jnp.concatenate([refs[-3][...], refs[-2][...]], axis=0).astype(F32)
     elif added == 2:
         total = total + jnp.where(step == 0, refs[-3][...], refs[-2][...]).astype(F32)
     out_ref[...] = total.astype(out_ref.dtype)
@@ -632,6 +634,8 @@
     extra = [] if extra is None else list(extra)
     if len(extra) == 1:
         specs.append(out)
+    elif len(extra) == 2 and not hidden_first:
+        specs += [pl.BlockSpec((HALF // 2, TILE), lambda i, s: (0, i))] * 2
     elif len(extra) == 2:
         specs.append(pl.BlockSpec((TILE, HALF), lambda i, s: (0, 0)))
         specs.append(pl.BlockSpec((TILE, HALF), lambda i, s: (jnp.maximum(i - 1, 0), 0)))
@@ -1138,7 +1142,8 @@
     in_send = order.run(lambda g, a: outer(send_half, g, a, False), grads, arrived)
     grad_home = list(order.wait(tuple(grad_home)))
     m_here, m_there = order.run(lambda *v: sort_groups(v), *grad_home)
-    back_got[0] = order.wait(back_got[0])
+    back_got[0], in_send = order.wait((back_got[0], in_send))
+    in_send = order.wait([in_send[: HALF // 2], in_send[HALF // 2 :]])
     back_got.append(hop(order.after(back_send[1]), "dp", 1))
     m_there = hop(order.after(m_there), "expert", 1)
 
@@ -1150,7 +1155,7 @@
     near = order.run(lambda *v: sum_home(*v, 0, pictures), rows, m_here, m_there)
     away = hop(near, "tensor", 1)
     back_got, dgate_next = order.wait((back_got, dgate_next))
-    in_got = hop(order.after(in_send), "dp", 1)
+    in_got = [hop(order.after(in_send[0]), "dp", 1)]
     away = order.wait(away)
     held, parts, sums, got = [], [], [], []
     for n, (lo, hi) in enumerate(groups):
@@ -1159,6 +1164,10 @@
             x, y, near, away, dgate, dgate_next, probs, ids_pad, narrow_all, cot, vectors, out_here, qkv, lse, qkv_w, *held,
         )
         parts.append(part)
+        if n == 0:
+            in_got[0] = order.wait(in_got[0])
+            in_got.append(hop(order.after(in_send[1]), "dp", 1))
+            part = order.after(part)
         got.append(hop(part, "tensor", 1))
         sums.append((grad_router, sums1, sums2))
     dy, dyb, dqkv = held
@@ -1168,16 +1177,16 @@
         projection_grads, a_rows, dqkv, dyb, o_rows, *routers, *ones, *twos
     )
     keep_half = 1 - send_half
+    got[0], in_got[1] = order.wait((got[0], in_got[1]))
+    total_got = hop(order.after(total_away), "expert", 1)
     grad_back = order.run(
         lambda h, g, b: outer(keep_half, h, g, True, b), hidden, grad_arrived, back_got
     )[None]
-    in_got, got[0] = order.wait((in_got, got[0]))
-    total_got = hop(order.after(total_away), "expert", 1)
-    grad_in = order.run(
-        lambda g, a, b: outer(keep_half, g, a, False, [b]), grads, arrived, in_got
-    )[None]
     total_got = order.wait(total_got)
     shards, leaving = chip_sum(order.wait(total + total_got.astype(F32)), BF)
+    grad_in = order.run(
+        lambda g, a, b: outer(keep_half, g, a, False, b), grads, arrived, in_got
+    )[None]
     shards, leaving, got = order.wait((shards, leaving, got))
     entering = hop(leaving, "dp", 1)
     out_other = hop(order.after(out_half), "tensor", 1)

time: 563 us -> 551 us (0.979)
  waiting for transfers between devices: 132 us -> 118 us
    ppermute x55 -> x56, waiting for transfers between devices: 132 us -> 118 us  [hop(): return lax.ppermute(value, axis, [(i, i ^ offset) for i in range(count)])]
    ppermute x55 -> x56, starting transfers between devices: 54.3 us -> 55.9 us  [hop(): return lax.ppermute(value, axis, [(i, i ^ offset) for i in range(count)])]
    unnamed x109 -> x115, local copies, waits for them, and re-layouts: 14.5 us -> 13.7 us
  transfers between devices with their start and end apart: 55 -> 56, of which waited for: 19 -> 17; matrix products, arithmetic and copies ran while one was open for 5% -> 5% of each run, Pallas kernels for 57% -> 58%
where the time goes in v6:
time: 551 us; the launch traced here: 542 us
  Pallas kernels  316 us (57%)
  waiting for transfers between devices  118 us (21%)
  starting transfers between devices  55.9 us (10%)
  local copies, waits for them, and re-layouts  39.8 us (7%)
  other arithmetic  10.3 us (2%)
    ppermute x56, waiting for transfers between devices, hop(): return lax.ppermute(value, axis, [(i, i ^ offset) for i in range(count)])  118 us
    pallas_call x4, Pallas kernels, expert_forward(): pl.pallas_call(forward_kernel, grid_spec=pltpu.PrefetchScalarGridSpec(num...  62.4 us
    ppermute x56, starting transfers between devices, hop(): return lax.ppermute(value, axis, [(i, i ^ offset) for i in range(count)])  55.9 us
    pallas_call x4, Pallas kernels, expert_backward(): pl.pallas_call(backward_kernel, grid_spec=pltpu.PrefetchScalarGridSpec(nu...  39 us
    pallas_call x4, Pallas kernels, outer(): pl.pallas_call(functools.partial(outer_kernel, chunks=len(wides), hidden_...  38.4 us
    pallas_call x2, Pallas kernels, attend_back(): pl.pallas_call(attend_back_kernel, grid_spec=pltpu.PrefetchScalarGridSpec...  34.6 us
    pallas_call x4, Pallas kernels, send_rows(): pl.pallas_call(functools.partial(send_kernel, parts=len(own[0]), chips=ch...  23.3 us
    pallas_call x8, Pallas kernels, add_halves(): pl.pallas_call(add_kernel, grid=(near.shape[0],), in_specs=[part, part],...  16.8 us
  transfers between devices with their start and end apart: 56, of which 17 were waited for; matrix products, arithmetic and copies ran while one was open for 5% of the time, Pallas kernels for 58%

profile of v6, /device:TPU:0, one launch (start us, length us, event | category | flops | bytes accessed | tf_op | source)
XLA Modules:
  0.0 541.7 jit_solution(10114694407663125743)
XLA Ops:
  6.4 4.1 collective-permute-start
  24.4 6.9 %image_rows.1 = (bf16[5,208,768]{2,1,0:T(8,128)(2,1)}, bf16[5,208,768]{2,1,0:T(8,128)(2,1)}, bf16[5,208,768]{2,1,0:T(8,128)(2,1)}) custom-call(s32[1]{0:T(128)} %bitcast.12.which_ref, bf16[985,768]{1,0:T(8,128)(2,1)} %tok_ref, bf16[985,768]{1,0:T(8,128)(2,1)} %cot_ref), custom_call_target="tpu_custom_call" | custom-call | flops 1000 | bytes 1000 | tf_op jit(solution)/shard_map/image_rows/pallas_call | solution.py:853
  32.4 9.9 %slot_rows.1 = (s32[5,208,2]{2,1,0:T(8,128)}, s32[8,1040]{1,0:T(8,128)}, s32[5,208,2]{2,1,0:T(8,128)}) custom-call(s32[1]{0:T(128)} %bitcast.13.here_ref, s32[985,2]{1,0:T(8,128)} %copy.59.ids_ref), custom_call_target="tpu_custom_call" | custom-call | flops 1000 | bytes 1000 | tf_op jit(solution)/shard_map/slot_rows/pallas_call | solution.py:897
  43.9 2.4 stacked.1.same_ref
  49.7 3.1 collective-permute-done.5.flip_ref
  52.8 3.5 assemble.1
  56.2 2.8 collective-permute-start.9
  63.3 8.3 %attend.2 = (bf16[5,208,768]{2,1,0:T(8,128)(2,1)}, bf16[5,208,1152]{2,1,0:T(8,128)(2,1)}, bf16[5,208,384]{2,1,0:T(8,128)(2,1)}, f32[5,208,128]{2,1,0:T(8,128)}, bf16[3,208,384]{2,1,0:T(8,128)(2,1)}) custom-call(bf16[5,208,768]{2,1,0:T(8,128)(2,1)} %get-tuple-element.1302.x_ref, f32[8,768]{1,0:T(8,128)} %vectors.1.vec_ref, ...), custom_call_target="tpu_custom_call" | custom-call | flops 1000 | bytes 1000 | tf_op jit(solution)/shard_map/attend/pallas_call | solution.py:286
  74.8 6.6 %attend.3 = (bf16[5,208,768]{2,1,0:T(8,128)(2,1)}, bf16[5,208,1152]{2,1,0:T(8,128)(2,1)}, bf16[5,208,384]{2,1,0:T(8,128)(2,1)}, f32[5,208,128]{2,1,0:T(8,128)}, bf16[2,208,384]{2,1,0:T(8,128)(2,1)}) custom-call(bf16[5,208,768]{2,1,0:T(8,128)(2,1)} %get-tuple-element.1302.x_ref, ...), custom_call_target="tpu_custom_call", output_to_operand_aliasing={{0}: (3, {}), {1}: (4, {}), {2}: (5, {}), {3}: (6, {})} | custom-call | flops 1000 | bytes 1000 | tf_op jit(solution)/shard_map/attend/pallas_call | solution.py:286
  83.4 28.3 %collective-permute-done.13.refs_9_ = bf16[1536,128]{1,0:T(8,128)(2,1)S(1)} collective-permute-done((bf16[1536,128]{1,0:T(8,128)(2,1)S(1)}, bf16[1536,128]{1,0:T(8,128)(2,1)S(1)}, u32[]{:S(2)}, u32[]{:S(2)}) %collective-permute-start.13) | collective-permute-done | bytes 393248 | tf_op jit(solution)/shard_map/ppermute | solution.py:41
  111.8 6.9 %route.2 = (f32[5,208,768]{2,1,0:T(8,128)}, f32[5,208,128]{2,1,0:T(8,128)}, f32[5,208,128]{2,1,0:T(8,128)}, bf16[3,208,768]{2,1,0:T(8,128)(2,1)}) custom-call(s32[1]{0:T(128)} %bitcast.12.which_ref, bf16[5,208,768]{2,1,0:T(8,128)(2,1)} %get-tuple-element.1302.x_ref, bf16[3,208,384]{2,1,0:T(8,128)(2,1)} %get-tuple-element.762.own_ref, ...), custom_call_target="tpu_custom_call" | custom-call | flops 1000 | bytes 1000 | tf_op jit(solution)/shard_map/route/pallas_call | solution.py:331
  118.9 5.4 route.3
  125.5 5.3 collective-permute-done.14.refs_10_
  133.9 6.9 %send_rows.2 = (bf16[2,312,768]{2,1,0:T(8,128)(2,1)}, bf16[2,312,768]{2,1,0:T(8,128)(2,1)}, bf16[2,312,768]{2,1,0:T(8,128)(2,1)}) custom-call(s32[2,624]{1,0:T(2,128)} %slice.97.refs_0_, s32[2,416]{1,0:T(2,128)} %slice.98.refs_1_, bf16[624,768]{1,0:T(8,128)(2,1)} %bitcast.59, bf16[416,768]{1,0:T(8,128)(2,1)} %bitcast.62, s32[2,624]{1,0:T(2,128)} %slice.99.refs_4_, ...), custom_call_target="tpu_custom_call" | custom-call | flops 1000 | bytes 1000 | tf_op jit(solution)/shard_map/send_rows/pallas_call | solution.py:389
  140.8 10.4 %collective-permute-done.17.refs_11_ = bf16[1536,128]{1,0:T(8,128)(2,1)S(1)} collective-permute-done((bf16[1536,128]{1,0:T(8,128)(2,1)S(1)}, bf16[1536,128]{1,0:T(8,128)(2,1)S(1)}, u32[]{:S(2)}, u32[]{:S(2)}) %collective-permute-start.17) | collective-permute-done | bytes 393248 | tf_op jit(solution)/shard_map/ppermute | solution.py:41
  154.7 4.4 send_rows.3.m_ref.refs_4_
  159.6 7.4 %send_gated.2 = (bf16[2,312,768]{2,1,0:T(8,128)(2,1)}, bf16[2,312,768]{2,1,0:T(8,128)(2,1)}, bf16[2,312,768]{2,1,0:T(8,128)(2,1)}) custom-call(s32[2,1040]{1,0:T(2,128)} %copy-done.50, bf16[1040,768]{1,0:T(8,128)(2,1)} %bitcast.55, f32[2,1040]{1,0:T(2,128)} %bitcast.68, s32[2,1040]{1,0:T(2,128)} %copy-done.51, ...), custom_call_target="tpu_custom_call" | custom-call | flops 1000 | bytes 1000 | tf_op jit(solution)/shard_map/send_gated/pallas_call | solution.py:389
  167.0 4.7 send_gated.3.z_ref.refs_4_
  171.7 21.9 %expert_forward.4 = (bf16[2,312,1536]{2,1,0:T(8,128)(2,1)}, bf16[2,312,1536]{2,1,0:T(8,128)(2,1)}, bf16[2,312,384]{2,1,0:T(8,128)(2,1)}, f32[2,312,384]{2,1,0:T(8,128)}) custom-call(s32[1]{0:T(128)} %bitcast.19.same_ref.which_ref, bf16[2,312,768]{2,1,0:T(8,128)(2,1)} %send_rows.3.m_ref.refs_4_, bf16[176,1536]{1,0:T(8,128)(2,1)} %copy-done, ...), custom_call_target="tpu_custom_call" | custom-call | flops 1000 | bytes 1000 | tf_op jit(solution)/shard_map/expert_forward/pallas_call | solution.py:542
  193.6 2.7 collective-permute-done.20.m_ref.refs_6_
  199.9 13.3 %expert_forward.5 = (bf16[2,312,1536]{2,1,0:T(8,128)(2,1)}, bf16[2,312,1536]{2,1,0:T(8,128)(2,1)}, bf16[2,312,384]{2,1,0:T(8,128)(2,1)}, f32[2,312,384]{2,1,0:T(8,128)}) custom-call(s32[1]{0:T(128)} %bitcast.19.same_ref.which_ref, bf16[2,312,768]{2,1,0:T(8,128)(2,1)} %copy-done.15, bf16[176,1536]{1,0:T(8,128)(2,1)} %copy-done, bf16[64,1536]{1,0:T(8,128)(2,1)} %copy-done.10, ...), custom_call_target="tpu_custom_call" | custom-call | flops 1000 | bytes 1000 | tf_op jit(solution)/shard_map/expert_forward/pallas_call | solution.py:542
  215.3 13.3 %expert_forward.6 = (bf16[2,312,1536]{2,1,0:T(8,128)(2,1)}, bf16[2,312,1536]{2,1,0:T(8,128)(2,1)}, bf16[2,312,384]{2,1,0:T(8,128)(2,1)}, f32[2,312,384]{2,1,0:T(8,128)}) custom-call(s32[1]{0:T(128)} %bitcast.19.same_ref.which_ref, bf16[2,312,768]{2,1,0:T(8,128)(2,1)} %copy-done.16, bf16[176,1536]{1,0:T(8,128)(2,1)} %copy-done, bf16[64,1536]{1,0:T(8,128)(2,1)} %copy-done.10, ...), custom_call_target="tpu_custom_call" | custom-call | flops 1000 | bytes 1000 | tf_op jit(solution)/shard_map/expert_forward/pallas_call | solution.py:542
  230.8 9.7 %collective-permute-done.24.z_ref.refs_6_ = bf16[2,312,768]{2,1,0:T(8,128)(2,1)S(1)} collective-permute-done((bf16[2,312,768]{2,1,0:T(8,128)(2,1)}, bf16[2,312,768]{2,1,0:T(8,128)(2,1)S(1)}, u32[]{:S(2)}, u32[]{:S(2)}) %collective-permute-start.24) | collective-permute-done | bytes 958496 | tf_op jit(solution)/shard_map/ppermute | solution.py:41
  240.5 13.9 %expert_forward.7 = (bf16[2,312,1536]{2,1,0:T(8,128)(2,1)}, bf16[2,312,1536]{2,1,0:T(8,128)(2,1)}, bf16[2,312,384]{2,1,0:T(8,128)(2,1)}, f32[2,312,384]{2,1,0:T(8,128)}) custom-call(s32[1]{0:T(128)} %bitcast.19.same_ref.which_ref, bf16[2,312,768]{2,1,0:T(8,128)(2,1)} %collective-permute-done.21.m_ref.refs_7_, bf16[176,1536]{1,0:T(8,128)(2,1)} %copy-done, ...), custom_call_target="tpu_custom_call" | custom-call | flops 1000 | bytes 1000 | tf_op jit(solution)/shard_map/expert_forward/pallas_call | solution.py:542
  257.3 9.9 %expert_backward.4 = (bf16[2,312,1536]{2,1,0:T(8,128)(2,1)}, bf16[2,312,384]{2,1,0:T(8,128)(2,1)}, f32[2,312,384]{2,1,0:T(8,128)}) custom-call(s32[1]{0:T(128)} %bitcast.19.same_ref.which_ref, bf16[2,312,768]{2,1,0:T(8,128)(2,1)} %send_gated.3.z_ref.refs_4_, bf16[2,312,1536]{2,1,0:T(8,128)(2,1)} %get-tuple-element.962.s_ref, bf16[176,1536]{1,0:T(8,128)(2,1)} %copy-done, ...), custom_call_target="tpu_custom_call" | custom-call | flops 1000 | bytes 1000 | tf_op jit(solution)/shard_map/expert_backward/pallas_call | solution.py:589
  272.0 9.7 %expert_backward.5 = (bf16[2,312,1536]{2,1,0:T(8,128)(2,1)}, bf16[2,312,384]{2,1,0:T(8,128)(2,1)}, f32[2,312,384]{2,1,0:T(8,128)}) custom-call(s32[1]{0:T(128)} %bitcast.19.same_ref.which_ref, bf16[2,312,768]{2,1,0:T(8,128)(2,1)} %copy-done.12, bf16[2,312,1536]{2,1,0:T(8,128)(2,1)} %get-tuple-element.988.s_ref, bf16[176,1536]{1,0:T(8,128)(2,1)} %copy-done, ...), custom_call_target="tpu_custom_call" | custom-call | flops 1000 | bytes 1000 | tf_op jit(solution)/shard_map/expert_backward/pallas_call | solution.py:589
  285.5 9.7 %expert_backward.6 = (bf16[2,312,1536]{2,1,0:T(8,128)(2,1)}, bf16[2,312,384]{2,1,0:T(8,128)(2,1)}, f32[2,312,384]{2,1,0:T(8,128)}) custom-call(s32[1]{0:T(128)} %bitcast.19.same_ref.which_ref, bf16[2,312,768]{2,1,0:T(8,128)(2,1)} %copy-done.13, bf16[2,312,1536]{2,1,0:T(8,128)(2,1)} %get-tuple-element.1014.s_ref, bf16[176,1536]{1,0:T(8,128)(2,1)} %copy-done, ...), custom_call_target="tpu_custom_call" | custom-call | flops 1000 | bytes 1000 | tf_op jit(solution)/shard_map/expert_backward/pallas_call | solution.py:589
  301.4 9.7 %expert_backward.7 = (bf16[2,312,1536]{2,1,0:T(8,128)(2,1)}, bf16[2,312,384]{2,1,0:T(8,128)(2,1)}, f32[2,312,384]{2,1,0:T(8,128)}) custom-call(s32[1]{0:T(128)} %bitcast.19.same_ref.which_ref, bf16[2,312,768]{2,1,0:T(8,128)(2,1)} %copy-done.14, bf16[2,312,1536]{2,1,0:T(8,128)(2,1)} %get-tuple-element.1042.s_ref, bf16[176,1536]{1,0:T(8,128)(2,1)} %copy-done, ...), custom_call_target="tpu_custom_call" | custom-call | flops 1000 | bytes 1000 | tf_op jit(solution)/shard_map/expert_backward/pallas_call | solution.py:589
  315.7 2.8 sort_groups.2
  321.4 9.6 %outer_send.2 = bf16[1536,384]{1,0:T(8,128)(2,1)} custom-call(s32[1]{0:T(128)} %bitcast.19.same_ref.which_ref, bf16[2,312,1536]{2,1,0:T(8,128)(2,1)} %get-tuple-element.1258.refs_0_, bf16[2,312,1536]{2,1,0:T(8,128)(2,1)} %get-tuple-element.1259.refs_1_, bf16[2,312,1536]{2,1,0:T(8,128)(2,1)} %get-tuple-element.1260.refs_2_, ...), custom_call_target="tpu_custom_call" | custom-call | flops 1000 | bytes 1000 | tf_op jit(solution)/shard_map/outer_send/pallas_call | solution.py:643
  342.8 8.8 %outer_send.3 = bf16[384,1536]{1,0:T(8,128)(2,1)} custom-call(s32[1]{0:T(128)} %bitcast.19.same_ref.which_ref, bf16[2,312,1536]{2,1,0:T(8,128)(2,1)} %get-tuple-element.1277.refs_0_, bf16[2,312,1536]{2,1,0:T(8,128)(2,1)} %get-tuple-element.1278.refs_1_, bf16[2,312,1536]{2,1,0:T(8,128)(2,1)} %get-tuple-element.1279.refs_2_, ...), custom_call_target="tpu_custom_call" | custom-call | flops 1000 | bytes 1000 | tf_op jit(solution)/shard_map/outer_send/pallas_call | solution.py:643
  351.6 3.2 collective-permute-done.37.refs_2_
  354.8 2.9 sort_groups.3
  361.7 15.3 %bring_home.1 = (bf16[5,208,384]{2,1,0:T(8,128)(2,1)}, f32[5,8,208]{2,1,0:T(8,128)}) custom-call(s32[1]{0:T(128)} %bitcast.12.which_ref, s32[5,208,2]{2,1,0:T(8,128)} %get-tuple-element.1157.rows_ref, f32[5,208,768]{2,1,0:T(8,128)} %get-tuple-element.1203.middle_ref.y_ref, bf16[5,208,768]{2,1,0:T(8,128)(2,1)} %get-tuple-element.1211.grad_ref.cot_ref, ...), custom_call_target="tpu_custom_call" | custom-call | flops 1000 | bytes 1000 | tf_op jit(solution)/shard_map/bring_home/pallas_call | solution.py:441
  378.0 7.9 %sum_home.1.near_ref = bf16[5,208,384]{2,1,0:T(8,128)(2,1)} custom-call(s32[5,208,2]{2,1,0:T(8,128)} %get-tuple-element.1157.rows_ref, bf16[4,312,384]{2,1,0:T(8,128)(2,1)} %get-tuple-element.1158.own_ref, bf16[4,312,384]{2,1,0:T(8,128)(2,1)} %copy-done.22), custom_call_target="tpu_custom_call" | custom-call | flops 1000 | bytes 1000 | tf_op jit(solution)/shard_map/sum_home/pallas_call | solution.py:468
  387.9 26.8 %collective-permute-done.43.dgate2_ref = f32[5,8,208]{2,1,0:T(8,128)S(1)} collective-permute-done((f32[5,8,208]{2,1,0:T(8,128)S(1)}, f32[5,8,208]{2,1,0:T(8,128)S(1)}, u32[]{:S(2)}, u32[]{:S(2)}) %collective-permute-start.43) | collective-permute-done | bytes 33312 | tf_op jit(solution)/shard_map/ppermute | solution.py:41
  416.2 19.8 %attend_back.2 = (f32[5,208,768]{2,1,0:T(8,128)}, bf16[5,208,768]{2,1,0:T(8,128)(2,1)}, bf16[5,208,1152]{2,1,0:T(8,128)(2,1)}, bf16[3,208,768]{2,1,0:T(8,128)(2,...) custom-call(s32[1]{0:T(128)} %bitcast.12.which_ref, bf16[5,208,768]{2,1,0:T(8,128)(2,1)} %get-tuple-element.1302.x_ref, ...), custom_call_target="tpu_custom_call" | custom-call | flops 1000 | bytes 1000 | tf_op jit(solution)/shard_map/attend_back/pallas_call | solution.py:758
  436.0 6.6 %collective-permute-done.45.refs_8_ = bf16[192,1536]{1,0:T(8,128)(2,1)S(1)} collective-permute-done((bf16[192,1536]{1,0:T(8,128)(2,1)S(1)}, bf16[192,1536]{1,0:T(8,128)(2,1)S(1)}, u32[]{:S(2)}, u32[]{:S(2)}) %collective-permute-start.45) | collective-permute-done | bytes 589856 | tf_op jit(solution)/shard_map/ppermute | solution.py:41
  442.7 2.7 collective-permute-start.47
  445.4 14.8 %attend_back.3 = (f32[5,208,768]{2,1,0:T(8,128)}, bf16[5,208,768]{2,1,0:T(8,128)(2,1)}, bf16[5,208,1152]{2,1,0:T(8,128)(2,1)}, bf16[2,208,768]{2,1,0:T(8,128)(2,...) custom-call(s32[1]{0:T(128)} %bitcast.12.which_ref, ...), custom_call_target="tpu_custom_call", output_to_operand_aliasing={{0}: (16, {}), {1}: (17, {}), {2}: (18, {})} | custom-call | flops 1000 | bytes 1000 | tf_op jit(solution)/shard_map/attend_back/pallas_call | solution.py:758
  460.2 11.1 %projection_grads.1 = (f32[2,4,48,1664]{3,2,1,0:T(8,128)}, bf16[2,4,48,1664]{3,2,1,0:T(8,128)(2,1)}) custom-call(s32[1]{0:T(128)} %bitcast.20.core_ref, bf16[5,208,768]{2,1,0:T(8,128)(2,1)} %get-tuple-element.1238.refs_0_, bf16[5,208,1152]{2,1,0:T(8,128)(2,1)} %get-tuple-element.1239.refs_1_, bf16[5,208,768]{2,1,0:T(8,128)(2,1)} %get-tuple-element.1240.refs_2_, ...), custom_call_target="tpu_custom_call" | custom-call | flops 1000 | bytes 1000 | tf_op jit(solution)/shard_map/projection_grads/pallas_call | solution.py:962
  471.3 5.2 collective-permute-done.47.refs_9_
  478.7 10.6 %outer_keep.2 = f32[1536,384]{1,0:T(8,128)} custom-call(s32[1]{0:T(128)S(6)} %sub.6.which_ref, bf16[2,312,1536]{2,1,0:T(8,128)(2,1)} %get-tuple-element.1258.refs_0_, bf16[2,312,1536]{2,1,0:T(8,128)(2,1)} %get-tuple-element.1259.refs_1_, bf16[2,312,1536]{2,1,0:T(8,128)(2,1)} %get-tuple-element.1260.refs_2_, ...), custom_call_target="tpu_custom_call" | custom-call | flops 1000 | bytes 1000 | tf_op jit(solution)/shard_map/outer_keep/pallas_call | solution.py:643
  497.9 9.4 %outer_keep.3 = f32[384,1536]{1,0:T(8,128)} custom-call(s32[1]{0:T(128)S(6)} %sub.6.which_ref, bf16[2,312,1536]{2,1,0:T(8,128)(2,1)} %get-tuple-element.1277.refs_0_, bf16[2,312,1536]{2,1,0:T(8,128)(2,1)} %get-tuple-element.1278.refs_1_, bf16[2,312,1536]{2,1,0:T(8,128)(2,1)} %get-tuple-element.1279.refs_2_, ...), custom_call_target="tpu_custom_call" | custom-call | flops 1000 | bytes 1000 | tf_op jit(solution)/shard_map/outer_keep/pallas_call | solution.py:643
  507.3 2.6 collective-permute-done.50
  515.4 5.1 token_back.2.refs_0_
  520.5 3.2 token_back.3
  527.8 5.2 collective-permute-done.53
  (261 shorter events, 125.4 us)
Async XLA Ops:
  20.9 26.2 %collective-permute-start.4 = (bf16[176,1536]{1,0:T(8,128)(2,1)S(1)}, bf16[176,1536]{1,0:T(8,128)(2,1)S(1)}, u32[]{:S(2)}, u32[]{:S(2)}) collective-permute-start(bf16[176,1536]{1,0:T(8,128)(2,1)S(1)} %fusion.3.refs_0_), channel_id=1, source_target_pairs={{0,16},{16,0},{1,17},{17,1},{2,18},{18,2},{3,19},{19,3},{4,20},{20... | collective-permute-start | bytes 1622024 | tf_op jit(solution)/shard_map/ppermute | solution.py:41
  21.0 22.1 %collective-permute-start.1 = (bf16[2,48,1664]{2,1,0:T(8,128)(2,1)}, bf16[2,48,1664]{2,1,0:T(8,128)(2,1)S(1)}, u32[]{:S(2)}, u32[]{:S(2)}) collective-permute-start(bf16[2,48,1664]{2,1,0:T(8,128)(2,1)} %cross.1.refs_0_), channel_id=1, source_target_pairs={{0,4},{2,6},{4,0},{6,2},{8,12},{10,14},{12,8},{14,10},{1,5},{3,7},... | collective-permute-start | bytes 958472 | tf_op jit(solution)/shard_map/ppermute | solution.py:41
  22.8 20.3 %collective-permute-start.2 = (bf16[2,48,1664]{2,1,0:T(8,128)(2,1)}, bf16[2,48,1664]{2,1,0:T(8,128)(2,1)S(1)}, u32[]{:S(2)}, u32[]{:S(2)}) collective-permute-start(bf16[2,48,1664]{2,1,0:T(8,128)(2,1)} %cross.1.refs_0_), channel_id=1, source_target_pairs={{0,8},{2,10},{4,12},{6,14},{8,0},{10,2},{12,4},{14,6},{1,9},{3,11}... | collective-permute-start | bytes 958472 | tf_op jit(solution)/shard_map/ppermute | solution.py:41
  24.3 18.8 %collective-permute-start.3 = (bf16[2,48,1664]{2,1,0:T(8,128)(2,1)}, bf16[2,48,1664]{2,1,0:T(8,128)(2,1)}, u32[]{:S(2)}, u32[]{:S(2)}) collective-permute-start(bf16[2,48,1664]{2,1,0:T(8,128)(2,1)} %cross.1.refs_0_), channel_id=1, source_target_pairs={{0,12},{2,14},{4,8},{6,10},{8,4},{10,6},{12,0},{14,2},{1,13},{3,15... | collective-permute-start | bytes 958472 | tf_op jit(solution)/shard_map/ppermute | solution.py:41
  47.2 14.9 %collective-permute-start.8 = (bf16[1040,768]{1,0:T(8,128)(2,1)}, bf16[1040,768]{1,0:T(8,128)(2,1)}, u32[]{:S(2)}, u32[]{:S(2)}) collective-permute-start(bf16[1040,768]{1,0:T(8,128)(2,1)} %bitcast.54), channel_id=1, source_target_pairs={{0,2},{2,0},{4,6},{6,4},{8,10},{10,8},{12,14},{14,12},{1,3},{3,1},... | collective-permute-start | bytes 4792328 | tf_op jit(solution)/shard_map/ppermute | solution.py:41
  47.7 14.3 %collective-permute-start.6 = (bf16[64,1536]{1,0:T(8,128)(2,1)S(1)}, bf16[64,1536]{1,0:T(8,128)(2,1)S(1)}, u32[]{:S(2)}, u32[]{:S(2)}) collective-permute-start(bf16[64,1536]{1,0:T(8,128)(2,1)S(1)} %fusion.11.refs_1_), channel_id=1, source_target_pairs={{0,16},{16,0},{1,17},{17,1},{2,18},{18,2},{3,19},{19,3},{4,20},{20... | collective-permute-start | bytes 589832 | tf_op jit(solution)/shard_map/ppermute | solution.py:41
  56.2 27.1 %collective-permute-start.9 = (bf16[768,384]{1,0:T(8,128)(2,1)}, bf16[768,384]{1,0:T(8,128)(2,1)S(1)}, u32[]{:S(2)}, u32[]{:S(2)}) collective-permute-start(bf16[768,384]{1,0:T(8,128)(2,1)} %get-tuple-element.1213.here_ref.out_w_ref), channel_id=1, source_target_pairs={{0,1},{1,0},{2,3},{3,2},{4,5},{5,4},{6,7},{7,6},{8,9},{9,8},{10,11... | collective-permute-start | bytes 1769480 | tf_op jit(solution)/shard_map/ppermute | solution.py:41
  71.7 40.0 %collective-permute-start.10 = (bf16[3,208,384]{2,1,0:T(8,128)(2,1)}, bf16[3,208,384]{2,1,0:T(8,128)(2,1)}, u32[]{:S(2)}, u32[]{:S(2)}) collective-permute-start(bf16[3,208,384]{2,1,0:T(8,128)(2,1)} %get-tuple-element.762.own_ref), channel_id=1, source_target_pairs={{0,1},{1,0},{2,3},{3,2},{4,5},{5,4},{6,7},{7,6},{8,9},{9,8},{10,11... | collective-permute-start | bytes 1437704 | tf_op jit(solution)/shard_map/ppermute | solution.py:41
  71.9 39.8 %collective-permute-start.12 = (bf16[144,1536]{1,0:T(8,128)(2,1)S(1)}, bf16[144,1536]{1,0:T(8,128)(2,1)S(1)}, u32[]{:S(2)}, u32[]{:S(2)}) collective-permute-start(bf16[144,1536]{1,0:T(8,128)(2,1)S(1)} %fusion.4.refs_2_), channel_id=1, source_target_pairs={{0,16},{16,0},{1,17},{17,1},{2,18},{18,2},{3,19},{19,3},{4,20},{20... | collective-permute-start | bytes 1327112 | tf_op jit(solution)/shard_map/ppermute | solution.py:41
  73.0 38.7 %collective-permute-start.13 = (bf16[1536,128]{1,0:T(8,128)(2,1)S(1)}, bf16[1536,128]{1,0:T(8,128)(2,1)S(1)}, u32[]{:S(2)}, u32[]{:S(2)}) collective-permute-start(bf16[1536,128]{1,0:T(8,128)(2,1)S(1)} %fusion.5.refs_6_), channel_id=1, source_target_pairs={{0,16},{16,0},{1,17},{17,1},{2,18},{18,2},{3,19},{19,3},{4,20},{20... | collective-permute-start | bytes 1179656 | tf_op jit(solution)/shard_map/ppermute | solution.py:41
  81.4 30.3 %collective-permute-start.11 = (bf16[2,208,384]{2,1,0:T(8,128)(2,1)}, bf16[2,208,384]{2,1,0:T(8,128)(2,1)S(1)}, u32[]{:S(2)}, u32[]{:S(2)}) collective-permute-start(bf16[2,208,384]{2,1,0:T(8,128)(2,1)} %get-tuple-element.779.own_ref), channel_id=1, source_target_pairs={{0,1},{1,0},{2,3},{3,2},{4,5},{5,4},{6,7},{7,6},{8,9},{9,8},{10,11... | collective-permute-start | bytes 958472 | tf_op jit(solution)/shard_map/ppermute | solution.py:41
  111.8 19.1 %collective-permute-start.14 = (bf16[1536,128]{1,0:T(8,128)(2,1)S(1)}, bf16[1536,128]{1,0:T(8,128)(2,1)S(1)}, u32[]{:S(2)}, u32[]{:S(2)}) collective-permute-start(bf16[1536,128]{1,0:T(8,128)(2,1)S(1)} %fusion.6.refs_7_), channel_id=1, source_target_pairs={{0,16},{16,0},{1,17},{17,1},{2,18},{18,2},{3,19},{19,3},{4,20},{20... | collective-permute-start | bytes 1179656 | tf_op jit(solution)/shard_map/ppermute | solution.py:41
  130.8 20.3 %collective-permute-start.17 = (bf16[1536,128]{1,0:T(8,128)(2,1)S(1)}, bf16[1536,128]{1,0:T(8,128)(2,1)S(1)}, u32[]{:S(2)}, u32[]{:S(2)}) collective-permute-start(bf16[1536,128]{1,0:T(8,128)(2,1)S(1)} %fusion.7.refs_8_), channel_id=1, source_target_pairs={{0,16},{16,0},{1,17},{17,1},{2,18},{18,2},{3,19},{19,3},{4,20},{20... | collective-permute-start | bytes 1179656 | tf_op jit(solution)/shard_map/ppermute | solution.py:41
  151.2 42.4 %collective-permute-start.19 = (bf16[2,312,768]{2,1,0:T(8,128)(2,1)}, bf16[2,312,768]{2,1,0:T(8,128)(2,1)S(1)}, u32[]{:S(2)}, u32[]{:S(2)}) collective-permute-start(bf16[2,312,768]{2,1,0:T(8,128)(2,1)} %get-tuple-element.877), channel_id=1, source_target_pairs={{0,4},{2,6},{4,0},{6,2},{8,12},{10,14},{12,8},{14,10},{1,5},{3,7},... | collective-permute-start | bytes 2875400 | tf_op jit(solution)/shard_map/ppermute | solution.py:41
  152.7 43.7 %collective-permute-start.20 = (bf16[2,312,768]{2,1,0:T(8,128)(2,1)}, bf16[2,312,768]{2,1,0:T(8,128)(2,1)S(1)}, u32[]{:S(2)}, u32[]{:S(2)}) collective-permute-start(bf16[2,312,768]{2,1,0:T(8,128)(2,1)} %get-tuple-element.879), channel_id=1, source_target_pairs={{0,8},{2,10},{4,12},{6,14},{8,0},{10,2},{12,4},{14,6},{1,9},{3,11}... | collective-permute-start | bytes 2875400 | tf_op jit(solution)/shard_map/ppermute | solution.py:41
  154.2 42.2 %collective-permute-start.21 = (bf16[2,312,768]{2,1,0:T(8,128)(2,1)}, bf16[2,312,768]{2,1,0:T(8,128)(2,1)}, u32[]{:S(2)}, u32[]{:S(2)}) collective-permute-start(bf16[2,312,768]{2,1,0:T(8,128)(2,1)} %get-tuple-element.881), channel_id=1, source_target_pairs={{0,12},{2,14},{4,8},{6,10},{8,4},{10,6},{12,0},{14,2},{1,13},{3,15... | collective-permute-start | bytes 2875400 | tf_op jit(solution)/shard_map/ppermute | solution.py:41
  196.4 34.4 %collective-permute-start.23 = (bf16[2,312,768]{2,1,0:T(8,128)(2,1)}, bf16[2,312,768]{2,1,0:T(8,128)(2,1)S(1)}, u32[]{:S(2)}, u32[]{:S(2)}) collective-permute-start(bf16[2,312,768]{2,1,0:T(8,128)(2,1)} %get-tuple-element.928), channel_id=1, source_target_pairs={{0,4},{2,6},{4,0},{6,2},{8,12},{10,14},{12,8},{14,10},{1,5},{3,7},... | collective-permute-start | bytes 2875400 | tf_op jit(solution)/shard_map/ppermute | solution.py:41
  197.7 42.8 %collective-permute-start.24 = (bf16[2,312,768]{2,1,0:T(8,128)(2,1)}, bf16[2,312,768]{2,1,0:T(8,128)(2,1)S(1)}, u32[]{:S(2)}, u32[]{:S(2)}) collective-permute-start(bf16[2,312,768]{2,1,0:T(8,128)(2,1)} %get-tuple-element.930), channel_id=1, source_target_pairs={{0,8},{2,10},{4,12},{6,14},{8,0},{10,2},{12,4},{14,6},{1,9},{3,11}... | collective-permute-start | bytes 2875400 | tf_op jit(solution)/shard_map/ppermute | solution.py:41
  198.8 41.7 %collective-permute-start.25 = (bf16[2,312,768]{2,1,0:T(8,128)(2,1)}, bf16[2,312,768]{2,1,0:T(8,128)(2,1)S(1)}, u32[]{:S(2)}, u32[]{:S(2)}) collective-permute-start(bf16[2,312,768]{2,1,0:T(8,128)(2,1)} %get-tuple-element.932), channel_id=1, source_target_pairs={{0,12},{2,14},{4,8},{6,10},{8,4},{10,6},{12,0},{14,2},{1,13},{3,15... | collective-permute-start | bytes 2875400 | tf_op jit(solution)/shard_map/ppermute | solution.py:41
  199.9 28.7 %collective-permute-start.22 = (bf16[2,312,384]{2,1,0:T(8,128)(2,1)}, bf16[2,312,384]{2,1,0:T(8,128)(2,1)}, u32[]{:S(2)}, u32[]{:S(2)}) collective-permute-start(bf16[2,312,384]{2,1,0:T(8,128)(2,1)} %get-tuple-element.923), channel_id=1, source_target_pairs={{0,1},{1,0},{2,3},{3,2},{4,5},{5,4},{6,7},{7,6},{8,9},{9,8},{10,11... | collective-permute-start | bytes 1437704 | tf_op jit(solution)/shard_map/ppermute | solution.py:41
  213.2 41.3 %collective-permute-start.26 = (bf16[2,312,384]{2,1,0:T(8,128)(2,1)}, bf16[2,312,384]{2,1,0:T(8,128)(2,1)S(1)}, u32[]{:S(2)}, u32[]{:S(2)}) collective-permute-start(bf16[2,312,384]{2,1,0:T(8,128)(2,1)} %get-tuple-element.955), channel_id=1, source_target_pairs={{0,1},{1,0},{2,3},{3,2},{4,5},{5,4},{6,7},{7,6},{8,9},{9,8},{10,11... | collective-permute-start | bytes 1437704 | tf_op jit(solution)/shard_map/ppermute | solution.py:41
  230.7 36.5 %collective-permute-start.27 = (bf16[2,312,384]{2,1,0:T(8,128)(2,1)}, bf16[2,312,384]{2,1,0:T(8,128)(2,1)}, u32[]{:S(2)}, u32[]{:S(2)}) collective-permute-start(bf16[2,312,384]{2,1,0:T(8,128)(2,1)} %get-tuple-element.981), channel_id=1, source_target_pairs={{0,1},{1,0},{2,3},{3,2},{4,5},{5,4},{6,7},{7,6},{8,9},{9,8},{10,11... | collective-permute-start | bytes 1437704 | tf_op jit(solution)/shard_map/ppermute | solution.py:41
  257.3 24.3 %collective-permute-start.28 = (bf16[2,312,384]{2,1,0:T(8,128)(2,1)S(1)}, bf16[2,312,384]{2,1,0:T(8,128)(2,1)S(1)}, u32[]{:S(2)}, u32[]{:S(2)}) collective-permute-start(bf16[2,312,384]{2,1,0:T(8,128)(2,1)S(1)} %copy-done.55), channel_id=1, source_target_pairs={{0,1},{1,0},{2,3},{3,2},{4,5},{5,4},{6,7},{7,6},{8,9},{9,8},{10,11... | collective-permute-start | bytes 1437704 | tf_op jit(solution)/shard_map/ppermute | solution.py:41
  269.4 27.8 %collective-permute-start.29 = (bf16[2,312,384]{2,1,0:T(8,128)(2,1)}, bf16[2,312,384]{2,1,0:T(8,128)(2,1)}, u32[]{:S(2)}, u32[]{:S(2)}) collective-permute-start(bf16[2,312,384]{2,1,0:T(8,128)(2,1)} %get-tuple-element.1033), channel_id=1, source_target_pairs={{0,1},{1,0},{2,3},{3,2},{4,5},{5,4},{6,7},{7,6},{8,9},{9,8},{10,11... | collective-permute-start | bytes 1437704 | tf_op jit(solution)/shard_map/ppermute | solution.py:41
  271.4 27.9 %collective-permute-start.30 = (bf16[2,312,384]{2,1,0:T(8,128)(2,1)S(1)}, bf16[2,312,384]{2,1,0:T(8,128)(2,1)S(1)}, u32[]{:S(2)}, u32[]{:S(2)}) collective-permute-start(bf16[2,312,384]{2,1,0:T(8,128)(2,1)S(1)} %copy-done.34), channel_id=1, source_target_pairs={{0,4},{2,6},{4,0},{6,2},{8,12},{10,14},{12,8},{14,10},{1,5},{3,7},... | collective-permute-start | bytes 1437704 | tf_op jit(solution)/shard_map/ppermute | solution.py:41
  284.5 26.6 %collective-permute-start.31 = (bf16[2,312,384]{2,1,0:T(8,128)(2,1)}, bf16[2,312,384]{2,1,0:T(8,128)(2,1)S(1)}, u32[]{:S(2)}, u32[]{:S(2)}) collective-permute-start(bf16[2,312,384]{2,1,0:T(8,128)(2,1)} %get-tuple-element.1061), channel_id=1, source_target_pairs={{0,1},{1,0},{2,3},{3,2},{4,5},{5,4},{6,7},{7,6},{8,9},{9,8},{10,11... | collective-permute-start | bytes 1437704 | tf_op jit(solution)/shard_map/ppermute | solution.py:41
  284.6 29.5 %collective-permute-start.32 = (bf16[2,312,384]{2,1,0:T(8,128)(2,1)S(1)}, bf16[2,312,384]{2,1,0:T(8,128)(2,1)S(1)}, u32[]{:S(2)}, u32[]{:S(2)}) collective-permute-start(bf16[2,312,384]{2,1,0:T(8,128)(2,1)S(1)} %copy-done.31), channel_id=1, source_target_pairs={{0,8},{2,10},{4,12},{6,14},{8,0},{10,2},{12,4},{14,6},{1,9},{3,11}... | collective-permute-start | bytes 1437704 | tf_op jit(solution)/shard_map/ppermute | solution.py:41
  295.2 18.9 %collective-permute-start.33 = (bf16[2,312,384]{2,1,0:T(8,128)(2,1)S(1)}, bf16[2,312,384]{2,1,0:T(8,128)(2,1)S(1)}, u32[]{:S(2)}, u32[]{:S(2)}) collective-permute-start(bf16[2,312,384]{2,1,0:T(8,128)(2,1)S(1)} %copy-done.32), channel_id=1, source_target_pairs={{0,12},{2,14},{4,8},{6,10},{8,4},{10,6},{12,0},{14,2},{1,13},{3,15... | collective-permute-start | bytes 1437704 | tf_op jit(solution)/shard_map/ppermute | solution.py:41
  299.4 19.1 %collective-permute-start.34 = (bf16[2,312,384]{2,1,0:T(8,128)(2,1)}, bf16[2,312,384]{2,1,0:T(8,128)(2,1)S(1)}, u32[]{:S(2)}, u32[]{:S(2)}) collective-permute-start(bf16[2,312,384]{2,1,0:T(8,128)(2,1)} %get-tuple-element.1081), channel_id=1, source_target_pairs={{0,1},{1,0},{2,3},{3,2},{4,5},{5,4},{6,7},{7,6},{8,9},{9,8},{10,11... | collective-permute-start | bytes 1437704 | tf_op jit(solution)/shard_map/ppermute | solution.py:41
  314.0 21.7 %collective-permute-start.35 = (bf16[2,312,384]{2,1,0:T(8,128)(2,1)}, bf16[2,312,384]{2,1,0:T(8,128)(2,1)S(1)}, u32[]{:S(2)}, u32[]{:S(2)}) collective-permute-start(bf16[2,312,384]{2,1,0:T(8,128)(2,1)} %get-tuple-element.1102), channel_id=1, source_target_pairs={{0,1},{1,0},{2,3},{3,2},{4,5},{5,4},{6,7},{7,6},{8,9},{9,8},{10,11... | collective-permute-start | bytes 1437704 | tf_op jit(solution)/shard_map/ppermute | solution.py:41
  334.2 17.3 %collective-permute-start.36 = (bf16[2,312,384]{2,1,0:T(8,128)(2,1)S(1)}, bf16[2,312,384]{2,1,0:T(8,128)(2,1)S(1)}, u32[]{:S(2)}, u32[]{:S(2)}) collective-permute-start(bf16[2,312,384]{2,1,0:T(8,128)(2,1)S(1)} %copy-done.35), channel_id=1, source_target_pairs={{0,4},{2,6},{4,0},{6,2},{8,12},{10,14},{12,8},{14,10},{1,5},{3,7},... | collective-permute-start | bytes 1437704 | tf_op jit(solution)/shard_map/ppermute | solution.py:41
  334.8 20.0 %collective-permute-start.37 = (bf16[2,312,384]{2,1,0:T(8,128)(2,1)}, bf16[2,312,384]{2,1,0:T(8,128)(2,1)}, u32[]{:S(2)}, u32[]{:S(2)}) collective-permute-start(bf16[2,312,384]{2,1,0:T(8,128)(2,1)} %add_halves.14), channel_id=1, source_target_pairs={{0,8},{2,10},{4,12},{6,14},{8,0},{10,2},{12,4},{14,6},{1,9},{3,11}... | collective-permute-start | bytes 1437704 | tf_op jit(solution)/shard_map/ppermute | solution.py:41
  338.6 16.2 %collective-permute-start.38 = (bf16[2,312,384]{2,1,0:T(8,128)(2,1)}, bf16[2,312,384]{2,1,0:T(8,128)(2,1)}, u32[]{:S(2)}, u32[]{:S(2)}) collective-permute-start(bf16[2,312,384]{2,1,0:T(8,128)(2,1)} %add_halves.15), channel_id=1, source_target_pairs={{0,12},{2,14},{4,8},{6,10},{8,4},{10,6},{12,0},{14,2},{1,13},{3,15... | collective-permute-start | bytes 1437704 | tf_op jit(solution)/shard_map/ppermute | solution.py:41
  340.6 17.1 %collective-permute-start.39 = (bf16[512,384]{1,0:T(8,128)(2,1)S(1)}, bf16[512,384]{1,0:T(8,128)(2,1)}, u32[]{:S(2)}, u32[]{:S(2)}) collective-permute-start(bf16[512,384]{1,0:T(8,128)(2,1)S(1)} %slice.102), channel_id=1, source_target_pairs={{0,16},{16,0},{1,17},{17,1},{2,18},{18,2},{3,19},{19,3},{4,20},{20... | collective-permute-start | bytes 1179656 | tf_op jit(solution)/shard_map/ppermute | solution.py:41
  342.8 17.9 %collective-permute-start.40 = (bf16[4,312,384]{2,1,0:T(8,128)(2,1)}, bf16[4,312,384]{2,1,0:T(8,128)(2,1)S(1)}, u32[]{:S(2)}, u32[]{:S(2)}) collective-permute-start(bf16[4,312,384]{2,1,0:T(8,128)(2,1)} %get-tuple-element.1141), channel_id=1, source_target_pairs={{0,2},{2,0},{4,6},{6,4},{8,10},{10,8},{12,14},{14,12},{1,3},{3,1},... | collective-permute-start | bytes 2875400 | tf_op jit(solution)/shard_map/ppermute | solution.py:41
  358.8 18.2 %collective-permute-start.41 = (bf16[4,312,384]{2,1,0:T(8,128)(2,1)}, bf16[4,312,384]{2,1,0:T(8,128)(2,1)S(1)}, u32[]{:S(2)}, u32[]{:S(2)}) collective-permute-start(bf16[4,312,384]{2,1,0:T(8,128)(2,1)} %get-tuple-element.1153), channel_id=1, source_target_pairs={{0,2},{2,0},{4,6},{6,4},{8,10},{10,8},{12,14},{14,12},{1,3},{3,1},... | collective-permute-start | bytes 2875400 | tf_op jit(solution)/shard_map/ppermute | solution.py:41
  358.8 55.9 %collective-permute-start.42 = (bf16[1024,384]{1,0:T(8,128)(2,1)}, bf16[1024,384]{1,0:T(8,128)(2,1)S(1)}, u32[]{:S(2)}, u32[]{:S(2)}) collective-permute-start(bf16[1024,384]{1,0:T(8,128)(2,1)} %slice.103), channel_id=1, source_target_pairs={{0,16},{16,0},{1,17},{17,1},{2,18},{18,2},{3,19},{19,3},{4,20},{20... | collective-permute-start | bytes 2359304 | tf_op jit(solution)/shard_map/ppermute | solution.py:41
  385.9 29.0 %collective-permute-start.44 = (bf16[5,208,384]{2,1,0:T(8,128)(2,1)}, bf16[5,208,384]{2,1,0:T(8,128)(2,1)S(1)}, u32[]{:S(2)}, u32[]{:S(2)}) collective-permute-start(bf16[5,208,384]{2,1,0:T(8,128)(2,1)} %sum_home.1.near_ref), channel_id=1, source_target_pairs={{0,1},{1,0},{2,3},{3,2},{4,5},{5,4},{6,7},{7,6},{8,9},{9,8},{10,11... | collective-permute-start | bytes 2396168 | tf_op jit(solution)/shard_map/ppermute | solution.py:41
  386.2 28.5 %collective-permute-start.43 = (f32[5,8,208]{2,1,0:T(8,128)S(1)}, f32[5,8,208]{2,1,0:T(8,128)S(1)}, u32[]{:S(2)}, u32[]{:S(2)}) collective-permute-start(f32[5,8,208]{2,1,0:T(8,128)S(1)} %copy-done.47), channel_id=1, source_target_pairs={{0,1},{1,0},{2,3},{3,2},{4,5},{5,4},{6,7},{7,6},{8,9},{9,8},{10,11... | collective-permute-start | bytes 99848 | tf_op jit(solution)/shard_map/ppermute | solution.py:41
  414.7 27.9 %collective-permute-start.45 = (bf16[192,1536]{1,0:T(8,128)(2,1)S(1)}, bf16[192,1536]{1,0:T(8,128)(2,1)S(1)}, u32[]{:S(2)}, u32[]{:S(2)}) collective-permute-start(bf16[192,1536]{1,0:T(8,128)(2,1)S(1)} %copy-done.29), channel_id=1, source_target_pairs={{0,16},{16,0},{1,17},{17,1},{2,18},{18,2},{3,19},{19,3},{4,20},{20... | collective-permute-start | bytes 1769480 | tf_op jit(solution)/shard_map/ppermute | solution.py:41
  442.7 36.0 %collective-permute-start.46 = (bf16[3,208,768]{2,1,0:T(8,128)(2,1)}, bf16[3,208,768]{2,1,0:T(8,128)(2,1)S(1)}, u32[]{:S(2)}, u32[]{:S(2)}) collective-permute-start(bf16[3,208,768]{2,1,0:T(8,128)(2,1)} %get-tuple-element.1295.own_ref), channel_id=1, source_target_pairs={{0,1},{1,0},{2,3},{3,2},{4,5},{5,4},{6,7},{7,6},{8,9},{9,8},{10,11... | collective-permute-start | bytes 2875400 | tf_op jit(solution)/shard_map/ppermute | solution.py:41
  442.7 33.8 %collective-permute-start.47 = (bf16[192,1536]{1,0:T(8,128)(2,1)S(1)}, bf16[192,1536]{1,0:T(8,128)(2,1)S(1)}, u32[]{:S(2)}, u32[]{:S(2)}) collective-permute-start(bf16[192,1536]{1,0:T(8,128)(2,1)S(1)} %copy-done.28), channel_id=1, source_target_pairs={{0,16},{16,0},{1,17},{17,1},{2,18},{18,2},{3,19},{19,3},{4,20},{20... | collective-permute-start | bytes 1769480 | tf_op jit(solution)/shard_map/ppermute | solution.py:41
  492.4 15.0 %collective-permute-start.51 = (bf16[2,48,1664]{2,1,0:T(8,128)(2,1)}, bf16[2,48,1664]{2,1,0:T(8,128)(2,1)S(1)}, u32[]{:S(2)}, u32[]{:S(2)}) collective-permute-start(bf16[2,48,1664]{2,1,0:T(8,128)(2,1)} %fusion.10), channel_id=1, source_target_pairs={{0,12},{2,14},{4,8},{6,10},{8,4},{10,6},{12,0},{14,2},{1,13},{3,15... | collective-permute-start | bytes 958472 | tf_op jit(solution)/shard_map/ppermute | solution.py:41
  494.7 15.2 %collective-permute-start.50 = (bf16[2,48,1664]{2,1,0:T(8,128)(2,1)}, bf16[2,48,1664]{2,1,0:T(8,128)(2,1)S(1)}, u32[]{:S(2)}, u32[]{:S(2)}) collective-permute-start(bf16[2,48,1664]{2,1,0:T(8,128)(2,1)} %get-tuple-element.1361), channel_id=1, source_target_pairs={{0,8},{2,10},{4,12},{6,14},{8,0},{10,2},{12,4},{14,6},{1,9},{3,11}... | collective-permute-start | bytes 958472 | tf_op jit(solution)/shard_map/ppermute | solution.py:41
  495.4 14.6 %collective-permute-start.49 = (bf16[2,48,1664]{2,1,0:T(8,128)(2,1)}, bf16[2,48,1664]{2,1,0:T(8,128)(2,1)S(1)}, u32[]{:S(2)}, u32[]{:S(2)}) collective-permute-start(bf16[2,48,1664]{2,1,0:T(8,128)(2,1)} %get-tuple-element.1360), channel_id=1, source_target_pairs={{0,4},{2,6},{4,0},{6,2},{8,12},{10,14},{12,8},{14,10},{1,5},{3,7},... | collective-permute-start | bytes 958472 | tf_op jit(solution)/shard_map/ppermute | solution.py:41
  496.8 15.9 %collective-permute-start.52 = (bf16[2,208,768]{2,1,0:T(8,128)(2,1)}, bf16[2,208,768]{2,1,0:T(8,128)(2,1)}, u32[]{:S(2)}, u32[]{:S(2)}) collective-permute-start(bf16[2,208,768]{2,1,0:T(8,128)(2,1)} %get-tuple-element.1303.own_ref), channel_id=1, source_target_pairs={{0,1},{1,0},{2,3},{3,2},{4,5},{5,4},{6,7},{7,6},{8,9},{9,8},{10,11... | collective-permute-start | bytes 1916936 | tf_op jit(solution)/shard_map/ppermute | solution.py:41
  512.7 21.9 %collective-permute-start.54 = (bf16[5,208,384]{2,1,0:T(8,128)(2,1)}, bf16[5,208,384]{2,1,0:T(8,128)(2,1)}, u32[]{:S(2)}, u32[]{:S(2)}) collective-permute-start(bf16[5,208,384]{2,1,0:T(8,128)(2,1)} %get-tuple-element.1311), channel_id=1, source_target_pairs={{0,1},{1,0},{2,3},{3,2},{4,5},{5,4},{6,7},{7,6},{8,9},{9,8},{10,11... | collective-permute-start | bytes 2396168 | tf_op jit(solution)/shard_map/ppermute | solution.py:41
  513.7 19.3 %collective-permute-start.53 = (bf16[48,1664]{1,0:T(8,128)(2,1)}, bf16[48,1664]{1,0:T(8,128)(2,1)S(1)}, u32[]{:S(2)}, u32[]{:S(2)}) collective-permute-start(bf16[48,1664]{1,0:T(8,128)(2,1)} %fusion.12), channel_id=1, source_target_pairs={{0,16},{16,0},{1,17},{17,1},{2,18},{18,2},{3,19},{19,3},{4,20},{20... | collective-permute-start | bytes 479240 | tf_op jit(solution)/shard_map/ppermute | solution.py:41
  (64 other events, 935.6 us)

commit v7 on v6

--- a/solution.py
+++ b/solution.py
@@ -21,7 +21,7 @@
 LANES = 128
 TILE = 512
 IN_CUTS = ((0, 176), (176, 240), (240, 384))
-BACK_CUTS = ((0, 128), (128, 256), (256, 384))
+BACK_CUTS = ((0, 128), (128, 384))
 TAIL_RATE = 0.305
 TAIL = (
     0.12163973686996697,
@@ -1041,7 +1041,6 @@
     vectors = order.run(lambda v: vectors_of(v, count), narrow_all)
     in_other[1] = order.wait(in_other[1])
     in_other.append(hop(order.after(in_own[2]), "dp", 1))
-    back_other = [hop(order.after(back_own[0]), "dp", 1)]
     rows_next, cot_next = order.wait((rows_next, cot_next))
     own_lanes, next_lanes = order.wait((lanes_of(rows_lane), lanes_of(rows_next)))
 
@@ -1054,8 +1053,8 @@
         got_parts.append(hop(o_part, "tensor", 1))
     a_rows, qkv, o_rows, lse = held
     out_there = order.wait(out_there)
-    got_parts, in_other[2], back_other[0] = order.wait((got_parts, in_other[2], back_other[0]))
-    back_other.append(hop(order.after(back_own[1]), "dp", 1))
+    got_parts, in_other[2] = order.wait((got_parts, in_other[2]))
+    back_other = [hop(order.after(back_own[0]), "dp", 1)]
     held, h_parts, h_next = [], [], []
     for n, (lo, hi) in enumerate(groups):
         *held, h_part = order.run(
@@ -1065,9 +1064,9 @@
         h_parts.append(h_part.reshape(-1, D))
         if n == len(groups) - 1:
             gates_lane = jnp.transpose(held[2].reshape(rows_all, LANES)[:, :2])
-            back_other[1], gates_lane = order.wait((back_other[1], gates_lane))
+            back_other[0], gates_lane = order.wait((back_other[0], gates_lane))
             h_parts[-1] = order.after(h_parts[-1])
-            back_other.append(hop(order.after(back_own[2]), "dp", 1))
+            back_other.append(hop(order.after(back_own[1]), "dp", 1))
         h_next.append(hop(h_parts[-1], "expert", 1))
     y, probs, gates = held
     gates_next = hop(order.after(gates_lane), "expert", 1)
@@ -1076,8 +1075,7 @@
     other = (next_lanes, h_next)
     far = list(range(1, chips))
     outgoing = order.run(lambda *v: send_rows(*v, capacity, far, False), own, other)
-    back_other[2] = order.wait(back_other[2])
-    arrived = [None] + [hop(order.after(o), "expert", 2 * c) for o, c in zip(outgoing, far)]
+    arrived = [None] + [hop(o, "expert", 2 * c) for o, c in zip(outgoing, far)]
     (arrived[0],) = order.run(lambda *v: send_rows(*v, capacity, [0], False), own, other)
     gates_next = order.wait(gates_next)
     own = ([rows_lane], [cot_here], [gates_lane])
@@ -1085,6 +1083,7 @@
     grad_outgoing = order.run(lambda *v: send_rows(*v, capacity, far, True), own, other)
     grad_arrived = [None] * chips
     (grad_arrived[0],) = order.run(lambda *v: send_rows(*v, capacity, [0], True), own, other)
+    back_other[1] = order.wait(back_other[1])
     weights = (*in_own, *in_other, *back_own, *back_other)
     same = flag(same)
 

time: 551 us -> 543 us (0.985)
  Pallas kernels: 316 us -> 308 us
    pallas_call x4, Pallas kernels: 62.4 us -> 53.7 us  [expert_forward(): pl.pallas_call(forward_kernel, grid_spec=pltpu.PrefetchScalarGridSpec(num...]
    ppermute x56 -> x55, starting transfers between devices: 55.9 us -> 54.6 us  [hop(): return lax.ppermute(value, axis, [(i, i ^ offset) for i in range(count)])]
    unnamed x115 -> x109, local copies, waits for them, and re-layouts: 13.7 us -> 14.5 us
    ppermute x56 -> x55, waiting for transfers between devices: 118 us -> 118 us  [hop(): return lax.ppermute(value, axis, [(i, i ^ offset) for i in range(count)])]
  transfers between devices with their start and end apart: 56 -> 55, of which waited for: 17 -> 19; matrix products, arithmetic and copies ran while one was open for 5% -> 5% of each run, Pallas kernels for 58% -> 56%
where the time goes in v7:
time: 543 us; the launch traced here: 532 us
  Pallas kernels  308 us (57%)
  waiting for transfers between devices  118 us (22%)
  starting transfers between devices  54.6 us (10%)
  local copies, waits for them, and re-layouts  39.7 us (7%)
  other arithmetic  10.3 us (2%)
    ppermute x55, waiting for transfers between devices, hop(): return lax.ppermute(value, axis, [(i, i ^ offset) for i in range(count)])  118 us
    ppermute x55, starting transfers between devices, hop(): return lax.ppermute(value, axis, [(i, i ^ offset) for i in range(count)])  54.6 us
    pallas_call x4, Pallas kernels, expert_forward(): pl.pallas_call(forward_kernel, grid_spec=pltpu.PrefetchScalarGridSpec(num...  53.7 us
    pallas_call x4, Pallas kernels, expert_backward(): pl.pallas_call(backward_kernel, grid_spec=pltpu.PrefetchScalarGridSpec(nu...  39.7 us
    pallas_call x4, Pallas kernels, outer(): pl.pallas_call(functools.partial(outer_kernel, chunks=len(wides), hidden_...  38.4 us
    pallas_call x2, Pallas kernels, attend_back(): pl.pallas_call(attend_back_kernel, grid_spec=pltpu.PrefetchScalarGridSpec...  34.6 us
    pallas_call x4, Pallas kernels, send_rows(): pl.pallas_call(functools.partial(send_kernel, parts=len(own[0]), chips=ch...  23.4 us
    pallas_call x8, Pallas kernels, add_halves(): pl.pallas_call(add_kernel, grid=(near.shape[0],), in_specs=[part, part],...  16.8 us
  transfers between devices with their start and end apart: 55, of which 19 were waited for; matrix products, arithmetic and copies ran while one was open for 5% of the time, Pallas kernels for 56%

profile of v7, /device:TPU:0, one launch (start us, length us, event | category | flops | bytes accessed | tf_op | source)
XLA Modules:
  0.0 531.9 jit_solution(11661873806901892875)
XLA Ops:
  6.4 4.1 collective-permute-start
  24.0 6.9 %image_rows.1 = (bf16[5,208,768]{2,1,0:T(8,128)(2,1)}, bf16[5,208,768]{2,1,0:T(8,128)(2,1)}, bf16[5,208,768]{2,1,0:T(8,128)(2,1)}) custom-call(s32[1]{0:T(128)} %bitcast.11.which_ref, bf16[985,768]{1,0:T(8,128)(2,1)} %tok_ref, bf16[985,768]{1,0:T(8,128)(2,1)} %cot_ref), custom_call_target="tpu_custom_call" | custom-call | flops 1000 | bytes 1000 | tf_op jit(solution)/shard_map/image_rows/pallas_call | solution.py:853
  32.0 9.9 %slot_rows.1 = (s32[5,208,2]{2,1,0:T(8,128)}, s32[8,1040]{1,0:T(8,128)}, s32[5,208,2]{2,1,0:T(8,128)}) custom-call(s32[1]{0:T(128)} %bitcast.12.here_ref, s32[985,2]{1,0:T(8,128)} %copy.59.ids_ref), custom_call_target="tpu_custom_call" | custom-call | flops 1000 | bytes 1000 | tf_op jit(solution)/shard_map/slot_rows/pallas_call | solution.py:897
  43.5 2.4 stacked.1.same_ref
  49.3 2.8 collective-permute-done.5.flip_ref
  52.1 3.4 assemble.1
  55.5 3.5 collective-permute-start.9
  63.3 8.3 %attend.2 = (bf16[5,208,768]{2,1,0:T(8,128)(2,1)}, bf16[5,208,1152]{2,1,0:T(8,128)(2,1)}, bf16[5,208,384]{2,1,0:T(8,128)(2,1)}, f32[5,208,128]{2,1,0:T(8,128)}, bf16[3,208,384]{2,1,0:T(8,128)(2,1)}) custom-call(bf16[5,208,768]{2,1,0:T(8,128)(2,1)} %get-tuple-element.1254.x_ref, f32[8,768]{1,0:T(8,128)} %vectors.1.vec_ref, ...), custom_call_target="tpu_custom_call" | custom-call | flops 1000 | bytes 1000 | tf_op jit(solution)/shard_map/attend/pallas_call | solution.py:286
  72.5 6.6 %attend.3 = (bf16[5,208,768]{2,1,0:T(8,128)(2,1)}, bf16[5,208,1152]{2,1,0:T(8,128)(2,1)}, bf16[5,208,384]{2,1,0:T(8,128)(2,1)}, f32[5,208,128]{2,1,0:T(8,128)}, bf16[2,208,384]{2,1,0:T(8,128)(2,1)}) custom-call(bf16[5,208,768]{2,1,0:T(8,128)(2,1)} %get-tuple-element.1254.x_ref, ...), custom_call_target="tpu_custom_call", output_to_operand_aliasing={{0}: (3, {}), {1}: (4, {}), {2}: (5, {}), {3}: (6, {})} | custom-call | flops 1000 | bytes 1000 | tf_op jit(solution)/shard_map/attend/pallas_call | solution.py:286
  80.5 14.4 %collective-permute-done.12.refs_5_ = bf16[144,1536]{1,0:T(8,128)(2,1)S(1)} collective-permute-done((bf16[144,1536]{1,0:T(8,128)(2,1)S(1)}, bf16[144,1536]{1,0:T(8,128)(2,1)S(1)}, u32[]{:S(2)}, u32[]{:S(2)}) %collective-permute-start.12) | collective-permute-done | bytes 442400 | tf_op jit(solution)/shard_map/ppermute | solution.py:41
  94.9 6.7 %collective-permute-done.11.got_ref = bf16[2,208,384]{2,1,0:T(8,128)(2,1)S(1)} collective-permute-done((bf16[2,208,384]{2,1,0:T(8,128)(2,1)}, bf16[2,208,384]{2,1,0:T(8,128)(2,1)S(1)}, u32[]{:S(2)}, u32[]{:S(2)}) %collective-permute-start.11) | collective-permute-done | bytes 319520 | tf_op jit(solution)/shard_map/ppermute | solution.py:41
  101.7 6.7 %route.2 = (f32[5,208,768]{2,1,0:T(8,128)}, f32[5,208,128]{2,1,0:T(8,128)}, f32[5,208,128]{2,1,0:T(8,128)}, bf16[3,208,768]{2,1,0:T(8,128)(2,1)}) custom-call(s32[1]{0:T(128)} %bitcast.11.which_ref, bf16[5,208,768]{2,1,0:T(8,128)(2,1)} %get-tuple-element.1254.x_ref, bf16[3,208,384]{2,1,0:T(8,128)(2,1)} %get-tuple-element.734.own_ref, ...), custom_call_target="tpu_custom_call" | custom-call | flops 1000 | bytes 1000 | tf_op jit(solution)/shard_map/route/pallas_call | solution.py:331
  108.5 5.3 %route.3 = (f32[5,208,768]{2,1,0:T(8,128)}, f32[5,208,128]{2,1,0:T(8,128)}, f32[5,208,128]{2,1,0:T(8,128)}, bf16[2,208,768]{2,1,0:T(8,128)(2,1)}) custom-call(s32[1]{0:T(128)} %bitcast.11.which_ref, bf16[5,208,768]{2,1,0:T(8,128)(2,1)} %get-tuple-element.1254.x_ref, ...), custom_call_target="tpu_custom_call", output_to_operand_aliasing={{0}: (9, {}), {1}: (10, {}), {2}: (11, {})} | custom-call | flops 1000 | bytes 1000 | tf_op jit(solution)/shard_map/route/pallas_call | solution.py:331
  115.1 6.5 %collective-permute-done.13.refs_8_ = bf16[1536,128]{1,0:T(8,128)(2,1)S(1)} collective-permute-done((bf16[1536,128]{1,0:T(8,128)(2,1)S(1)}, bf16[1536,128]{1,0:T(8,128)(2,1)S(1)}, u32[]{:S(2)}, u32[]{:S(2)}) %collective-permute-start.13) | collective-permute-done | bytes 393248 | tf_op jit(solution)/shard_map/ppermute | solution.py:41
  124.7 6.9 %send_rows.2 = (bf16[2,312,768]{2,1,0:T(8,128)(2,1)}, bf16[2,312,768]{2,1,0:T(8,128)(2,1)}, bf16[2,312,768]{2,1,0:T(8,128)(2,1)}) custom-call(s32[2,624]{1,0:T(2,128)} %slice.92.refs_0_, s32[2,416]{1,0:T(2,128)} %slice.93.refs_1_, bf16[624,768]{1,0:T(8,128)(2,1)} %bitcast.57, bf16[416,768]{1,0:T(8,128)(2,1)} %bitcast.60, s32[2,624]{1,0:T(2,128)} %slice.94.refs_4_, ...), custom_call_target="tpu_custom_call" | custom-call | flops 1000 | bytes 1000 | tf_op jit(solution)/shard_map/send_rows/pallas_call | solution.py:389
  135.1 4.4 send_rows.3.m_ref.refs_4_
  140.1 7.4 %send_gated.2 = (bf16[2,312,768]{2,1,0:T(8,128)(2,1)}, bf16[2,312,768]{2,1,0:T(8,128)(2,1)}, bf16[2,312,768]{2,1,0:T(8,128)(2,1)}) custom-call(s32[2,1040]{1,0:T(2,128)} %copy-done.47, bf16[1040,768]{1,0:T(8,128)(2,1)} %bitcast.53, f32[2,1040]{1,0:T(2,128)} %bitcast.66, s32[2,1040]{1,0:T(2,128)} %copy-done.48, ...), custom_call_target="tpu_custom_call" | custom-call | flops 1000 | bytes 1000 | tf_op jit(solution)/shard_map/send_gated/pallas_call | solution.py:389
  147.5 4.7 send_gated.3.z_ref.refs_4_
  152.2 17.2 %collective-permute-done.17.refs_9_ = bf16[1536,256]{1,0:T(8,128)(2,1)S(1)} collective-permute-done((bf16[1536,256]{1,0:T(8,128)(2,1)S(1)}, bf16[1536,256]{1,0:T(8,128)(2,1)S(1)}, u32[]{:S(2)}, u32[]{:S(2)}) %collective-permute-start.17) | collective-permute-done | bytes 786464 | tf_op jit(solution)/shard_map/ppermute | solution.py:41
  170.3 13.4 %expert_forward.4 = (bf16[2,312,1536]{2,1,0:T(8,128)(2,1)}, bf16[2,312,1536]{2,1,0:T(8,128)(2,1)}, bf16[2,312,384]{2,1,0:T(8,128)(2,1)}, f32[2,312,384]{2,1,0:T(8,128)}) custom-call(s32[1]{0:T(128)} %bitcast.18.same_ref.which_ref, bf16[2,312,768]{2,1,0:T(8,128)(2,1)} %send_rows.3.m_ref.refs_4_, bf16[176,1536]{1,0:T(8,128)(2,1)} %copy-done.2, ...), custom_call_target="tpu_custom_call" | custom-call | flops 1000 | bytes 1000 | tf_op jit(solution)/shard_map/expert_forward/pallas_call | solution.py:542
  187.6 13.3 %expert_forward.5 = (bf16[2,312,1536]{2,1,0:T(8,128)(2,1)}, bf16[2,312,1536]{2,1,0:T(8,128)(2,1)}, bf16[2,312,384]{2,1,0:T(8,128)(2,1)}, f32[2,312,384]{2,1,0:T(8,128)}) custom-call(s32[1]{0:T(128)} %bitcast.18.same_ref.which_ref, bf16[2,312,768]{2,1,0:T(8,128)(2,1)} %copy-done.13, bf16[176,1536]{1,0:T(8,128)(2,1)} %copy-done.2, bf16[64,1536]{1,0:T(8,128)(2,1)} %copy-done.8, ...), custom_call_target="tpu_custom_call" | custom-call | flops 1000 | bytes 1000 | tf_op jit(solution)/shard_map/expert_forward/pallas_call | solution.py:542
  203.0 13.2 %expert_forward.6 = (bf16[2,312,1536]{2,1,0:T(8,128)(2,1)}, bf16[2,312,1536]{2,1,0:T(8,128)(2,1)}, bf16[2,312,384]{2,1,0:T(8,128)(2,1)}, f32[2,312,384]{2,1,0:T(8,128)}) custom-call(s32[1]{0:T(128)} %bitcast.18.same_ref.which_ref, bf16[2,312,768]{2,1,0:T(8,128)(2,1)} %collective-permute-done.19.m_ref.refs_6_, bf16[176,1536]{1,0:T(8,128)(2,1)} %copy-done.2, ...), custom_call_target="tpu_custom_call" | custom-call | flops 1000 | bytes 1000 | tf_op jit(solution)/shard_map/expert_forward/pallas_call | solution.py:542
  218.3 10.7 %collective-permute-done.23.z_ref.refs_6_ = bf16[2,312,768]{2,1,0:T(8,128)(2,1)S(1)} collective-permute-done((bf16[2,312,768]{2,1,0:T(8,128)(2,1)}, bf16[2,312,768]{2,1,0:T(8,128)(2,1)S(1)}, u32[]{:S(2)}, u32[]{:S(2)}) %collective-permute-start.23) | collective-permute-done | bytes 958496 | tf_op jit(solution)/shard_map/ppermute | solution.py:41
  229.0 13.9 %expert_forward.7 = (bf16[2,312,1536]{2,1,0:T(8,128)(2,1)}, bf16[2,312,1536]{2,1,0:T(8,128)(2,1)}, bf16[2,312,384]{2,1,0:T(8,128)(2,1)}, f32[2,312,384]{2,1,0:T(8,128)}) custom-call(s32[1]{0:T(128)} %bitcast.18.same_ref.which_ref, bf16[2,312,768]{2,1,0:T(8,128)(2,1)} %collective-permute-done.20.m_ref.refs_7_, bf16[176,1536]{1,0:T(8,128)(2,1)} %copy-done.2, ...), custom_call_target="tpu_custom_call" | custom-call | flops 1000 | bytes 1000 | tf_op jit(solution)/shard_map/expert_forward/pallas_call | solution.py:542
  245.8 10.1 %expert_backward.4 = (bf16[2,312,1536]{2,1,0:T(8,128)(2,1)}, bf16[2,312,384]{2,1,0:T(8,128)(2,1)}, f32[2,312,384]{2,1,0:T(8,128)}) custom-call(s32[1]{0:T(128)} %bitcast.18.same_ref.which_ref, bf16[2,312,768]{2,1,0:T(8,128)(2,1)} %send_gated.3.z_ref.refs_4_, bf16[2,312,1536]{2,1,0:T(8,128)(2,1)} %get-tuple-element.922.s_ref, bf16[176,1536]{1,0:T(8,128)(2,1)} %copy-done.2, ...), custom_call_target="tpu_custom_call" | custom-call | flops 1000 | bytes 1000 | tf_op jit(solution)/shard_map/expert_backward/pallas_call | solution.py:589
  261.0 9.9 %expert_backward.5 = (bf16[2,312,1536]{2,1,0:T(8,128)(2,1)}, bf16[2,312,384]{2,1,0:T(8,128)(2,1)}, f32[2,312,384]{2,1,0:T(8,128)}) custom-call(s32[1]{0:T(128)} %bitcast.18.same_ref.which_ref, bf16[2,312,768]{2,1,0:T(8,128)(2,1)} %copy-done.10, bf16[2,312,1536]{2,1,0:T(8,128)(2,1)} %get-tuple-element.946.s_ref, bf16[176,1536]{1,0:T(8,128)(2,1)} %copy-done.2, ...), custom_call_target="tpu_custom_call" | custom-call | flops 1000 | bytes 1000 | tf_op jit(solution)/shard_map/expert_backward/pallas_call | solution.py:589
  275.6 9.9 %expert_backward.6 = (bf16[2,312,1536]{2,1,0:T(8,128)(2,1)}, bf16[2,312,384]{2,1,0:T(8,128)(2,1)}, f32[2,312,384]{2,1,0:T(8,128)}) custom-call(s32[1]{0:T(128)} %bitcast.18.same_ref.which_ref, bf16[2,312,768]{2,1,0:T(8,128)(2,1)} %copy-done.11, bf16[2,312,1536]{2,1,0:T(8,128)(2,1)} %get-tuple-element.970.s_ref, bf16[176,1536]{1,0:T(8,128)(2,1)} %copy-done.2, ...), custom_call_target="tpu_custom_call" | custom-call | flops 1000 | bytes 1000 | tf_op jit(solution)/shard_map/expert_backward/pallas_call | solution.py:589
  290.5 9.9 %expert_backward.7 = (bf16[2,312,1536]{2,1,0:T(8,128)(2,1)}, bf16[2,312,384]{2,1,0:T(8,128)(2,1)}, f32[2,312,384]{2,1,0:T(8,128)}) custom-call(s32[1]{0:T(128)} %bitcast.18.same_ref.which_ref, bf16[2,312,768]{2,1,0:T(8,128)(2,1)} %copy-done.12, bf16[2,312,1536]{2,1,0:T(8,128)(2,1)} %get-tuple-element.996.s_ref, bf16[176,1536]{1,0:T(8,128)(2,1)} %copy-done.2, ...), custom_call_target="tpu_custom_call" | custom-call | flops 1000 | bytes 1000 | tf_op jit(solution)/shard_map/expert_backward/pallas_call | solution.py:589
  304.9 2.9 sort_groups.2
  310.6 9.6 %outer_send.2 = bf16[1536,384]{1,0:T(8,128)(2,1)} custom-call(s32[1]{0:T(128)} %bitcast.18.same_ref.which_ref, bf16[2,312,1536]{2,1,0:T(8,128)(2,1)} %get-tuple-element.1210.refs_0_, bf16[2,312,1536]{2,1,0:T(8,128)(2,1)} %get-tuple-element.1211.refs_1_, bf16[2,312,1536]{2,1,0:T(8,128)(2,1)} %get-tuple-element.1212.refs_2_, ...), custom_call_target="tpu_custom_call" | custom-call | flops 1000 | bytes 1000 | tf_op jit(solution)/shard_map/outer_send/pallas_call | solution.py:643
  329.8 2.5 collective-permute-start.38
  332.3 8.8 %outer_send.3 = bf16[384,1536]{1,0:T(8,128)(2,1)} custom-call(s32[1]{0:T(128)} %bitcast.18.same_ref.which_ref, bf16[2,312,1536]{2,1,0:T(8,128)(2,1)} %get-tuple-element.1229.refs_0_, bf16[2,312,1536]{2,1,0:T(8,128)(2,1)} %get-tuple-element.1230.refs_1_, bf16[2,312,1536]{2,1,0:T(8,128)(2,1)} %get-tuple-element.1231.refs_2_, ...), custom_call_target="tpu_custom_call" | custom-call | flops 1000 | bytes 1000 | tf_op jit(solution)/shard_map/outer_send/pallas_call | solution.py:643
  344.8 2.9 sort_groups.3
  351.4 15.3 %bring_home.1 = (bf16[5,208,384]{2,1,0:T(8,128)(2,1)}, f32[5,8,208]{2,1,0:T(8,128)}) custom-call(s32[1]{0:T(128)} %bitcast.11.which_ref, s32[5,208,2]{2,1,0:T(8,128)} %get-tuple-element.1109.rows_ref, f32[5,208,768]{2,1,0:T(8,128)} %get-tuple-element.1155.middle_ref.y_ref, bf16[5,208,768]{2,1,0:T(8,128)(2,1)} %get-tuple-element.1163.grad_ref.cot_ref, ...), custom_call_target="tpu_custom_call" | custom-call | flops 1000 | bytes 1000 | tf_op jit(solution)/shard_map/bring_home/pallas_call | solution.py:441
  367.7 7.9 %sum_home.1.near_ref = bf16[5,208,384]{2,1,0:T(8,128)(2,1)} custom-call(s32[5,208,2]{2,1,0:T(8,128)} %get-tuple-element.1109.rows_ref, bf16[4,312,384]{2,1,0:T(8,128)(2,1)} %get-tuple-element.1110.own_ref, bf16[4,312,384]{2,1,0:T(8,128)(2,1)} %copy-done.19), custom_call_target="tpu_custom_call" | custom-call | flops 1000 | bytes 1000 | tf_op jit(solution)/shard_map/sum_home/pallas_call | solution.py:468
  377.6 27.2 %collective-permute-done.42.dgate2_ref = f32[5,8,208]{2,1,0:T(8,128)S(1)} collective-permute-done((f32[5,8,208]{2,1,0:T(8,128)S(1)}, f32[5,8,208]{2,1,0:T(8,128)S(1)}, u32[]{:S(2)}, u32[]{:S(2)}) %collective-permute-start.42) | collective-permute-done | bytes 33312 | tf_op jit(solution)/shard_map/ppermute | solution.py:41
  406.3 19.8 %attend_back.2 = (f32[5,208,768]{2,1,0:T(8,128)}, bf16[5,208,768]{2,1,0:T(8,128)(2,1)}, bf16[5,208,1152]{2,1,0:T(8,128)(2,1)}, bf16[3,208,768]{2,1,0:T(8,128)(2,...) custom-call(s32[1]{0:T(128)} %bitcast.11.which_ref, bf16[5,208,768]{2,1,0:T(8,128)(2,1)} %get-tuple-element.1254.x_ref, ...), custom_call_target="tpu_custom_call" | custom-call | flops 1000 | bytes 1000 | tf_op jit(solution)/shard_map/attend_back/pallas_call | solution.py:758
  426.1 6.6 %collective-permute-done.44.refs_8_ = bf16[192,1536]{1,0:T(8,128)(2,1)S(1)} collective-permute-done((bf16[192,1536]{1,0:T(8,128)(2,1)S(1)}, bf16[192,1536]{1,0:T(8,128)(2,1)S(1)}, u32[]{:S(2)}, u32[]{:S(2)}) %collective-permute-start.44) | collective-permute-done | bytes 589856 | tf_op jit(solution)/shard_map/ppermute | solution.py:41
  432.6 2.8 collective-permute-start.46
  435.4 14.8 %attend_back.3 = (f32[5,208,768]{2,1,0:T(8,128)}, bf16[5,208,768]{2,1,0:T(8,128)(2,1)}, bf16[5,208,1152]{2,1,0:T(8,128)(2,1)}, bf16[2,208,768]{2,1,0:T(8,128)(2,...) custom-call(s32[1]{0:T(128)} %bitcast.11.which_ref, ...), custom_call_target="tpu_custom_call", output_to_operand_aliasing={{0}: (16, {}), {1}: (17, {}), {2}: (18, {})} | custom-call | flops 1000 | bytes 1000 | tf_op jit(solution)/shard_map/attend_back/pallas_call | solution.py:758
  450.3 11.1 %projection_grads.1 = (f32[2,4,48,1664]{3,2,1,0:T(8,128)}, bf16[2,4,48,1664]{3,2,1,0:T(8,128)(2,1)}) custom-call(s32[1]{0:T(128)} %bitcast.19.core_ref, bf16[5,208,768]{2,1,0:T(8,128)(2,1)} %get-tuple-element.1190.refs_0_, bf16[5,208,1152]{2,1,0:T(8,128)(2,1)} %get-tuple-element.1191.refs_1_, bf16[5,208,768]{2,1,0:T(8,128)(2,1)} %get-tuple-element.1192.refs_2_, ...), custom_call_target="tpu_custom_call" | custom-call | flops 1000 | bytes 1000 | tf_op jit(solution)/shard_map/projection_grads/pallas_call | solution.py:962
  461.3 5.1 collective-permute-done.46.refs_9_
  468.7 10.6 %outer_keep.2 = f32[1536,384]{1,0:T(8,128)} custom-call(s32[1]{0:T(128)S(6)} %sub.6.which_ref, bf16[2,312,1536]{2,1,0:T(8,128)(2,1)} %get-tuple-element.1210.refs_0_, bf16[2,312,1536]{2,1,0:T(8,128)(2,1)} %get-tuple-element.1211.refs_1_, bf16[2,312,1536]{2,1,0:T(8,128)(2,1)} %get-tuple-element.1212.refs_2_, ...), custom_call_target="tpu_custom_call" | custom-call | flops 1000 | bytes 1000 | tf_op jit(solution)/shard_map/outer_keep/pallas_call | solution.py:643
  488.0 9.4 %outer_keep.3 = f32[384,1536]{1,0:T(8,128)} custom-call(s32[1]{0:T(128)S(6)} %sub.6.which_ref, bf16[2,312,1536]{2,1,0:T(8,128)(2,1)} %get-tuple-element.1229.refs_0_, bf16[2,312,1536]{2,1,0:T(8,128)(2,1)} %get-tuple-element.1230.refs_1_, bf16[2,312,1536]{2,1,0:T(8,128)(2,1)} %get-tuple-element.1231.refs_2_, ...), custom_call_target="tpu_custom_call" | custom-call | flops 1000 | bytes 1000 | tf_op jit(solution)/shard_map/outer_keep/pallas_call | solution.py:643
  497.3 2.7 collective-permute-done.49
  505.6 5.1 token_back.2.refs_0_
  510.7 3.2 token_back.3
  518.0 5.1 collective-permute-done.52
  (252 shorter events, 124.8 us)
Async XLA Ops:
  20.5 25.9 %collective-permute-start.4 = (bf16[176,1536]{1,0:T(8,128)(2,1)S(1)}, bf16[176,1536]{1,0:T(8,128)(2,1)S(1)}, u32[]{:S(2)}, u32[]{:S(2)}) collective-permute-start(bf16[176,1536]{1,0:T(8,128)(2,1)S(1)} %fusion.4.refs_0_), channel_id=1, source_target_pairs={{0,16},{16,0},{1,17},{17,1},{2,18},{18,2},{3,19},{19,3},{4,20},{20... | collective-permute-start | bytes 1622024 | tf_op jit(solution)/shard_map/ppermute | solution.py:41
  20.5 22.1 %collective-permute-start.1 = (bf16[2,48,1664]{2,1,0:T(8,128)(2,1)}, bf16[2,48,1664]{2,1,0:T(8,128)(2,1)S(1)}, u32[]{:S(2)}, u32[]{:S(2)}) collective-permute-start(bf16[2,48,1664]{2,1,0:T(8,128)(2,1)} %cross.1.refs_0_), channel_id=1, source_target_pairs={{0,4},{2,6},{4,0},{6,2},{8,12},{10,14},{12,8},{14,10},{1,5},{3,7},... | collective-permute-start | bytes 958472 | tf_op jit(solution)/shard_map/ppermute | solution.py:41
  22.1 20.6 %collective-permute-start.2 = (bf16[2,48,1664]{2,1,0:T(8,128)(2,1)}, bf16[2,48,1664]{2,1,0:T(8,128)(2,1)S(1)}, u32[]{:S(2)}, u32[]{:S(2)}) collective-permute-start(bf16[2,48,1664]{2,1,0:T(8,128)(2,1)} %cross.1.refs_0_), channel_id=1, source_target_pairs={{0,8},{2,10},{4,12},{6,14},{8,0},{10,2},{12,4},{14,6},{1,9},{3,11}... | collective-permute-start | bytes 958472 | tf_op jit(solution)/shard_map/ppermute | solution.py:41
  23.6 19.1 %collective-permute-start.3 = (bf16[2,48,1664]{2,1,0:T(8,128)(2,1)}, bf16[2,48,1664]{2,1,0:T(8,128)(2,1)}, u32[]{:S(2)}, u32[]{:S(2)}) collective-permute-start(bf16[2,48,1664]{2,1,0:T(8,128)(2,1)} %cross.1.refs_0_), channel_id=1, source_target_pairs={{0,12},{2,14},{4,8},{6,10},{8,4},{10,6},{12,0},{14,2},{1,13},{3,15... | collective-permute-start | bytes 958472 | tf_op jit(solution)/shard_map/ppermute | solution.py:41
  46.4 15.6 %collective-permute-start.8 = (bf16[1040,768]{1,0:T(8,128)(2,1)}, bf16[1040,768]{1,0:T(8,128)(2,1)}, u32[]{:S(2)}, u32[]{:S(2)}) collective-permute-start(bf16[1040,768]{1,0:T(8,128)(2,1)} %bitcast.52), channel_id=1, source_target_pairs={{0,2},{2,0},{4,6},{6,4},{8,10},{10,8},{12,14},{14,12},{1,3},{3,1},... | collective-permute-start | bytes 4792328 | tf_op jit(solution)/shard_map/ppermute | solution.py:41
  47.0 15.0 %collective-permute-start.6 = (bf16[64,1536]{1,0:T(8,128)(2,1)S(1)}, bf16[64,1536]{1,0:T(8,128)(2,1)S(1)}, u32[]{:S(2)}, u32[]{:S(2)}) collective-permute-start(bf16[64,1536]{1,0:T(8,128)(2,1)S(1)} %fusion.10.refs_1_), channel_id=1, source_target_pairs={{0,16},{16,0},{1,17},{17,1},{2,18},{18,2},{3,19},{19,3},{4,20},{20... | collective-permute-start | bytes 589832 | tf_op jit(solution)/shard_map/ppermute | solution.py:41
  55.5 25.0 %collective-permute-start.9 = (bf16[768,384]{1,0:T(8,128)(2,1)}, bf16[768,384]{1,0:T(8,128)(2,1)S(1)}, u32[]{:S(2)}, u32[]{:S(2)}) collective-permute-start(bf16[768,384]{1,0:T(8,128)(2,1)} %get-tuple-element.1165.here_ref.out_w_ref), channel_id=1, source_target_pairs={{0,1},{1,0},{2,3},{3,2},{4,5},{5,4},{6,7},{7,6},{8,9},{9,8},{10,11... | collective-permute-start | bytes 1769480 | tf_op jit(solution)/shard_map/ppermute | solution.py:41
  71.6 30.0 %collective-permute-start.10 = (bf16[3,208,384]{2,1,0:T(8,128)(2,1)}, bf16[3,208,384]{2,1,0:T(8,128)(2,1)}, u32[]{:S(2)}, u32[]{:S(2)}) collective-permute-start(bf16[3,208,384]{2,1,0:T(8,128)(2,1)} %get-tuple-element.734.own_ref), channel_id=1, source_target_pairs={{0,1},{1,0},{2,3},{3,2},{4,5},{5,4},{6,7},{7,6},{8,9},{9,8},{10,11... | collective-permute-start | bytes 1437704 | tf_op jit(solution)/shard_map/ppermute | solution.py:41
  71.8 23.1 %collective-permute-start.12 = (bf16[144,1536]{1,0:T(8,128)(2,1)S(1)}, bf16[144,1536]{1,0:T(8,128)(2,1)S(1)}, u32[]{:S(2)}, u32[]{:S(2)}) collective-permute-start(bf16[144,1536]{1,0:T(8,128)(2,1)S(1)} %fusion.5.refs_2_), channel_id=1, source_target_pairs={{0,16},{16,0},{1,17},{17,1},{2,18},{18,2},{3,19},{19,3},{4,20},{20... | collective-permute-start | bytes 1327112 | tf_op jit(solution)/shard_map/ppermute | solution.py:41
  79.2 22.4 %collective-permute-start.11 = (bf16[2,208,384]{2,1,0:T(8,128)(2,1)}, bf16[2,208,384]{2,1,0:T(8,128)(2,1)S(1)}, u32[]{:S(2)}, u32[]{:S(2)}) collective-permute-start(bf16[2,208,384]{2,1,0:T(8,128)(2,1)} %get-tuple-element.751.own_ref), channel_id=1, source_target_pairs={{0,1},{1,0},{2,3},{3,2},{4,5},{5,4},{6,7},{7,6},{8,9},{9,8},{10,11... | collective-permute-start | bytes 958472 | tf_op jit(solution)/shard_map/ppermute | solution.py:41
  101.6 19.9 %collective-permute-start.13 = (bf16[1536,128]{1,0:T(8,128)(2,1)S(1)}, bf16[1536,128]{1,0:T(8,128)(2,1)S(1)}, u32[]{:S(2)}, u32[]{:S(2)}) collective-permute-start(bf16[1536,128]{1,0:T(8,128)(2,1)S(1)} %fusion.6.refs_6_), channel_id=1, source_target_pairs={{0,16},{16,0},{1,17},{17,1},{2,18},{18,2},{3,19},{19,3},{4,20},{20... | collective-permute-start | bytes 1179656 | tf_op jit(solution)/shard_map/ppermute | solution.py:41
  108.4 13.1 %collective-permute-start.14 = (bf16[624,768]{1,0:T(8,128)(2,1)}, bf16[624,768]{1,0:T(8,128)(2,1)S(1)}, u32[]{:S(2)}, u32[]{:S(2)}) collective-permute-start(bf16[624,768]{1,0:T(8,128)(2,1)} %bitcast.56), channel_id=1, source_target_pairs={{0,2},{2,0},{4,6},{6,4},{8,10},{10,8},{12,14},{14,12},{1,3},{3,1},... | collective-permute-start | bytes 2875400 | tf_op jit(solution)/shard_map/ppermute | solution.py:41
  131.6 52.0 %collective-permute-start.18 = (bf16[2,312,768]{2,1,0:T(8,128)(2,1)}, bf16[2,312,768]{2,1,0:T(8,128)(2,1)S(1)}, u32[]{:S(2)}, u32[]{:S(2)}) collective-permute-start(bf16[2,312,768]{2,1,0:T(8,128)(2,1)} %get-tuple-element.845), channel_id=1, source_target_pairs={{0,4},{2,6},{4,0},{6,2},{8,12},{10,14},{12,8},{14,10},{1,5},{3,7},... | collective-permute-start | bytes 2875400 | tf_op jit(solution)/shard_map/ppermute | solution.py:41
  133.1 50.6 %collective-permute-start.19 = (bf16[2,312,768]{2,1,0:T(8,128)(2,1)}, bf16[2,312,768]{2,1,0:T(8,128)(2,1)}, u32[]{:S(2)}, u32[]{:S(2)}) collective-permute-start(bf16[2,312,768]{2,1,0:T(8,128)(2,1)} %get-tuple-element.846), channel_id=1, source_target_pairs={{0,8},{2,10},{4,12},{6,14},{8,0},{10,2},{12,4},{14,6},{1,9},{3,11}... | collective-permute-start | bytes 2875400 | tf_op jit(solution)/shard_map/ppermute | solution.py:41
  134.6 49.0 %collective-permute-start.20 = (bf16[2,312,768]{2,1,0:T(8,128)(2,1)}, bf16[2,312,768]{2,1,0:T(8,128)(2,1)}, u32[]{:S(2)}, u32[]{:S(2)}) collective-permute-start(bf16[2,312,768]{2,1,0:T(8,128)(2,1)} %get-tuple-element.847), channel_id=1, source_target_pairs={{0,12},{2,14},{4,8},{6,10},{8,4},{10,6},{12,0},{14,2},{1,13},{3,15... | collective-permute-start | bytes 2875400 | tf_op jit(solution)/shard_map/ppermute | solution.py:41
  135.1 34.2 %collective-permute-start.17 = (bf16[1536,256]{1,0:T(8,128)(2,1)S(1)}, bf16[1536,256]{1,0:T(8,128)(2,1)S(1)}, u32[]{:S(2)}, u32[]{:S(2)}) collective-permute-start(bf16[1536,256]{1,0:T(8,128)(2,1)S(1)} %fusion.1.refs_7_), channel_id=1, source_target_pairs={{0,16},{16,0},{1,17},{17,1},{2,18},{18,2},{3,19},{19,3},{4,20},{20... | collective-permute-start | bytes 2359304 | tf_op jit(solution)/shard_map/ppermute | solution.py:41
  183.7 34.6 %collective-permute-start.22 = (bf16[2,312,768]{2,1,0:T(8,128)(2,1)}, bf16[2,312,768]{2,1,0:T(8,128)(2,1)S(1)}, u32[]{:S(2)}, u32[]{:S(2)}) collective-permute-start(bf16[2,312,768]{2,1,0:T(8,128)(2,1)} %get-tuple-element.890), channel_id=1, source_target_pairs={{0,4},{2,6},{4,0},{6,2},{8,12},{10,14},{12,8},{14,10},{1,5},{3,7},... | collective-permute-start | bytes 2875400 | tf_op jit(solution)/shard_map/ppermute | solution.py:41
  185.3 43.7 %collective-permute-start.23 = (bf16[2,312,768]{2,1,0:T(8,128)(2,1)}, bf16[2,312,768]{2,1,0:T(8,128)(2,1)S(1)}, u32[]{:S(2)}, u32[]{:S(2)}) collective-permute-start(bf16[2,312,768]{2,1,0:T(8,128)(2,1)} %get-tuple-element.892), channel_id=1, source_target_pairs={{0,8},{2,10},{4,12},{6,14},{8,0},{10,2},{12,4},{14,6},{1,9},{3,11}... | collective-permute-start | bytes 2875400 | tf_op jit(solution)/shard_map/ppermute | solution.py:41
  186.8 42.2 %collective-permute-start.24 = (bf16[2,312,768]{2,1,0:T(8,128)(2,1)}, bf16[2,312,768]{2,1,0:T(8,128)(2,1)S(1)}, u32[]{:S(2)}, u32[]{:S(2)}) collective-permute-start(bf16[2,312,768]{2,1,0:T(8,128)(2,1)} %get-tuple-element.894), channel_id=1, source_target_pairs={{0,12},{2,14},{4,8},{6,10},{8,4},{10,6},{12,0},{14,2},{1,13},{3,15... | collective-permute-start | bytes 2875400 | tf_op jit(solution)/shard_map/ppermute | solution.py:41
  187.6 28.6 %collective-permute-start.21 = (bf16[2,312,384]{2,1,0:T(8,128)(2,1)}, bf16[2,312,384]{2,1,0:T(8,128)(2,1)}, u32[]{:S(2)}, u32[]{:S(2)}) collective-permute-start(bf16[2,312,384]{2,1,0:T(8,128)(2,1)} %get-tuple-element.885), channel_id=1, source_target_pairs={{0,1},{1,0},{2,3},{3,2},{4,5},{5,4},{6,7},{7,6},{8,9},{9,8},{10,11... | collective-permute-start | bytes 1437704 | tf_op jit(solution)/shard_map/ppermute | solution.py:41
  200.9 42.1 %collective-permute-start.25 = (bf16[2,312,384]{2,1,0:T(8,128)(2,1)}, bf16[2,312,384]{2,1,0:T(8,128)(2,1)S(1)}, u32[]{:S(2)}, u32[]{:S(2)}) collective-permute-start(bf16[2,312,384]{2,1,0:T(8,128)(2,1)} %get-tuple-element.915), channel_id=1, source_target_pairs={{0,1},{1,0},{2,3},{3,2},{4,5},{5,4},{6,7},{7,6},{8,9},{9,8},{10,11... | collective-permute-start | bytes 1437704 | tf_op jit(solution)/shard_map/ppermute | solution.py:41
  218.3 37.7 %collective-permute-start.26 = (bf16[2,312,384]{2,1,0:T(8,128)(2,1)}, bf16[2,312,384]{2,1,0:T(8,128)(2,1)}, u32[]{:S(2)}, u32[]{:S(2)}) collective-permute-start(bf16[2,312,384]{2,1,0:T(8,128)(2,1)} %get-tuple-element.939), channel_id=1, source_target_pairs={{0,1},{1,0},{2,3},{3,2},{4,5},{5,4},{6,7},{7,6},{8,9},{9,8},{10,11... | collective-permute-start | bytes 1437704 | tf_op jit(solution)/shard_map/ppermute | solution.py:41
  245.8 25.0 %collective-permute-start.27 = (bf16[2,312,384]{2,1,0:T(8,128)(2,1)S(1)}, bf16[2,312,384]{2,1,0:T(8,128)(2,1)S(1)}, u32[]{:S(2)}, u32[]{:S(2)}) collective-permute-start(bf16[2,312,384]{2,1,0:T(8,128)(2,1)S(1)} %copy-done.52), channel_id=1, source_target_pairs={{0,1},{1,0},{2,3},{3,2},{4,5},{5,4},{6,7},{7,6},{8,9},{9,8},{10,11... | collective-permute-start | bytes 1437704 | tf_op jit(solution)/shard_map/ppermute | solution.py:41
  258.1 28.3 %collective-permute-start.28 = (bf16[2,312,384]{2,1,0:T(8,128)(2,1)}, bf16[2,312,384]{2,1,0:T(8,128)(2,1)}, u32[]{:S(2)}, u32[]{:S(2)}) collective-permute-start(bf16[2,312,384]{2,1,0:T(8,128)(2,1)} %get-tuple-element.987), channel_id=1, source_target_pairs={{0,1},{1,0},{2,3},{3,2},{4,5},{5,4},{6,7},{7,6},{8,9},{9,8},{10,11... | collective-permute-start | bytes 1437704 | tf_op jit(solution)/shard_map/ppermute | solution.py:41
  260.1 28.4 %collective-permute-start.29 = (bf16[2,312,384]{2,1,0:T(8,128)(2,1)S(1)}, bf16[2,312,384]{2,1,0:T(8,128)(2,1)S(1)}, u32[]{:S(2)}, u32[]{:S(2)}) collective-permute-start(bf16[2,312,384]{2,1,0:T(8,128)(2,1)S(1)} %copy-done.30), channel_id=1, source_target_pairs={{0,4},{2,6},{4,0},{6,2},{8,12},{10,14},{12,8},{14,10},{1,5},{3,7},... | collective-permute-start | bytes 1437704 | tf_op jit(solution)/shard_map/ppermute | solution.py:41
  273.7 26.6 %collective-permute-start.30 = (bf16[2,312,384]{2,1,0:T(8,128)(2,1)}, bf16[2,312,384]{2,1,0:T(8,128)(2,1)S(1)}, u32[]{:S(2)}, u32[]{:S(2)}) collective-permute-start(bf16[2,312,384]{2,1,0:T(8,128)(2,1)} %get-tuple-element.1013), channel_id=1, source_target_pairs={{0,1},{1,0},{2,3},{3,2},{4,5},{5,4},{6,7},{7,6},{8,9},{9,8},{10,11... | collective-permute-start | bytes 1437704 | tf_op jit(solution)/shard_map/ppermute | solution.py:41
  273.8 29.5 %collective-permute-start.31 = (bf16[2,312,384]{2,1,0:T(8,128)(2,1)S(1)}, bf16[2,312,384]{2,1,0:T(8,128)(2,1)S(1)}, u32[]{:S(2)}, u32[]{:S(2)}) collective-permute-start(bf16[2,312,384]{2,1,0:T(8,128)(2,1)S(1)} %copy-done.28), channel_id=1, source_target_pairs={{0,8},{2,10},{4,12},{6,14},{8,0},{10,2},{12,4},{14,6},{1,9},{3,11}... | collective-permute-start | bytes 1437704 | tf_op jit(solution)/shard_map/ppermute | solution.py:41
  285.5 17.9 %collective-permute-start.32 = (bf16[2,312,384]{2,1,0:T(8,128)(2,1)S(1)}, bf16[2,312,384]{2,1,0:T(8,128)(2,1)S(1)}, u32[]{:S(2)}, u32[]{:S(2)}) collective-permute-start(bf16[2,312,384]{2,1,0:T(8,128)(2,1)S(1)} %copy-done.29), channel_id=1, source_target_pairs={{0,12},{2,14},{4,8},{6,10},{8,4},{10,6},{12,0},{14,2},{1,13},{3,15... | collective-permute-start | bytes 1437704 | tf_op jit(solution)/shard_map/ppermute | solution.py:41
  288.5 19.3 %collective-permute-start.33 = (bf16[2,312,384]{2,1,0:T(8,128)(2,1)}, bf16[2,312,384]{2,1,0:T(8,128)(2,1)S(1)}, u32[]{:S(2)}, u32[]{:S(2)}) collective-permute-start(bf16[2,312,384]{2,1,0:T(8,128)(2,1)} %get-tuple-element.1033), channel_id=1, source_target_pairs={{0,1},{1,0},{2,3},{3,2},{4,5},{5,4},{6,7},{7,6},{8,9},{9,8},{10,11... | collective-permute-start | bytes 1437704 | tf_op jit(solution)/shard_map/ppermute | solution.py:41
  303.3 22.9 %collective-permute-start.34 = (bf16[2,312,384]{2,1,0:T(8,128)(2,1)}, bf16[2,312,384]{2,1,0:T(8,128)(2,1)S(1)}, u32[]{:S(2)}, u32[]{:S(2)}) collective-permute-start(bf16[2,312,384]{2,1,0:T(8,128)(2,1)} %get-tuple-element.1054), channel_id=1, source_target_pairs={{0,1},{1,0},{2,3},{3,2},{4,5},{5,4},{6,7},{7,6},{8,9},{9,8},{10,11... | collective-permute-start | bytes 1437704 | tf_op jit(solution)/shard_map/ppermute | solution.py:41
  323.5 17.6 %collective-permute-start.35 = (bf16[2,312,384]{2,1,0:T(8,128)(2,1)S(1)}, bf16[2,312,384]{2,1,0:T(8,128)(2,1)S(1)}, u32[]{:S(2)}, u32[]{:S(2)}) collective-permute-start(bf16[2,312,384]{2,1,0:T(8,128)(2,1)S(1)} %copy-done.32), channel_id=1, source_target_pairs={{0,4},{2,6},{4,0},{6,2},{8,12},{10,14},{12,8},{14,10},{1,5},{3,7},... | collective-permute-start | bytes 1437704 | tf_op jit(solution)/shard_map/ppermute | solution.py:41
  324.4 18.8 %collective-permute-start.36 = (bf16[2,312,384]{2,1,0:T(8,128)(2,1)}, bf16[2,312,384]{2,1,0:T(8,128)(2,1)}, u32[]{:S(2)}, u32[]{:S(2)}) collective-permute-start(bf16[2,312,384]{2,1,0:T(8,128)(2,1)} %add_halves.14), channel_id=1, source_target_pairs={{0,8},{2,10},{4,12},{6,14},{8,0},{10,2},{12,4},{14,6},{1,9},{3,11}... | collective-permute-start | bytes 1437704 | tf_op jit(solution)/shard_map/ppermute | solution.py:41
  329.0 15.8 %collective-permute-start.37 = (bf16[2,312,384]{2,1,0:T(8,128)(2,1)}, bf16[2,312,384]{2,1,0:T(8,128)(2,1)}, u32[]{:S(2)}, u32[]{:S(2)}) collective-permute-start(bf16[2,312,384]{2,1,0:T(8,128)(2,1)} %add_halves.15), channel_id=1, source_target_pairs={{0,12},{2,14},{4,8},{6,10},{8,4},{10,6},{12,0},{14,2},{1,13},{3,15... | collective-permute-start | bytes 1437704 | tf_op jit(solution)/shard_map/ppermute | solution.py:41
  329.8 17.9 %collective-permute-start.38 = (bf16[512,384]{1,0:T(8,128)(2,1)S(1)}, bf16[512,384]{1,0:T(8,128)(2,1)}, u32[]{:S(2)}, u32[]{:S(2)}) collective-permute-start(bf16[512,384]{1,0:T(8,128)(2,1)S(1)} %slice.97), channel_id=1, source_target_pairs={{0,16},{16,0},{1,17},{17,1},{2,18},{18,2},{3,19},{19,3},{4,20},{20... | collective-permute-start | bytes 1179656 | tf_op jit(solution)/shard_map/ppermute | solution.py:41
  332.3 18.1 %collective-permute-start.39 = (bf16[4,312,384]{2,1,0:T(8,128)(2,1)}, bf16[4,312,384]{2,1,0:T(8,128)(2,1)S(1)}, u32[]{:S(2)}, u32[]{:S(2)}) collective-permute-start(bf16[4,312,384]{2,1,0:T(8,128)(2,1)} %get-tuple-element.1093), channel_id=1, source_target_pairs={{0,2},{2,0},{4,6},{6,4},{8,10},{10,8},{12,14},{14,12},{1,3},{3,1},... | collective-permute-start | bytes 2875400 | tf_op jit(solution)/shard_map/ppermute | solution.py:41
  348.8 17.9 %collective-permute-start.40 = (bf16[4,312,384]{2,1,0:T(8,128)(2,1)}, bf16[4,312,384]{2,1,0:T(8,128)(2,1)S(1)}, u32[]{:S(2)}, u32[]{:S(2)}) collective-permute-start(bf16[4,312,384]{2,1,0:T(8,128)(2,1)} %get-tuple-element.1105), channel_id=1, source_target_pairs={{0,2},{2,0},{4,6},{6,4},{8,10},{10,8},{12,14},{14,12},{1,3},{3,1},... | collective-permute-start | bytes 2875400 | tf_op jit(solution)/shard_map/ppermute | solution.py:41
  348.9 55.9 %collective-permute-start.41 = (bf16[1024,384]{1,0:T(8,128)(2,1)}, bf16[1024,384]{1,0:T(8,128)(2,1)S(1)}, u32[]{:S(2)}, u32[]{:S(2)}) collective-permute-start(bf16[1024,384]{1,0:T(8,128)(2,1)} %slice.98), channel_id=1, source_target_pairs={{0,16},{16,0},{1,17},{17,1},{2,18},{18,2},{3,19},{19,3},{4,20},{20... | collective-permute-start | bytes 2359304 | tf_op jit(solution)/shard_map/ppermute | solution.py:41
  375.6 29.3 %collective-permute-start.43 = (bf16[5,208,384]{2,1,0:T(8,128)(2,1)}, bf16[5,208,384]{2,1,0:T(8,128)(2,1)S(1)}, u32[]{:S(2)}, u32[]{:S(2)}) collective-permute-start(bf16[5,208,384]{2,1,0:T(8,128)(2,1)} %sum_home.1.near_ref), channel_id=1, source_target_pairs={{0,1},{1,0},{2,3},{3,2},{4,5},{5,4},{6,7},{7,6},{8,9},{9,8},{10,11... | collective-permute-start | bytes 2396168 | tf_op jit(solution)/shard_map/ppermute | solution.py:41
  375.8 28.9 %collective-permute-start.42 = (f32[5,8,208]{2,1,0:T(8,128)S(1)}, f32[5,8,208]{2,1,0:T(8,128)S(1)}, u32[]{:S(2)}, u32[]{:S(2)}) collective-permute-start(f32[5,8,208]{2,1,0:T(8,128)S(1)} %copy-done.44), channel_id=1, source_target_pairs={{0,1},{1,0},{2,3},{3,2},{4,5},{5,4},{6,7},{7,6},{8,9},{9,8},{10,11... | collective-permute-start | bytes 99848 | tf_op jit(solution)/shard_map/ppermute | solution.py:41
  404.8 27.9 %collective-permute-start.44 = (bf16[192,1536]{1,0:T(8,128)(2,1)S(1)}, bf16[192,1536]{1,0:T(8,128)(2,1)S(1)}, u32[]{:S(2)}, u32[]{:S(2)}) collective-permute-start(bf16[192,1536]{1,0:T(8,128)(2,1)S(1)} %copy-done.26), channel_id=1, source_target_pairs={{0,16},{16,0},{1,17},{17,1},{2,18},{18,2},{3,19},{19,3},{4,20},{20... | collective-permute-start | bytes 1769480 | tf_op jit(solution)/shard_map/ppermute | solution.py:41
  432.6 36.0 %collective-permute-start.45 = (bf16[3,208,768]{2,1,0:T(8,128)(2,1)}, bf16[3,208,768]{2,1,0:T(8,128)(2,1)S(1)}, u32[]{:S(2)}, u32[]{:S(2)}) collective-permute-start(bf16[3,208,768]{2,1,0:T(8,128)(2,1)} %get-tuple-element.1247.own_ref), channel_id=1, source_target_pairs={{0,1},{1,0},{2,3},{3,2},{4,5},{5,4},{6,7},{7,6},{8,9},{9,8},{10,11... | collective-permute-start | bytes 2875400 | tf_op jit(solution)/shard_map/ppermute | solution.py:41
  432.6 33.8 %collective-permute-start.46 = (bf16[192,1536]{1,0:T(8,128)(2,1)S(1)}, bf16[192,1536]{1,0:T(8,128)(2,1)S(1)}, u32[]{:S(2)}, u32[]{:S(2)}) collective-permute-start(bf16[192,1536]{1,0:T(8,128)(2,1)S(1)} %copy-done.25), channel_id=1, source_target_pairs={{0,16},{16,0},{1,17},{17,1},{2,18},{18,2},{3,19},{19,3},{4,20},{20... | collective-permute-start | bytes 1769480 | tf_op jit(solution)/shard_map/ppermute | solution.py:41
  482.3 15.0 %collective-permute-start.50 = (bf16[2,48,1664]{2,1,0:T(8,128)(2,1)}, bf16[2,48,1664]{2,1,0:T(8,128)(2,1)S(1)}, u32[]{:S(2)}, u32[]{:S(2)}) collective-permute-start(bf16[2,48,1664]{2,1,0:T(8,128)(2,1)} %fusion.9), channel_id=1, source_target_pairs={{0,12},{2,14},{4,8},{6,10},{8,4},{10,6},{12,0},{14,2},{1,13},{3,15... | collective-permute-start | bytes 958472 | tf_op jit(solution)/shard_map/ppermute | solution.py:41
  485.1 14.9 %collective-permute-start.49 = (bf16[2,48,1664]{2,1,0:T(8,128)(2,1)}, bf16[2,48,1664]{2,1,0:T(8,128)(2,1)S(1)}, u32[]{:S(2)}, u32[]{:S(2)}) collective-permute-start(bf16[2,48,1664]{2,1,0:T(8,128)(2,1)} %get-tuple-element.1313), channel_id=1, source_target_pairs={{0,8},{2,10},{4,12},{6,14},{8,0},{10,2},{12,4},{14,6},{1,9},{3,11}... | collective-permute-start | bytes 958472 | tf_op jit(solution)/shard_map/ppermute | solution.py:41
  485.4 14.6 %collective-permute-start.48 = (bf16[2,48,1664]{2,1,0:T(8,128)(2,1)}, bf16[2,48,1664]{2,1,0:T(8,128)(2,1)S(1)}, u32[]{:S(2)}, u32[]{:S(2)}) collective-permute-start(bf16[2,48,1664]{2,1,0:T(8,128)(2,1)} %get-tuple-element.1312), channel_id=1, source_target_pairs={{0,4},{2,6},{4,0},{6,2},{8,12},{10,14},{12,8},{14,10},{1,5},{3,7},... | collective-permute-start | bytes 958472 | tf_op jit(solution)/shard_map/ppermute | solution.py:41
  486.7 16.1 %collective-permute-start.51 = (bf16[2,208,768]{2,1,0:T(8,128)(2,1)}, bf16[2,208,768]{2,1,0:T(8,128)(2,1)}, u32[]{:S(2)}, u32[]{:S(2)}) collective-permute-start(bf16[2,208,768]{2,1,0:T(8,128)(2,1)} %get-tuple-element.1255.own_ref), channel_id=1, source_target_pairs={{0,1},{1,0},{2,3},{3,2},{4,5},{5,4},{6,7},{7,6},{8,9},{9,8},{10,11... | collective-permute-start | bytes 1916936 | tf_op jit(solution)/shard_map/ppermute | solution.py:41
  502.8 22.1 %collective-permute-start.53 = (bf16[5,208,384]{2,1,0:T(8,128)(2,1)}, bf16[5,208,384]{2,1,0:T(8,128)(2,1)}, u32[]{:S(2)}, u32[]{:S(2)}) collective-permute-start(bf16[5,208,384]{2,1,0:T(8,128)(2,1)} %get-tuple-element.1263), channel_id=1, source_target_pairs={{0,1},{1,0},{2,3},{3,2},{4,5},{5,4},{6,7},{7,6},{8,9},{9,8},{10,11... | collective-permute-start | bytes 2396168 | tf_op jit(solution)/shard_map/ppermute | solution.py:41
  503.7 19.3 %collective-permute-start.52 = (bf16[48,1664]{1,0:T(8,128)(2,1)}, bf16[48,1664]{1,0:T(8,128)(2,1)S(1)}, u32[]{:S(2)}, u32[]{:S(2)}) collective-permute-start(bf16[48,1664]{1,0:T(8,128)(2,1)} %fusion.11), channel_id=1, source_target_pairs={{0,16},{16,0},{1,17},{17,1},{2,18},{18,2},{3,19},{19,3},{4,20},{20... | collective-permute-start | bytes 479240 | tf_op jit(solution)/shard_map/ppermute | solution.py:41
  (60 other events, 831.3 us)
